TPU v7x, 32 devices: a whole 2x2x4 slice. The times are simulated.
32 devices in a mesh: dp: 8 (over z, x), shard: 4 (over y, core).
Axes of the slice: x: 2, y: 2, z: 4, core: 2. Of those that a mesh axis runs over, the one named last changes fastest.
Arguments:
- tokens: bfloat16 [8192, 2048], P('dp'), may hold values from -6 to 6
- block_ids: int32 [8, 1024], P('dp'), may hold values from 0 to 7, never falling along the last dimension, each value on 1 to 256 neighbouring positions
- cotangent: bfloat16 [8192, 2048], P('dp'), may hold values from -12 to 12
- gain_first: float32 [2048], P('dp'), may hold values from 0.3 to 2.5
- w_query: float32 [2048, 2048], P('dp', 'shard'), may hold values from -0.125 to 0.125
- w_key: float32 [2048, 512], P('dp', 'shard'), may hold values from -0.125 to 0.125
- w_value: float32 [2048, 512], P('dp', 'shard'), may hold values from -0.125 to 0.125
- w_output: float32 [2048, 2048], P('shard', 'dp'), may hold values from -2 to 2
- gain_second: float32 [2048], P('dp'), may hold values from 0.3 to 2.5
- w_gate: float32 [2048, 8192], P('dp', 'shard'), may hold values from -0.125 to 0.125
- w_up: float32 [2048, 8192], P('dp', 'shard'), may hold values from -0.125 to 0.125
- w_down: float32 [8192, 2048], P('shard', 'dp'), may hold values from -0.0625 to 0.0625
- moment_first: float32 [2048], P('dp'), may hold values from -6 to 6
- moment_query: float32 [2048, 2048], P('dp', 'shard'), may hold values from -4 to 4
- moment_key: float32 [2048, 512], P('dp', 'shard'), may hold values from -4 to 4
- moment_value: float32 [2048, 512], P('dp', 'shard'), may hold values from -4 to 4
- moment_output: float32 [2048, 2048], P('shard', 'dp'), may hold values from -4 to 4
- moment_second: float32 [2048], P('dp'), may hold values from -6 to 6
- moment_gate: float32 [2048, 8192], P('dp', 'shard'), may hold values from -4 to 4
- moment_up: float32 [2048, 8192], P('dp', 'shard'), may hold values from -4 to 4
- moment_down: float32 [8192, 2048], P('shard', 'dp'), may hold values from -4 to 4
- step: int32 [], replicated, may hold values from 1000 to 1999
- rate: float32 [], replicated, may hold values from 0.6 to 1.2
Outputs:
- output: bfloat16 [8192, 2048], P('dp')
- input_grad: float32 [8192, 2048], P('dp')
- global_norm: float32 [], replicated
- momentum_first: float32 [2048], P('dp')
- momentum_query: float32 [2048, 2048], P('dp', 'shard')
- momentum_key: float32 [2048, 512], P('dp', 'shard')
- momentum_value: float32 [2048, 512], P('dp', 'shard')
- momentum_output: float32 [2048, 2048], P('shard', 'dp')
- momentum_second: float32 [2048], P('dp')
- momentum_gate: float32 [2048, 8192], P('dp', 'shard')
- momentum_up: float32 [2048, 8192], P('dp', 'shard')
- momentum_down: float32 [8192, 2048], P('shard', 'dp')
- updated_first: float32 [2048], P('dp')
- updated_query: float32 [2048, 2048], P('dp', 'shard')
- updated_key: float32 [2048, 512], P('dp', 'shard')
- updated_value: float32 [2048, 512], P('dp', 'shard')
- updated_output: float32 [2048, 2048], P('shard', 'dp')
- updated_second: float32 [2048], P('dp')
- updated_gate: float32 [2048, 8192], P('dp', 'shard')
- updated_up: float32 [2048, 8192], P('dp', 'shard')
- updated_down: float32 [8192, 2048], P('shard', 'dp')
Inputs may be any that keep to these rules, and one draw needn't show every extreme that they name: `block_ids`: along each row the block numbers never fall, every number 0 to 7 appears, and a block holds 1 to 256 positions.
All inputs are finite; a program needn't handle non-finite values.
Results may differ from a plain program's by a relative error of at most 0.02.
Values may be sent and summed in bfloat16 or wider, within the bound.
A program may use at most 256 MiB of HBM per device.

v0:
```python
import math

import jax
import jax.numpy as jnp
from jax import lax
from jax.sharding import PartitionSpec as P

H = 32
KV = 8
HD = 64
CLIP = 4096
WARMUP = 2000


EPS = 1e-05
THETA = 10000000.0
NEGATIVE = -1e30


def inverse_rms(values):
    return lax.rsqrt(jnp.mean(values * values, axis=1, keepdims=True) + EPS)


def norm_back(values, inverse, gain, grad_normed):
    scaled = grad_normed * gain[None, :]
    gain_grad = jnp.sum(grad_normed * values * inverse, axis=0)
    grad_values = inverse * scaled - values * inverse**3 * jnp.mean(
        scaled * values, axis=1, keepdims=True
    )
    return (gain_grad, grad_values)


def angle_table(count, length):
    positions = (jnp.arange(count, dtype=jnp.int32) % length).astype(jnp.float32)
    powers = -2.0 * jnp.arange(HD // 2, dtype=jnp.float32) / HD
    angles = positions[:, None] * jnp.power(THETA, powers)[None, :]
    return (jnp.cos(angles)[:, None, :], jnp.sin(angles)[:, None, :])


def rotate(values, cosine, sine):
    half = values.shape[-1] // 2
    first = values[..., :half]
    second = values[..., half:]
    return jnp.concatenate(
        [first * cosine - second * sine, second * cosine + first * sine], axis=-1
    )


def unrotate(grads, cosine, sine):
    half = grads.shape[-1] // 2
    first = grads[..., :half]
    second = grads[..., half:]
    return jnp.concatenate(
        [first * cosine + second * sine, second * cosine - first * sine], axis=-1
    )


def to_items(values, seqs, length):
    shaped = values.reshape((seqs, length) + values.shape[1:])
    moved = jnp.moveaxis(shaped, 2, 1)
    return moved.reshape((seqs * values.shape[1], length) + values.shape[2:])


def from_items(items, seqs):
    groups = items.shape[0] // seqs
    shaped = items.reshape((seqs, groups) + items.shape[1:])
    moved = jnp.moveaxis(shaped, 1, 2)
    return moved.reshape((seqs * items.shape[1], groups) + items.shape[2:])


def item_scores(query, key, blocks, scale):
    scores = jnp.einsum("qgd,jd->gqj", query, key, preferred_element_type=jnp.float32) * scale
    allowed = blocks[None, :] <= blocks[:, None]
    return jnp.where(allowed[None], scores, NEGATIVE)


def attend_forward(scale):

    def run(parts):
        query, key, value, blocks = parts
        scores = item_scores(query, key, blocks, scale)
        peak = jnp.max(scores, axis=2, keepdims=True)
        weights = jnp.exp(scores - peak)
        total = jnp.sum(weights, axis=2, keepdims=True)
        probs = (weights / total).astype(jnp.bfloat16)
        mixed = jnp.einsum("gqj,jd->qgd", probs, value, preferred_element_type=jnp.float32)
        return (mixed.astype(jnp.bfloat16), peak, total)

    return run


def attend_backward(scale):

    def run(parts):
        query, key, value, blocks, peak, total, grad_mixed = parts
        scores = item_scores(query, key, blocks, scale)
        probs = jnp.exp(scores - peak) / total
        probs_low = probs.astype(jnp.bfloat16)
        grad_value = jnp.einsum(
            "gqj,qgd->jd", probs_low, grad_mixed, preferred_element_type=jnp.float32
        )
        grad_probs = jnp.einsum(
            "qgd,jd->gqj", grad_mixed, value, preferred_element_type=jnp.float32
        )
        grad_scores = (
            probs * (grad_probs - jnp.sum(probs * grad_probs, axis=2, keepdims=True))
        ).astype(jnp.bfloat16)
        grad_query = (
            jnp.einsum("gqj,jd->qgd", grad_scores, key, preferred_element_type=jnp.float32) * scale
        )
        grad_key = (
            jnp.einsum("gqj,qgd->jd", grad_scores, query, preferred_element_type=jnp.float32)
            * scale
        )
        return (grad_query, grad_key, grad_value)

    return run


def on_device(
    tokens,
    block_ids,
    cotangent,
    gain_first,
    w_query,
    w_key,
    w_value,
    w_output,
    gain_second,
    w_gate,
    w_up,
    w_down,
    moment_first,
    moment_query,
    moment_key,
    moment_value,
    moment_output,
    moment_second,
    moment_gate,
    moment_up,
    moment_down,
    step,
    rate,
):
    seqs, length = block_ids.shape
    count = tokens.shape[0]
    scale = 1.0 / math.sqrt(HD)
    group = H // KV
    (
        gain_one,
        query_weight,
        key_weight,
        value_weight,
        output_weight,
        gain_two,
        gate_weight,
        up_weight,
        down_weight,
    ) = (
        lax.all_gather(gain_first.astype(jnp.bfloat16), "dp", axis=0, tiled=True),
        lax.all_gather(w_query.astype(jnp.bfloat16), "dp", axis=0, tiled=True),
        lax.all_gather(w_key.astype(jnp.bfloat16), "dp", axis=0, tiled=True),
        lax.all_gather(w_value.astype(jnp.bfloat16), "dp", axis=0, tiled=True),
        lax.all_gather(w_output.astype(jnp.bfloat16), "dp", axis=1, tiled=True),
        lax.all_gather(gain_second.astype(jnp.bfloat16), "dp", axis=0, tiled=True),
        lax.all_gather(w_gate.astype(jnp.bfloat16), "dp", axis=0, tiled=True),
        lax.all_gather(w_up.astype(jnp.bfloat16), "dp", axis=0, tiled=True),
        lax.all_gather(w_down.astype(jnp.bfloat16), "dp", axis=1, tiled=True),
    )
    heads_local = query_weight.shape[1] // HD
    kv_local = key_weight.shape[1] // HD
    inputs = tokens.astype(jnp.float32)
    inverse_first = inverse_rms(inputs)
    gain_one_wide = gain_one.astype(jnp.float32)
    normed = (inputs * inverse_first * gain_one_wide[None, :]).astype(jnp.bfloat16)
    cosine, sine = angle_table(count, length)
    query = rotate(
        jnp.dot(normed, query_weight, preferred_element_type=jnp.float32).reshape(
            count, heads_local, HD
        ),
        cosine,
        sine,
    ).astype(jnp.bfloat16)
    key = rotate(
        jnp.dot(normed, key_weight, preferred_element_type=jnp.float32).reshape(
            count, kv_local, HD
        ),
        cosine,
        sine,
    ).astype(jnp.bfloat16)
    value = (
        jnp.dot(normed, value_weight, preferred_element_type=jnp.float32)
        .astype(jnp.bfloat16)
        .reshape(count, kv_local, HD)
    )
    query_items = to_items(query.reshape(count, kv_local, group, HD), seqs, length)
    key_items = to_items(key, seqs, length)
    value_items = to_items(value, seqs, length)
    block_items = jnp.repeat(block_ids, kv_local, axis=0)
    mixed_items, peak, total = lax.map(
        attend_forward(scale), (query_items, key_items, value_items, block_items)
    )
    mixed = from_items(mixed_items, seqs).reshape(count, heads_local * HD)
    hidden = inputs + lax.psum(
        jnp.dot(mixed, output_weight, preferred_element_type=jnp.float32).astype(jnp.bfloat16),
        "shard",
    ).astype(jnp.float32)
    inverse_second = inverse_rms(hidden)
    gain_two_wide = gain_two.astype(jnp.float32)
    normed_two = (hidden * inverse_second * gain_two_wide[None, :]).astype(jnp.bfloat16)
    gate = jnp.dot(normed_two, gate_weight, preferred_element_type=jnp.float32)
    up = jnp.dot(normed_two, up_weight, preferred_element_type=jnp.float32)
    sigmoid_gate = jax.nn.sigmoid(gate)
    activated = (gate * sigmoid_gate * up).astype(jnp.bfloat16)
    result = hidden + lax.psum(
        jnp.dot(activated, down_weight, preferred_element_type=jnp.float32).astype(jnp.bfloat16),
        "shard",
    ).astype(jnp.float32)
    output = result.astype(jnp.bfloat16)
    grad_result = cotangent.astype(jnp.float32)
    grad_down_weight = jnp.einsum(
        "tf,td->fd", activated, cotangent, preferred_element_type=jnp.float32
    )
    grad_act = jnp.einsum("td,fd->tf", cotangent, down_weight, preferred_element_type=jnp.float32)
    grad_gate_in = (grad_act * up * sigmoid_gate * (1.0 + gate * (1.0 - sigmoid_gate))).astype(
        jnp.bfloat16
    )
    grad_up_in = (grad_act * gate * sigmoid_gate).astype(jnp.bfloat16)
    grad_gate_weight = jnp.einsum(
        "tc,tf->cf", normed_two, grad_gate_in, preferred_element_type=jnp.float32
    )
    grad_up_weight = jnp.einsum(
        "tc,tf->cf", normed_two, grad_up_in, preferred_element_type=jnp.float32
    )
    partial_two = jnp.einsum(
        "tf,cf->tc", grad_gate_in, gate_weight, preferred_element_type=jnp.float32
    ) + jnp.einsum("tf,cf->tc", grad_up_in, up_weight, preferred_element_type=jnp.float32)
    grad_normed_two = lax.psum(partial_two.astype(jnp.bfloat16), "shard").astype(jnp.float32)
    gain_grad_two, grad_through = norm_back(hidden, inverse_second, gain_two_wide, grad_normed_two)
    grad_hidden = grad_result + grad_through
    grad_hidden_low = grad_hidden.astype(jnp.bfloat16)
    grad_output_weight = jnp.einsum(
        "tk,td->kd", mixed, grad_hidden_low, preferred_element_type=jnp.float32
    )
    grad_mixed = jnp.einsum(
        "td,kd->tk", grad_hidden_low, output_weight, preferred_element_type=jnp.float32
    ).astype(jnp.bfloat16)
    grad_mixed_items = to_items(grad_mixed.reshape(count, kv_local, group, HD), seqs, length)
    grad_query_items, grad_key_items, grad_value_items = lax.map(
        attend_backward(scale),
        (query_items, key_items, value_items, block_items, peak, total, grad_mixed_items),
    )
    grad_query_in = (
        unrotate(from_items(grad_query_items, seqs).reshape(count, heads_local, HD), cosine, sine)
        .astype(jnp.bfloat16)
        .reshape(count, heads_local * HD)
    )
    grad_key_in = (
        unrotate(from_items(grad_key_items, seqs), cosine, sine)
        .astype(jnp.bfloat16)
        .reshape(count, kv_local * HD)
    )
    grad_value_in = (
        from_items(grad_value_items, seqs).astype(jnp.bfloat16).reshape(count, kv_local * HD)
    )
    grad_query_weight = jnp.einsum(
        "tc,tk->ck", normed, grad_query_in, preferred_element_type=jnp.float32
    )
    grad_key_weight = jnp.einsum(
        "tc,tk->ck", normed, grad_key_in, preferred_element_type=jnp.float32
    )
    grad_value_weight = jnp.einsum(
        "tc,tk->ck", normed, grad_value_in, preferred_element_type=jnp.float32
    )
    partial_one = jnp.einsum(
        "tk,ck->tc", grad_query_in, query_weight, preferred_element_type=jnp.float32
    )
    partial_one = partial_one + jnp.einsum(
        "tk,ck->tc", grad_key_in, key_weight, preferred_element_type=jnp.float32
    )
    partial_one = partial_one + jnp.einsum(
        "tk,ck->tc", grad_value_in, value_weight, preferred_element_type=jnp.float32
    )
    grad_normed = lax.psum(partial_one.astype(jnp.bfloat16), "shard").astype(jnp.float32)
    gain_grad_one, grad_inner = norm_back(inputs, inverse_first, gain_one_wide, grad_normed)
    input_grad = grad_hidden + grad_inner
    owned = (
        lax.psum_scatter(
            gain_grad_one.astype(jnp.bfloat16), "dp", scatter_dimension=0, tiled=True
        ).astype(jnp.float32),
        lax.psum_scatter(
            grad_query_weight.astype(jnp.bfloat16), "dp", scatter_dimension=0, tiled=True
        ).astype(jnp.float32),
        lax.psum_scatter(
            grad_key_weight.astype(jnp.bfloat16), "dp", scatter_dimension=0, tiled=True
        ).astype(jnp.float32),
        lax.psum_scatter(
            grad_value_weight.astype(jnp.bfloat16), "dp", scatter_dimension=0, tiled=True
        ).astype(jnp.float32),
        lax.psum_scatter(
            grad_output_weight.astype(jnp.bfloat16), "dp", scatter_dimension=1, tiled=True
        ).astype(jnp.float32),
        lax.psum_scatter(
            gain_grad_two.astype(jnp.bfloat16), "dp", scatter_dimension=0, tiled=True
        ).astype(jnp.float32),
        lax.psum_scatter(
            grad_gate_weight.astype(jnp.bfloat16), "dp", scatter_dimension=0, tiled=True
        ).astype(jnp.float32),
        lax.psum_scatter(
            grad_up_weight.astype(jnp.bfloat16), "dp", scatter_dimension=0, tiled=True
        ).astype(jnp.float32),
        lax.psum_scatter(
            grad_down_weight.astype(jnp.bfloat16), "dp", scatter_dimension=1, tiled=True
        ).astype(jnp.float32),
    )
    first_shard = (lax.axis_index("shard") == 0).astype(jnp.float32)
    squares = first_shard * (jnp.sum(owned[0] * owned[0]) + jnp.sum(owned[5] * owned[5]))
    for position in (1, 2, 3, 4, 6, 7, 8):
        squares = squares + jnp.sum(owned[position] * owned[position])
    global_norm = jnp.sqrt(lax.psum(squares, ("dp", "shard")))
    factor = jnp.minimum(1.0, CLIP / global_norm)
    rate_now = rate * jnp.minimum(1.0, (step.astype(jnp.float32) + 1.0) / WARMUP)
    masters = (gain_first, w_query, w_key, w_value, w_output, gain_second, w_gate, w_up, w_down)
    moments = (
        moment_first,
        moment_query,
        moment_key,
        moment_value,
        moment_output,
        moment_second,
        moment_gate,
        moment_up,
        moment_down,
    )
    momenta = [0.5 * moment + 0.5 * (factor * gradient) for moment, gradient in zip(moments, owned)]
    updated = [master - rate_now * momentum for master, momentum in zip(masters, momenta)]
    return (
        output,
        input_grad,
        global_norm,
        momenta[0],
        momenta[1],
        momenta[2],
        momenta[3],
        momenta[4],
        momenta[5],
        momenta[6],
        momenta[7],
        momenta[8],
        updated[0],
        updated[1],
        updated[2],
        updated[3],
        updated[4],
        updated[5],
        updated[6],
        updated[7],
        updated[8],
    )


def solution(mesh):
    in_specs = (
        P("dp", None),
        P("dp", None),
        P("dp", None),
        P("dp"),
        P("dp", "shard"),
        P("dp", "shard"),
        P("dp", "shard"),
        P("shard", "dp"),
        P("dp"),
        P("dp", "shard"),
        P("dp", "shard"),
        P("shard", "dp"),
        P("dp"),
        P("dp", "shard"),
        P("dp", "shard"),
        P("dp", "shard"),
        P("shard", "dp"),
        P("dp"),
        P("dp", "shard"),
        P("dp", "shard"),
        P("shard", "dp"),
        P(),
        P(),
    )
    out_specs = (
        P("dp", None),
        P("dp", None),
        P(),
        P("dp"),
        P("dp", "shard"),
        P("dp", "shard"),
        P("dp", "shard"),
        P("shard", "dp"),
        P("dp"),
        P("dp", "shard"),
        P("dp", "shard"),
        P("shard", "dp"),
        P("dp"),
        P("dp", "shard"),
        P("dp", "shard"),
        P("dp", "shard"),
        P("shard", "dp"),
        P("dp"),
        P("dp", "shard"),
        P("dp", "shard"),
        P("shard", "dp"),
    )
    return jax.shard_map(
        on_device, mesh=mesh, in_specs=in_specs, out_specs=out_specs, check_vma=False
    )
```

profile of v0, /device:TPU:0, one launch (start us, length us, event | category | flops | bytes accessed | tf_op | source)
XLA Modules:
  0.0 1819.1 jit_solution(10321602777745166804)
XLA Ops:
  11.8 22.4 %all-gather = bf16[8,1,256]{2,1,0:T(2,128)(2,1)S(1)} all-gather(bf16[1,1,256]{2,1,0:T(2,128)(2,1)S(1)} %reshape.331), channel_id=1, replica_groups=mesh['dp'=8,'shard'=4] {'dp'}, dimensions={0}, use_global_device_ids=true | all-gather | bytes 4608 | tf_op jit(solution)/shard_map/all_gather | solution.py:160
  38.9 32.9 %all_gather.28 = bf16[2048,128]{1,0:T(8,128)(2,1)S(1)} all-gather(bf16[256,128]{1,0:T(8,128)(2,1)S(1)} %convert_element_type.243), channel_id=1, replica_groups=mesh['dp'=8,'shard'=4] {'dp'}, dimensions={0}, use_global_device_ids=true | all-gather | bytes 589824 | tf_op jit(solution)/shard_map/all_gather | solution.py:163
  72.8 31.7 %all_gather.29 = bf16[2048,128]{1,0:T(8,128)(2,1)S(1)} all-gather(bf16[256,128]{1,0:T(8,128)(2,1)S(1)} %convert_element_type.245), channel_id=1, replica_groups=mesh['dp'=8,'shard'=4] {'dp'}, dimensions={0}, use_global_device_ids=true | all-gather | bytes 589824 | tf_op jit(solution)/shard_map/all_gather | solution.py:162
  110.5 5.3 fusion.111
  116.8 30.4 %while.28 = (s32[]{:T(128)}, bf16[2,1024,4,64]{1,3,2,0:T(8,128)(2,1)}, f32[2,4,1024,1]{2,1,3,0:T(4,128)}, f32[2,4,1024,1]{2,1,3,0:T(4,128)}, bf16[2,1024,64]{1,2...) while((s32[]{:T(128)}, ...), condition=%wide.region_4.5_spmd, body=%wide.region_1.4_spmd.sunk | while | flops 1125376000 | bytes 64387236 | solution.py:200
  126.0 5.1 fusion.180
  141.1 5.1 fusion.180
  147.2 6.7 convolution_convert_fusion.4
  160.8 16.6 all-gather.1
  177.3 59.9 %all-reduce.8.cloned.1.call-done = bf16[1024,2048]{1,0:T(8,128)(2,1)} async-done(((bf16[1024,2048]{1,0:T(8,128)(2,1)}), bf16[1024,2048]{1,0:T(8,128)(2,1)}) %all-reduce.8.cloned.1.call-update) | async-done | bytes 4194320 | tf_op jit(solution)/shard_map/psum | solution.py:204
  237.2 5.0 multiply_reduce_fusion
  243.2 4.6 multiply_convert_fusion.3
  247.8 117.3 %all-gather.12.cloned.1.call-done = bf16[2048,2048]{1,0:T(8,128)(2,1)} async-done(((bf16[256,2048]{1,0:T(8,128)(2,1)}), bf16[2048,2048]{1,0:T(8,128)(2,1)}) %all-gather.12.cloned.1.call-update) | async-done | bytes 8388624 | tf_op jit(solution)/shard_map/all_gather | solution.py:166
  365.1 14.5 fusion.112
  379.6 111.4 %all-gather.14.cloned.1.call-done = bf16[2048,2048]{1,0:T(8,128)(2,1)} async-done(((bf16[256,2048]{1,0:T(8,128)(2,1)}), bf16[2048,2048]{1,0:T(8,128)(2,1)}) %all-gather.14.cloned.1.call-update) | async-done | bytes 8388624 | tf_op jit(solution)/shard_map/all_gather | solution.py:167
  491.0 14.5 fusion.113
  505.5 111.8 %all-gather.16.cloned.1.call-done = bf16[2048,2048]{1,0:T(8,128)(2,1)} async-done(((bf16[2048,256]{1,0:T(8,128)(2,1)}), bf16[2048,2048]{1,0:T(8,128)(2,1)}) %all-gather.16.cloned.1.call-update) | async-done | bytes 8388624 | tf_op jit(solution)/shard_map/all_gather | solution.py:168
  617.3 22.1 %multiply_convert_fusion = (bf16[1024,2048]{1,0:T(8,128)(2,1)}, bf16[1024,2048]{1,0:T(8,128)(2,1)}, bf16[1024,2048]{1,0:T(8,128)(2,1)}) fusion(f32[1024,2048]{1,0:T(8,128)} %fusion.112, f32[1024,2048]{1,0:T(8,128)} %fusion.113, bf16[1024,2048]{1,0:T(8,128)(2,1)} %param.29, bf16[2048,2048]{1,0:T(8,128)(2,1)} %all-gather.16.cloned.1.call-done), kind=kOutput, calls=%fused_computation.96 | convolution fusion | flops 8623489024 | bytes 41943040 | tf_op jit(solution)/shard_map/td,fd->tf/dot_general | solution.py:224
  639.4 14.7 fusion.114
  654.1 12.2 add_convert_fusion.1
  666.4 83.8 %all-reduce.10.cloned.1.call-done = bf16[1024,2048]{1,0:T(8,128)(2,1)} async-done(((bf16[1024,2048]{1,0:T(8,128)(2,1)}), bf16[1024,2048]{1,0:T(8,128)(2,1)}) %all-reduce.10.cloned.1.call-update) | async-done | bytes 4194320 | tf_op jit(solution)/shard_map/psum | solution.py:238
  750.1 8.8 fusion.65
  758.9 5.2 fusion.62
  767.5 79.0 %while.29 = (s32[]{:T(128)}, f32[2,1024,4,64]{1,3,2,0:T(8,128)}, f32[2,1024,64]{1,2,0:T(8,128)}, bf16[2,1024,64]{1,2,0:T(8,128)(2,1)}, bf16[2,1024,64]{1,2,0:T(8...) while((s32[]{:T(128)}, f32[2,1024,4,64]{1,3,2,0:T(8,128)}, ...), condition=%wide.region_12.13_spmd, body=%wide.region_10.12_spmd.sunk | while | flops 2727669760 | bytes 159401328 | solution.py:249
  767.5 8.1 fusion.189
  778.4 11.7 fusion.190
  790.1 8.0 fusion.191
  807.0 8.1 fusion.189
  817.8 11.7 fusion.190
  829.5 8.0 fusion.191
  852.1 13.9 convolution_convert_fusion.3
  877.6 6.0 convolution_convert_fusion.6
  883.6 7.0 convolution_convert_fusion.5
  890.8 14.0 convolution_convert_fusion.2
  905.3 14.1 convolution_convert_fusion.1
  919.4 14.1 convolution_convert_fusion
  937.6 41.8 %reduce-scatter.12.cloned.1.call-done = bf16[256,128]{1,0:T(8,128)(2,1)} async-done(((bf16[2048,128]{1,0:T(8,128)(2,1)}), bf16[256,128]{1,0:T(8,128)(2,1)}) %reduce-scatter.12.cloned.1.call-update) | async-done | bytes 65552 | tf_op jit(solution)/shard_map/reduce_scatter | solution.py:297
  980.9 153.2 %all-reduce.12.cloned.1.call-done = (bf16[1024,2048]{1,0:T(8,128)(2,1)}, bf16[1024,2048]{1,0:T(8,128)(2,1)}) async-done(((bf16[1024,2048]{1,0:T(8,128)(2,1)}, bf16[1024,2048]{1,0:T(8,128)(2,1)}), (bf16[1024,2048]{1,0:T(8,128)(2,1)}, bf16[1024,2048]{1,0:T(8,128)(2,1)})) %all-reduce.12.cloned.1.call-update) | async-done | bytes 8388624 | tf_op jit(solution)/shard_map/psum | solution.py:215
  1134.1 5.6 fusion.72
  1139.8 22.3 %all-reduce.2 = (bf16[2048]{0:T(1024)(128)(2,1)S(1)}, bf16[2048]{0:T(1024)(128)(2,1)S(1)}) all-reduce(bf16[2048]{0:T(1024)(128)(2,1)S(1)} %get-tuple-element.132, bf16[2048]{0:T(1024)(128)(2,1)S(1)} %copy-done.43), channel_id=2, replica_groups=mesh['dp'=8,'shard'=4] {'dp'}, use_global_device_ids=true, to_apply=%region_16.17.clone | all-reduce | flops 4096 | bytes 16384
  1164.1 41.8 %reduce-scatter.8.cloned.1.call-done = bf16[256,512]{1,0:T(8,128)(2,1)} async-done(((bf16[2048,512]{1,0:T(8,128)(2,1)}), bf16[256,512]{1,0:T(8,128)(2,1)}) %reduce-scatter.8.cloned.1.call-update) | async-done | bytes 262160 | tf_op jit(solution)/shard_map/reduce_scatter | solution.py:291
  1209.5 67.7 %reduce-scatter.14.cloned.1.call-done = bf16[512,256]{1,0:T(8,128)(2,1)} async-done(((bf16[512,2048]{1,0:T(8,128)(2,1)}), bf16[512,256]{1,0:T(8,128)(2,1)}) %reduce-scatter.14.cloned.1.call-update) | async-done | bytes 262160 | tf_op jit(solution)/shard_map/reduce_scatter | solution.py:300
  1280.1 148.8 %reduce-scatter.16.cloned.1.call-done = bf16[256,2048]{1,0:T(8,128)(2,1)} async-done(((bf16[2048,2048]{1,0:T(8,128)(2,1)}), bf16[256,2048]{1,0:T(8,128)(2,1)}) %reduce-scatter.16.cloned.1.call-update) | async-done | bytes 1048592 | tf_op jit(solution)/shard_map/reduce_scatter | solution.py:306
  1431.9 148.9 %reduce-scatter.18.cloned.1.call-done = bf16[256,2048]{1,0:T(8,128)(2,1)} async-done(((bf16[2048,2048]{1,0:T(8,128)(2,1)}), bf16[256,2048]{1,0:T(8,128)(2,1)}) %reduce-scatter.18.cloned.1.call-update) | async-done | bytes 1048592 | tf_op jit(solution)/shard_map/reduce_scatter | solution.py:309
  1583.9 148.9 %reduce-scatter.20.cloned.1.call-done = bf16[2048,256]{1,0:T(8,128)(2,1)} async-done(((bf16[2048,2048]{1,0:T(8,128)(2,1)}), bf16[2048,256]{1,0:T(8,128)(2,1)}) %reduce-scatter.20.cloned.1.call-update) | async-done | bytes 1048592 | tf_op jit(solution)/shard_map/reduce_scatter | solution.py:312
  1735.9 14.7 fusion.60
  1750.7 39.0 %psum.39 = f32[]{:T(128)} all-reduce(f32[]{:T(128)S(6)} %add.221), channel_id=1, replica_groups=mesh['dp'=8,'shard'=4] {'dp','shard'}, use_global_device_ids=true, to_apply=%region_35.36 | all-reduce | flops 1 | bytes 8 | tf_op jit(solution)/shard_map/psum | solution.py:320
  1801.5 4.4 multiply_subtract_fusion.2
  (245 shorter events, 120.0 us)
Async XLA Ops:
  7.2 103.3 %all-gather.8.cloned.1.call-start = ((), (), s32[]{:S(2)}) async-start(), calls=%async_computation.7 | async-start | bytes 2359296 | tf_op jit(solution)/shard_map/all_gather | solution.py:161
  9.0 138.2 %all-gather.10.cloned.1.call-start = ((), (), s32[]{:S(2)}) async-start(), calls=%async_computation.8 | async-start | bytes 2359296 | tf_op jit(solution)/shard_map/all_gather | solution.py:164
  10.9 226.4 %all-reduce.8.cloned.1.call-start = ((), (), s32[]{:S(2)}) async-start(), calls=%async_computation.9 | async-start | bytes 8388608 | tf_op jit(solution)/shard_map/psum | solution.py:204
  11.0 93.5 %copy-start = (bf16[1024,2048]{1,0:T(8,128)(2,1)S(1)}, bf16[1024,2048]{1,0:T(8,128)(2,1)}, u32[]{:S(2)}) copy-start(bf16[1024,2048]{1,0:T(8,128)(2,1)} %param.27) | copy-start | bytes 12582916
  34.3 72.8 %copy-start.38 = (f32[8,1,256]{2,1,0:T(1,128)}, f32[8,1,256]{2,1,0:T(1,128)S(1)}, u32[]{:S(2)}) copy-start(f32[8,1,256]{2,1,0:T(1,128)S(1)} %convert_element_type.295) | copy-start | bytes 24580
  38.0 71.1 %copy-start.40 = (f32[1024]{0:T(1024)}, f32[1024]{0:T(1024)S(1)}, u32[]{:S(2)}) copy-start(f32[1024]{0:T(1024)S(1)} %get-tuple-element.218) | copy-start | bytes 12292
  71.7 37.3 %copy-start.15 = (bf16[2048,128]{1,0:T(8,128)(2,1)}, bf16[2048,128]{1,0:T(8,128)(2,1)S(1)}, u32[]{:S(2)}) copy-start(bf16[2048,128]{1,0:T(8,128)(2,1)S(1)} %all_gather.28) | copy-start | bytes 1572868
  147.2 7.9 copy-start.9
  154.0 211.2 %all-gather.12.cloned.1.call-start = ((), (), s32[]{:S(2)}) async-start(), calls=%async_computation.10 | async-start | bytes 9437184 | tf_op jit(solution)/shard_map/all_gather | solution.py:166
  155.2 335.8 %all-gather.14.cloned.1.call-start = ((), (), s32[]{:S(2)}) async-start(), calls=%async_computation.11 | async-start | bytes 9437184 | tf_op jit(solution)/shard_map/all_gather | solution.py:167
  157.9 459.3 %all-gather.16.cloned.1.call-start = ((), (), s32[]{:S(2)}) async-start(), calls=%async_computation.12 | async-start | bytes 9437184 | tf_op jit(solution)/shard_map/all_gather | solution.py:168
  160.7 589.4 %all-reduce.10.cloned.1.call-start = ((), (), s32[]{:S(2)}) async-start(), calls=%async_computation.13 | async-start | bytes 8388608 | tf_op jit(solution)/shard_map/psum | solution.py:238
  639.4 14.7 copy-start.48
  639.4 14.7 copy-start.54
  666.3 269.8 %reduce-scatter.10.cloned.1.call-start = ((), (), s32[]{:S(2)}) async-start(), calls=%async_computation.15 | async-start | bytes 589824 | tf_op jit(solution)/shard_map/reduce_scatter | solution.py:294
  750.1 8.8 copy-start.2
  750.1 8.8 copy-start.4
  750.1 8.8 copy-start.8
  767.5 79.0 %copy-start.23 = (f32[1024,32]{0,1:T(8,128)S(1)}, f32[1024,32]{0,1:T(8,128)}, u32[]{:S(2)}) copy-start(f32[1024,32]{0,1:T(8,128)} %copy-done.22) | copy-start | bytes 393220
  767.5 79.0 %copy-start.25 = (f32[1024,32]{0,1:T(8,128)S(1)}, f32[1024,32]{0,1:T(8,128)}, u32[]{:S(2)}) copy-start(f32[1024,32]{0,1:T(8,128)} %copy-done.24) | copy-start | bytes 393220
  790.1 8.1 copy-start.28
  829.5 8.1 copy-start.28
  852.0 127.5 %reduce-scatter.12.cloned.1.call-start = ((), (), s32[]{:S(2)}) async-start(), calls=%async_computation.16 | async-start | bytes 589824 | tf_op jit(solution)/shard_map/reduce_scatter | solution.py:297
  852.0 14.0 copy-start.30
  852.0 14.4 copy-start.6
  852.1 14.4 copy-start.37
  868.6 265.5 %all-reduce.12.cloned.1.call-start = ((), (), s32[]{:S(2)}) async-start(), calls=%async_computation.21 | async-start | bytes 16777216 | tf_op jit(solution)/shard_map/psum | solution.py:215
  877.3 328.6 %reduce-scatter.8.cloned.1.call-start = ((), (), s32[]{:S(2)}) async-start(), calls=%async_computation.14 | async-start | bytes 2359296 | tf_op jit(solution)/shard_map/reduce_scatter | solution.py:291
  883.6 393.6 %reduce-scatter.14.cloned.1.call-start = ((), (), s32[]{:S(2)}) async-start(), calls=%async_computation.17 | async-start | bytes 2359296 | tf_op jit(solution)/shard_map/reduce_scatter | solution.py:300
  890.7 538.2 %reduce-scatter.16.cloned.1.call-start = ((), (), s32[]{:S(2)}) async-start(), calls=%async_computation.18 | async-start | bytes 9437184 | tf_op jit(solution)/shard_map/reduce_scatter | solution.py:306
  904.8 676.1 %reduce-scatter.18.cloned.1.call-start = ((), (), s32[]{:S(2)}) async-start(), calls=%async_computation.19 | async-start | bytes 9437184 | tf_op jit(solution)/shard_map/reduce_scatter | solution.py:309
  919.4 813.5 %reduce-scatter.20.cloned.1.call-start = ((), (), s32[]{:S(2)}) async-start(), calls=%async_computation.20 | async-start | bytes 9437184 | tf_op jit(solution)/shard_map/reduce_scatter | solution.py:312
  933.5 200.6 %copy-start.39 = (f32[8,1,256]{2,1,0:T(1,128)S(1)}, f32[8,1,256]{2,1,0:T(1,128)}, u32[]{:S(2)}) copy-start(f32[8,1,256]{2,1,0:T(1,128)} %copy-done.38) | copy-start | bytes 24580
  933.5 200.6 %copy-start.41 = (f32[1024]{0:T(1024)S(1)}, f32[1024]{0:T(1024)}, u32[]{:S(2)}) copy-start(f32[1024]{0:T(1024)} %copy-done.40) | copy-start | bytes 12292
  933.5 206.3 %copy-start.43 = (bf16[2048]{0:T(1024)(128)(2,1)S(1)}, bf16[2048]{0:T(1024)(128)(2,1)}, u32[]{:S(2)}) copy-start(bf16[2048]{0:T(1024)(128)(2,1)} %get-tuple-element.130) | copy-start | bytes 12292
  933.5 802.4 %copy-start.42 = (f32[1024]{0:T(1024)S(1)}, f32[1024]{0:T(1024)}, u32[]{:S(2)}) copy-start(f32[1024]{0:T(1024)} %get-tuple-element.217) | copy-start | bytes 12292
  1162.1 573.8 %copy-start.46 = (bf16[2048]{0:T(1024)(128)(2,1)}, bf16[2048]{0:T(1024)(128)(2,1)S(1)}, u32[]{:S(2)}) copy-start(bf16[2048]{0:T(1024)(128)(2,1)S(1)} %get-tuple-element.173) | copy-start | bytes 12292
  1162.1 573.8 %copy-start.47 = (bf16[2048]{0:T(1024)(128)(2,1)}, bf16[2048]{0:T(1024)(128)(2,1)S(1)}, u32[]{:S(2)}) copy-start(bf16[2048]{0:T(1024)(128)(2,1)S(1)} %get-tuple-element.172) | copy-start | bytes 12292
  1735.9 57.5 %copy-start.31 = (bf16[256,512]{1,0:T(8,128)(2,1)S(1)}, bf16[256,512]{1,0:T(8,128)(2,1)}, u32[]{:S(2)}) copy-start(bf16[256,512]{1,0:T(8,128)(2,1)} %reduce-scatter.8.cloned.1.call-done) | copy-start | bytes 786436
  1735.9 59.9 %copy-start.34 = (f32[256,128]{1,0:T(8,128)S(1)}, f32[256,128]{1,0:T(8,128)}, u32[]{:S(2)}) copy-start(f32[256,128]{1,0:T(8,128)} %param.32) | copy-start | bytes 393220
  1735.9 65.5 %copy-start.12 = (f32[256,2048]{1,0:T(8,128)S(1)}, f32[256,2048]{1,0:T(8,128)}, u32[]{:S(2)}) copy-start(f32[256,2048]{1,0:T(8,128)} %param.36) | copy-start | bytes 6291460
  1735.9 65.5 %copy-start.19 = (bf16[256,2048]{1,0:T(8,128)(2,1)S(1)}, bf16[256,2048]{1,0:T(8,128)(2,1)}, u32[]{:S(2)}) copy-start(bf16[256,2048]{1,0:T(8,128)(2,1)} %reduce-scatter.16.cloned.1.call-done) | copy-start | bytes 3145732
  1790.5 15.5 copy-start.13
  1790.5 15.5 copy-start.20
  1790.5 15.4 copy-start.26
  1801.4 7.4 copy-start.14
  1801.5 7.4 copy-start.21
  1801.5 7.3 copy-start.27
  (31 other events, 121.2 us)
Sparse Core Ops, SparseCore 0:
  10.7 58.7 all-gather.7
  72.2 52.4 all-gather.9
  154.1 83.1 all-reduce.7
  240.0 125.0 all-gather.11
  367.9 123.0 all-gather.13
  493.7 123.5 all-gather.15
  666.4 83.6 all-reduce.9
  852.1 62.0 reduce-scatter.9
  918.5 60.9 reduce-scatter.11
  981.9 152.2 all-reduce.11
  1138.2 67.5 reduce-scatter.7
  1209.8 67.3 reduce-scatter.13
  1280.8 148.0 reduce-scatter.15
  1432.8 148.0 reduce-scatter.17
  1584.4 148.4 reduce-scatter.19
where the time goes:
time: 1830 us; the launch traced here: 1820 us
  waiting for transfers between devices  1240 us (68%)
  matrix products  253 us (14%)
  blocking collectives  165 us (9%)
  other arithmetic  126 us (7%)
  between operations  24.5 us (1%)
    psum x1, waiting for transfers between devices, on_device(): lax.psum(jnp.dot(activated, down_weight, preferred_element_type=jnp.float...  153 us
    reduce_scatter x1, waiting for transfers between devices, on_device(): lax.psum_scatter(grad_up_weight.astype(jnp.bfloat16), 'dp', scatter_dimen...  149 us
    reduce_scatter x1, waiting for transfers between devices, on_device(): lax.psum_scatter(grad_down_weight.astype(jnp.bfloat16), 'dp', scatter_dim...  149 us
    reduce_scatter x1, waiting for transfers between devices, on_device(): lax.psum_scatter(grad_gate_weight.astype(jnp.bfloat16), 'dp', scatter_dim...  149 us
    all_gather x1, waiting for transfers between devices, on_device(): lax.all_gather(w_gate.astype(jnp.bfloat16), 'dp', axis=0, tiled=True)  117 us
    all_gather x1, waiting for transfers between devices, on_device(): lax.all_gather(w_down.astype(jnp.bfloat16), 'dp', axis=1, tiled=True)  112 us
    all_gather x1, waiting for transfers between devices, on_device(): lax.all_gather(w_up.astype(jnp.bfloat16), 'dp', axis=0, tiled=True)  111 us
    psum x1, waiting for transfers between devices, on_device(): lax.psum(partial_two.astype(jnp.bfloat16), 'shard').astype(jnp.float32)  83.8 us
  transfers between devices with their start and end apart: 15, of which 12 were waited for; matrix products, arithmetic and copies ran while one was open for 11% of the time, Pallas kernels for 0%

commit v1 on v0

v1 whole, which is shorter than its diff:
```python
import math

import jax
import jax.numpy as jnp
from jax import lax
from jax.sharding import PartitionSpec as P

H = 32
KV = 8
HD = 64
CLIP = 4096
WARMUP = 2000

EPS = 1e-05
THETA = 10000000.0
NEGATIVE = -1e30
CHUNKS = 2

BF = jnp.bfloat16
F32 = jnp.float32


def inverse_rms(values):
    return lax.rsqrt(jnp.mean(values * values, axis=-1, keepdims=True) + EPS)


def norm_back(values, inverse, gain, grad_normed):
    scaled = grad_normed * gain
    gain_grad = jnp.sum(grad_normed * values * inverse, axis=0)
    grad_values = inverse * scaled - values * inverse**3 * jnp.mean(
        scaled * values, axis=-1, keepdims=True
    )
    return (gain_grad, grad_values)


def angle_table(length):
    positions = jnp.arange(length, dtype=jnp.int32).astype(F32)
    powers = -2.0 * jnp.arange(HD // 2, dtype=F32) / HD
    angles = positions[:, None] * jnp.power(THETA, powers)[None, :]
    return (jnp.cos(angles)[None, :, None, :], jnp.sin(angles)[None, :, None, :])


def rotate(values, cosine, sine):
    half = values.shape[-1] // 2
    first = values[..., :half]
    second = values[..., half:]
    return jnp.concatenate(
        [first * cosine - second * sine, second * cosine + first * sine], axis=-1
    )


def unrotate(grads, cosine, sine):
    half = grads.shape[-1] // 2
    first = grads[..., :half]
    second = grads[..., half:]
    return jnp.concatenate(
        [first * cosine + second * sine, second * cosine - first * sine], axis=-1
    )


def item_scores(query, key, blocks, scale):
    scores = jnp.einsum("qgd,jd->gqj", query, key, preferred_element_type=F32) * scale
    allowed = blocks[None, :] <= blocks[:, None]
    return jnp.where(allowed[None], scores, NEGATIVE)


def attend_forward(scale):

    def run(parts):
        query, key, value, blocks = parts
        scores = item_scores(query, key, blocks, scale)
        peak = jnp.max(scores, axis=2, keepdims=True)
        weights = jnp.exp(scores - peak)
        total = jnp.sum(weights, axis=2, keepdims=True)
        probs = (weights / total).astype(BF)
        mixed = jnp.einsum("gqj,jd->qgd", probs, value, preferred_element_type=F32)
        return (mixed.astype(BF), peak, total)

    return run


def attend_backward(scale):

    def run(parts):
        query, key, value, blocks, peak, total, grad_mixed = parts
        scores = item_scores(query, key, blocks, scale)
        probs = jnp.exp(scores - peak) / total
        probs_low = probs.astype(BF)
        grad_value = jnp.einsum("gqj,qgd->jd", probs_low, grad_mixed, preferred_element_type=F32)
        grad_probs = jnp.einsum("qgd,jd->gqj", grad_mixed, value, preferred_element_type=F32)
        grad_scores = (
            probs * (grad_probs - jnp.sum(probs * grad_probs, axis=2, keepdims=True))
        ).astype(BF)
        grad_query = (
            jnp.einsum("gqj,jd->qgd", grad_scores, key, preferred_element_type=F32) * scale
        )
        grad_key = jnp.einsum("gqj,qgd->jd", grad_scores, query, preferred_element_type=F32) * scale
        return (grad_query, grad_key, grad_value)

    return run


def build(dps, shards):
    total = dps * shards
    axes = ("dp", "shard")
    zgroups = [[i for i in range(dps) if i % 2 == p] for p in (0, 1)]

    def swap(values, dx, ds):
        pairs = [
            (i, ((i // shards) ^ dx) * shards + ((i % shards) ^ ds)) for i in range(total)
        ]
        return lax.ppermute(values, axes, pairs)

    def gather(piece):
        return lax.all_gather(piece, "dp", axis=0, tiled=True, axis_index_groups=zgroups)

    def scatter(whole):
        return lax.psum_scatter(
            whole, "dp", scatter_dimension=0, tiled=True, axis_index_groups=zgroups
        )

    def sum_to_owner(partial):
        even = partial[:, 0::2]
        odd = partial[:, 1::2].astype(BF)
        paired = even.astype(F32) + swap(odd, 0, 1).astype(F32)
        low = paired.astype(BF)
        from_y = swap(low[0, 1], 0, 2)
        from_x = swap(low[1, 0], 1, 0)
        from_d = swap(low[1, 1], 1, 2)
        return paired[0, 0] + from_y.astype(F32) + from_x.astype(F32) + from_d.astype(F32)

    def spread(own):
        from_y = swap(own, 0, 2)
        from_x = swap(own, 1, 0)
        from_d = swap(own, 1, 2)
        mine = jnp.stack([own, from_y, from_x, from_d])
        theirs = swap(mine, 0, 1)
        return jnp.stack([mine, theirs], axis=1).reshape((2, shards) + own.shape)

    def on_device(
        tokens,
        block_ids,
        cotangent,
        gain_first,
        w_query,
        w_key,
        w_value,
        w_output,
        gain_second,
        w_gate,
        w_up,
        w_down,
        moment_first,
        moment_query,
        moment_key,
        moment_value,
        moment_output,
        moment_second,
        moment_gate,
        moment_up,
        moment_down,
        step,
        rate,
    ):
        length = block_ids.shape[1]
        width = tokens.shape[1]
        scale = 1.0 / math.sqrt(HD)
        group = H // KV
        dp = lax.axis_index("dp")
        me = lax.axis_index("shard")
        x = lax.rem(dp, 2)
        core = lax.rem(me, 2)
        quarter = length // shards
        rows = w_query.shape[0]

        def half(values, which):
            size = values.shape[1] // 2
            return lax.dynamic_slice_in_dim(values, which * size, size, axis=1)

        def ordered(mine, theirs, axis=0):
            first = jnp.where(x == 0, mine, theirs)
            second = jnp.where(x == 0, theirs, mine)
            return jnp.concatenate([first, second], axis=axis)

        low_q = w_query.astype(BF)
        low_k = w_key.astype(BF)
        low_v = w_value.astype(BF)
        low_o = w_output.astype(BF).T
        low_g = w_gate.astype(BF)
        low_u = w_up.astype(BF)
        low_d = w_down.astype(BF).T

        def attn_half(which):
            return jnp.concatenate([half(low_q, which), half(low_k, which), half(low_v, which)], axis=1)

        cols = low_q.shape[1] // 2 + low_k.shape[1]
        gains = jnp.stack([gain_first, gain_second]).astype(BF)
        gains = jnp.pad(gains, ((0, 14), (0, cols - rows)))
        sent = swap(jnp.concatenate([attn_half(1 - x), gains], axis=0), 1, 0)
        piece = jnp.concatenate(
            [ordered(attn_half(x), sent[:rows]), ordered(gains, sent[rows:])], axis=0
        )
        groups = dps // 2
        packed = gather(piece).reshape(groups, 2 * rows + 32, cols)
        qkv_weight = packed[:, : 2 * rows].reshape(width, cols)
        tails = packed[:, 2 * rows :].reshape(groups, 2, 16, cols)
        gain_one = tails[:, :, 0, :rows].reshape(width).astype(F32)
        gain_two = tails[:, :, 1, :rows].reshape(width).astype(F32)

        out_weight = gather(ordered(half(low_o, x), swap(half(low_o, 1 - x), 1, 0)))
        size = low_g.shape[1] // 2 // CHUNKS

        def ffn_part(which, j):
            return jnp.concatenate(
                [half(low, which)[:, j * size : (j + 1) * size] for low in (low_g, low_u, low_d)],
                axis=1,
            )

        ffn_weights = []
        for j in range(CHUNKS):
            ffn_weights.append(gather(ordered(ffn_part(x, j), swap(ffn_part(1 - x, j), 1, 0))))

        start = core * (length // 2)
        got = swap(lax.dynamic_slice_in_dim(tokens, start, length // 2, axis=0), 1, 0)
        got_other = swap(got, 0, 1)
        other_tokens = jnp.where(
            core == 0,
            jnp.concatenate([got, got_other], axis=0),
            jnp.concatenate([got_other, got], axis=0),
        )
        both = jnp.stack([tokens, other_tokens])
        blocks = jnp.concatenate([block_ids, swap(block_ids, 1, 0)], axis=0)

        def to_relative(values):
            parts = [
                lax.dynamic_slice_in_dim(values, (me ^ ds) * quarter, quarter, axis=1)
                for ds in range(shards)
            ]
            return jnp.stack(parts, axis=1)

        def to_natural(values):
            parts = [
                lax.dynamic_index_in_dim(values, me ^ q, axis=1, keepdims=False)
                for q in range(shards)
            ]
            return jnp.concatenate(parts, axis=1)

        cot_own = to_relative(cotangent[None])[0]
        cot_got = swap(cot_own[0::2], 1, 0)
        cot_core = swap(cot_got, 0, 1)
        cot_other = jnp.stack([cot_got, cot_core], axis=1).reshape(cot_own.shape)
        cot_rel = jnp.stack([cot_own, cot_other]).reshape(2 * length, width)

        inputs = both.astype(F32)
        inverse_first = inverse_rms(inputs)
        normed = (inputs * inverse_first * gain_one).astype(BF).reshape(2 * length, width)
        cosine, sine = angle_table(length)
        lin = jnp.dot(normed, qkv_weight, preferred_element_type=F32)
        lin = lin.reshape(2, length, cols // HD, HD)
        query = rotate(lin[:, :, :group], cosine, sine).astype(BF)
        key = rotate(lin[:, :, group : group + 1], cosine, sine).astype(BF)[:, :, 0]
        value = lin[:, :, group + 1].astype(BF)
        mixed, peak, total_w = lax.map(attend_forward(scale), (query, key, value, blocks))
        mixed_rel = to_relative(mixed.reshape(2, length, group * HD)).reshape(2 * length, group * HD)
        partial = jnp.einsum("tk,dk->td", mixed_rel, out_weight, preferred_element_type=F32)
        summed = sum_to_owner(partial.astype(BF).reshape(2, shards, quarter, width))
        tokens_own = lax.dynamic_slice_in_dim(tokens, me * quarter, quarter, axis=0).astype(F32)
        hidden = tokens_own + summed
        inverse_second = inverse_rms(hidden)
        normed_two_own = (hidden * inverse_second * gain_two).astype(BF)
        normed_two = spread(normed_two_own).reshape(2 * length, width)

        grads_ffn = []
        partial_two = None
        result = None
        for j in range(CHUNKS):
            weight = ffn_weights[j]
            w_gu, w_dt = weight[:, : 2 * size], weight[:, 2 * size :]
            gate_up = jnp.dot(normed_two, w_gu, preferred_element_type=F32)
            gate, up = gate_up[:, :size], gate_up[:, size:]
            grad_act = jnp.dot(cot_rel, w_dt, preferred_element_type=F32)
            sig = jax.nn.sigmoid(gate)
            activated = (gate * sig * up).astype(BF)
            grad_gate_in = (grad_act * up * sig * (1.0 + gate * (1.0 - sig))).astype(BF)
            grad_up_in = (grad_act * gate * sig).astype(BF)
            grad_gu = jnp.concatenate([grad_gate_in, grad_up_in], axis=1)
            part = jnp.einsum("tf,cf->tc", grad_gu, w_gu, preferred_element_type=F32)
            partial_two = part if partial_two is None else partial_two + part
            part = jnp.einsum("tf,cf->tc", activated, w_dt, preferred_element_type=F32)
            result = part if result is None else result + part
            d_gu = jnp.einsum("tc,tf->cf", normed_two, grad_gu, preferred_element_type=F32)
            d_dt = jnp.einsum("tc,tf->cf", cot_rel, activated, preferred_element_type=F32)
            grads_ffn.append(scatter(jnp.concatenate([d_gu.astype(BF), d_dt.astype(BF)], axis=1)))

        shape = (2, shards, quarter, width)
        grad_normed_two = sum_to_owner(partial_two.astype(BF).reshape(shape))
        cot_mine = cot_own[0].astype(F32)
        gain_grad_two, grad_through = norm_back(hidden, inverse_second, gain_two, grad_normed_two)
        grad_hidden = cot_mine + grad_through
        grad_hidden_rel = spread(grad_hidden.astype(BF)).reshape(2 * length, width)

        def to_sequence(own):
            from_y = swap(own, 0, 2)
            mine = jnp.stack([own, from_y])
            theirs = swap(mine, 0, 1)
            rel = jnp.stack([mine, theirs], axis=1).reshape((1, shards) + own.shape)
            return to_natural(rel)[0]

        output_own = (hidden + sum_to_owner(result.astype(BF).reshape(shape))).astype(BF)
        output = to_sequence(output_own)

        d_out = jnp.einsum("td,tk->dk", grad_hidden_rel, mixed_rel, preferred_element_type=F32)
        grad_out = scatter(d_out.astype(BF))
        grad_mixed = jnp.dot(grad_hidden_rel, out_weight, preferred_element_type=F32).astype(BF)
        grad_mixed = to_natural(grad_mixed.reshape(2, shards, quarter, group * HD))
        grad_query, grad_key, grad_value = lax.map(
            attend_backward(scale),
            (
                query,
                key,
                value,
                blocks,
                peak,
                total_w,
                grad_mixed.reshape(2, length, group, HD),
            ),
        )
        grad_qkv = jnp.concatenate(
            [
                unrotate(grad_query, cosine, sine).astype(BF),
                unrotate(grad_key[:, :, None], cosine, sine).astype(BF),
                grad_value[:, :, None].astype(BF),
            ],
            axis=2,
        ).reshape(2, length, cols)
        d_qkv = jnp.einsum(
            "tc,tk->ck", normed, grad_qkv.reshape(2 * length, cols), preferred_element_type=F32
        )
        grad_qkv_w = scatter(d_qkv.astype(BF))
        partial_one = jnp.einsum(
            "tk,ck->tc",
            to_relative(grad_qkv).reshape(2 * length, cols),
            qkv_weight,
            preferred_element_type=F32,
        )
        grad_normed = sum_to_owner(partial_one.astype(BF).reshape(shape))
        inverse_own = inverse_rms(tokens_own)
        gain_grad_one, grad_inner = norm_back(tokens_own, inverse_own, gain_one, grad_normed)
        input_grad = to_sequence((grad_hidden + grad_inner).astype(BF)).astype(F32)

        def owned_halves(piece):
            keep = lax.dynamic_slice_in_dim(piece, x * rows, rows, axis=0)
            send = lax.dynamic_slice_in_dim(piece, (1 - x) * rows, rows, axis=0)
            return keep, swap(send, 1, 0)

        def joined(mine, theirs):
            return ordered(mine, theirs, axis=1).astype(F32)

        mine, theirs = owned_halves(grad_qkv_w)
        qc = group * HD
        own_q = joined(mine[:, :qc], theirs[:, :qc])
        own_k = joined(mine[:, qc : qc + HD], theirs[:, qc : qc + HD])
        own_v = joined(mine[:, qc + HD :], theirs[:, qc + HD :])
        mine, theirs = owned_halves(grad_out)
        own_o = joined(mine, theirs).T
        pairs = [owned_halves(piece) for piece in grads_ffn]
        own_gud = []
        for part in range(3):
            cut = slice(part * size, (part + 1) * size)
            own_gud.append(
                joined(
                    jnp.concatenate([m[:, cut] for m, t in pairs], axis=1),
                    jnp.concatenate([t[:, cut] for m, t in pairs], axis=1),
                )
            )
        own_g, own_u, own_d = own_gud[0], own_gud[1], own_gud[2].T
        gain_grads = lax.psum(jnp.stack([gain_grad_one, gain_grad_two]), axes)
        gain_grads = lax.dynamic_slice_in_dim(gain_grads, dp * rows, rows, axis=1)
        owned = (gain_grads[0], own_q, own_k, own_v, own_o, gain_grads[1], own_g, own_u, own_d)

        first_shard = (me == 0).astype(F32)
        squares = first_shard * (jnp.sum(owned[0] * owned[0]) + jnp.sum(owned[5] * owned[5]))
        for position in (1, 2, 3, 4, 6, 7, 8):
            squares = squares + jnp.sum(owned[position] * owned[position])
        global_norm = jnp.sqrt(lax.psum(squares, axes))
        factor = jnp.minimum(1.0, CLIP / global_norm)
        rate_now = rate * jnp.minimum(1.0, (step.astype(F32) + 1.0) / WARMUP)
        masters = (gain_first, w_query, w_key, w_value, w_output, gain_second, w_gate, w_up, w_down)
        moments = (
            moment_first,
            moment_query,
            moment_key,
            moment_value,
            moment_output,
            moment_second,
            moment_gate,
            moment_up,
            moment_down,
        )
        momenta = [
            0.5 * moment + 0.5 * (factor * gradient) for moment, gradient in zip(moments, owned)
        ]
        updated = [master - rate_now * momentum for master, momentum in zip(masters, momenta)]
        return (output, input_grad, global_norm, *momenta, *updated)

    return on_device


def solution(mesh):
    rows, both, back = P("dp"), P("dp", "shard"), P("shard", "dp")
    tokens = P("dp", None)
    params = (rows, both, both, both, back, rows, both, both, back)
    in_specs = (tokens, tokens, tokens, *params, *params, P(), P())
    out_specs = (tokens, tokens, P(), *params, *params)
    return jax.shard_map(
        build(mesh.shape["dp"], mesh.shape["shard"]),
        mesh=mesh,
        in_specs=in_specs,
        out_specs=out_specs,
        check_vma=False,
    )
```

time: 1830 us -> 1120 us (0.61)
  waiting for transfers between devices: 1240 us -> 430 us
  local copies, waits for them, and re-layouts: 12.7 us -> 101 us
  blocking collectives: 165 us -> 81.5 us
  other arithmetic: 126 us -> 193 us
  starting transfers between devices: 1.24 us -> 41.5 us
    reduce_scatter x7 -> x4, waiting for transfers between devices: 598 us -> 0.97 us  [scatter(): lax.psum_scatter(whole, 'dp', scatter_dimension=0, tiled=True, axis_index...]
    ppermute x0 -> x41, waiting for transfers between devices: none -> 429 us  [swap(): return lax.ppermute(values, axes, pairs)]
    all_gather x5 -> x4, waiting for transfers between devices: 341 us -> 0.04 us  [gather(): lax.all_gather(piece, 'dp', axis=0, tiled=True, axis_index_groups=zgroups)]
    psum x3 -> x0, waiting for transfers between devices: 297 us -> none  [the longest x1 153 us: on_device(): lax.psum(jnp.dot(activated, down_weight, preferred_element_type=jnp.float...]
    all_gather x4 -> x0, blocking collectives: 104 us -> none  [the longest x1 32.9 us: on_device(): lax.all_gather(w_value.astype(jnp.bfloat16), 'dp', axis=0, tiled=True)]
    psum x1 -> x2, blocking collectives: 39 us -> 81.5 us  [the longest x1 41 us: on_device(): global_norm = jnp.sqrt(lax.psum(squares, axes))]
    ppermute x0 -> x41, starting transfers between devices: none -> 41.2 us  [swap(): return lax.ppermute(values, axes, pairs)]
    another operation x7 -> x24, other arithmetic: 1.76 us -> 37.9 us  [the longest x4 17.3 us: spread(): return jnp.stack([mine, theirs], axis=1).reshape((2, shards) + own.shape)]
  transfers between devices with their start and end apart: 15 -> 49, of which waited for: 12 -> 27; matrix products, arithmetic and copies ran while one was open for 11% -> 38% of each run, Pallas kernels for 0% -> 0%
where the time goes in v1:
time: 1120 us; the launch traced here: 1110 us
  waiting for transfers between devices  430 us (38%)
  matrix products  240 us (21%)
  other arithmetic  193 us (17%)
  local copies, waits for them, and re-layouts  101 us (9%)
  blocking collectives  81.5 us (7%)
  starting transfers between devices  41.5 us (4%)
  between operations  24.8 us (2%)
    ppermute x41, waiting for transfers between devices, swap(): return lax.ppermute(values, axes, pairs)  429 us
    ppermute x41, starting transfers between devices, swap(): return lax.ppermute(values, axes, pairs)  41.2 us
    psum x1, blocking collectives, on_device(): global_norm = jnp.sqrt(lax.psum(squares, axes))  41 us
    psum x1, blocking collectives, on_device(): gain_grads = lax.psum(jnp.stack([gain_grad_one, gain_grad_two]), axes)  40.6 us
    unnamed x205, local copies, waits for them, and re-layouts  38.5 us
    dot_general x4, matrix products, item_scores(): jnp.einsum('qgd,jd->gqj', query, key, preferred_element_type=F32) * scale  29.6 us
    dot_general x2, matrix products, on_device(): part = jnp.einsum('tf,cf->tc', grad_gu, w_gu, preferred_element_type=F32)  28.6 us
    dot_general x2, matrix products, on_device(): gate_up = jnp.dot(normed_two, w_gu, preferred_element_type=F32)  27.2 us
  transfers between devices with their start and end apart: 49, of which 27 were waited for; matrix products, arithmetic and copies ran while one was open for 38% of the time, Pallas kernels for 0%

profile of v1, /device:TPU:0, one launch (start us, length us, event | category | flops | bytes accessed | tf_op | source)
XLA Modules:
  0.0 1112.9 jit_solution(13904813660430027450)
XLA Ops:
  40.6 32.5 %collective-permute-done = bf16[512,2048]{1,0:T(8,128)(2,1)} collective-permute-done((bf16[512,2048]{1,0:T(8,128)(2,1)}, bf16[512,2048]{1,0:T(8,128)(2,1)}, u32[]{:S(2)}, u32[]{:S(2)}) %collective-permute-start) | collective-permute-done | bytes 2097184 | tf_op jit(solution)/shard_map/ppermute | solution.py:112
  78.5 14.4 %collective-permute-done.13 = bf16[256,1536]{0,1:T(8,128)(2,1)} collective-permute-done((bf16[256,1536]{0,1:T(8,128)(2,1)}, bf16[256,1536]{0,1:T(8,128)(2,1)}, u32[]{:S(2)}, u32[]{:S(2)}) %collective-permute-start.13) | collective-permute-done | bytes 786464 | tf_op jit(solution)/shard_map/ppermute | solution.py:112
  92.9 15.0 %collective-permute-done.14 = bf16[256,1536]{0,1:T(8,128)(2,1)S(1)} collective-permute-done((bf16[256,1536]{0,1:T(8,128)(2,1)}, bf16[256,1536]{0,1:T(8,128)(2,1)S(1)}, u32[]{:S(2)}, u32[]{:S(2)}) %collective-permute-start.14) | collective-permute-done | bytes 786464 | tf_op jit(solution)/shard_map/ppermute | solution.py:112
  132.3 25.2 %while.28 = (s32[]{:T(128)}, bf16[2,1024,4,64]{1,3,2,0:T(8,128)(2,1)S(1)}, f32[2,4,1024,1]{2,1,3,0:T(4,128)S(1)}, f32[2,4,1024,1]{2,1,3,0:T(4,128)S(1)}, bf16[2,...) while((s32[]{:T(128)}, ...), condition=%wide.region_4.5_spmd, body=%wide.region_1.4_spmd.sunk | while | flops 1125376000 | bytes 55998564 | solution.py:263
  164.8 7.3 collective-permute-done.5
  172.0 7.7 convert_add_fusion.3
  188.1 18.9 %collective-permute-done.6 = bf16[256,2048]{1,0:T(8,128)(2,1)} collective-permute-done((bf16[256,2048]{1,0:T(8,128)(2,1)}, bf16[256,2048]{1,0:T(8,128)(2,1)}, u32[]{:S(2)}, u32[]{:S(2)}) %collective-permute-start.6) | collective-permute-done | bytes 1048608 | tf_op jit(solution)/shard_map/ppermute | solution.py:112
  209.2 21.5 %collective-permute-done.8 = bf16[256,2048]{1,0:T(8,128)(2,1)} collective-permute-done((bf16[256,2048]{1,0:T(8,128)(2,1)}, bf16[256,2048]{1,0:T(8,128)(2,1)}, u32[]{:S(2)}, u32[]{:S(2)}) %collective-permute-start.8) | collective-permute-done | bytes 1048608 | tf_op jit(solution)/shard_map/ppermute | solution.py:112
  242.3 19.0 %collective-permute-done.9 = bf16[256,2048]{1,0:T(8,128)(2,1)S(1)} collective-permute-done((bf16[256,2048]{1,0:T(8,128)(2,1)S(1)}, bf16[256,2048]{1,0:T(8,128)(2,1)S(1)}, u32[]{:S(2)}, u32[]{:S(2)}) %collective-permute-start.9) | collective-permute-done | bytes 1048608 | tf_op jit(solution)/shard_map/ppermute | solution.py:112
  263.5 22.6 %collective-permute-done.11 = bf16[256,2048]{1,0:T(8,128)(2,1)S(1)} collective-permute-done((bf16[256,2048]{1,0:T(8,128)(2,1)S(1)}, bf16[256,2048]{1,0:T(8,128)(2,1)S(1)}, u32[]{:S(2)}, u32[]{:S(2)}) %collective-permute-start.11) | collective-permute-done | bytes 1048608 | tf_op jit(solution)/shard_map/ppermute | solution.py:112
  286.9 41.7 %collective-permute-done.21 = bf16[2,256,2048]{2,1,0:T(8,128)(2,1)S(1)} collective-permute-done((bf16[2,256,2048]{2,1,0:T(8,128)(2,1)S(1)}, bf16[2,256,2048]{2,1,0:T(8,128)(2,1)S(1)}, u32[]{:S(2)}, u32[]{:S(2)}) %collective-permute-start.21) | collective-permute-done | bytes 2097184 | tf_op jit(solution)/shard_map/ppermute | solution.py:112
  339.0 6.4 pad_maximum_fusion.1
  345.3 14.5 %fusion.67 = f32[2048,1024]{0,1:T(8,128)} fusion(bf16[2048,2048]{1,0:T(8,128)(2,1)} %bitcast.475, bf16[2048,1536]{0,1:T(8,128)(2,1)} %all-gather.9.cloned.1.call-done), kind=kOutput, calls=%fused_computation.121 | convolution fusion | flops 8589934592 | bytes 20971520 | tf_op jit(solution)/shard_map/dot_general | solution.py:279
  359.8 12.7 %fusion.63 = f32[2048,1024]{0,1:T(8,128)S(1)} fusion(bf16[2048,2048]{1,0:T(8,128)(2,1)} %bitcast.476, bf16[2048,1536]{0,1:T(8,128)(2,1)} %all-gather.11.cloned.1.call-done), kind=kOutput, calls=%fused_computation.117 | convolution fusion | flops 8589934592 | bytes 20971520 | tf_op jit(solution)/shard_map/dot_general | solution.py:279
  372.5 11.7 %multiply_convert_fusion.3 = (bf16[2048,512]{0,1:T(8,128)(2,1)}, bf16[2048,512]{0,1:T(8,128)(2,1)}, bf16[2048,512]{0,1:T(8,128)(2,1)}) fusion(f32[2048,1024]{0,1:T(8,128)S(1)} %copy-done.90, bf16[2048,2048]{1,0:T(8,128)(2,1)} %bitcast.469, bf16[2048,1536]{0,1:T(8,128)(2,1)S(1)} %copy-done.86), kind=kOutput, calls=%fused_computation.104 | convolution fusion | flops 4311744512 | bytes 25165824 | tf_op jit(solution)/shard_map/dot_general | solution.py:281
  384.2 11.0 multiply_convert_fusion.1
  395.2 11.9 %fusion.65 = f32[2048,2048]{1,0:T(8,128)} fusion(bf16[2048,1536]{0,1:T(8,128)(2,1)S(1)} %copy-done.86, bf16[2048,512]{0,1:T(8,128)(2,1)S(1)} %copy-done.93, bf16[2048,512]{0,1:T(8,128)(2,1)S(1)} %copy-done.91), kind=kOutput, calls=%fused_computation.119 | convolution fusion | flops 8598323200 | bytes 25165824 | tf_op jit(solution)/shard_map/tf,cf->tc/dot_general | solution.py:287
  407.1 16.7 %add_convert_fusion = bf16[2048,2048]{1,0:T(8,128)(2,1)} fusion(f32[2048,2048]{1,0:T(8,128)} %fusion.65, bf16[2048,1536]{0,1:T(8,128)(2,1)} %all-gather.11.cloned.1.call-done, bf16[2048,512]{0,1:T(8,128)(2,1)} %get-tuple-element.256, bf16[2048,512]{0,1:T(8,128)(2,1)} %get-tuple-element.255), kind=kOutput, calls=%fused_computation.73 | convolution fusion | flops 8606711808 | bytes 33554432 | tf_op jit(solution)/shard_map/tf,cf->tc/dot_general | solution.py:287
  428.9 8.1 fusion.103
  437.0 15.1 %add_convert_fusion.1 = bf16[2048,2048]{1,0:T(8,128)(2,1)} fusion(f32[2048,2048]{1,0:T(8,128)} %fusion.103, bf16[2048,512]{0,1:T(8,128)(2,1)} %get-tuple-element.263, bf16[2048,1536]{0,1:T(8,128)(2,1)} %all-gather.11.cloned.1.call-done), kind=kOutput, calls=%fused_computation.74 | convolution fusion | flops 4303355904 | bytes 29360128 | tf_op jit(solution)/shard_map/tf,cf->tc/dot_general | solution.py:289
  452.1 13.9 %convolution_convert_fusion.3 = bf16[2048,1024]{0,1:T(8,128)(2,1)} fusion(bf16[2048,2048]{1,0:T(8,128)(2,1)} %bitcast.477, bf16[2048,512]{0,1:T(8,128)(2,1)} %get-tuple-element.258, bf16[2048,512]{0,1:T(8,128)(2,1)S(1)} %copy-done.92), kind=kOutput, calls=%fused_computation.115 | convolution fusion | flops 8600420352 | bytes 16777216 | tf_op jit(solution)/shard_map/tc,tf->cf/dot_general | solution.py:291
  473.4 5.9 pad_maximum_fusion.4
  479.4 9.4 convert_add_fusion.1
  502.0 15.3 %collective-permute-done.24 = bf16[256,2048]{1,0:T(8,128)(2,1)} collective-permute-done((bf16[256,2048]{1,0:T(8,128)(2,1)}, bf16[256,2048]{1,0:T(8,128)(2,1)}, u32[]{:S(2)}, u32[]{:S(2)}) %collective-permute-start.24) | collective-permute-done | bytes 1048608 | tf_op jit(solution)/shard_map/ppermute | solution.py:112
  519.1 21.7 %collective-permute-done.26 = bf16[256,2048]{1,0:T(8,128)(2,1)} collective-permute-done((bf16[256,2048]{1,0:T(8,128)(2,1)S(1)}, bf16[256,2048]{1,0:T(8,128)(2,1)}, u32[]{:S(2)}, u32[]{:S(2)}) %collective-permute-start.26) | collective-permute-done | bytes 1048608 | tf_op jit(solution)/shard_map/ppermute | solution.py:112
  545.0 15.9 %collective-permute-done.16 = bf16[256,2048]{1,0:T(8,128)(2,1)S(1)} collective-permute-done((bf16[256,2048]{1,0:T(8,128)(2,1)S(1)}, bf16[256,2048]{1,0:T(8,128)(2,1)S(1)}, u32[]{:S(2)}, u32[]{:S(2)}) %collective-permute-start.16) | collective-permute-done | bytes 1048608 | tf_op jit(solution)/shard_map/ppermute | solution.py:112
  562.5 22.1 %collective-permute-done.18 = bf16[256,2048]{1,0:T(8,128)(2,1)S(1)} collective-permute-done((bf16[256,2048]{1,0:T(8,128)(2,1)S(1)}, bf16[256,2048]{1,0:T(8,128)(2,1)S(1)}, u32[]{:S(2)}, u32[]{:S(2)}) %collective-permute-start.18) | collective-permute-done | bytes 1048608 | tf_op jit(solution)/shard_map/ppermute | solution.py:112
  592.1 21.7 %collective-permute-done.27 = bf16[256,2048]{1,0:T(8,128)(2,1)S(1)} collective-permute-done((bf16[256,2048]{1,0:T(8,128)(2,1)S(1)}, bf16[256,2048]{1,0:T(8,128)(2,1)S(1)}, u32[]{:S(2)}, u32[]{:S(2)}) %collective-permute-start.27) | collective-permute-done | bytes 1048608 | tf_op jit(solution)/shard_map/ppermute | solution.py:112
  615.4 21.1 %collective-permute-done.29 = bf16[256,2048]{1,0:T(8,128)(2,1)S(1)} collective-permute-done((bf16[256,2048]{1,0:T(8,128)(2,1)S(1)}, bf16[256,2048]{1,0:T(8,128)(2,1)S(1)}, u32[]{:S(2)}, u32[]{:S(2)}) %collective-permute-start.29) | collective-permute-done | bytes 1048608 | tf_op jit(solution)/shard_map/ppermute | solution.py:112
  640.3 12.6 %convolution_convert_fusion.2 = bf16[2048,1024]{0,1:T(8,128)(2,1)S(1)} fusion(bf16[2048,2048]{1,0:T(8,128)(2,1)} %bitcast.478, bf16[2048,512]{0,1:T(8,128)(2,1)} %get-tuple-element.256, bf16[2048,512]{0,1:T(8,128)(2,1)} %get-tuple-element.255), kind=kOutput, calls=%fused_computation.114 | convolution fusion | flops 8600420352 | bytes 16777216 | tf_op jit(solution)/shard_map/tc,tf->cf/dot_general | solution.py:291
  653.6 8.1 convolution_convert_fusion.4
  665.2 13.4 %collective-permute-done.19 = bf16[256,2048]{1,0:T(8,128)(2,1)S(1)} collective-permute-done((bf16[256,2048]{1,0:T(8,128)(2,1)S(1)}, bf16[256,2048]{1,0:T(8,128)(2,1)S(1)}, u32[]{:S(2)}, u32[]{:S(2)}) %collective-permute-start.19) | collective-permute-done | bytes 1048608 | tf_op jit(solution)/shard_map/ppermute | solution.py:112
  680.9 6.4 pad_maximum_fusion.3
  687.2 8.4 copy.140
  702.3 77.8 %while.29 = (s32[]{:T(128)}, f32[2,1024,4,64]{1,3,2,0:T(8,128)}, f32[2,1024,64]{1,2,0:T(8,128)}, bf16[2,1024,64]{1,2,0:T(8,128)(2,1)}, bf16[2,1024,64]{1,2,0:T(8...) while((s32[]{:T(128)}, f32[2,1024,4,64]{1,3,2,0:T(8,128)}, ...), condition=%wide.region_10.11_spmd, body=%wide.region_8.10_spmd.sunk | while | flops 2727669760 | bytes 158352688 | solution.py:316
  702.7 8.2 fusion.212
  712.9 11.9 %fusion.213 = (f32[4,1024]{1,0:T(4,128)S(1)}, f32[4,1024,1024]{1,2,0:T(8,128)S(1)}) fusion(f32[1024,1024,4]{1,0,2:T(8,128)} %fusion.212, f32[4,1024]{1,0:T(4,128)} %get-tuple-element.533, f32[4,1024]{1,0:T(4,128)} %get-tuple-element.534, bf16[2,1024,4,64]{1,3,2,0:T(8,128)(2,1)} %get-tuple-element.594, s32[]{:T(128)} %get-tuple-element.576, ...), kind=kOutput, calls=%fused_computation.26.clone.1 | convolution fusion | flops 562032640 | bytes 35308544 | tf_op jit(solution)/shard_map/while/body/eval_jaxpr/qgd,jd->gqj/dot_general | solution.py:62
  724.8 8.0 fusion.214
  741.3 8.2 fusion.212
  751.5 11.8 %fusion.213 = (f32[4,1024]{1,0:T(4,128)S(1)}, f32[4,1024,1024]{1,2,0:T(8,128)S(1)}) fusion(f32[1024,1024,4]{1,0,2:T(8,128)} %fusion.212, f32[4,1024]{1,0:T(4,128)} %get-tuple-element.533, f32[4,1024]{1,0:T(4,128)} %get-tuple-element.534, bf16[2,1024,4,64]{1,3,2,0:T(8,128)(2,1)} %get-tuple-element.594, s32[]{:T(128)} %get-tuple-element.576, ...), kind=kOutput, calls=%fused_computation.26.clone.1 | convolution fusion | flops 562032640 | bytes 35308544 | tf_op jit(solution)/shard_map/while/body/eval_jaxpr/qgd,jd->gqj/dot_general | solution.py:62
  763.3 8.2 fusion.214
  823.6 5.9 convolution_convert_fusion.6
  841.2 28.8 %collective-permute-done.38 = bf16[256,256]{1,0:T(8,128)(2,1)S(1)} collective-permute-done((bf16[256,256]{1,0:T(8,128)(2,1)S(1)}, bf16[256,256]{1,0:T(8,128)(2,1)S(1)}, u32[]{:S(2)}, u32[]{:S(2)}) %collective-permute-start.38) | collective-permute-done | bytes 131104 | tf_op jit(solution)/shard_map/ppermute | solution.py:112
  873.5 9.0 convert_add_fusion
  897.0 38.8 %collective-permute-done.37 = bf16[256,384]{1,0:T(8,128)(2,1)S(1)} collective-permute-done((bf16[256,384]{1,0:T(8,128)(2,1)S(1)}, bf16[256,384]{1,0:T(8,128)(2,1)S(1)}, u32[]{:S(2)}, u32[]{:S(2)}) %collective-permute-start.37) | collective-permute-done | bytes 196640 | tf_op jit(solution)/shard_map/ppermute | solution.py:112
  947.7 40.6 %psum.14 = f32[2,2048]{1,0:T(2,128)} all-reduce(f32[2,2048]{1,0:T(2,128)} %pad_maximum_fusion.48), channel_id=1, replica_groups=mesh['dp'=8,'shard'=4] {'dp','shard'}, use_global_device_ids=true, to_apply=%region_14.15 | all-reduce | flops 4096 | bytes 32768 | tf_op jit(solution)/shard_map/psum | solution.py:377
  998.9 41.0 %psum.15 = f32[]{:T(128)} all-reduce(f32[]{:T(128)S(6)} %add.352), channel_id=1, replica_groups=mesh['dp'=8,'shard'=4] {'dp','shard'}, use_global_device_ids=true, to_apply=%region_28.29 | all-reduce | flops 1 | bytes 8 | tf_op jit(solution)/shard_map/psum | solution.py:385
  1052.2 17.0 %collective-permute-done.35 = bf16[256,2048]{1,0:T(8,128)(2,1)S(1)} collective-permute-done((bf16[256,2048]{1,0:T(8,128)(2,1)S(1)}, bf16[256,2048]{1,0:T(8,128)(2,1)S(1)}, u32[]{:S(2)}, u32[]{:S(2)}) %collective-permute-start.35) | collective-permute-done | bytes 1048608 | tf_op jit(solution)/shard_map/ppermute | solution.py:112
  (494 shorter events, 345.4 us)
Async XLA Ops:
  7.2 105.0 %all-gather.5.cloned.1.call-start = ((), (), s32[]{:S(2)}) async-start(), calls=%async_computation.4 | async-start | bytes 2088960 | tf_op jit(solution)/shard_map/all_gather | solution.py:115
  11.9 8.2 collective-permute-start.2
  21.0 139.3 %all-gather.7.cloned.1.call-start = ((), (), s32[]{:S(2)}) async-start(), calls=%async_computation.5 | async-start | bytes 1310720 | tf_op jit(solution)/shard_map/all_gather | solution.py:115
  24.3 48.9 %collective-permute-start = (bf16[512,2048]{1,0:T(8,128)(2,1)}, bf16[512,2048]{1,0:T(8,128)(2,1)}, u32[]{:S(2)}, u32[]{:S(2)}) collective-permute-start(bf16[512,2048]{1,0:T(8,128)(2,1)} %constant_dynamic-slice_fusion.35), channel_id=1, source_target_pairs={{0,4},{1,5},{2,6},{3,7},{4,0},{5,1},{6,2},{7,3},{8,12},{9,13},{10,... | collective-permute-start | bytes 6291464 | tf_op jit(solution)/shard_map/ppermute | solution.py:112
  26.0 52.5 %collective-permute-start.3 = (s32[1,1024]{1,0:T(1,128)S(1)}, s32[1,1024]{1,0:T(1,128)S(1)}, u32[]{:S(2)}, u32[]{:S(2)}) collective-permute-start(s32[1,1024]{1,0:T(1,128)S(1)} %copy-done.81), channel_id=1, source_target_pairs={{0,4},{1,5},{2,6},{3,7},{4,0},{5,1},{6,2},{7,3},{8,12},{9,13},{10,... | collective-permute-start | bytes 12296 | tf_op jit(solution)/shard_map/ppermute | solution.py:112
  26.6 49.5 %collective-permute-start.4 = (bf16[256,256]{1,0:T(8,128)(2,1)S(1)}, bf16[256,256]{1,0:T(8,128)(2,1)}, u32[]{:S(2)}, u32[]{:S(2)}) collective-permute-start(bf16[256,256]{1,0:T(8,128)(2,1)S(1)} %dynamic-slice_bitcast_fusion.16), channel_id=1, source_target_pairs={{0,4},{1,5},{2,6},{3,7},{4,0},{5,1},{6,2},{7,3},{8,12},{9,13},{10,... | collective-permute-start | bytes 393224 | tf_op jit(solution)/shard_map/ppermute | solution.py:112
  37.6 55.2 %collective-permute-start.13 = (bf16[256,1536]{0,1:T(8,128)(2,1)}, bf16[256,1536]{0,1:T(8,128)(2,1)}, u32[]{:S(2)}, u32[]{:S(2)}) collective-permute-start(bf16[256,1536]{0,1:T(8,128)(2,1)} %pad_maximum_fusion.30), channel_id=1, source_target_pairs={{0,4},{1,5},{2,6},{3,7},{4,0},{5,1},{6,2},{7,3},{8,12},{9,13},{10,... | collective-permute-start | bytes 2359304 | tf_op jit(solution)/shard_map/ppermute | solution.py:112
  39.2 68.7 %collective-permute-start.14 = (bf16[256,1536]{0,1:T(8,128)(2,1)}, bf16[256,1536]{0,1:T(8,128)(2,1)S(1)}, u32[]{:S(2)}, u32[]{:S(2)}) collective-permute-start(bf16[256,1536]{0,1:T(8,128)(2,1)} %pad_maximum_fusion.32), channel_id=1, source_target_pairs={{0,4},{1,5},{2,6},{3,7},{4,0},{5,1},{6,2},{7,3},{8,12},{9,13},{10,... | collective-permute-start | bytes 2359304 | tf_op jit(solution)/shard_map/ppermute | solution.py:112
  73.1 44.5 %collective-permute-start.1 = (bf16[512,2048]{1,0:T(8,128)(2,1)}, bf16[512,2048]{1,0:T(8,128)(2,1)}, u32[]{:S(2)}, u32[]{:S(2)}) collective-permute-start(bf16[512,2048]{1,0:T(8,128)(2,1)} %collective-permute-done), channel_id=1, source_target_pairs={{0,1},{1,0},{2,3},{3,2},{4,5},{5,4},{6,7},{7,6},{8,9},{9,8},{10,11... | collective-permute-start | bytes 6291464 | tf_op jit(solution)/shard_map/ppermute | solution.py:112
  77.7 267.6 %all-gather.9.cloned.1.call-start = ((), (), s32[]{:S(2)}) async-start(), calls=%async_computation.6 | async-start | bytes 7864320 | tf_op jit(solution)/shard_map/all_gather | solution.py:115
  112.1 247.8 %all-gather.11.cloned.1.call-start = ((), (), s32[]{:S(2)}) async-start(), calls=%async_computation.7 | async-start | bytes 7864320 | tf_op jit(solution)/shard_map/all_gather | solution.py:115
  164.7 7.4 collective-permute-start.5
  181.5 25.5 %collective-permute-start.6 = (bf16[256,2048]{1,0:T(8,128)(2,1)}, bf16[256,2048]{1,0:T(8,128)(2,1)}, u32[]{:S(2)}, u32[]{:S(2)}) collective-permute-start(bf16[256,2048]{1,0:T(8,128)(2,1)} %get-tuple-element.291), channel_id=1, source_target_pairs={{0,2},{1,3},{2,0},{3,1},{4,6},{5,7},{6,4},{7,5},{8,10},{9,11},{10,... | collective-permute-start | bytes 3145736 | tf_op jit(solution)/shard_map/ppermute | solution.py:112
  182.8 26.4 %collective-permute-start.7 = (bf16[256,2048]{1,0:T(8,128)(2,1)}, bf16[256,2048]{1,0:T(8,128)(2,1)}, u32[]{:S(2)}, u32[]{:S(2)}) collective-permute-start(bf16[256,2048]{1,0:T(8,128)(2,1)} %get-tuple-element.293), channel_id=1, source_target_pairs={{0,4},{1,5},{2,6},{3,7},{4,0},{5,1},{6,2},{7,3},{8,12},{9,13},{10,... | collective-permute-start | bytes 3145736 | tf_op jit(solution)/shard_map/ppermute | solution.py:112
  184.3 46.3 %collective-permute-start.8 = (bf16[256,2048]{1,0:T(8,128)(2,1)}, bf16[256,2048]{1,0:T(8,128)(2,1)}, u32[]{:S(2)}, u32[]{:S(2)}) collective-permute-start(bf16[256,2048]{1,0:T(8,128)(2,1)} %get-tuple-element.292), channel_id=1, source_target_pairs={{0,6},{1,7},{2,4},{3,5},{4,2},{5,3},{6,0},{7,1},{8,14},{9,15},{10,... | collective-permute-start | bytes 3145736 | tf_op jit(solution)/shard_map/ppermute | solution.py:112
  188.1 641.5 %reduce-scatter.9.cloned.1.call-start = ((), (), s32[]{:S(2)}) async-start(), calls=%async_computation.10 | async-start | bytes 7864320 | tf_op jit(solution)/shard_map/reduce_scatter | solution.py:118
  236.0 25.3 %collective-permute-start.9 = (bf16[256,2048]{1,0:T(8,128)(2,1)S(1)}, bf16[256,2048]{1,0:T(8,128)(2,1)S(1)}, u32[]{:S(2)}, u32[]{:S(2)}) collective-permute-start(bf16[256,2048]{1,0:T(8,128)(2,1)S(1)} %multiply_convert_fusion.6), channel_id=1, source_target_pairs={{0,2},{1,3},{2,0},{3,1},{4,6},{5,7},{6,4},{7,5},{8,10},{9,11},{10,... | collective-permute-start | bytes 3145736 | tf_op jit(solution)/shard_map/ppermute | solution.py:112
  237.4 26.1 %collective-permute-start.10 = (bf16[256,2048]{1,0:T(8,128)(2,1)S(1)}, bf16[256,2048]{1,0:T(8,128)(2,1)S(1)}, u32[]{:S(2)}, u32[]{:S(2)}) collective-permute-start(bf16[256,2048]{1,0:T(8,128)(2,1)S(1)} %multiply_convert_fusion.6), channel_id=1, source_target_pairs={{0,4},{1,5},{2,6},{3,7},{4,0},{5,1},{6,2},{7,3},{8,12},{9,13},{10,... | collective-permute-start | bytes 3145736 | tf_op jit(solution)/shard_map/ppermute | solution.py:112
  238.9 47.2 %collective-permute-start.11 = (bf16[256,2048]{1,0:T(8,128)(2,1)S(1)}, bf16[256,2048]{1,0:T(8,128)(2,1)S(1)}, u32[]{:S(2)}, u32[]{:S(2)}) collective-permute-start(bf16[256,2048]{1,0:T(8,128)(2,1)S(1)} %multiply_convert_fusion.6), channel_id=1, source_target_pairs={{0,6},{1,7},{2,4},{3,5},{4,2},{5,3},{6,0},{7,1},{8,14},{9,15},{10,... | collective-permute-start | bytes 3145736 | tf_op jit(solution)/shard_map/ppermute | solution.py:112
  240.6 87.9 %collective-permute-start.21 = (bf16[2,256,2048]{2,1,0:T(8,128)(2,1)S(1)}, bf16[2,256,2048]{2,1,0:T(8,128)(2,1)S(1)}, u32[]{:S(2)}, u32[]{:S(2)}) collective-permute-start(bf16[2,256,2048]{2,1,0:T(8,128)(2,1)S(1)} %slice.292), channel_id=1, source_target_pairs={{0,4},{1,5},{2,6},{3,7},{4,0},{5,1},{6,2},{7,3},{8,12},{9,13},{10,... | collective-permute-start | bytes 6291464 | tf_op jit(solution)/shard_map/ppermute | solution.py:112
  286.8 50.2 %collective-permute-start.12 = (bf16[4,256,2048]{2,1,0:T(8,128)(2,1)S(1)}, bf16[4,256,2048]{2,1,0:T(8,128)(2,1)S(1)}, u32[]{:S(2)}, u32[]{:S(2)}) collective-permute-start(bf16[4,256,2048]{2,1,0:T(8,128)(2,1)S(1)} %get-tuple-element.290), channel_id=1, source_target_pairs={{0,1},{1,0},{2,3},{3,2},{4,5},{5,4},{6,7},{7,6},{8,9},{9,8},{10,11... | collective-permute-start | bytes 12582920 | tf_op jit(solution)/shard_map/ppermute | solution.py:112
  428.8 50.6 %collective-permute-start.23 = (bf16[2,2,256,2048]{3,2,1,0:T(8,128)(2,1)}, bf16[2,2,256,2048]{3,2,1,0:T(8,128)(2,1)}, u32[]{:S(2)}, u32[]{:S(2)}) collective-permute-start(bf16[2,2,256,2048]{3,2,1,0:T(8,128)(2,1)} %slice.294), channel_id=1, source_target_pairs={{0,1},{1,0},{2,3},{3,2},{4,5},{5,4},{6,7},{7,6},{8,9},{9,8},{10,11... | collective-permute-start | bytes 12582920 | tf_op jit(solution)/shard_map/ppermute | solution.py:112
  468.3 25.6 %collective-permute-start.15 = (bf16[2,2,256,2048]{3,2,1,0:T(8,128)(2,1)}, bf16[2,2,256,2048]{3,2,1,0:T(8,128)(2,1)}, u32[]{:S(2)}, u32[]{:S(2)}) collective-permute-start(bf16[2,2,256,2048]{3,2,1,0:T(8,128)(2,1)} %slice.287), channel_id=1, source_target_pairs={{0,1},{1,0},{2,3},{3,2},{4,5},{5,4},{6,7},{7,6},{8,9},{9,8},{10,11... | collective-permute-start | bytes 12582920 | tf_op jit(solution)/shard_map/ppermute | solution.py:112
  479.3 352.9 %reduce-scatter.11.cloned.1.call-start = ((), (), s32[]{:S(2)}) async-start(), calls=%async_computation.11 | async-start | bytes 7864320 | tf_op jit(solution)/shard_map/reduce_scatter | solution.py:118
  490.4 26.8 %collective-permute-start.24 = (bf16[256,2048]{1,0:T(8,128)(2,1)}, bf16[256,2048]{1,0:T(8,128)(2,1)}, u32[]{:S(2)}, u32[]{:S(2)}) collective-permute-start(bf16[256,2048]{1,0:T(8,128)(2,1)} %get-tuple-element.275), channel_id=1, source_target_pairs={{0,2},{1,3},{2,0},{3,1},{4,6},{5,7},{6,4},{7,5},{8,10},{9,11},{10,... | collective-permute-start | bytes 3145736 | tf_op jit(solution)/shard_map/ppermute | solution.py:112
  491.2 27.8 %collective-permute-start.25 = (bf16[256,2048]{1,0:T(8,128)(2,1)}, bf16[256,2048]{1,0:T(8,128)(2,1)}, u32[]{:S(2)}, u32[]{:S(2)}) collective-permute-start(bf16[256,2048]{1,0:T(8,128)(2,1)} %get-tuple-element.277), channel_id=1, source_target_pairs={{0,4},{1,5},{2,6},{3,7},{4,0},{5,1},{6,2},{7,3},{8,12},{9,13},{10,... | collective-permute-start | bytes 3145736 | tf_op jit(solution)/shard_map/ppermute | solution.py:112
  492.6 48.2 %collective-permute-start.26 = (bf16[256,2048]{1,0:T(8,128)(2,1)S(1)}, bf16[256,2048]{1,0:T(8,128)(2,1)}, u32[]{:S(2)}, u32[]{:S(2)}) collective-permute-start(bf16[256,2048]{1,0:T(8,128)(2,1)S(1)} %get-tuple-element.276), channel_id=1, source_target_pairs={{0,6},{1,7},{2,4},{3,5},{4,2},{5,3},{6,0},{7,1},{8,14},{9,15},{10,... | collective-permute-start | bytes 3145736 | tf_op jit(solution)/shard_map/ppermute | solution.py:112
  499.7 61.1 %collective-permute-start.16 = (bf16[256,2048]{1,0:T(8,128)(2,1)S(1)}, bf16[256,2048]{1,0:T(8,128)(2,1)S(1)}, u32[]{:S(2)}, u32[]{:S(2)}) collective-permute-start(bf16[256,2048]{1,0:T(8,128)(2,1)S(1)} %get-tuple-element.286), channel_id=1, source_target_pairs={{0,2},{1,3},{2,0},{3,1},{4,6},{5,7},{6,4},{7,5},{8,10},{9,11},{10,... | collective-permute-start | bytes 3145736 | tf_op jit(solution)/shard_map/ppermute | solution.py:112
  500.6 61.8 %collective-permute-start.17 = (bf16[256,2048]{1,0:T(8,128)(2,1)S(1)}, bf16[256,2048]{1,0:T(8,128)(2,1)S(1)}, u32[]{:S(2)}, u32[]{:S(2)}) collective-permute-start(bf16[256,2048]{1,0:T(8,128)(2,1)S(1)} %get-tuple-element.288), channel_id=1, source_target_pairs={{0,4},{1,5},{2,6},{3,7},{4,0},{5,1},{6,2},{7,3},{8,12},{9,13},{10,... | collective-permute-start | bytes 3145736 | tf_op jit(solution)/shard_map/ppermute | solution.py:112
  517.3 67.3 %collective-permute-start.18 = (bf16[256,2048]{1,0:T(8,128)(2,1)S(1)}, bf16[256,2048]{1,0:T(8,128)(2,1)S(1)}, u32[]{:S(2)}, u32[]{:S(2)}) collective-permute-start(bf16[256,2048]{1,0:T(8,128)(2,1)S(1)} %get-tuple-element.287), channel_id=1, source_target_pairs={{0,6},{1,7},{2,4},{3,5},{4,2},{5,3},{6,0},{7,1},{8,14},{9,15},{10,... | collective-permute-start | bytes 3145736 | tf_op jit(solution)/shard_map/ppermute | solution.py:112
  588.6 25.2 %collective-permute-start.27 = (bf16[256,2048]{1,0:T(8,128)(2,1)S(1)}, bf16[256,2048]{1,0:T(8,128)(2,1)S(1)}, u32[]{:S(2)}, u32[]{:S(2)}) collective-permute-start(bf16[256,2048]{1,0:T(8,128)(2,1)S(1)} %get-tuple-element.238), channel_id=1, source_target_pairs={{0,2},{1,3},{2,0},{3,1},{4,6},{5,7},{6,4},{7,5},{8,10},{9,11},{10,... | collective-permute-start | bytes 3145736 | tf_op jit(solution)/shard_map/ppermute | solution.py:112
  589.3 26.1 %collective-permute-start.28 = (bf16[256,2048]{1,0:T(8,128)(2,1)S(1)}, bf16[256,2048]{1,0:T(8,128)(2,1)S(1)}, u32[]{:S(2)}, u32[]{:S(2)}) collective-permute-start(bf16[256,2048]{1,0:T(8,128)(2,1)S(1)} %get-tuple-element.238), channel_id=1, source_target_pairs={{0,4},{1,5},{2,6},{3,7},{4,0},{5,1},{6,2},{7,3},{8,12},{9,13},{10,... | collective-permute-start | bytes 3145736 | tf_op jit(solution)/shard_map/ppermute | solution.py:112
  590.6 45.9 %collective-permute-start.29 = (bf16[256,2048]{1,0:T(8,128)(2,1)S(1)}, bf16[256,2048]{1,0:T(8,128)(2,1)S(1)}, u32[]{:S(2)}, u32[]{:S(2)}) collective-permute-start(bf16[256,2048]{1,0:T(8,128)(2,1)S(1)} %get-tuple-element.238), channel_id=1, source_target_pairs={{0,6},{1,7},{2,4},{3,5},{4,2},{5,3},{6,0},{7,1},{8,14},{9,15},{10,... | collective-permute-start | bytes 3145736 | tf_op jit(solution)/shard_map/ppermute | solution.py:112
  640.3 40.6 %collective-permute-start.30 = (bf16[4,256,2048]{2,1,0:T(8,128)(2,1)}, bf16[4,256,2048]{2,1,0:T(8,128)(2,1)}, u32[]{:S(2)}, u32[]{:S(2)}) collective-permute-start(bf16[4,256,2048]{2,1,0:T(8,128)(2,1)} %get-tuple-element.273), channel_id=1, source_target_pairs={{0,1},{1,0},{2,3},{3,2},{4,5},{5,4},{6,7},{7,6},{8,9},{9,8},{10,11... | collective-permute-start | bytes 12582920 | tf_op jit(solution)/shard_map/ppermute | solution.py:112
  653.0 25.6 %collective-permute-start.19 = (bf16[256,2048]{1,0:T(8,128)(2,1)S(1)}, bf16[256,2048]{1,0:T(8,128)(2,1)S(1)}, u32[]{:S(2)}, u32[]{:S(2)}) collective-permute-start(bf16[256,2048]{1,0:T(8,128)(2,1)S(1)} %get-tuple-element.306), channel_id=1, source_target_pairs={{0,2},{1,3},{2,0},{3,1},{4,6},{5,7},{6,4},{7,5},{8,10},{9,11},{10,... | collective-permute-start | bytes 3145736 | tf_op jit(solution)/shard_map/ppermute | solution.py:112
  665.2 169.8 %reduce-scatter.7.cloned.1.call-start = ((), (), s32[]{:S(2)}) async-start(), calls=%async_computation.9 | async-start | bytes 1310720 | tf_op jit(solution)/shard_map/reduce_scatter | solution.py:118
  680.9 134.9 %collective-permute-start.20 = (bf16[2,256,2048]{2,1,0:T(8,128)(2,1)}, bf16[2,256,2048]{2,1,0:T(8,128)(2,1)}, u32[]{:S(2)}, u32[]{:S(2)}) collective-permute-start(bf16[2,256,2048]{2,1,0:T(8,128)(2,1)} %get-tuple-element.308), channel_id=1, source_target_pairs={{0,1},{1,0},{2,3},{3,2},{4,5},{5,4},{6,7},{7,6},{8,9},{9,8},{10,11... | collective-permute-start | bytes 6291464 | tf_op jit(solution)/shard_map/ppermute | solution.py:112
  803.5 70.0 %collective-permute-start.31 = (bf16[2,2,256,2048]{3,2,1,0:T(8,128)(2,1)}, bf16[2,2,256,2048]{3,2,1,0:T(8,128)(2,1)}, u32[]{:S(2)}, u32[]{:S(2)}) collective-permute-start(bf16[2,2,256,2048]{3,2,1,0:T(8,128)(2,1)} %slice.304), channel_id=1, source_target_pairs={{0,1},{1,0},{2,3},{3,2},{4,5},{5,4},{6,7},{7,6},{8,9},{9,8},{10,11... | collective-permute-start | bytes 12582920 | tf_op jit(solution)/shard_map/ppermute | solution.py:112
  807.6 83.6 %reduce-scatter.5.cloned.1.call-start = ((), (), s32[]{:S(2)}) async-start(), calls=%async_computation.8 | async-start | bytes 1966080 | tf_op jit(solution)/shard_map/reduce_scatter | solution.py:118
  830.7 41.1 %collective-permute-start.39 = (bf16[256,1536]{0,1:T(8,128)(2,1)S(1)}, bf16[256,1536]{0,1:T(8,128)(2,1)S(1)}, u32[]{:S(2)}, u32[]{:S(2)}) collective-permute-start(bf16[256,1536]{0,1:T(8,128)(2,1)S(1)} %constant_dynamic-slice_fusion.10), channel_id=1, source_target_pairs={{0,4},{1,5},{2,6},{3,7},{4,0},{5,1},{6,2},{7,3},{8,12},{9,13},{10,... | collective-permute-start | bytes 2359304 | tf_op jit(solution)/shard_map/ppermute | solution.py:112
  833.4 39.1 %collective-permute-start.40 = (bf16[256,1536]{0,1:T(8,128)(2,1)S(1)}, bf16[256,1536]{0,1:T(8,128)(2,1)S(1)}, u32[]{:S(2)}, u32[]{:S(2)}) collective-permute-start(bf16[256,1536]{0,1:T(8,128)(2,1)S(1)} %constant_dynamic-slice_fusion.9), channel_id=1, source_target_pairs={{0,4},{1,5},{2,6},{3,7},{4,0},{5,1},{6,2},{7,3},{8,12},{9,13},{10,... | collective-permute-start | bytes 2359304 | tf_op jit(solution)/shard_map/ppermute | solution.py:112
  835.9 34.1 %collective-permute-start.38 = (bf16[256,256]{1,0:T(8,128)(2,1)S(1)}, bf16[256,256]{1,0:T(8,128)(2,1)S(1)}, u32[]{:S(2)}, u32[]{:S(2)}) collective-permute-start(bf16[256,256]{1,0:T(8,128)(2,1)S(1)} %constant_dynamic-slice_fusion.11), channel_id=1, source_target_pairs={{0,4},{1,5},{2,6},{3,7},{4,0},{5,1},{6,2},{7,3},{8,12},{9,13},{10,... | collective-permute-start | bytes 393224 | tf_op jit(solution)/shard_map/ppermute | solution.py:112
  884.2 55.8 %collective-permute-start.32 = (bf16[256,2048]{1,0:T(8,128)(2,1)}, bf16[256,2048]{1,0:T(8,128)(2,1)S(1)}, u32[]{:S(2)}, u32[]{:S(2)}) collective-permute-start(bf16[256,2048]{1,0:T(8,128)(2,1)} %get-tuple-element.269), channel_id=1, source_target_pairs={{0,2},{1,3},{2,0},{3,1},{4,6},{5,7},{6,4},{7,5},{8,10},{9,11},{10,... | collective-permute-start | bytes 3145736 | tf_op jit(solution)/shard_map/ppermute | solution.py:112
  884.8 55.2 %collective-permute-start.33 = (bf16[256,2048]{1,0:T(8,128)(2,1)}, bf16[256,2048]{1,0:T(8,128)(2,1)S(1)}, u32[]{:S(2)}, u32[]{:S(2)}) collective-permute-start(bf16[256,2048]{1,0:T(8,128)(2,1)} %get-tuple-element.271), channel_id=1, source_target_pairs={{0,4},{1,5},{2,6},{3,7},{4,0},{5,1},{6,2},{7,3},{8,12},{9,13},{10,... | collective-permute-start | bytes 3145736 | tf_op jit(solution)/shard_map/ppermute | solution.py:112
  886.1 53.9 %collective-permute-start.34 = (bf16[256,2048]{1,0:T(8,128)(2,1)}, bf16[256,2048]{1,0:T(8,128)(2,1)}, u32[]{:S(2)}, u32[]{:S(2)}) collective-permute-start(bf16[256,2048]{1,0:T(8,128)(2,1)} %get-tuple-element.270), channel_id=1, source_target_pairs={{0,6},{1,7},{2,4},{3,5},{4,2},{5,3},{6,0},{7,1},{8,14},{9,15},{10,... | collective-permute-start | bytes 3145736 | tf_op jit(solution)/shard_map/ppermute | solution.py:112
  892.2 43.7 %collective-permute-start.37 = (bf16[256,384]{1,0:T(8,128)(2,1)S(1)}, bf16[256,384]{1,0:T(8,128)(2,1)S(1)}, u32[]{:S(2)}, u32[]{:S(2)}) collective-permute-start(bf16[256,384]{1,0:T(8,128)(2,1)S(1)} %constant_dynamic-slice_fusion.12), channel_id=1, source_target_pairs={{0,4},{1,5},{2,6},{3,7},{4,0},{5,1},{6,2},{7,3},{8,12},{9,13},{10,... | collective-permute-start | bytes 589832 | tf_op jit(solution)/shard_map/ppermute | solution.py:112
  1044.7 24.4 %collective-permute-start.35 = (bf16[256,2048]{1,0:T(8,128)(2,1)S(1)}, bf16[256,2048]{1,0:T(8,128)(2,1)S(1)}, u32[]{:S(2)}, u32[]{:S(2)}) collective-permute-start(bf16[256,2048]{1,0:T(8,128)(2,1)S(1)} %fusion.80), channel_id=1, source_target_pairs={{0,2},{1,3},{2,0},{3,1},{4,6},{5,7},{6,4},{7,5},{8,10},{9,11},{10,... | collective-permute-start | bytes 3145736 | tf_op jit(solution)/shard_map/ppermute | solution.py:112
  1071.4 26.4 %collective-permute-start.36 = (bf16[2,256,2048]{2,1,0:T(8,128)(2,1)}, bf16[2,256,2048]{2,1,0:T(8,128)(2,1)}, u32[]{:S(2)}, u32[]{:S(2)}) collective-permute-start(bf16[2,256,2048]{2,1,0:T(8,128)(2,1)} %get-tuple-element.305), channel_id=1, source_target_pairs={{0,1},{1,0},{2,3},{3,2},{4,5},{5,4},{6,7},{7,6},{8,9},{9,8},{10,11... | collective-permute-start | bytes 6291464 | tf_op jit(solution)/shard_map/ppermute | solution.py:112
  (107 other events, 1276.6 us)
Sparse Core Ops, SparseCore 0:
  21.2 40.1 all-gather.4
  77.9 29.4 all-gather.6
  112.2 116.5 all-gather.8
  230.8 113.5 all-gather.10
  479.5 111.0 reduce-scatter.8
  665.3 111.7 reduce-scatter.10
  807.7 27.2 reduce-scatter.6
  838.0 33.9 reduce-scatter.4

commit v2 on v1

v2 whole, which is shorter than its diff:
```python
import functools

import jax
import jax.numpy as jnp
from jax import lax
from jax.experimental import pallas as pl
from jax.experimental.pallas import tpu as pltpu
from jax.sharding import PartitionSpec as P

H = 32
KV = 8
CLIP = 4096
WARMUP = 2000
THETA = 10000000.0
CHUNKS = 2
MESH = pl.DeviceIdType.MESH


BF = jnp.bfloat16
F32 = jnp.float32
HD = 64
EPS = 1e-05
NEGATIVE = -1e30
VMEM = 48 << 20

def dot(a, b, ca, cb):
    return lax.dot_general(a, b, (((ca,), (cb,)), ((), ())), preferred_element_type=F32)

def swap_halves(v):
    n = v.shape[1]
    lane = lax.broadcasted_iota(jnp.int32, v.shape, 1)
    return jnp.where(lane % HD < HD // 2, pltpu.roll(v, n - HD // 2, 1), pltpu.roll(v, HD // 2, 1))

def qkv_body(tok_ref, gain_ref, w_ref, cos_ref, sin_ref, normed_ref, q_ref, k_ref, v_ref):
    x = tok_ref[...].astype(F32)
    inv = lax.rsqrt(jnp.mean(x * x, axis=1, keepdims=True) + EPS)
    normed = (x * inv * gain_ref[...]).astype(BF)
    normed_ref[...] = normed
    lin = dot(normed, w_ref[...], 1, 0)
    heads = q_ref.shape[0]
    qc = heads * HD
    rot = lin * cos_ref[...] + swap_halves(lin) * sin_ref[...]
    for h in range(heads):
        q_ref[h] = (rot[:, h * HD : (h + 1) * HD]).astype(BF)
    k_ref[...] = rot[:, qc : qc + HD].astype(BF)
    v_ref[...] = rot[:, qc + HD :].astype(BF)

def qkv(tokens, gain, weight, cos, sin, heads, tile=256):
    count, width = tokens.shape
    cols = weight.shape[1]
    length = cos.shape[0]
    per = length // tile
    full = lambda i: (0, 0)
    row = lambda i: (i, 0)
    return pl.pallas_call(
        qkv_body,
        grid=(count // tile,),
        in_specs=[
            pl.BlockSpec((tile, width), row),
            pl.BlockSpec((1, width), full),
            pl.BlockSpec((width, cols), full),
            pl.BlockSpec((tile, cols), lambda i: (i % per, 0)),
            pl.BlockSpec((tile, cols), lambda i: (i % per, 0)),
        ],
        out_specs=[
            pl.BlockSpec((tile, width), row),
            pl.BlockSpec((heads, tile, HD), lambda i: (0, i, 0)),
            pl.BlockSpec((tile, HD), row),
            pl.BlockSpec((tile, HD), row),
        ],
        out_shape=[
            jax.ShapeDtypeStruct((count, width), BF),
            jax.ShapeDtypeStruct((heads, count, HD), BF),
            jax.ShapeDtypeStruct((count, HD), BF),
            jax.ShapeDtypeStruct((count, HD), BF),
        ],
        compiler_params=pltpu.CompilerParams(vmem_limit_bytes=VMEM),
        cost_estimate=pl.CostEstimate(flops=2 * count * width * cols, bytes_accessed=4 * count * width, transcendentals=0),
        name="qkv_rope",
    )(tokens, gain, weight, cos, sin)

def fwd_body(limits, q_ref, k_ref, v_ref, brow_ref, bcol_ref, o_ref, lse_ref):
    heads, tile, _ = q_ref.shape
    i = pl.program_id(1)
    def run(keys):
        k = k_ref[:keys]
        v = v_ref[:keys]
        allowed = brow_ref[0][:, :keys] <= bcol_ref[...]
        outs = []
        lses = []
        for h in range(heads):
            s = dot(q_ref[h] * BF(0.125), k, 1, 1)
            s = jnp.where(allowed, s, NEGATIVE)
            m = jnp.max(s, axis=1, keepdims=True)
            p = jnp.exp(s - m)
            l = jnp.sum(p, axis=1, keepdims=True)
            o = dot(p.astype(BF), v, 1, 0) / l
            outs.append(o.astype(BF))
            lses.append(m + jnp.log(l))
        o_ref[...] = jnp.concatenate(outs, axis=1)
        lse_ref[...] = jnp.concatenate(lses, axis=1)
    for n, keys in enumerate(limits):
        @pl.when(i == n)
        def _(keys=keys):
            run(keys)

def attend(q, k, v, brow, bcol, length, tile=256, most=256):
    heads, count, _ = q.shape
    seqs = count // length
    per = length // tile
    limits = tuple(min(length, (n + 1) * tile + most) for n in range(per))
    return pl.pallas_call(
        functools.partial(fwd_body, limits),
        grid=(seqs, per),
        in_specs=[
            pl.BlockSpec((heads, tile, HD), lambda b, i: (0, b * per + i, 0)),
            pl.BlockSpec((length, HD), lambda b, i: (b, 0)),
            pl.BlockSpec((length, HD), lambda b, i: (b, 0)),
            pl.BlockSpec((1, 1, length), lambda b, i: (b, 0, 0)),
            pl.BlockSpec((tile, 1), lambda b, i: (b * per + i, 0)),
        ],
        out_specs=[
            pl.BlockSpec((tile, heads * HD), lambda b, i: (b * per + i, 0)),
            pl.BlockSpec((tile, heads), lambda b, i: (b * per + i, 0)),
        ],
        out_shape=[
            jax.ShapeDtypeStruct((count, heads * HD), BF),
            jax.ShapeDtypeStruct((count, heads), F32),
        ],
        compiler_params=pltpu.CompilerParams(vmem_limit_bytes=VMEM),
        cost_estimate=pl.CostEstimate(flops=4 * heads * count * length * HD * 4, bytes_accessed=count * 2048, transcendentals=heads * count * length),
        name="attend",
    )(q, k, v, brow, bcol)

def bwd_body(limits, q_ref, k_ref, v_ref, brow_ref, bcol_ref, lse_ref, do_ref, cos_ref, sin_ref, kcos_ref, ksin_ref, dq_ref, dkv_ref, dk_acc, dv_acc):
    heads, tile, _ = q_ref.shape
    i = pl.program_id(1)
    @pl.when(i == 0)
    def _():
        dk_acc[...] = jnp.zeros_like(dk_acc)
        dv_acc[...] = jnp.zeros_like(dv_acc)
    def run(keys):
        k = k_ref[:keys]
        v = v_ref[:keys]
        allowed = brow_ref[0][:, :keys] <= bcol_ref[...]
        dqs = []
        dk = jnp.zeros((HD, keys), F32)
        dv = jnp.zeros((HD, keys), F32)
        for h in range(heads):
            q = q_ref[h] * BF(0.125)
            do = do_ref[:, h * HD : (h + 1) * HD]
            s = dot(q, k, 1, 1)
            s = jnp.where(allowed, s, NEGATIVE)
            p = jnp.exp(s - lse_ref[:, h : h + 1])
            dp = dot(do, v, 1, 1)
            pdp = p * dp
            delta = jnp.sum(pdp, axis=1, keepdims=True)
            ds = (pdp - p * delta).astype(BF)
            dqs.append(dot(ds, k, 1, 0) * 0.125)
            dk = dk + dot(q, ds, 0, 0)
            dv = dv + dot(do, p.astype(BF), 0, 0)
        dk_acc[:, :keys] += dk
        dv_acc[:, :keys] += dv
        dq = jnp.concatenate(dqs, axis=1)
        dq_ref[...] = (dq * cos_ref[...] - swap_halves(dq) * sin_ref[...]).astype(BF)
    for n, keys in enumerate(limits):
        @pl.when(i == n)
        def _(keys=keys):
            run(keys)
    @pl.when(i == len(limits) - 1)
    def _():
        both = jnp.concatenate([dk_acc[...], dv_acc[...]], axis=0).T
        dkv_ref[...] = (both * kcos_ref[...] - swap_halves(both) * ksin_ref[...]).astype(BF)

def attend_back(q, k, v, brow, bcol, lse, do, cos, sin, length, tile=256, most=256):
    heads, count, _ = q.shape
    seqs = count // length
    per = length // tile
    qc = heads * HD
    limits = tuple(min(length, (n + 1) * tile + most) for n in range(per))
    rowm = lambda b, i: (b * per + i, 0)
    return pl.pallas_call(
        functools.partial(bwd_body, limits),
        grid=(seqs, per),
        in_specs=[
            pl.BlockSpec((heads, tile, HD), lambda b, i: (0, b * per + i, 0)),
            pl.BlockSpec((length, HD), lambda b, i: (b, 0)),
            pl.BlockSpec((length, HD), lambda b, i: (b, 0)),
            pl.BlockSpec((1, 1, length), lambda b, i: (b, 0, 0)),
            pl.BlockSpec((tile, 1), rowm),
            pl.BlockSpec((tile, heads), rowm),
            pl.BlockSpec((tile, qc), rowm),
            pl.BlockSpec((tile, qc), lambda b, i: (i, 0)),
            pl.BlockSpec((tile, qc), lambda b, i: (i, 0)),
            pl.BlockSpec((length, 2 * HD), lambda b, i: (0, qc // (2 * HD))),
            pl.BlockSpec((length, 2 * HD), lambda b, i: (0, qc // (2 * HD))),
        ],
        out_specs=[
            pl.BlockSpec((tile, qc), rowm),
            pl.BlockSpec((length, 2 * HD), lambda b, i: (b, 0)),
        ],
        out_shape=[
            jax.ShapeDtypeStruct((count, qc), BF),
            jax.ShapeDtypeStruct((count, 2 * HD), BF),
        ],
        scratch_shapes=[pltpu.VMEM((HD, length), F32), pltpu.VMEM((HD, length), F32)],
        compiler_params=pltpu.CompilerParams(vmem_limit_bytes=VMEM),
        cost_estimate=pl.CostEstimate(flops=10 * heads * count * length * HD * 4, bytes_accessed=count * 4096, transcendentals=heads * count * length),
        name="attend_back",
    )(q, k, v, brow, bcol, lse, do, cos, sin, cos, sin)

def rope_tables(length, heads):
    positions = jnp.arange(length, dtype=jnp.int32).astype(F32)
    powers = -2.0 * jnp.arange(HD // 2, dtype=F32) / HD
    angles = positions[:, None] * jnp.power(THETA, powers)[None, :]
    c = jnp.cos(angles); s = jnp.sin(angles)
    cos = jnp.concatenate([jnp.tile(jnp.concatenate([c, c], axis=1), (1, heads + 1)), jnp.ones((length, HD), F32)], axis=1)
    sin = jnp.concatenate([jnp.tile(jnp.concatenate([-s, s], axis=1), (1, heads + 1)), jnp.zeros((length, HD), F32)], axis=1)
    return cos, sin

def up_body(first, last, n2_ref, cot_ref, w_ref, *rest):
    if first:
        act_ref, dgu_ref, part_ref = rest
    else:
        prev_ref, act_ref, dgu_ref, part_ref = rest
    size = act_ref.shape[1]
    gu = dot(n2_ref[...], w_ref[:, : 2 * size], 1, 0)
    da = dot(cot_ref[...], w_ref[:, 2 * size :], 1, 0)
    gate, up = gu[:, :size], gu[:, size:]
    sig = 1.0 / (1.0 + jnp.exp(-gate))
    gs = gate * sig
    act_ref[...] = (gs * up).astype(BF)
    dg = (da * up * sig * (1.0 + gate * (1.0 - sig))).astype(BF)
    du = (da * gs).astype(BF)
    dgu = jnp.concatenate([dg, du], axis=1)
    dgu_ref[...] = dgu
    part = dot(dgu, w_ref[:, : 2 * size], 1, 1)
    if not first:
        part = part + prev_ref[...]
    part_ref[...] = part.astype(part_ref.dtype)

def up_back(n2, cot, weight, prev, last, tile=256):
    count, width = n2.shape
    size = weight.shape[1] // 3
    row = lambda i: (i, 0)
    full = lambda i: (0, 0)
    ins = [n2, cot, weight] + ([] if prev is None else [prev])
    specs = [pl.BlockSpec((tile, width), row), pl.BlockSpec((tile, width), row), pl.BlockSpec((width, 3 * size), full, pipeline_mode=pl.Buffered(1))]
    if prev is not None:
        specs.append(pl.BlockSpec((tile, width), row))
    return pl.pallas_call(
        functools.partial(up_body, prev is None, last),
        grid=(count // tile,),
        in_specs=specs,
        out_specs=[pl.BlockSpec((tile, size), row), pl.BlockSpec((tile, 2 * size), row), pl.BlockSpec((tile, width), row)],
        out_shape=[jax.ShapeDtypeStruct((count, size), BF), jax.ShapeDtypeStruct((count, 2 * size), BF), jax.ShapeDtypeStruct((count, width), BF if last else F32)],
        compiler_params=pltpu.CompilerParams(vmem_limit_bytes=VMEM),
        cost_estimate=pl.CostEstimate(flops=2 * count * width * size * 5, bytes_accessed=12 * count * width, transcendentals=count * size),
        name="swiglu_part",
    )(*ins)

def grad_body(n2_ref, cot_ref, dgu_ref, act_ref, o_ref):
    size = act_ref.shape[1]
    o_ref[:, : 2 * size] = dot(n2_ref[...], dgu_ref[...], 0, 0).astype(BF)
    o_ref[:, 2 * size :] = dot(cot_ref[...], act_ref[...], 0, 0).astype(BF)

def ffn_grads(n2, cot, dgu, act, tile=256):
    count, width = n2.shape
    size = act.shape[1]
    col = lambda i: (0, i)
    full = lambda i: (0, 0)
    return pl.pallas_call(
        grad_body,
        grid=(width // tile,),
        in_specs=[pl.BlockSpec((count, tile), col), pl.BlockSpec((count, tile), col), pl.BlockSpec((count, 2 * size), full, pipeline_mode=pl.Buffered(1)), pl.BlockSpec((count, size), full, pipeline_mode=pl.Buffered(1))],
        out_specs=pl.BlockSpec((tile, 3 * size), lambda i: (i, 0)),
        out_shape=jax.ShapeDtypeStruct((width, 3 * size), BF),
        compiler_params=pltpu.CompilerParams(vmem_limit_bytes=VMEM),
        cost_estimate=pl.CostEstimate(flops=2 * count * width * size * 3, bytes_accessed=8 * count * width, transcendentals=0),
        name="swiglu_grads",
    )(n2, cot, dgu, act)

def out_body(*refs):
    count = len(refs) // 2
    total = dot(refs[0][...], refs[count][...], 1, 1)
    for j in range(1, count):
        total = total + dot(refs[j][...], refs[count + j][...], 1, 1)
    refs[-1][...] = total.astype(BF)


def down(acts, weights, tile=256):
    count, size = acts[0].shape
    width = weights[0].shape[0]
    row = lambda i: (i, 0)
    return pl.pallas_call(
        out_body,
        grid=(count // tile,),
        in_specs=[pl.BlockSpec((tile, size), row) for _ in acts]
        + [
            pl.BlockSpec((width, size), lambda i: (0, 2), pipeline_mode=pl.Buffered(1))
            for _ in weights
        ],
        out_specs=pl.BlockSpec((tile, width), row),
        out_shape=jax.ShapeDtypeStruct((count, width), BF),
        compiler_params=pltpu.CompilerParams(vmem_limit_bytes=VMEM),
        cost_estimate=pl.CostEstimate(
            flops=2 * count * width * size * len(acts),
            bytes_accessed=8 * count * width,
            transcendentals=0,
        ),
        name="swiglu_down",
    )(*acts, *weights)


def sum_body(dps, shards, x_ref, o_ref, slots, send, recv):
    total = dps * shards
    me = lax.axis_index("dp") * shards + lax.axis_index("shard")
    barrier = pltpu.get_barrier_semaphore()

    def device(p):
        target = lax.rem(me + p, total)
        return (target // shards, lax.rem(target, shards))

    def greet(p, carry):
        pl.semaphore_signal(barrier, inc=1, device_id=device(p), device_id_type=MESH)
        return carry

    lax.fori_loop(1, total, greet, 0)
    slots[me] = x_ref[...]
    pl.semaphore_wait(barrier, total - 1)

    def copy(p):
        return pltpu.make_async_remote_copy(
            src_ref=x_ref,
            dst_ref=slots.at[me],
            send_sem=send.at[p],
            recv_sem=recv.at[p],
            device_id=device(p),
            device_id_type=MESH,
        )

    def start(p, carry):
        copy(p).start()
        return carry

    def finish(p, carry):
        copy(p).wait()
        return carry

    lax.fori_loop(1, total, start, 0)
    lax.fori_loop(1, total, finish, 0)
    o_ref[...] = lax.fori_loop(
        0, total, lambda i, acc: acc + slots[i], jnp.zeros(x_ref.shape, F32)
    )


def sum_all(values, dps, shards, number):
    total = dps * shards
    return pl.pallas_call(
        functools.partial(sum_body, dps, shards),
        in_specs=[pl.BlockSpec(memory_space=pltpu.VMEM)],
        out_specs=pl.BlockSpec(memory_space=pltpu.VMEM),
        out_shape=jax.ShapeDtypeStruct(values.shape, F32),
        scratch_shapes=[
            pltpu.VMEM((total,) + values.shape, F32),
            pltpu.SemaphoreType.DMA((total,)),
            pltpu.SemaphoreType.DMA((total,)),
        ],
        compiler_params=pltpu.CompilerParams(collective_id=number, has_side_effects=True),
        name="sum_all",
    )(values)


def after(value, *others):
    return lax.optimization_barrier((value,) + others)[0]


def inverse_rms(values):
    return lax.rsqrt(jnp.mean(values * values, axis=-1, keepdims=True) + EPS)


def norm_back(values, inverse, gain, grad_normed):
    scaled = grad_normed * gain
    gain_grad = jnp.sum(grad_normed * values * inverse, axis=0)
    grad_values = inverse * scaled - values * inverse**3 * jnp.mean(
        scaled * values, axis=-1, keepdims=True
    )
    return (gain_grad, grad_values)


def build(dps, shards):
    total = dps * shards
    axes = ("dp", "shard")
    zgroups = [[i for i in range(dps) if i % 2 == p] for p in (0, 1)]

    def swap(values, dx, ds):
        pairs = [
            (i, ((i // shards) ^ dx) * shards + ((i % shards) ^ ds)) for i in range(total)
        ]
        return lax.ppermute(values, axes, pairs)

    def gather(piece):
        return lax.all_gather(piece, "dp", axis=0, tiled=True, axis_index_groups=zgroups)

    def scatter(whole):
        return lax.psum_scatter(
            whole, "dp", scatter_dimension=0, tiled=True, axis_index_groups=zgroups
        )

    def sum_to_owner(partial):
        even = partial[:, 0::2]
        odd = partial[:, 1::2].astype(BF)
        paired = even.astype(F32) + swap(odd, 0, 1).astype(F32)
        low = paired.astype(BF)
        from_y = swap(low[0, 1], 0, 2)
        from_x = swap(low[1, 0], 1, 0)
        from_d = swap(low[1, 1], 1, 2)
        return paired[0, 0] + from_y.astype(F32) + from_x.astype(F32) + from_d.astype(F32)

    def spread(own):
        from_y = swap(own, 0, 2)
        from_x = swap(own, 1, 0)
        from_d = swap(own, 1, 2)
        mine = jnp.stack([own, from_y, from_x, from_d])
        theirs = swap(mine, 0, 1)
        return jnp.stack([mine, theirs], axis=1).reshape((2, shards) + own.shape)

    def on_device(
        tokens,
        block_ids,
        cotangent,
        gain_first,
        w_query,
        w_key,
        w_value,
        w_output,
        gain_second,
        w_gate,
        w_up,
        w_down,
        moment_first,
        moment_query,
        moment_key,
        moment_value,
        moment_output,
        moment_second,
        moment_gate,
        moment_up,
        moment_down,
        step,
        rate,
    ):
        length = block_ids.shape[1]
        width = tokens.shape[1]
        group = H // KV
        dp = lax.axis_index("dp")
        me = lax.axis_index("shard")
        x = lax.rem(dp, 2)
        quarter = length // shards
        rows = w_query.shape[0]

        def half(values, which):
            size = values.shape[1] // 2
            return lax.dynamic_slice_in_dim(values, which * size, size, axis=1)

        def ordered(mine, theirs, axis=0):
            first = jnp.where(x == 0, mine, theirs)
            second = jnp.where(x == 0, theirs, mine)
            return jnp.concatenate([first, second], axis=axis)

        low_q = w_query.astype(BF)
        low_k = w_key.astype(BF)
        low_v = w_value.astype(BF)
        low_o = w_output.astype(BF).T
        low_g = w_gate.astype(BF)
        low_u = w_up.astype(BF)
        low_d = w_down.astype(BF).T

        def attn_half(which):
            return jnp.concatenate([half(low_q, which), half(low_k, which), half(low_v, which)], axis=1)

        cols = low_q.shape[1] // 2 + low_k.shape[1]
        gains = jnp.stack([gain_first, gain_second]).astype(BF)
        gains = jnp.pad(gains, ((0, 14), (0, cols - rows)))
        sent = swap(jnp.concatenate([attn_half(1 - x), gains], axis=0), 1, 0)
        piece = jnp.concatenate(
            [ordered(attn_half(x), sent[:rows]), ordered(gains, sent[rows:])], axis=0
        )
        groups = dps // 2
        packed = gather(piece).reshape(groups, 2 * rows + 32, cols)
        qkv_weight = packed[:, : 2 * rows].reshape(width, cols)
        tails = packed[:, 2 * rows :].reshape(groups, 2, 16, cols)
        gain_one = tails[:, :, 0, :rows].reshape(1, width).astype(F32)
        gain_two = tails[:, :, 1, :rows].reshape(1, width).astype(F32)

        tokens_mine = lax.dynamic_slice_in_dim(tokens, me * quarter, quarter, axis=0)
        tokens_x = swap(after(tokens_mine, sent), 1, 0)
        out_x = swap(after(half(low_o, 1 - x), sent), 1, 0)
        out_weight = gather(ordered(half(low_o, x), out_x))
        size = low_g.shape[1] // 2 // CHUNKS

        def ffn_part(which, j):
            return jnp.concatenate(
                [half(low, which)[:, j * size : (j + 1) * size] for low in (low_g, low_u, low_d)],
                axis=1,
            )

        ffn_weights = []
        previous = (tokens_x, out_x)
        for j in range(CHUNKS):
            ffn_x = swap(after(ffn_part(1 - x, j), *previous), 1, 0)
            previous = (ffn_x,)
            ffn_weights.append(gather(ordered(ffn_part(x, j), ffn_x)))

        def natural_index(values):
            return jnp.concatenate(
                [
                    lax.dynamic_index_in_dim(values, me ^ q, axis=0, keepdims=False)
                    for q in range(shards)
                ],
                axis=0,
            )

        def rest_of(from_x):
            from_xy = swap(from_x, 0, 2)
            pair = jnp.stack([from_x, from_xy])
            return jnp.stack([pair, swap(pair, 0, 1)], axis=1).reshape((shards,) + from_x.shape)

        both = jnp.concatenate([tokens, natural_index(rest_of(tokens_x))], axis=0)
        blocks = jnp.concatenate([block_ids, swap(block_ids, 1, 0)], axis=0)
        block_rows = blocks[:, None, :]
        block_cols = blocks.reshape(2 * length, 1)

        def to_relative(values):
            values = values.reshape(2, length, values.shape[-1])
            parts = [
                lax.dynamic_slice_in_dim(values, (me ^ ds) * quarter, quarter, axis=1)
                for ds in range(shards)
            ]
            return jnp.stack(parts, axis=1)

        def to_natural(values):
            parts = [
                lax.dynamic_index_in_dim(values, me ^ q, axis=1, keepdims=False)
                for q in range(shards)
            ]
            return jnp.concatenate(parts, axis=1)

        cot_own = jnp.stack(
            [
                lax.dynamic_slice_in_dim(cotangent, (me ^ ds) * quarter, quarter, axis=0)
                for ds in range(shards)
            ]
        )
        cot_x = swap(after(cot_own[0], *previous), 1, 0)
        cot_rel = jnp.concatenate([cot_own, rest_of(cot_x)], axis=0).reshape(2 * length, width)

        cosine, sine = rope_tables(length, group)
        normed, query, key, value = qkv(both, gain_one, qkv_weight, cosine, sine, group)
        mixed, lse = attend(query, key, value, block_rows, block_cols, length)
        mixed_rel = to_relative(mixed).reshape(2 * length, group * HD)
        partial = jnp.einsum("tk,dk->td", mixed_rel, out_weight, preferred_element_type=F32)
        summed = sum_to_owner(partial.astype(BF).reshape(2, shards, quarter, width))
        tokens_own = lax.dynamic_slice_in_dim(tokens, me * quarter, quarter, axis=0).astype(F32)
        hidden = tokens_own + summed
        inverse_second = inverse_rms(hidden)
        normed_two_own = (hidden * inverse_second * gain_two).astype(BF)
        normed_two = spread(normed_two_own).reshape(2 * length, width)

        shape = (2, shards, quarter, width)
        grads_ffn = []
        acts = []
        partial_two = None
        for j in range(CHUNKS):
            last = j == CHUNKS - 1
            act, grad_gu, partial_two = up_back(
                normed_two, cot_rel, ffn_weights[j], partial_two, last
            )
            acts.append(act)
            grads_ffn.append(scatter(ffn_grads(normed_two, cot_rel, grad_gu, act)))
        grad_normed_two = sum_to_owner(partial_two.reshape(shape))
        cot_mine = cot_own[0].astype(F32)
        gain_grad_two, grad_through = norm_back(hidden, inverse_second, gain_two, grad_normed_two)
        grad_hidden = cot_mine + grad_through
        grad_hidden_rel = spread(grad_hidden.astype(BF)).reshape(2 * length, width)

        def to_sequence(own):
            from_y = swap(own, 0, 2)
            mine = jnp.stack([own, from_y])
            theirs = swap(mine, 0, 1)
            rel = jnp.stack([mine, theirs], axis=1).reshape((1, shards) + own.shape)
            return to_natural(rel)[0]

        result = after(down(acts, ffn_weights), grad_hidden_rel)
        output_own = (hidden + sum_to_owner(result.reshape(shape))).astype(BF)
        output = to_sequence(output_own)

        d_out = jnp.einsum("td,tk->dk", grad_hidden_rel, mixed_rel, preferred_element_type=F32)
        grad_out = scatter(d_out.astype(BF))
        grad_mixed = jnp.dot(grad_hidden_rel, out_weight, preferred_element_type=F32).astype(BF)
        grad_mixed = to_natural(grad_mixed.reshape(2, shards, quarter, group * HD))
        grad_q, grad_kv = attend_back(
            query,
            key,
            value,
            block_rows,
            block_cols,
            lse,
            grad_mixed.reshape(2 * length, group * HD),
            cosine,
            sine,
            length,
        )
        grad_qkv = jnp.concatenate([grad_q, grad_kv], axis=1)
        d_qkv = jnp.einsum(
            "tc,tk->ck", normed, grad_qkv, preferred_element_type=F32
        ).astype(BF)
        grad_qkv_w = scatter(d_qkv)
        partial_one = jnp.einsum(
            "tk,ck->tc",
            after(to_relative(grad_qkv).reshape(2 * length, cols), d_qkv),
            qkv_weight,
            preferred_element_type=F32,
        )
        grad_normed = sum_to_owner(partial_one.astype(BF).reshape(shape))
        inverse_own = inverse_rms(tokens_own)
        gain_grad_one, grad_inner = norm_back(tokens_own, inverse_own, gain_one, grad_normed)
        input_grad = to_sequence((grad_hidden + grad_inner).astype(BF)).astype(F32)

        def owned_halves(piece):
            keep = lax.dynamic_slice_in_dim(piece, x * rows, rows, axis=0)
            send = lax.dynamic_slice_in_dim(piece, (1 - x) * rows, rows, axis=0)
            return keep, swap(send, 1, 0)

        def joined(mine, theirs):
            return ordered(mine, theirs, axis=1).astype(F32)

        mine, theirs = owned_halves(grad_qkv_w)
        qc = group * HD
        own_q = joined(mine[:, :qc], theirs[:, :qc])
        own_k = joined(mine[:, qc : qc + HD], theirs[:, qc : qc + HD])
        own_v = joined(mine[:, qc + HD :], theirs[:, qc + HD :])
        mine, theirs = owned_halves(grad_out)
        own_o = joined(mine, theirs).T
        pairs = [owned_halves(piece) for piece in grads_ffn]
        own_gud = []
        for part in range(3):
            cut = slice(part * size, (part + 1) * size)
            own_gud.append(
                joined(
                    jnp.concatenate([m[:, cut] for m, t in pairs], axis=1),
                    jnp.concatenate([t[:, cut] for m, t in pairs], axis=1),
                )
            )
        own_g, own_u, own_d = own_gud[0], own_gud[1], own_gud[2].T
        gain_grads = sum_all(
            jnp.stack([gain_grad_one, gain_grad_two]).reshape(-1, 128), dps, shards, 1
        ).reshape(2, width)
        gain_grads = lax.dynamic_slice_in_dim(gain_grads, dp * rows, rows, axis=1)
        owned = (gain_grads[0], own_q, own_k, own_v, own_o, gain_grads[1], own_g, own_u, own_d)

        first_shard = (me == 0).astype(F32)
        squares = first_shard * (jnp.sum(owned[0] * owned[0]) + jnp.sum(owned[5] * owned[5]))
        for position in (1, 2, 3, 4, 6, 7, 8):
            squares = squares + jnp.sum(owned[position] * owned[position])
        squares = sum_all(jnp.broadcast_to(squares, (8, 128)), dps, shards, 2)
        global_norm = jnp.sqrt(squares[0, 0])
        factor = jnp.minimum(1.0, CLIP / global_norm)
        rate_now = rate * jnp.minimum(1.0, (step.astype(F32) + 1.0) / WARMUP)
        masters = (gain_first, w_query, w_key, w_value, w_output, gain_second, w_gate, w_up, w_down)
        moments = (
            moment_first,
            moment_query,
            moment_key,
            moment_value,
            moment_output,
            moment_second,
            moment_gate,
            moment_up,
            moment_down,
        )
        momenta = [
            0.5 * moment + 0.5 * (factor * gradient) for moment, gradient in zip(moments, owned)
        ]
        updated = [master - rate_now * momentum for master, momentum in zip(masters, momenta)]
        return (output, input_grad, global_norm, *momenta, *updated)

    return on_device


def solution(mesh):
    rows, both, back = P("dp"), P("dp", "shard"), P("shard", "dp")
    tokens = P("dp", None)
    params = (rows, both, both, both, back, rows, both, both, back)
    in_specs = (tokens, tokens, tokens, *params, *params, P(), P())
    out_specs = (tokens, tokens, P(), *params, *params)
    return jax.shard_map(
        build(mesh.shape["dp"], mesh.shape["shard"]),
        mesh=mesh,
        in_specs=in_specs,
        out_specs=out_specs,
        check_vma=False,
    )
```

time: 1120 us -> 943 us (0.84)
  Pallas kernels: 0 us -> 225 us
  matrix products: 240 us -> 27.3 us
  blocking collectives: 81.5 us -> 0 us
  waiting for transfers between devices: 430 us -> 362 us
  other arithmetic: 193 us -> 135 us
  local copies, waits for them, and re-layouts: 101 us -> 121 us
    pallas_call x0 -> x10, Pallas kernels: none -> 225 us  [the longest x2 59.5 us: up_back(): pl.pallas_call(functools.partial(up_body, prev is None, last), grid=(coun...]
    dot_general x29 -> x2, matrix products: 227 us -> 14.1 us  [the longest x1 9.34 us: on_device(): jnp.einsum('tc,tk->ck', normed, grad_qkv, preferred_element_type=F32)]
    psum x2 -> x0, blocking collectives: 81.5 us -> none  [the longest x1 41 us: on_device(): global_norm = jnp.sqrt(lax.psum(squares, axes))]
    ppermute x41 -> x43, waiting for transfers between devices: 429 us -> 362 us  [swap(): return lax.ppermute(values, axes, pairs)]
    convert_element_type x5 -> x3, other arithmetic: 19.9 us -> 3.4 us  [the longest x1 3.39 us: on_device(): output_own = (hidden + sum_to_owner(result.reshape(shape))).astype(BF)]
    dynamic_slice x16 -> x0, local copies, waits for them, and re-layouts: 13 us -> none  [the longest x6 9.24 us: to_relative(): lax.dynamic_slice_in_dim(values, (me ^ ds) * quarter, quarter, axis=1)]
    unnamed x205 -> x208, local copies, waits for them, and re-layouts: 38.5 us -> 48 us
    ppermute x41 -> x43, starting transfers between devices: 41.2 us -> 40.7 us  [swap(): return lax.ppermute(values, axes, pairs)]
  transfers between devices with their start and end apart: 49 -> 51, of which waited for: 27 -> 28; matrix products, arithmetic and copies ran while one was open for 38% -> 27% of each run, Pallas kernels for 0% -> 24%
where the time goes in v2:
time: 943 us; the launch traced here: 936 us
  waiting for transfers between devices  362 us (38%)
  Pallas kernels  225 us (24%)
  other arithmetic  135 us (14%)
  local copies, waits for them, and re-layouts  121 us (13%)
  starting transfers between devices  41.5 us (4%)
  matrix products  27.3 us (3%)
  between operations  24.7 us (3%)
    ppermute x43, waiting for transfers between devices, swap(): return lax.ppermute(values, axes, pairs)  362 us
    pallas_call x2, Pallas kernels, up_back(): pl.pallas_call(functools.partial(up_body, prev is None, last), grid=(coun...  59.5 us
    pallas_call x2, Pallas kernels, sum_all(): pl.pallas_call(functools.partial(sum_body, dps, shards), in_specs=[pl.Blo...  53.5 us
    unnamed x208, local copies, waits for them, and re-layouts  48 us
    ppermute x43, starting transfers between devices, swap(): return lax.ppermute(values, axes, pairs)  40.7 us
    pallas_call x2, Pallas kernels, ffn_grads(): pl.pallas_call(grad_body, grid=(width // tile,), in_specs=[pl.BlockSpec((...  37 us
    pallas_call x1, Pallas kernels, attend_back(): pl.pallas_call(functools.partial(bwd_body, limits), grid=(seqs, per), in_...  29 us
    add x3, other arithmetic, sum_to_owner(): paired = even.astype(F32) + swap(odd, 0, 1).astype(F32)  22.7 us
  transfers between devices with their start and end apart: 51, of which 28 were waited for; matrix products, arithmetic and copies ran while one was open for 27% of the time, Pallas kernels for 24%

profile of v2, /device:TPU:0, one launch (start us, length us, event | category | flops | bytes accessed | tf_op | source)
XLA Modules:
  0.0 936.3 jit_solution(3446769762841274655)
XLA Ops:
  36.0 8.5 collective-permute-done.1
  52.8 15.3 %collective-permute-done.2 = bf16[256,2048]{1,0:T(8,128)(2,1)S(1)} collective-permute-done((bf16[256,2048]{1,0:T(8,128)(2,1)}, bf16[256,2048]{1,0:T(8,128)(2,1)S(1)}, u32[]{:S(2)}, u32[]{:S(2)}) %collective-permute-start.2) | collective-permute-done | bytes 1048608 | tf_op jit(solution)/shard_map/ppermute | solution.py:400
  74.1 4.8 constant_dynamic-update-slice_fusion
  85.5 7.2 collective-permute-done.14
  105.9 13.9 %qkv_rope.1 = (bf16[2048,2048]{1,0:T(8,128)(2,1)}, bf16[4,2048,64]{2,1,0:T(8,128)(2,1)}, bf16[2048,64]{1,0:T(8,128)(2,1)S(1)}, bf16[2048,64]{1,0:T(8,128)(2,1)S(1)}) custom-call(bf16[2048,2048]{1,0:T(8,128)(2,1)} %bitcast_dynamic-update-slice_fusion.4.tok_ref, f32[1,2048]{1,0:T(1,128)S(1)} %reshape.214.gain_ref, bf16[2048,384]{1,0:T(8,128)(2,1)S(1)} %bitcast.239, ...), custom_call_target="tpu_custom_call" | custom-call | flops 3221225472 | bytes 16777216 | tf_op jit(solution)/shard_map/qkv_rope/pallas_call | solution.py:55
  119.8 17.9 %attend.1 = (bf16[2048,256]{1,0:T(8,128)(2,1)S(1)}, f32[2048,4]{1,0:T(8,128)S(1)}) custom-call(bf16[4,2048,64]{2,1,0:T(8,128)(2,1)} %get-tuple-element.43.q_ref, bf16[2048,64]{1,0:T(8,128)(2,1)S(1)} %get-tuple-element.44.k_ref, bf16[2048,64]{1,0:T(8,128)(2,1)S(1)} %get-tuple-element.45.v_ref, s32[2,1,1024]{2,1,0:T(1,128)S(1)} %broadcast_in_dim.4.brow_ref, ...), custom_call_target="tpu_custom_call" | custom-call | flops 8589934592 | bytes 4194304 | tf_op jit(solution)/shard_map/attend/pallas_call | solution.py:112
  139.0 3.9 convolution_convert_fusion.1
  145.2 5.4 collective-permute-done.6
  150.6 9.1 convert_add_fusion.3
  159.7 3.7 slice_bitcast_fusion.15
  168.6 20.4 %collective-permute-done.7 = bf16[256,2048]{1,0:T(8,128)(2,1)} collective-permute-done((bf16[256,2048]{1,0:T(8,128)(2,1)}, bf16[256,2048]{1,0:T(8,128)(2,1)}, u32[]{:S(2)}, u32[]{:S(2)}) %collective-permute-start.7) | collective-permute-done | bytes 1048608 | tf_op jit(solution)/shard_map/ppermute | solution.py:400
  190.9 21.7 %collective-permute-done.9 = bf16[256,2048]{1,0:T(8,128)(2,1)} collective-permute-done((bf16[256,2048]{1,0:T(8,128)(2,1)}, bf16[256,2048]{1,0:T(8,128)(2,1)}, u32[]{:S(2)}, u32[]{:S(2)}) %collective-permute-start.9) | collective-permute-done | bytes 1048608 | tf_op jit(solution)/shard_map/ppermute | solution.py:400
  221.8 20.1 %collective-permute-done.10 = bf16[256,2048]{1,0:T(8,128)(2,1)S(1)} collective-permute-done((bf16[256,2048]{1,0:T(8,128)(2,1)S(1)}, bf16[256,2048]{1,0:T(8,128)(2,1)S(1)}, u32[]{:S(2)}, u32[]{:S(2)}) %collective-permute-start.10) | collective-permute-done | bytes 1048608 | tf_op jit(solution)/shard_map/ppermute | solution.py:400
  243.9 22.8 %collective-permute-done.12 = bf16[256,2048]{1,0:T(8,128)(2,1)S(1)} collective-permute-done((bf16[256,2048]{1,0:T(8,128)(2,1)S(1)}, bf16[256,2048]{1,0:T(8,128)(2,1)S(1)}, u32[]{:S(2)}, u32[]{:S(2)}) %collective-permute-start.12) | collective-permute-done | bytes 1048608 | tf_op jit(solution)/shard_map/ppermute | solution.py:400
  269.2 17.3 %collective-permute-done.16 = bf16[256,2048]{1,0:T(8,128)(2,1)S(1)} collective-permute-done((bf16[256,2048]{1,0:T(8,128)(2,1)S(1)}, bf16[256,2048]{1,0:T(8,128)(2,1)S(1)}, u32[]{:S(2)}, u32[]{:S(2)}) %collective-permute-start.16) | collective-permute-done | bytes 1048608 | tf_op jit(solution)/shard_map/ppermute | solution.py:400
  287.4 22.1 %collective-permute-done.17 = bf16[256,2048]{1,0:T(8,128)(2,1)S(1)} collective-permute-done((bf16[256,2048]{1,0:T(8,128)(2,1)S(1)}, bf16[256,2048]{1,0:T(8,128)(2,1)S(1)}, u32[]{:S(2)}, u32[]{:S(2)}) %collective-permute-start.17) | collective-permute-done | bytes 1048608 | tf_op jit(solution)/shard_map/ppermute | solution.py:400
  310.1 3.9 collective-permute-done.18
  320.1 7.6 pad_maximum_fusion
  327.7 8.4 copy.62
  336.1 29.3 %swiglu_part.2 = (bf16[2048,512]{1,0:T(8,128)(2,1)S(1)}, bf16[2048,1024]{1,0:T(8,128)(2,1)}, f32[2048,2048]{1,0:T(8,128)}) custom-call(bf16[2048,2048]{1,0:T(8,128)(2,1)} %bitcast.260, bf16[2048,2048]{1,0:T(8,128)(2,1)} %bitcast.298, bf16[2048,1536]{1,0:T(8,128)(2,1)} %all-gather.9.cloned.1.call-done.w_ref.refs_2_), custom_call_target="tpu_custom_call" | custom-call | flops 21474836480 | bytes 50331648 | tf_op jit(solution)/shard_map/swiglu_part/pallas_call | solution.py:251
  365.4 18.5 %swiglu_grads.2 = bf16[2048,1536]{1,0:T(8,128)(2,1)} custom-call(bf16[2048,2048]{1,0:T(8,128)(2,1)} %bitcast.261, bf16[2048,2048]{1,0:T(8,128)(2,1)} %bitcast.299, bf16[2048,1024]{1,0:T(8,128)(2,1)} %get-tuple-element.61.dgu_ref, bf16[2048,512]{1,0:T(8,128)(2,1)S(1)} %get-tuple-element.51.refs_0_.act_ref), custom_call_target="tpu_custom_call" | custom-call | flops 12884901888 | bytes 33554432 | tf_op jit(solution)/shard_map/swiglu_grads/pallas_call | solution.py:272
  385.3 30.3 %swiglu_part.3 = (bf16[2048,512]{1,0:T(8,128)(2,1)S(1)}, bf16[2048,1024]{1,0:T(8,128)(2,1)}, bf16[2048,2048]{1,0:T(8,128)(2,1)}) custom-call(bf16[2048,2048]{1,0:T(8,128)(2,1)} %bitcast.262, bf16[2048,2048]{1,0:T(8,128)(2,1)} %bitcast.300, bf16[2048,1536]{1,0:T(8,128)(2,1)} %all-gather.11.cloned.1.call-done.w_ref.refs_3_, f32[2048,2048]{1,0:T(8,128)} %get-tuple-element.52.rest_0_), custom_call_target="tpu_custom_call" | custom-call | flops 21474836480 | bytes 50331648 | tf_op jit(solution)/shard_map/swiglu_part/pallas_call | solution.py:251
  415.6 5.6 slice.214
  421.3 18.5 %swiglu_grads.3 = bf16[2048,1536]{1,0:T(8,128)(2,1)} custom-call(bf16[2048,2048]{1,0:T(8,128)(2,1)} %bitcast.263, bf16[2048,2048]{1,0:T(8,128)(2,1)} %bitcast.301, bf16[2048,1024]{1,0:T(8,128)(2,1)} %get-tuple-element.62.dgu_ref, bf16[2048,512]{1,0:T(8,128)(2,1)S(1)} %get-tuple-element.53.refs_1_.act_ref), custom_call_target="tpu_custom_call" | custom-call | flops 12884901888 | bytes 33554432 | tf_op jit(solution)/shard_map/swiglu_grads/pallas_call | solution.py:272
  440.1 8.0 convert_add_fusion.2
  453.9 22.0 %collective-permute-done.20 = bf16[256,2048]{1,0:T(8,128)(2,1)S(1)} collective-permute-done((bf16[256,2048]{1,0:T(8,128)(2,1)S(1)}, bf16[256,2048]{1,0:T(8,128)(2,1)S(1)}, u32[]{:S(2)}, u32[]{:S(2)}) %collective-permute-start.20) | collective-permute-done | bytes 1048608 | tf_op jit(solution)/shard_map/ppermute | solution.py:400
  477.3 22.3 %collective-permute-done.22 = bf16[256,2048]{1,0:T(8,128)(2,1)S(1)} collective-permute-done((bf16[256,2048]{1,0:T(8,128)(2,1)S(1)}, bf16[256,2048]{1,0:T(8,128)(2,1)S(1)}, u32[]{:S(2)}, u32[]{:S(2)}) %collective-permute-start.22) | collective-permute-done | bytes 1048608 | tf_op jit(solution)/shard_map/ppermute | solution.py:400
  506.6 21.7 %collective-permute-done.23 = bf16[256,2048]{1,0:T(8,128)(2,1)S(1)} collective-permute-done((bf16[256,2048]{1,0:T(8,128)(2,1)S(1)}, bf16[256,2048]{1,0:T(8,128)(2,1)S(1)}, u32[]{:S(2)}, u32[]{:S(2)}) %collective-permute-start.23) | collective-permute-done | bytes 1048608 | tf_op jit(solution)/shard_map/ppermute | solution.py:400
  530.0 21.2 %collective-permute-done.25 = bf16[256,2048]{1,0:T(8,128)(2,1)S(1)} collective-permute-done((bf16[256,2048]{1,0:T(8,128)(2,1)S(1)}, bf16[256,2048]{1,0:T(8,128)(2,1)S(1)}, u32[]{:S(2)}, u32[]{:S(2)}) %collective-permute-start.25) | collective-permute-done | bytes 1048608 | tf_op jit(solution)/shard_map/ppermute | solution.py:400
  553.6 7.2 collective-permute-done.26
  562.8 7.8 pad_maximum_fusion.1
  570.6 8.6 copy.65
  579.1 5.8 convolution_convert_fusion.4
  586.4 29.0 %attend_back.1 = (bf16[2048,256]{1,0:T(8,128)(2,1)S(1)}, bf16[2048,128]{1,0:T(8,128)(2,1)S(1)}) custom-call(bf16[4,2048,64]{2,1,0:T(8,128)(2,1)} %get-tuple-element.43.q_ref, bf16[2048,64]{1,0:T(8,128)(2,1)S(1)} %copy-done.5, bf16[2048,64]{1,0:T(8,128)(2,1)S(1)} %copy-done.7, s32[2,1,1024]{2,1,0:T(1,128)S(1)} %broadcast_in_dim.4.brow_ref, ...), custom_call_target="tpu_custom_call" | custom-call | flops 21474836480 | bytes 8388608 | tf_op jit(solution)/shard_map/attend_back/pallas_call | solution.py:182
  624.3 9.3 convolution_convert_fusion.2
  633.7 4.8 convolution_convert_fusion
  650.8 13.8 %swiglu_down.1 = bf16[2048,2048]{1,0:T(8,128)(2,1)} custom-call(bf16[2048,512]{1,0:T(8,128)(2,1)S(1)} %copy-done.9, bf16[2048,512]{1,0:T(8,128)(2,1)S(1)} %copy-done.11, bf16[2048,1536]{1,0:T(8,128)(2,1)} %all-gather.9.cloned.1.call-done.w_ref.refs_2_, bf16[2048,1536]{1,0:T(8,128)(2,1)} %all-gather.11.cloned.1.call-done.w_ref.refs_3_), custom_call_target="tpu_custom_call" | custom-call | flops 8589934592 | bytes 33554432 | tf_op jit(solution)/shard_map/swiglu_down/pallas_call | solution.py:295
  664.6 4.8 slice.220
  679.6 31.9 %collective-permute-done.40 = bf16[256,256]{1,0:T(8,128)(2,1)S(1)} collective-permute-done((bf16[256,256]{1,0:T(8,128)(2,1)S(1)}, bf16[256,256]{1,0:T(8,128)(2,1)S(1)}, u32[]{:S(2)}, u32[]{:S(2)}) %collective-permute-start.40) | collective-permute-done | bytes 131104 | tf_op jit(solution)/shard_map/ppermute | solution.py:400
  729.2 5.6 convert_add_fusion
  739.9 10.7 %fusion.61 = (bf16[2,2,256,2048]{3,2,1,0:T(8,128)(2,1)}, f32[2,2,256,2048]{3,2,1,0:T(8,128)}) fusion(bf16[2,2,256,2048]{3,2,1,0:T(8,128)(2,1)} %collective-permute-done.27, bf16[2,4,256,2048]{3,2,1,0:T(8,128)(2,1)} %bitcast.257), kind=kLoop, calls=%fused_computation.265 | loop fusion | flops 8388608 | bytes 20971520 | tf_op jit(solution)/shard_map/convert_element_type | solution.py:414
  750.6 3.7 slice_bitcast_fusion.9
  755.9 27.7 %collective-permute-done.34 = bf16[256,2048]{1,0:T(8,128)(2,1)S(1)} collective-permute-done((bf16[256,2048]{1,0:T(8,128)(2,1)}, bf16[256,2048]{1,0:T(8,128)(2,1)S(1)}, u32[]{:S(2)}, u32[]{:S(2)}) %collective-permute-start.34) | collective-permute-done | bytes 1048608 | tf_op jit(solution)/shard_map/ppermute | solution.py:400
  792.7 42.5 %sum_all.2 = f32[32,128]{1,0:T(8,128)} custom-call(f32[32,128]{1,0:T(8,128)} %reshape.212.x_ref), custom_call_target="tpu_custom_call" | custom-call | tf_op jit(solution)/shard_map/sum_all/pallas_call | solution.py:359
  844.2 11.0 %sum_all.3 = f32[8,128]{1,0:T(8,128)} custom-call(f32[8,128]{1,0:T(8,128)} %broadcast_in_dim.5.x_ref), custom_call_target="tpu_custom_call" | custom-call | tf_op jit(solution)/shard_map/sum_all/pallas_call | solution.py:359
  881.9 5.6 collective-permute-done.37
  890.6 18.5 %collective-permute-done.31 = bf16[256,2048]{1,0:T(8,128)(2,1)} collective-permute-done((bf16[256,2048]{1,0:T(8,128)(2,1)S(1)}, bf16[256,2048]{1,0:T(8,128)(2,1)}, u32[]{:S(2)}, u32[]{:S(2)}) %collective-permute-start.31) | collective-permute-done | bytes 1048608 | tf_op jit(solution)/shard_map/ppermute | solution.py:400
  921.8 3.9 fusion
  (426 shorter events, 228.0 us)
Async XLA Ops:
  7.2 88.6 %all-gather.5.cloned.1.call-start = ((), (), s32[]{:S(2)}) async-start(), calls=%async_computation.4 | async-start | bytes 2088960 | tf_op jit(solution)/shard_map/all_gather | solution.py:403
  11.8 8.2 collective-permute-start
  20.0 24.5 %collective-permute-start.1 = (bf16[256,2048]{1,0:T(8,128)(2,1)S(1)}, bf16[256,2048]{1,0:T(8,128)(2,1)}, u32[]{:S(2)}, u32[]{:S(2)}) collective-permute-start(bf16[256,2048]{1,0:T(8,128)(2,1)S(1)} %get-tuple-element.42), channel_id=1, source_target_pairs={{0,4},{1,5},{2,6},{3,7},{4,0},{5,1},{6,2},{7,3},{8,12},{9,13},{10,... | collective-permute-start | bytes 3145736 | tf_op jit(solution)/shard_map/ppermute | solution.py:400
  22.7 116.3 %all-gather.7.cloned.1.call-start = ((), (), s32[]{:S(2)}) async-start(), calls=%async_computation.5 | async-start | bytes 1310720 | tf_op jit(solution)/shard_map/all_gather | solution.py:403
  22.8 61.3 %collective-permute-start.4 = (s32[1,1024]{1,0:T(1,128)S(1)}, s32[1,1024]{1,0:T(1,128)S(1)}, u32[]{:S(2)}, u32[]{:S(2)}) collective-permute-start(s32[1,1024]{1,0:T(1,128)S(1)} %copy-done.87), channel_id=1, source_target_pairs={{0,4},{1,5},{2,6},{3,7},{4,0},{5,1},{6,2},{7,3},{8,12},{9,13},{10,... | collective-permute-start | bytes 12296 | tf_op jit(solution)/shard_map/ppermute | solution.py:400
  44.5 23.6 %collective-permute-start.2 = (bf16[256,2048]{1,0:T(8,128)(2,1)}, bf16[256,2048]{1,0:T(8,128)(2,1)S(1)}, u32[]{:S(2)}, u32[]{:S(2)}) collective-permute-start(bf16[256,2048]{1,0:T(8,128)(2,1)} %collective-permute-done.1), channel_id=1, source_target_pairs={{0,2},{1,3},{2,0},{3,1},{4,6},{5,7},{6,4},{7,5},{8,10},{9,11},{10,... | collective-permute-start | bytes 3145736 | tf_op jit(solution)/shard_map/ppermute | solution.py:400
  71.6 27.3 %collective-permute-start.3 = (bf16[2,256,2048]{2,1,0:T(8,128)(2,1)}, bf16[2,256,2048]{2,1,0:T(8,128)(2,1)}, u32[]{:S(2)}, u32[]{:S(2)}) collective-permute-start(bf16[2,256,2048]{2,1,0:T(8,128)(2,1)} %get-tuple-element.166), channel_id=1, source_target_pairs={{0,1},{1,0},{2,3},{3,2},{4,5},{5,4},{6,7},{7,6},{8,9},{9,8},{10,11... | collective-permute-start | bytes 6291464 | tf_op jit(solution)/shard_map/ppermute | solution.py:400
  72.3 263.7 %all-gather.9.cloned.1.call-start = ((), (), s32[]{:S(2)}) async-start(), calls=%async_computation.6 | async-start | bytes 7864320 | tf_op jit(solution)/shard_map/all_gather | solution.py:403
  72.4 20.3 %collective-permute-start.14 = (bf16[256,1536]{1,0:T(8,128)(2,1)}, bf16[256,1536]{1,0:T(8,128)(2,1)}, u32[]{:S(2)}, u32[]{:S(2)}) collective-permute-start(bf16[256,1536]{1,0:T(8,128)(2,1)} %pad_maximum_fusion.21), channel_id=1, source_target_pairs={{0,4},{1,5},{2,6},{3,7},{4,0},{5,1},{6,2},{7,3},{8,12},{9,13},{10,... | collective-permute-start | bytes 2359304 | tf_op jit(solution)/shard_map/ppermute | solution.py:400
  95.4 289.9 %all-gather.11.cloned.1.call-start = ((), (), s32[]{:S(2)}) async-start(), calls=%async_computation.7 | async-start | bytes 7864320 | tf_op jit(solution)/shard_map/all_gather | solution.py:403
  143.3 7.4 collective-permute-start.6
  144.0 22.9 %collective-permute-start.15 = (bf16[256,1536]{1,0:T(8,128)(2,1)S(1)}, bf16[256,1536]{1,0:T(8,128)(2,1)S(1)}, u32[]{:S(2)}, u32[]{:S(2)}) collective-permute-start(bf16[256,1536]{1,0:T(8,128)(2,1)S(1)} %pad_maximum_fusion.20), channel_id=1, source_target_pairs={{0,4},{1,5},{2,6},{3,7},{4,0},{5,1},{6,2},{7,3},{8,12},{9,13},{10,... | collective-permute-start | bytes 2359304 | tf_op jit(solution)/shard_map/ppermute | solution.py:400
  163.5 25.5 %collective-permute-start.7 = (bf16[256,2048]{1,0:T(8,128)(2,1)}, bf16[256,2048]{1,0:T(8,128)(2,1)}, u32[]{:S(2)}, u32[]{:S(2)}) collective-permute-start(bf16[256,2048]{1,0:T(8,128)(2,1)} %get-tuple-element.150), channel_id=1, source_target_pairs={{0,2},{1,3},{2,0},{3,1},{4,6},{5,7},{6,4},{7,5},{8,10},{9,11},{10,... | collective-permute-start | bytes 3145736 | tf_op jit(solution)/shard_map/ppermute | solution.py:400
  164.6 26.4 %collective-permute-start.8 = (bf16[256,2048]{1,0:T(8,128)(2,1)}, bf16[256,2048]{1,0:T(8,128)(2,1)}, u32[]{:S(2)}, u32[]{:S(2)}) collective-permute-start(bf16[256,2048]{1,0:T(8,128)(2,1)} %get-tuple-element.152), channel_id=1, source_target_pairs={{0,4},{1,5},{2,6},{3,7},{4,0},{5,1},{6,2},{7,3},{8,12},{9,13},{10,... | collective-permute-start | bytes 3145736 | tf_op jit(solution)/shard_map/ppermute | solution.py:400
  166.1 46.5 %collective-permute-start.9 = (bf16[256,2048]{1,0:T(8,128)(2,1)}, bf16[256,2048]{1,0:T(8,128)(2,1)}, u32[]{:S(2)}, u32[]{:S(2)}) collective-permute-start(bf16[256,2048]{1,0:T(8,128)(2,1)} %get-tuple-element.151), channel_id=1, source_target_pairs={{0,6},{1,7},{2,4},{3,5},{4,2},{5,3},{6,0},{7,1},{8,14},{9,15},{10,... | collective-permute-start | bytes 3145736 | tf_op jit(solution)/shard_map/ppermute | solution.py:400
  168.5 501.2 %reduce-scatter.9.cloned.1.call-start = ((), (), s32[]{:S(2)}) async-start(), calls=%async_computation.10 | async-start | bytes 7864320 | tf_op jit(solution)/shard_map/reduce_scatter | solution.py:406
  216.6 25.3 %collective-permute-start.10 = (bf16[256,2048]{1,0:T(8,128)(2,1)S(1)}, bf16[256,2048]{1,0:T(8,128)(2,1)S(1)}, u32[]{:S(2)}, u32[]{:S(2)}) collective-permute-start(bf16[256,2048]{1,0:T(8,128)(2,1)S(1)} %multiply_convert_fusion), channel_id=1, source_target_pairs={{0,2},{1,3},{2,0},{3,1},{4,6},{5,7},{6,4},{7,5},{8,10},{9,11},{10,... | collective-permute-start | bytes 3145736 | tf_op jit(solution)/shard_map/ppermute | solution.py:400
  217.8 26.1 %collective-permute-start.11 = (bf16[256,2048]{1,0:T(8,128)(2,1)S(1)}, bf16[256,2048]{1,0:T(8,128)(2,1)S(1)}, u32[]{:S(2)}, u32[]{:S(2)}) collective-permute-start(bf16[256,2048]{1,0:T(8,128)(2,1)S(1)} %multiply_convert_fusion), channel_id=1, source_target_pairs={{0,4},{1,5},{2,6},{3,7},{4,0},{5,1},{6,2},{7,3},{8,12},{9,13},{10,... | collective-permute-start | bytes 3145736 | tf_op jit(solution)/shard_map/ppermute | solution.py:400
  219.3 47.4 %collective-permute-start.12 = (bf16[256,2048]{1,0:T(8,128)(2,1)S(1)}, bf16[256,2048]{1,0:T(8,128)(2,1)S(1)}, u32[]{:S(2)}, u32[]{:S(2)}) collective-permute-start(bf16[256,2048]{1,0:T(8,128)(2,1)S(1)} %multiply_convert_fusion), channel_id=1, source_target_pairs={{0,6},{1,7},{2,4},{3,5},{4,2},{5,3},{6,0},{7,1},{8,14},{9,15},{10,... | collective-permute-start | bytes 3145736 | tf_op jit(solution)/shard_map/ppermute | solution.py:400
  220.4 66.1 %collective-permute-start.16 = (bf16[256,2048]{1,0:T(8,128)(2,1)S(1)}, bf16[256,2048]{1,0:T(8,128)(2,1)S(1)}, u32[]{:S(2)}, u32[]{:S(2)}) collective-permute-start(bf16[256,2048]{1,0:T(8,128)(2,1)S(1)} %get-tuple-element.50), channel_id=1, source_target_pairs={{0,4},{1,5},{2,6},{3,7},{4,0},{5,1},{6,2},{7,3},{8,12},{9,13},{10,... | collective-permute-start | bytes 3145736 | tf_op jit(solution)/shard_map/ppermute | solution.py:400
  269.2 46.3 %collective-permute-start.13 = (bf16[4,256,2048]{2,1,0:T(8,128)(2,1)S(1)}, bf16[4,256,2048]{2,1,0:T(8,128)(2,1)S(1)}, u32[]{:S(2)}, u32[]{:S(2)}) collective-permute-start(bf16[4,256,2048]{2,1,0:T(8,128)(2,1)S(1)} %get-tuple-element.149), channel_id=1, source_target_pairs={{0,1},{1,0},{2,3},{3,2},{4,5},{5,4},{6,7},{7,6},{8,9},{9,8},{10,11... | collective-permute-start | bytes 12582920 | tf_op jit(solution)/shard_map/ppermute | solution.py:400
  286.5 23.0 %collective-permute-start.17 = (bf16[256,2048]{1,0:T(8,128)(2,1)S(1)}, bf16[256,2048]{1,0:T(8,128)(2,1)S(1)}, u32[]{:S(2)}, u32[]{:S(2)}) collective-permute-start(bf16[256,2048]{1,0:T(8,128)(2,1)S(1)} %collective-permute-done.16), channel_id=1, source_target_pairs={{0,2},{1,3},{2,0},{3,1},{4,6},{5,7},{6,4},{7,5},{8,10},{9,11},{10,... | collective-permute-start | bytes 3145736 | tf_op jit(solution)/shard_map/ppermute | solution.py:400
  385.2 288.1 %reduce-scatter.11.cloned.1.call-start = ((), (), s32[]{:S(2)}) async-start(), calls=%async_computation.11 | async-start | bytes 7864320 | tf_op jit(solution)/shard_map/reduce_scatter | solution.py:406
  421.1 19.0 %collective-permute-start.19 = (bf16[2,2,256,2048]{3,2,1,0:T(8,128)(2,1)}, bf16[2,2,256,2048]{3,2,1,0:T(8,128)(2,1)}, u32[]{:S(2)}, u32[]{:S(2)}) collective-permute-start(bf16[2,2,256,2048]{3,2,1,0:T(8,128)(2,1)} %slice.214), channel_id=1, source_target_pairs={{0,1},{1,0},{2,3},{3,2},{4,5},{5,4},{6,7},{7,6},{8,9},{9,8},{10,11... | collective-permute-start | bytes 12582920 | tf_op jit(solution)/shard_map/ppermute | solution.py:400
  439.8 237.2 %reduce-scatter.7.cloned.1.call-start = ((), (), s32[]{:S(2)}) async-start(), calls=%async_computation.9 | async-start | bytes 1310720 | tf_op jit(solution)/shard_map/reduce_scatter | solution.py:406
  450.4 25.6 %collective-permute-start.20 = (bf16[256,2048]{1,0:T(8,128)(2,1)S(1)}, bf16[256,2048]{1,0:T(8,128)(2,1)S(1)}, u32[]{:S(2)}, u32[]{:S(2)}) collective-permute-start(bf16[256,2048]{1,0:T(8,128)(2,1)S(1)} %get-tuple-element.145), channel_id=1, source_target_pairs={{0,2},{1,3},{2,0},{3,1},{4,6},{5,7},{6,4},{7,5},{8,10},{9,11},{10,... | collective-permute-start | bytes 3145736 | tf_op jit(solution)/shard_map/ppermute | solution.py:400
  451.3 26.0 %collective-permute-start.21 = (bf16[256,2048]{1,0:T(8,128)(2,1)S(1)}, bf16[256,2048]{1,0:T(8,128)(2,1)S(1)}, u32[]{:S(2)}, u32[]{:S(2)}) collective-permute-start(bf16[256,2048]{1,0:T(8,128)(2,1)S(1)} %get-tuple-element.147), channel_id=1, source_target_pairs={{0,4},{1,5},{2,6},{3,7},{4,0},{5,1},{6,2},{7,3},{8,12},{9,13},{10,... | collective-permute-start | bytes 3145736 | tf_op jit(solution)/shard_map/ppermute | solution.py:400
  452.5 47.2 %collective-permute-start.22 = (bf16[256,2048]{1,0:T(8,128)(2,1)S(1)}, bf16[256,2048]{1,0:T(8,128)(2,1)S(1)}, u32[]{:S(2)}, u32[]{:S(2)}) collective-permute-start(bf16[256,2048]{1,0:T(8,128)(2,1)S(1)} %get-tuple-element.146), channel_id=1, source_target_pairs={{0,6},{1,7},{2,4},{3,5},{4,2},{5,3},{6,0},{7,1},{8,14},{9,15},{10,... | collective-permute-start | bytes 3145736 | tf_op jit(solution)/shard_map/ppermute | solution.py:400
  503.2 25.2 %collective-permute-start.23 = (bf16[256,2048]{1,0:T(8,128)(2,1)S(1)}, bf16[256,2048]{1,0:T(8,128)(2,1)S(1)}, u32[]{:S(2)}, u32[]{:S(2)}) collective-permute-start(bf16[256,2048]{1,0:T(8,128)(2,1)S(1)} %get-tuple-element.114), channel_id=1, source_target_pairs={{0,2},{1,3},{2,0},{3,1},{4,6},{5,7},{6,4},{7,5},{8,10},{9,11},{10,... | collective-permute-start | bytes 3145736 | tf_op jit(solution)/shard_map/ppermute | solution.py:400
  503.9 26.1 %collective-permute-start.24 = (bf16[256,2048]{1,0:T(8,128)(2,1)S(1)}, bf16[256,2048]{1,0:T(8,128)(2,1)S(1)}, u32[]{:S(2)}, u32[]{:S(2)}) collective-permute-start(bf16[256,2048]{1,0:T(8,128)(2,1)S(1)} %get-tuple-element.114), channel_id=1, source_target_pairs={{0,4},{1,5},{2,6},{3,7},{4,0},{5,1},{6,2},{7,3},{8,12},{9,13},{10,... | collective-permute-start | bytes 3145736 | tf_op jit(solution)/shard_map/ppermute | solution.py:400
  505.0 46.3 %collective-permute-start.25 = (bf16[256,2048]{1,0:T(8,128)(2,1)S(1)}, bf16[256,2048]{1,0:T(8,128)(2,1)S(1)}, u32[]{:S(2)}, u32[]{:S(2)}) collective-permute-start(bf16[256,2048]{1,0:T(8,128)(2,1)S(1)} %get-tuple-element.114), channel_id=1, source_target_pairs={{0,6},{1,7},{2,4},{3,5},{4,2},{5,3},{6,0},{7,1},{8,14},{9,15},{10,... | collective-permute-start | bytes 3145736 | tf_op jit(solution)/shard_map/ppermute | solution.py:400
  553.6 7.2 collective-permute-start.26
  620.5 99.0 %reduce-scatter.5.cloned.1.call-start = ((), (), s32[]{:S(2)}) async-start(), calls=%async_computation.8 | async-start | bytes 1966080 | tf_op jit(solution)/shard_map/reduce_scatter | solution.py:406
  643.1 86.1 %collective-permute-start.33 = (bf16[2,2,256,2048]{3,2,1,0:T(8,128)(2,1)}, bf16[2,2,256,2048]{3,2,1,0:T(8,128)(2,1)}, u32[]{:S(2)}, u32[]{:S(2)}) collective-permute-start(bf16[2,2,256,2048]{3,2,1,0:T(8,128)(2,1)} %slice.226), channel_id=1, source_target_pairs={{0,1},{1,0},{2,3},{3,2},{4,5},{5,4},{6,7},{7,6},{8,9},{9,8},{10,11... | collective-permute-start | bytes 12582920 | tf_op jit(solution)/shard_map/ppermute | solution.py:400
  669.4 70.5 %collective-permute-start.27 = (bf16[2,2,256,2048]{3,2,1,0:T(8,128)(2,1)}, bf16[2,2,256,2048]{3,2,1,0:T(8,128)(2,1)}, u32[]{:S(2)}, u32[]{:S(2)}) collective-permute-start(bf16[2,2,256,2048]{3,2,1,0:T(8,128)(2,1)} %slice.220), channel_id=1, source_target_pairs={{0,1},{1,0},{2,3},{3,2},{4,5},{5,4},{6,7},{7,6},{8,9},{9,8},{10,11... | collective-permute-start | bytes 12582920 | tf_op jit(solution)/shard_map/ppermute | solution.py:400
  671.9 41.2 %collective-permute-start.41 = (bf16[256,1536]{1,0:T(8,128)(2,1)}, bf16[256,1536]{1,0:T(8,128)(2,1)}, u32[]{:S(2)}, u32[]{:S(2)}) collective-permute-start(bf16[256,1536]{1,0:T(8,128)(2,1)} %constant_dynamic-slice_fusion.8), channel_id=1, source_target_pairs={{0,4},{1,5},{2,6},{3,7},{4,0},{5,1},{6,2},{7,3},{8,12},{9,13},{10,... | collective-permute-start | bytes 2359304 | tf_op jit(solution)/shard_map/ppermute | solution.py:400
  675.6 38.8 %collective-permute-start.42 = (bf16[256,1536]{1,0:T(8,128)(2,1)}, bf16[256,1536]{1,0:T(8,128)(2,1)}, u32[]{:S(2)}, u32[]{:S(2)}) collective-permute-start(bf16[256,1536]{1,0:T(8,128)(2,1)} %constant_dynamic-slice_fusion.7), channel_id=1, source_target_pairs={{0,4},{1,5},{2,6},{3,7},{4,0},{5,1},{6,2},{7,3},{8,12},{9,13},{10,... | collective-permute-start | bytes 2359304 | tf_op jit(solution)/shard_map/ppermute | solution.py:400
  678.0 33.5 %collective-permute-start.40 = (bf16[256,256]{1,0:T(8,128)(2,1)S(1)}, bf16[256,256]{1,0:T(8,128)(2,1)S(1)}, u32[]{:S(2)}, u32[]{:S(2)}) collective-permute-start(bf16[256,256]{1,0:T(8,128)(2,1)S(1)} %constant_dynamic-slice_fusion.9), channel_id=1, source_target_pairs={{0,4},{1,5},{2,6},{3,7},{4,0},{5,1},{6,2},{7,3},{8,12},{9,13},{10,... | collective-permute-start | bytes 393224 | tf_op jit(solution)/shard_map/ppermute | solution.py:400
  736.4 47.3 %collective-permute-start.34 = (bf16[256,2048]{1,0:T(8,128)(2,1)}, bf16[256,2048]{1,0:T(8,128)(2,1)S(1)}, u32[]{:S(2)}, u32[]{:S(2)}) collective-permute-start(bf16[256,2048]{1,0:T(8,128)(2,1)} %get-tuple-element.133), channel_id=1, source_target_pairs={{0,2},{1,3},{2,0},{3,1},{4,6},{5,7},{6,4},{7,5},{8,10},{9,11},{10,... | collective-permute-start | bytes 3145736 | tf_op jit(solution)/shard_map/ppermute | solution.py:400
  736.6 48.1 %collective-permute-start.35 = (bf16[256,2048]{1,0:T(8,128)(2,1)}, bf16[256,2048]{1,0:T(8,128)(2,1)S(1)}, u32[]{:S(2)}, u32[]{:S(2)}) collective-permute-start(bf16[256,2048]{1,0:T(8,128)(2,1)} %get-tuple-element.135), channel_id=1, source_target_pairs={{0,4},{1,5},{2,6},{3,7},{4,0},{5,1},{6,2},{7,3},{8,12},{9,13},{10,... | collective-permute-start | bytes 3145736 | tf_op jit(solution)/shard_map/ppermute | solution.py:400
  738.0 48.7 %collective-permute-start.36 = (bf16[256,2048]{1,0:T(8,128)(2,1)S(1)}, bf16[256,2048]{1,0:T(8,128)(2,1)S(1)}, u32[]{:S(2)}, u32[]{:S(2)}) collective-permute-start(bf16[256,2048]{1,0:T(8,128)(2,1)S(1)} %get-tuple-element.134), channel_id=1, source_target_pairs={{0,6},{1,7},{2,4},{3,5},{4,2},{5,3},{6,0},{7,1},{8,14},{9,15},{10,... | collective-permute-start | bytes 3145736 | tf_op jit(solution)/shard_map/ppermute | solution.py:400
  754.3 108.1 %collective-permute-start.28 = (bf16[256,2048]{1,0:T(8,128)(2,1)}, bf16[256,2048]{1,0:T(8,128)(2,1)}, u32[]{:S(2)}, u32[]{:S(2)}) collective-permute-start(bf16[256,2048]{1,0:T(8,128)(2,1)} %get-tuple-element.140), channel_id=1, source_target_pairs={{0,2},{1,3},{2,0},{3,1},{4,6},{5,7},{6,4},{7,5},{8,10},{9,11},{10,... | collective-permute-start | bytes 3145736 | tf_op jit(solution)/shard_map/ppermute | solution.py:400
  754.5 107.9 %collective-permute-start.29 = (bf16[256,2048]{1,0:T(8,128)(2,1)}, bf16[256,2048]{1,0:T(8,128)(2,1)}, u32[]{:S(2)}, u32[]{:S(2)}) collective-permute-start(bf16[256,2048]{1,0:T(8,128)(2,1)} %get-tuple-element.142), channel_id=1, source_target_pairs={{0,4},{1,5},{2,6},{3,7},{4,0},{5,1},{6,2},{7,3},{8,12},{9,13},{10,... | collective-permute-start | bytes 3145736 | tf_op jit(solution)/shard_map/ppermute | solution.py:400
  783.6 78.8 %collective-permute-start.30 = (bf16[256,2048]{1,0:T(8,128)(2,1)}, bf16[256,2048]{1,0:T(8,128)(2,1)}, u32[]{:S(2)}, u32[]{:S(2)}) collective-permute-start(bf16[256,2048]{1,0:T(8,128)(2,1)} %get-tuple-element.141), channel_id=1, source_target_pairs={{0,6},{1,7},{2,4},{3,5},{4,2},{5,3},{6,0},{7,1},{8,14},{9,15},{10,... | collective-permute-start | bytes 3145736 | tf_op jit(solution)/shard_map/ppermute | solution.py:400
  861.2 26.3 %collective-permute-start.37 = (bf16[256,2048]{1,0:T(8,128)(2,1)}, bf16[256,2048]{1,0:T(8,128)(2,1)}, u32[]{:S(2)}, u32[]{:S(2)}) collective-permute-start(bf16[256,2048]{1,0:T(8,128)(2,1)} %fusion.12), channel_id=1, source_target_pairs={{0,2},{1,3},{2,0},{3,1},{4,6},{5,7},{6,4},{7,5},{8,10},{9,11},{10,... | collective-permute-start | bytes 3145736 | tf_op jit(solution)/shard_map/ppermute | solution.py:400
  865.9 43.2 %collective-permute-start.31 = (bf16[256,2048]{1,0:T(8,128)(2,1)S(1)}, bf16[256,2048]{1,0:T(8,128)(2,1)}, u32[]{:S(2)}, u32[]{:S(2)}) collective-permute-start(bf16[256,2048]{1,0:T(8,128)(2,1)S(1)} %fusion.23), channel_id=1, source_target_pairs={{0,2},{1,3},{2,0},{3,1},{4,6},{5,7},{6,4},{7,5},{8,10},{9,11},{10,... | collective-permute-start | bytes 3145736 | tf_op jit(solution)/shard_map/ppermute | solution.py:400
  889.4 29.3 %collective-permute-start.38 = (bf16[2,256,2048]{2,1,0:T(8,128)(2,1)S(1)}, bf16[2,256,2048]{2,1,0:T(8,128)(2,1)S(1)}, u32[]{:S(2)}, u32[]{:S(2)}) collective-permute-start(bf16[2,256,2048]{2,1,0:T(8,128)(2,1)S(1)} %get-tuple-element.160), channel_id=1, source_target_pairs={{0,1},{1,0},{2,3},{3,2},{4,5},{5,4},{6,7},{7,6},{8,9},{9,8},{10,11... | collective-permute-start | bytes 6291464 | tf_op jit(solution)/shard_map/ppermute | solution.py:400
  910.8 9.5 %collective-permute-start.32 = (bf16[2,256,2048]{2,1,0:T(8,128)(2,1)S(1)}, bf16[2,256,2048]{2,1,0:T(8,128)(2,1)S(1)}, u32[]{:S(2)}, u32[]{:S(2)}) collective-permute-start(bf16[2,256,2048]{2,1,0:T(8,128)(2,1)S(1)} %get-tuple-element.162), channel_id=1, source_target_pairs={{0,1},{1,0},{2,3},{3,2},{4,5},{5,4},{6,7},{7,6},{8,9},{9,8},{10,11... | collective-permute-start | bytes 6291464 | tf_op jit(solution)/shard_map/ppermute | solution.py:400
  (97 other events, 671.5 us)
Sparse Core Ops, SparseCore 0:
  22.8 39.0 all-gather.4
  72.5 28.9 all-gather.6
  103.6 114.8 all-gather.8
  220.5 113.6 all-gather.10
  385.3 111.0 reduce-scatter.8
  498.6 111.2 reduce-scatter.10
  620.6 27.4 reduce-scatter.6
  650.5 33.9 reduce-scatter.4

commit v3 on v2

--- a/solution.py
+++ b/solution.py
@@ -259,26 +259,36 @@
         name="swiglu_part",
     )(*ins)
 
-def grad_body(n2_ref, cot_ref, dgu_ref, act_ref, o_ref):
-    size = act_ref.shape[1]
-    o_ref[:, : 2 * size] = dot(n2_ref[...], dgu_ref[...], 0, 0).astype(BF)
-    o_ref[:, 2 * size :] = dot(cot_ref[...], act_ref[...], 0, 0).astype(BF)
+def grad_body(n2a, n2b, cota, cotb, dgua, dgub, acta, actb, o_ref):
+    size = acta.shape[1]
+    gu = dot(n2a[...], dgua[...], 0, 0) + dot(n2b[...], dgub[...], 0, 0)
+    o_ref[:, : 2 * size] = gu.astype(BF)
+    dt = dot(cota[...], acta[...], 0, 0) + dot(cotb[...], actb[...], 0, 0)
+    o_ref[:, 2 * size :] = dt.astype(BF)
+
 
 def ffn_grads(n2, cot, dgu, act, tile=256):
-    count, width = n2.shape
-    size = act.shape[1]
+    count, width = n2[0].shape
+    size = act[0].shape[1]
     col = lambda i: (0, i)
     full = lambda i: (0, 0)
     return pl.pallas_call(
         grad_body,
         grid=(width // tile,),
-        in_specs=[pl.BlockSpec((count, tile), col), pl.BlockSpec((count, tile), col), pl.BlockSpec((count, 2 * size), full, pipeline_mode=pl.Buffered(1)), pl.BlockSpec((count, size), full, pipeline_mode=pl.Buffered(1))],
+        in_specs=[pl.BlockSpec((count, tile), col)] * 4
+        + [pl.BlockSpec((count, 2 * size), full, pipeline_mode=pl.Buffered(1))] * 2
+        + [pl.BlockSpec((count, size), full, pipeline_mode=pl.Buffered(1))] * 2,
         out_specs=pl.BlockSpec((tile, 3 * size), lambda i: (i, 0)),
         out_shape=jax.ShapeDtypeStruct((width, 3 * size), BF),
         compiler_params=pltpu.CompilerParams(vmem_limit_bytes=VMEM),
-        cost_estimate=pl.CostEstimate(flops=2 * count * width * size * 3, bytes_accessed=8 * count * width, transcendentals=0),
+        cost_estimate=pl.CostEstimate(
+            flops=4 * count * width * size * 3,
+            bytes_accessed=16 * count * width,
+            transcendentals=0,
+        ),
         name="swiglu_grads",
-    )(n2, cot, dgu, act)
+    )(*n2, *cot, *dgu, *act)
+
 
 def out_body(*refs):
     count = len(refs) // 2
@@ -371,8 +381,8 @@
     )(values)
 
 
-def after(value, *others):
-    return lax.optimization_barrier((value,) + others)[0]
+def after(*values):
+    return lax.optimization_barrier(values)
 
 
 def inverse_rms(values):
@@ -407,23 +417,34 @@
             whole, "dp", scatter_dimension=0, tiled=True, axis_index_groups=zgroups
         )
 
-    def sum_to_owner(partial):
-        even = partial[:, 0::2]
-        odd = partial[:, 1::2].astype(BF)
-        paired = even.astype(F32) + swap(odd, 0, 1).astype(F32)
-        low = paired.astype(BF)
-        from_y = swap(low[0, 1], 0, 2)
-        from_x = swap(low[1, 0], 1, 0)
-        from_d = swap(low[1, 1], 1, 2)
-        return paired[0, 0] + from_y.astype(F32) + from_x.astype(F32) + from_d.astype(F32)
-
-    def spread(own):
+
+    def sum_to_owner(even, odd, between=None):
+        got = swap(odd, 0, 1)
+
+        def pair(k):
+            return even[k].astype(F32) + got[k].astype(F32)
+
+        from_d = swap(pair(3).astype(BF), 1, 2)
+        from_y = swap(pair(1).astype(BF), 0, 2)
+        from_x = swap(pair(2).astype(BF), 1, 0)
+        filler = None
+        if between is not None:
+            filler = between(got)
+            from_d, from_y, from_x, filler = after(from_d, from_y, from_x, filler)
+        result = pair(0) + from_y.astype(F32) + from_x.astype(F32) + from_d.astype(F32)
+        return result if between is None else (result, filler)
+
+    def spread(own, between=None):
+        from_d = swap(own, 1, 2)
         from_y = swap(own, 0, 2)
         from_x = swap(own, 1, 0)
-        from_d = swap(own, 1, 2)
+        if between is not None:
+            filler = between(own)
+            from_d, from_y, from_x, filler = after(from_d, from_y, from_x, filler)
+            mine = jnp.stack([own, from_y, from_x, from_d])
+            return mine, swap(mine, 0, 1), filler
         mine = jnp.stack([own, from_y, from_x, from_d])
-        theirs = swap(mine, 0, 1)
-        return jnp.stack([mine, theirs], axis=1).reshape((2, shards) + own.shape)
+        return mine, swap(mine, 0, 1)
 
     def on_device(
         tokens,
@@ -468,16 +489,41 @@
             second = jnp.where(x == 0, theirs, mine)
             return jnp.concatenate([first, second], axis=axis)
 
+        def natural(parts):
+            stacked = jnp.stack(parts)
+            return jnp.concatenate(
+                [
+                    lax.dynamic_index_in_dim(stacked, me ^ q, axis=0, keepdims=False)
+                    for q in range(shards)
+                ],
+                axis=0,
+            )
+
+        def cut(values, ds):
+            return lax.dynamic_slice_in_dim(values, (me ^ ds) * quarter, quarter, axis=0)
+
+        def halves(own, other):
+            return [
+                jnp.stack([cut(own, dc), cut(own, dc + 2), cut(other, dc), cut(other, dc + 2)])
+                for dc in (0, 1)
+            ]
+
+        def streams(mine, theirs):
+            return [
+                natural([mine[k], theirs[k], mine[k + 1], theirs[k + 1]]) for k in (0, 2)
+            ]
+
+        def flat(values):
+            return values.reshape(-1, values.shape[-1])
+
         low_q = w_query.astype(BF)
         low_k = w_key.astype(BF)
         low_v = w_value.astype(BF)
-        low_o = w_output.astype(BF).T
-        low_g = w_gate.astype(BF)
-        low_u = w_up.astype(BF)
-        low_d = w_down.astype(BF).T
 
         def attn_half(which):
-            return jnp.concatenate([half(low_q, which), half(low_k, which), half(low_v, which)], axis=1)
+            return jnp.concatenate(
+                [half(low_q, which), half(low_k, which), half(low_v, which)], axis=1
+            )
 
         cols = low_q.shape[1] // 2 + low_k.shape[1]
         gains = jnp.stack([gain_first, gain_second]).astype(BF)
@@ -493,10 +539,14 @@
         gain_one = tails[:, :, 0, :rows].reshape(1, width).astype(F32)
         gain_two = tails[:, :, 1, :rows].reshape(1, width).astype(F32)
 
-        tokens_mine = lax.dynamic_slice_in_dim(tokens, me * quarter, quarter, axis=0)
-        tokens_x = swap(after(tokens_mine, sent), 1, 0)
-        out_x = swap(after(half(low_o, 1 - x), sent), 1, 0)
-        out_weight = gather(ordered(half(low_o, x), out_x))
+        low_o, w_g, w_u, w_d = after((w_output, w_gate, w_up, w_down), sent)[0]
+        low_o = low_o.astype(BF).T
+        low_g = w_g.astype(BF)
+        low_u = w_u.astype(BF)
+        low_d = w_d.astype(BF).T
+        tokens_x = swap(after(cut(tokens, 0), sent)[0], 1, 0)
+        blocks_x = swap(block_ids, 1, 0)
+        out_x = swap(half(low_o, 1 - x), 1, 0)
         size = low_g.shape[1] // 2 // CHUNKS
 
         def ffn_part(which, j):
@@ -505,124 +555,136 @@
                 axis=1,
             )
 
-        ffn_weights = []
-        previous = (tokens_x, out_x)
-        for j in range(CHUNKS):
-            ffn_x = swap(after(ffn_part(1 - x, j), *previous), 1, 0)
-            previous = (ffn_x,)
-            ffn_weights.append(gather(ordered(ffn_part(x, j), ffn_x)))
-
-        def natural_index(values):
-            return jnp.concatenate(
-                [
-                    lax.dynamic_index_in_dim(values, me ^ q, axis=0, keepdims=False)
-                    for q in range(shards)
-                ],
-                axis=0,
-            )
-
         def rest_of(from_x):
             from_xy = swap(from_x, 0, 2)
-            pair = jnp.stack([from_x, from_xy])
-            return jnp.stack([pair, swap(pair, 0, 1)], axis=1).reshape((shards,) + from_x.shape)
-
-        both = jnp.concatenate([tokens, natural_index(rest_of(tokens_x))], axis=0)
-        blocks = jnp.concatenate([block_ids, swap(block_ids, 1, 0)], axis=0)
-        block_rows = blocks[:, None, :]
-        block_cols = blocks.reshape(2 * length, 1)
-
-        def to_relative(values):
-            values = values.reshape(2, length, values.shape[-1])
-            parts = [
-                lax.dynamic_slice_in_dim(values, (me ^ ds) * quarter, quarter, axis=1)
-                for ds in range(shards)
-            ]
-            return jnp.stack(parts, axis=1)
-
-        def to_natural(values):
-            parts = [
-                lax.dynamic_index_in_dim(values, me ^ q, axis=1, keepdims=False)
-                for q in range(shards)
-            ]
-            return jnp.concatenate(parts, axis=1)
-
-        cot_own = jnp.stack(
-            [
-                lax.dynamic_slice_in_dim(cotangent, (me ^ ds) * quarter, quarter, axis=0)
-                for ds in range(shards)
-            ]
-        )
-        cot_x = swap(after(cot_own[0], *previous), 1, 0)
-        cot_rel = jnp.concatenate([cot_own, rest_of(cot_x)], axis=0).reshape(2 * length, width)
+            other = swap(jnp.stack([from_x, from_xy]), 0, 1)
+            return [from_x, other[0], from_xy, other[1]]
+
+        out_weight = gather(ordered(half(low_o, x), out_x))
+        send_first, _, _ = after(ffn_part(1 - x, 0), tokens_x, out_x)
+        first_x = swap(send_first, 1, 0)
+        ffn_weights = [gather(ordered(ffn_part(x, 0), first_x))]
+        cot_x = swap(after(cut(cotangent, 0), first_x)[0], 1, 0)
+        second_x = swap(after(ffn_part(1 - x, 1), cot_x)[0], 1, 0)
+        ffn_weights.append(gather(ordered(ffn_part(x, 1), second_x)))
 
         cosine, sine = rope_tables(length, group)
-        normed, query, key, value = qkv(both, gain_one, qkv_weight, cosine, sine, group)
-        mixed, lse = attend(query, key, value, block_rows, block_cols, length)
-        mixed_rel = to_relative(mixed).reshape(2 * length, group * HD)
-        partial = jnp.einsum("tk,dk->td", mixed_rel, out_weight, preferred_element_type=F32)
-        summed = sum_to_owner(partial.astype(BF).reshape(2, shards, quarter, width))
-        tokens_own = lax.dynamic_slice_in_dim(tokens, me * quarter, quarter, axis=0).astype(F32)
+
+        def forward(own_tokens, own_blocks):
+            normed, query, key, value = qkv(own_tokens, gain_one, qkv_weight, cosine, sine, group)
+            block_rows = own_blocks[:, None, :]
+            block_cols = own_blocks.reshape(length, 1)
+            mixed, lse = attend(query, key, value, block_rows, block_cols, length)
+            return normed, mixed, (query, key, value, block_rows, block_cols, lse)
+
+        normed_own, mixed_own, saved_own = forward(tokens, block_ids)
+        other_tokens = natural(rest_of(tokens_x))
+        other_tokens, _, _ = after(other_tokens, cot_x, mixed_own)
+        normed_other, mixed_other, saved_other = forward(other_tokens, blocks_x)
+        cot_rest = rest_of(cot_x)
+        mixed_own, mixed_other, cot_rest, second_x = after(
+            mixed_own, mixed_other, cot_rest, second_x
+        )
+        cot_mine = flat(jnp.stack([cut(cotangent, 0), cut(cotangent, 2), cot_rest[0], cot_rest[2]]))
+        cot_theirs = flat(
+            jnp.stack([cut(cotangent, 1), cut(cotangent, 3), cot_rest[1], cot_rest[3]])
+        )
+        mixed_mine, mixed_theirs = halves(mixed_own, mixed_other)
+
+        def project(values, weight):
+            partial = jnp.einsum("atk,dk->atd", values, weight, preferred_element_type=F32)
+            return partial.astype(BF)
+
+        summed = sum_to_owner(project(mixed_mine, out_weight), project(mixed_theirs, out_weight))
+        tokens_own = cut(tokens, 0).astype(F32)
         hidden = tokens_own + summed
         inverse_second = inverse_rms(hidden)
-        normed_two_own = (hidden * inverse_second * gain_two).astype(BF)
-        normed_two = spread(normed_two_own).reshape(2 * length, width)
-
-        shape = (2, shards, quarter, width)
-        grads_ffn = []
-        acts = []
-        partial_two = None
+        mine, theirs = spread((hidden * inverse_second * gain_two).astype(BF))
+        two_mine, two_theirs = flat(mine), flat(theirs)
+
+        shape = (4, quarter, width)
+        acts_mine = []
+        acts_theirs = []
+        part_mine = part_theirs = None
+        first_grads = None
         for j in range(CHUNKS):
             last = j == CHUNKS - 1
-            act, grad_gu, partial_two = up_back(
-                normed_two, cot_rel, ffn_weights[j], partial_two, last
+            weight = ffn_weights[j]
+            theirs_in = two_theirs
+            if first_grads is not None:
+                theirs_in, first_grads = after(two_theirs, first_grads)
+            act_theirs, gu_theirs, part_theirs = up_back(
+                theirs_in, cot_theirs, weight, part_theirs, last
             )
-            acts.append(act)
-            grads_ffn.append(scatter(ffn_grads(normed_two, cot_rel, grad_gu, act)))
-        grad_normed_two = sum_to_owner(partial_two.reshape(shape))
-        cot_mine = cot_own[0].astype(F32)
+            mine_in = two_mine
+            if last:
+                mine_in, part_theirs = after(two_mine, part_theirs)
+            act_mine, gu_mine, part_mine = up_back(mine_in, cot_mine, weight, part_mine, last)
+            acts_mine.append(act_mine)
+            acts_theirs.append(act_theirs)
+
+            def part_grads(token=None):
+                gu = gu_mine if token is None else after(gu_mine, token)[0]
+                return ffn_grads(
+                    (two_mine, two_theirs),
+                    (cot_mine, cot_theirs),
+                    (gu, gu_theirs),
+                    (act_mine, act_theirs),
+                )
+
+            if not last:
+                first_grads = part_grads()
+        grad_normed_two, last_grads = sum_to_owner(
+            part_mine.reshape(shape), part_theirs.reshape(shape), part_grads
+        )
+        first_piece = scatter(first_grads)
+        last_piece = scatter(last_grads)
         gain_grad_two, grad_through = norm_back(hidden, inverse_second, gain_two, grad_normed_two)
-        grad_hidden = cot_mine + grad_through
-        grad_hidden_rel = spread(grad_hidden.astype(BF)).reshape(2 * length, width)
+        grad_hidden = cut(cotangent, 0).astype(F32) + grad_through
+
+        def outputs(token):
+            return tuple(
+                down([after(a, token)[0] for a in acts], ffn_weights)
+                for acts in (acts_mine, acts_theirs)
+            )
+
+        gh_mine, gh_theirs, (out_mine, out_theirs) = spread(grad_hidden.astype(BF), outputs)
 
         def to_sequence(own):
-            from_y = swap(own, 0, 2)
-            mine = jnp.stack([own, from_y])
-            theirs = swap(mine, 0, 1)
-            rel = jnp.stack([mine, theirs], axis=1).reshape((1, shards) + own.shape)
-            return to_natural(rel)[0]
-
-        result = after(down(acts, ffn_weights), grad_hidden_rel)
-        output_own = (hidden + sum_to_owner(result.reshape(shape))).astype(BF)
-        output = to_sequence(output_own)
-
-        d_out = jnp.einsum("td,tk->dk", grad_hidden_rel, mixed_rel, preferred_element_type=F32)
+            pair = jnp.stack([own, swap(own, 0, 2)])
+            other = swap(pair, 0, 1)
+            return natural([pair[0], other[0], pair[1], other[1]])
+
+        grad_mixed_mine = project(gh_mine, out_weight.T)
+        grad_mixed_theirs = project(gh_theirs, out_weight.T)
+        grad_mixed = streams(grad_mixed_mine, grad_mixed_theirs)
+        grad_mixed, first_piece = after(grad_mixed, first_piece)
+        backs = [
+            attend_back(*saved, grad_mixed[k], cosine, sine, length)
+            for k, saved in enumerate((saved_own, saved_other))
+        ]
+        grad_qkv = [jnp.concatenate(pair, axis=1) for pair in backs]
+        d_out = jnp.einsum("atd,atk->dk", gh_mine, mixed_mine, preferred_element_type=F32)
+        d_out = d_out + jnp.einsum(
+            "atd,atk->dk", gh_theirs, mixed_theirs, preferred_element_type=F32
+        )
         grad_out = scatter(d_out.astype(BF))
-        grad_mixed = jnp.dot(grad_hidden_rel, out_weight, preferred_element_type=F32).astype(BF)
-        grad_mixed = to_natural(grad_mixed.reshape(2, shards, quarter, group * HD))
-        grad_q, grad_kv = attend_back(
-            query,
-            key,
-            value,
-            block_rows,
-            block_cols,
-            lse,
-            grad_mixed.reshape(2 * length, group * HD),
-            cosine,
-            sine,
-            length,
-        )
-        grad_qkv = jnp.concatenate([grad_q, grad_kv], axis=1)
-        d_qkv = jnp.einsum(
-            "tc,tk->ck", normed, grad_qkv, preferred_element_type=F32
-        ).astype(BF)
+        d_qkv = jnp.einsum("tc,tk->ck", normed_own, grad_qkv[0], preferred_element_type=F32)
+        d_qkv = d_qkv + jnp.einsum(
+            "tc,tk->ck", normed_other, grad_qkv[1], preferred_element_type=F32
+        )
+        d_qkv = d_qkv.astype(BF)
         grad_qkv_w = scatter(d_qkv)
-        partial_one = jnp.einsum(
-            "tk,ck->tc",
-            after(to_relative(grad_qkv).reshape(2 * length, cols), d_qkv),
-            qkv_weight,
-            preferred_element_type=F32,
-        )
-        grad_normed = sum_to_owner(partial_one.astype(BF).reshape(shape))
+        gq_mine, gq_theirs = halves(*grad_qkv)
+        gq_mine, gq_theirs, _ = after(gq_mine, gq_theirs, d_qkv)
+        grad_normed, last_piece = sum_to_owner(
+            project(gq_mine, qkv_weight), project(gq_theirs, qkv_weight), lambda token: last_piece
+        )
+
+        out_theirs, _ = after(out_theirs, gh_theirs)
+        output_own = hidden + sum_to_owner(out_mine.reshape(shape), out_theirs.reshape(shape))
+        output = to_sequence(output_own.astype(BF))
+
         inverse_own = inverse_rms(tokens_own)
         gain_grad_one, grad_inner = norm_back(tokens_own, inverse_own, gain_one, grad_normed)
         input_grad = to_sequence((grad_hidden + grad_inner).astype(BF)).astype(F32)
@@ -635,35 +697,40 @@
         def joined(mine, theirs):
             return ordered(mine, theirs, axis=1).astype(F32)
 
+        first_piece, _ = after(first_piece, d_qkv)
+        pairs = [owned_halves(first_piece), owned_halves(last_piece)]
+        grad_out, pairs = after(grad_out, pairs)
+        mine, theirs = owned_halves(grad_out)
+        grad_qkv_w, theirs = after(grad_qkv_w, theirs)
+        own_o = joined(mine, theirs).T
+        own_gud = []
+        for part in range(3):
+            span = slice(part * size, (part + 1) * size)
+            own_gud.append(
+                joined(
+                    jnp.concatenate([m[:, span] for m, t in pairs], axis=1),
+                    jnp.concatenate([t[:, span] for m, t in pairs], axis=1),
+                )
+            )
+        own_g, own_u, own_d = own_gud[0], own_gud[1], own_gud[2].T
+        gain_grads = jnp.stack([gain_grad_one, gain_grad_two]).reshape(-1, 128)
+        gain_grads, output = after(gain_grads, output)
+        gain_grads = sum_all(gain_grads, dps, shards, 1).reshape(2, width)
+        gain_grads = lax.dynamic_slice_in_dim(gain_grads, dp * rows, rows, axis=1)
         mine, theirs = owned_halves(grad_qkv_w)
         qc = group * HD
         own_q = joined(mine[:, :qc], theirs[:, :qc])
         own_k = joined(mine[:, qc : qc + HD], theirs[:, qc : qc + HD])
         own_v = joined(mine[:, qc + HD :], theirs[:, qc + HD :])
-        mine, theirs = owned_halves(grad_out)
-        own_o = joined(mine, theirs).T
-        pairs = [owned_halves(piece) for piece in grads_ffn]
-        own_gud = []
-        for part in range(3):
-            cut = slice(part * size, (part + 1) * size)
-            own_gud.append(
-                joined(
-                    jnp.concatenate([m[:, cut] for m, t in pairs], axis=1),
-                    jnp.concatenate([t[:, cut] for m, t in pairs], axis=1),
-                )
-            )
-        own_g, own_u, own_d = own_gud[0], own_gud[1], own_gud[2].T
-        gain_grads = sum_all(
-            jnp.stack([gain_grad_one, gain_grad_two]).reshape(-1, 128), dps, shards, 1
-        ).reshape(2, width)
-        gain_grads = lax.dynamic_slice_in_dim(gain_grads, dp * rows, rows, axis=1)
         owned = (gain_grads[0], own_q, own_k, own_v, own_o, gain_grads[1], own_g, own_u, own_d)
 
         first_shard = (me == 0).astype(F32)
         squares = first_shard * (jnp.sum(owned[0] * owned[0]) + jnp.sum(owned[5] * owned[5]))
         for position in (1, 2, 3, 4, 6, 7, 8):
             squares = squares + jnp.sum(owned[position] * owned[position])
-        squares = sum_all(jnp.broadcast_to(squares, (8, 128)), dps, shards, 2)
+        squares = jnp.broadcast_to(squares, (8, 128))
+        squares, input_grad = after(squares, input_grad)
+        squares = sum_all(squares, dps, shards, 2)
         global_norm = jnp.sqrt(squares[0, 0])
         factor = jnp.minimum(1.0, CLIP / global_norm)
         rate_now = rate * jnp.minimum(1.0, (step.astype(F32) + 1.0) / WARMUP)

time: 943 us -> 798 us (0.85)
  waiting for transfers between devices: 362 us -> 277 us
  local copies, waits for them, and re-layouts: 121 us -> 76.7 us
  Pallas kernels: 225 us -> 214 us
  other arithmetic: 135 us -> 124 us
    ppermute x43, waiting for transfers between devices: 362 us -> 272 us  [swap(): return lax.ppermute(values, axes, pairs)]
    pallas_call x2, Pallas kernels: 53.5 us -> 27.4 us  [sum_all(): pl.pallas_call(functools.partial(sum_body, dps, shards), in_specs=[pl.Blo...]
    add x3 -> x0, other arithmetic: 22.7 us -> none  [sum_to_owner(): paired = even.astype(F32) + swap(odd, 0, 1).astype(F32)]
    unnamed x208 -> x249, local copies, waits for them, and re-layouts: 48 us -> 30 us
    another operation x7 -> x5, local copies, waits for them, and re-layouts: 20.3 us -> 5.87 us  [the longest x1 4.11 us: on_device(): jnp.stack([cut(cotangent, 1), cut(cotangent, 3), cot_rest[1], cot_rest[3]])]
    pallas_call x2 -> x4, Pallas kernels: 59.5 us -> 70.9 us  [up_back(): pl.pallas_call(functools.partial(up_body, prev is None, last), grid=(coun...]
    another operation x17 -> x16, other arithmetic: 34.7 us -> 23.8 us  [the longest x2 5.47 us: to_sequence(): pair = jnp.stack([own, swap(own, 0, 2)])]
    dot_general x5 -> x10, matrix products: 27.3 us -> 33.7 us  [the longest x6 19.5 us: project(): jnp.einsum('atk,dk->atd', values, weight, preferred_element_type=F32)]
  transfers between devices with their start and end apart: 51 -> 51, of which waited for: 28 -> 24; matrix products, arithmetic and copies ran while one was open for 27% -> 23% of each run, Pallas kernels for 24% -> 25%
where the time goes in v3:
time: 798 us; the launch traced here: 791 us
  waiting for transfers between devices  277 us (35%)
  Pallas kernels  214 us (27%)
  other arithmetic  124 us (16%)
  local copies, waits for them, and re-layouts  76.7 us (10%)
  starting transfers between devices  41.2 us (5%)
  matrix products  33.7 us (4%)
  between operations  24.9 us (3%)
    ppermute x43, waiting for transfers between devices, swap(): return lax.ppermute(values, axes, pairs)  272 us
    pallas_call x4, Pallas kernels, up_back(): pl.pallas_call(functools.partial(up_body, prev is None, last), grid=(coun...  70.9 us
    ppermute x43, starting transfers between devices, swap(): return lax.ppermute(values, axes, pairs)  39.9 us
    pallas_call x2, Pallas kernels, ffn_grads(): pl.pallas_call(grad_body, grid=(width // tile,), in_specs=[pl.BlockSpec((...  36.3 us
    unnamed x249, local copies, waits for them, and re-layouts  30 us
    pallas_call x2, Pallas kernels, attend_back(): pl.pallas_call(functools.partial(bwd_body, limits), grid=(seqs, per), in_...  29.6 us
    pallas_call x2, Pallas kernels, sum_all(): pl.pallas_call(functools.partial(sum_body, dps, shards), in_specs=[pl.Blo...  27.4 us
    dot_general x6, matrix products, project(): jnp.einsum('atk,dk->atd', values, weight, preferred_element_type=F32)  19.5 us
  transfers between devices with their start and end apart: 51, of which 24 were waited for; matrix products, arithmetic and copies ran while one was open for 23% of the time, Pallas kernels for 25%

profile of v3, /device:TPU:0, one launch (start us, length us, event | category | flops | bytes accessed | tf_op | source)
XLA Modules:
  0.0 790.7 jit_solution(16827872359334541237)
XLA Ops:
  14.9 5.2 collective-permute-done
  25.2 4.1 dynamic-slice_bitcast_fusion.9
  42.0 8.1 %collective-permute-done.1 = bf16[256,2048]{1,0:T(8,128)(2,1)} collective-permute-done((bf16[256,2048]{1,0:T(8,128)(2,1)S(1)}, bf16[256,2048]{1,0:T(8,128)(2,1)}, u32[]{:S(2)}, u32[]{:S(2)}) %collective-permute-start.1) | collective-permute-done | bytes 1048608 | tf_op jit(solution)/shard_map/ppermute | solution.py:410
  77.3 14.3 %collective-permute-done.6 = bf16[256,2048]{1,0:T(8,128)(2,1)} collective-permute-done((bf16[256,2048]{1,0:T(8,128)(2,1)S(1)}, bf16[256,2048]{1,0:T(8,128)(2,1)}, u32[]{:S(2)}, u32[]{:S(2)}) %collective-permute-start.6) | collective-permute-done | bytes 1048608 | tf_op jit(solution)/shard_map/ppermute | solution.py:410
  97.8 8.1 %qkv_rope.2 = (bf16[1024,2048]{1,0:T(8,128)(2,1)}, bf16[4,1024,64]{2,1,0:T(8,128)(2,1)S(1)}, bf16[1024,64]{1,0:T(8,128)(2,1)S(1)}, bf16[1024,64]{1,0:T(8,128)(2,1)S(1)}) custom-call(bf16[1024,2048]{1,0:T(8,128)(2,1)} %tok_ref.1, f32[1,2048]{1,0:T(1,128)S(1)} %reshape.244.gain_ref, bf16[2048,384]{1,0:T(8,128)(2,1)S(1)} %bitcast.256, ...), custom_call_target="tpu_custom_call" | custom-call | flops 1610612736 | bytes 8388608 | tf_op jit(solution)/shard_map/qkv_rope/pallas_call | solution.py:55
  105.9 8.2 %attend.2 = (bf16[1024,256]{1,0:T(8,128)(2,1)S(1)}, f32[1024,4]{1,0:T(8,128)S(1)}) custom-call(bf16[4,1024,64]{2,1,0:T(8,128)(2,1)S(1)} %get-tuple-element.104.q_ref, bf16[1024,64]{1,0:T(8,128)(2,1)S(1)} %get-tuple-element.105.k_ref, bf16[1024,64]{1,0:T(8,128)(2,1)S(1)} %get-tuple-element.106.v_ref, s32[1,1,1024]{2,1,0:T(1,128)S(1)} %bitcast.261, ...), custom_call_target="tpu_custom_call" | custom-call | flops 4294967296 | bytes 2097152 | tf_op jit(solution)/shard_map/attend/pallas_call | solution.py:112
  123.1 7.9 qkv_rope.3
  131.0 8.4 %attend.3 = (bf16[1024,256]{1,0:T(8,128)(2,1)S(1)}, f32[1024,4]{1,0:T(8,128)S(1)}) custom-call(bf16[4,1024,64]{2,1,0:T(8,128)(2,1)S(1)} %get-tuple-element.117.q_ref, bf16[1024,64]{1,0:T(8,128)(2,1)S(1)} %get-tuple-element.118.k_ref, bf16[1024,64]{1,0:T(8,128)(2,1)S(1)} %get-tuple-element.119.v_ref, s32[1,1,1024]{2,1,0:T(1,128)S(1)} %bitcast.264, ...), custom_call_target="tpu_custom_call" | custom-call | flops 4294967296 | bytes 2097152 | tf_op jit(solution)/shard_map/attend/pallas_call | solution.py:112
  147.4 5.4 collective-permute-done.11
  162.5 19.1 %collective-permute-done.12 = bf16[256,2048]{1,0:T(8,128)(2,1)} collective-permute-done((bf16[256,2048]{1,0:T(8,128)(2,1)}, bf16[256,2048]{1,0:T(8,128)(2,1)}, u32[]{:S(2)}, u32[]{:S(2)}) %collective-permute-start.12) | collective-permute-done | bytes 1048608 | tf_op jit(solution)/shard_map/ppermute | solution.py:410
  183.0 22.3 %collective-permute-done.14 = bf16[256,2048]{1,0:T(8,128)(2,1)} collective-permute-done((bf16[256,2048]{1,0:T(8,128)(2,1)}, bf16[256,2048]{1,0:T(8,128)(2,1)}, u32[]{:S(2)}, u32[]{:S(2)}) %collective-permute-start.14) | collective-permute-done | bytes 1048608 | tf_op jit(solution)/shard_map/ppermute | solution.py:410
  205.3 3.8 multiply_reduce_fusion.2
  213.1 21.4 %collective-permute-done.15 = bf16[256,2048]{1,0:T(8,128)(2,1)S(1)} collective-permute-done((bf16[256,2048]{1,0:T(8,128)(2,1)S(1)}, bf16[256,2048]{1,0:T(8,128)(2,1)S(1)}, u32[]{:S(2)}, u32[]{:S(2)}) %collective-permute-start.15) | collective-permute-done | bytes 1048608 | tf_op jit(solution)/shard_map/ppermute | solution.py:410
  236.3 21.1 %collective-permute-done.17 = bf16[256,2048]{1,0:T(8,128)(2,1)S(1)} collective-permute-done((bf16[256,2048]{1,0:T(8,128)(2,1)S(1)}, bf16[256,2048]{1,0:T(8,128)(2,1)S(1)}, u32[]{:S(2)}, u32[]{:S(2)}) %collective-permute-start.17) | collective-permute-done | bytes 1048608 | tf_op jit(solution)/shard_map/ppermute | solution.py:410
  266.9 17.1 %swiglu_part.4 = (bf16[1024,512]{1,0:T(8,128)(2,1)S(1)}, bf16[1024,1024]{1,0:T(8,128)(2,1)S(1)}, f32[1024,2048]{1,0:T(8,128)}) custom-call(bf16[1024,2048]{1,0:T(8,128)(2,1)} %bitcast.40.n2_ref.n2a, bf16[1024,2048]{1,0:T(8,128)(2,1)} %bitcast.277, bf16[2048,1536]{1,0:T(8,128)(2,1)} %all-gather.9.cloned.1.call-done.w_ref.refs_2_), custom_call_target="tpu_custom_call" | custom-call | flops 10737418240 | bytes 25165824 | tf_op jit(solution)/shard_map/swiglu_part/pallas_call | solution.py:251
  284.0 17.4 %swiglu_part.5 = (bf16[1024,512]{1,0:T(8,128)(2,1)S(1)}, bf16[1024,1024]{1,0:T(8,128)(2,1)S(1)}, f32[1024,2048]{1,0:T(8,128)}) custom-call(bf16[1024,2048]{1,0:T(8,128)(2,1)} %bitcast.41.n2_ref.n2b, bf16[1024,2048]{1,0:T(8,128)(2,1)} %bitcast.273, bf16[2048,1536]{1,0:T(8,128)(2,1)} %all-gather.9.cloned.1.call-done.w_ref.refs_2_), custom_call_target="tpu_custom_call" | custom-call | flops 10737418240 | bytes 25165824 | tf_op jit(solution)/shard_map/swiglu_part/pallas_call | solution.py:251
  302.8 18.2 %swiglu_grads.2 = bf16[2048,1536]{1,0:T(8,128)(2,1)} custom-call(bf16[1024,2048]{1,0:T(8,128)(2,1)} %bitcast.40.n2_ref.n2a, bf16[1024,2048]{1,0:T(8,128)(2,1)} %bitcast.41.n2_ref.n2b, bf16[1024,2048]{1,0:T(8,128)(2,1)} %bitcast.278, bf16[1024,2048]{1,0:T(8,128)(2,1)} %bitcast.274, bf16[1024,1024]{1,0:T(8,128)(2,1)S(1)} %get-tuple-element.128.dgua, ...), custom_call_target="tpu_custom_call" | custom-call | flops 12884901888 | bytes 33554432 | tf_op jit(solution)/shard_map/swiglu_grads/pallas_call | solution.py:275
  322.0 4.0 all-gather.11.cloned.1.call-done.w_ref.refs_3_
  326.0 18.1 %swiglu_part.6 = (bf16[1024,512]{1,0:T(8,128)(2,1)S(1)}, bf16[1024,1024]{1,0:T(8,128)(2,1)S(1)}, bf16[1024,2048]{1,0:T(8,128)(2,1)}) custom-call(bf16[1024,2048]{1,0:T(8,128)(2,1)} %bitcast.41.n2_ref.n2b, bf16[1024,2048]{1,0:T(8,128)(2,1)} %bitcast.275, bf16[2048,1536]{1,0:T(8,128)(2,1)} %all-gather.11.cloned.1.call-done.w_ref.refs_3_, ...), custom_call_target="tpu_custom_call" | custom-call | flops 10737418240 | bytes 25165824 | tf_op jit(solution)/shard_map/swiglu_part/pallas_call | solution.py:251
  345.5 18.3 %swiglu_part.7 = (bf16[1024,512]{1,0:T(8,128)(2,1)S(1)}, bf16[1024,1024]{1,0:T(8,128)(2,1)S(1)}, bf16[1024,2048]{1,0:T(8,128)(2,1)}) custom-call(bf16[1024,2048]{1,0:T(8,128)(2,1)} %bitcast.40.n2_ref.n2a, bf16[1024,2048]{1,0:T(8,128)(2,1)} %bitcast.279, bf16[2048,1536]{1,0:T(8,128)(2,1)} %all-gather.11.cloned.1.call-done.w_ref.refs_3_, ...), custom_call_target="tpu_custom_call" | custom-call | flops 10737418240 | bytes 25165824 | tf_op jit(solution)/shard_map/swiglu_part/pallas_call | solution.py:251
  363.8 6.4 fusion.25
  373.6 18.2 %swiglu_grads.3 = bf16[2048,1536]{1,0:T(8,128)(2,1)} custom-call(bf16[1024,2048]{1,0:T(8,128)(2,1)} %bitcast.40.n2_ref.n2a, bf16[1024,2048]{1,0:T(8,128)(2,1)} %bitcast.41.n2_ref.n2b, bf16[1024,2048]{1,0:T(8,128)(2,1)} %bitcast.280, bf16[1024,2048]{1,0:T(8,128)(2,1)} %bitcast.276, bf16[1024,1024]{1,0:T(8,128)(2,1)S(1)} %get-tuple-element.140.dgua, ...), custom_call_target="tpu_custom_call" | custom-call | flops 12884901888 | bytes 33554432 | tf_op jit(solution)/shard_map/swiglu_grads/pallas_call | solution.py:275
  391.8 5.6 collective-permute-done.20
  397.4 21.6 %collective-permute-done.21 = bf16[256,2048]{1,0:T(8,128)(2,1)} collective-permute-done((bf16[256,2048]{1,0:T(8,128)(2,1)}, bf16[256,2048]{1,0:T(8,128)(2,1)}, u32[]{:S(2)}, u32[]{:S(2)}) %collective-permute-start.21) | collective-permute-done | bytes 1048608 | tf_op jit(solution)/shard_map/ppermute | solution.py:410
  419.1 4.4 multiply_reduce_fusion.1
  429.1 8.4 %swiglu_down.3 = bf16[1024,2048]{1,0:T(8,128)(2,1)} custom-call(bf16[1024,512]{1,0:T(8,128)(2,1)S(1)} %copy-done.3, bf16[1024,512]{1,0:T(8,128)(2,1)S(1)} %copy-done.5, bf16[2048,1536]{1,0:T(8,128)(2,1)} %all-gather.9.cloned.1.call-done.w_ref.refs_2_, bf16[2048,1536]{1,0:T(8,128)(2,1)} %all-gather.11.cloned.1.call-done.w_ref.refs_3_), custom_call_target="tpu_custom_call" | custom-call | flops 4294967296 | bytes 16777216 | tf_op jit(solution)/shard_map/swiglu_down/pallas_call | solution.py:305
  437.5 8.4 %swiglu_down.2 = bf16[1024,2048]{1,0:T(8,128)(2,1)} custom-call(bf16[1024,512]{1,0:T(8,128)(2,1)S(1)} %copy-done.1, bf16[1024,512]{1,0:T(8,128)(2,1)S(1)} %copy-done.7, bf16[2048,1536]{1,0:T(8,128)(2,1)} %all-gather.9.cloned.1.call-done.w_ref.refs_2_, bf16[2048,1536]{1,0:T(8,128)(2,1)} %all-gather.11.cloned.1.call-done.w_ref.refs_3_), custom_call_target="tpu_custom_call" | custom-call | flops 4294967296 | bytes 16777216 | tf_op jit(solution)/shard_map/swiglu_down/pallas_call | solution.py:305
  445.9 6.7 collective-permute-done.23
  452.6 21.4 %collective-permute-done.24 = bf16[256,2048]{1,0:T(8,128)(2,1)S(1)} collective-permute-done((bf16[256,2048]{1,0:T(8,128)(2,1)S(1)}, bf16[256,2048]{1,0:T(8,128)(2,1)S(1)}, u32[]{:S(2)}, u32[]{:S(2)}) %collective-permute-start.24) | collective-permute-done | bytes 1048608 | tf_op jit(solution)/shard_map/ppermute | solution.py:410
  476.8 3.8 convolution_convert_fusion.5
  494.7 14.6 %attend_back.2 = (bf16[1024,256]{1,0:T(8,128)(2,1)S(1)}, bf16[1024,128]{1,0:T(8,128)(2,1)S(1)}) custom-call(bf16[4,1024,64]{2,1,0:T(8,128)(2,1)S(1)} %copy-done.16, bf16[1024,64]{1,0:T(8,128)(2,1)S(1)} %get-tuple-element.105.k_ref, bf16[1024,64]{1,0:T(8,128)(2,1)S(1)} %copy-done.20, s32[1,1,1024]{2,1,0:T(1,128)S(1)} %bitcast.262, s32[1024,1]{1,0:T(8,128)S(1)} %copy-done.9, ...), custom_call_target="tpu_custom_call" | custom-call | flops 10737418240 | bytes 4194304 | tf_op jit(solution)/shard_map/attend_back/pallas_call | solution.py:182
  509.4 15.0 %attend_back.3 = (bf16[1024,256]{1,0:T(8,128)(2,1)S(1)}, bf16[1024,128]{1,0:T(8,128)(2,1)S(1)}) custom-call(bf16[4,1024,64]{2,1,0:T(8,128)(2,1)S(1)} %copy-done.18, bf16[1024,64]{1,0:T(8,128)(2,1)S(1)} %copy-done.22, bf16[1024,64]{1,0:T(8,128)(2,1)S(1)} %copy-done.24, s32[1,1,1024]{2,1,0:T(1,128)S(1)} %bitcast.265, s32[1024,1]{1,0:T(8,128)S(1)} %copy-done.11, ...), custom_call_target="tpu_custom_call" | custom-call | flops 10737418240 | bytes 4194304 | tf_op jit(solution)/shard_map/attend_back/pallas_call | solution.py:182
  533.3 4.4 convolution_convert_fusion
  538.2 4.5 fusion.19
  549.9 4.6 fusion.1
  558.3 10.0 %collective-permute-done.32 = bf16[256,2048]{1,0:T(8,128)(2,1)} collective-permute-done((bf16[256,2048]{1,0:T(8,128)(2,1)}, bf16[256,2048]{1,0:T(8,128)(2,1)}, u32[]{:S(2)}, u32[]{:S(2)}) %collective-permute-start.32) | collective-permute-done | bytes 1048608 | tf_op jit(solution)/shard_map/ppermute | solution.py:410
  570.5 21.4 %collective-permute-done.34 = bf16[256,2048]{1,0:T(8,128)(2,1)} collective-permute-done((bf16[256,2048]{1,0:T(8,128)(2,1)S(1)}, bf16[256,2048]{1,0:T(8,128)(2,1)}, u32[]{:S(2)}, u32[]{:S(2)}) %collective-permute-start.34) | collective-permute-done | bytes 1048608 | tf_op jit(solution)/shard_map/ppermute | solution.py:410
  591.9 3.7 fusion.24
  597.0 4.5 fusion.43
  616.2 28.2 %collective-permute-done.35 = bf16[256,2048]{1,0:T(8,128)(2,1)} collective-permute-done((bf16[256,2048]{1,0:T(8,128)(2,1)S(1)}, bf16[256,2048]{1,0:T(8,128)(2,1)}, u32[]{:S(2)}, u32[]{:S(2)}) %collective-permute-start.35) | collective-permute-done | bytes 1048608 | tf_op jit(solution)/shard_map/ppermute | solution.py:410
  647.1 17.5 %collective-permute-done.29 = bf16[256,2048]{1,0:T(8,128)(2,1)} collective-permute-done((bf16[256,2048]{1,0:T(8,128)(2,1)}, bf16[256,2048]{1,0:T(8,128)(2,1)}, u32[]{:S(2)}, u32[]{:S(2)}) %collective-permute-start.29) | collective-permute-done | bytes 1048608 | tf_op jit(solution)/shard_map/ppermute | solution.py:410
  668.7 4.1 fusion.16
  674.8 10.2 %collective-permute-done.38 = bf16[256,1536]{1,0:T(8,128)(2,1)} collective-permute-done((bf16[256,1536]{1,0:T(8,128)(2,1)}, bf16[256,1536]{1,0:T(8,128)(2,1)}, u32[]{:S(2)}, u32[]{:S(2)}) %collective-permute-start.38) | collective-permute-done | bytes 786464 | tf_op jit(solution)/shard_map/ppermute | solution.py:410
  707.5 14.0 %sum_all.2 = f32[32,128]{1,0:T(8,128)} custom-call(f32[32,128]{1,0:T(8,128)} %reshape.241.x_ref), custom_call_target="tpu_custom_call" | custom-call | tf_op jit(solution)/shard_map/sum_all/pallas_call | solution.py:369
  738.2 3.9 maximum_convert_fusion
  742.8 13.4 %sum_all.3 = f32[8,128]{1,0:T(8,128)} custom-call(f32[8,128]{1,0:T(8,128)} %broadcast_in_dim.8.x_ref), custom_call_target="tpu_custom_call" | custom-call | tf_op jit(solution)/shard_map/sum_all/pallas_call | solution.py:369
  758.7 4.5 multiply_subtract_fusion
  769.2 4.4 multiply_subtract_fusion.1
  (478 shorter events, 227.3 us)
Async XLA Ops:
  7.2 87.4 %all-gather.5.cloned.1.call-start = ((), (), s32[]{:S(2)}) async-start(), calls=%async_computation.4 | async-start | bytes 2088960 | tf_op jit(solution)/shard_map/all_gather | solution.py:413
  11.8 8.2 %collective-permute-start = (bf16[272,384]{1,0:T(8,128)(2,1)S(1)}, bf16[272,384]{1,0:T(8,128)(2,1)S(1)}, u32[]{:S(2)}, u32[]{:S(2)}) collective-permute-start(bf16[272,384]{1,0:T(8,128)(2,1)S(1)} %pad_maximum_fusion.42), channel_id=1, source_target_pairs={{0,4},{1,5},{2,6},{3,7},{4,0},{5,1},{6,2},{7,3},{8,12},{9,13},{10,... | collective-permute-start | bytes 626696 | tf_op jit(solution)/shard_map/ppermute | solution.py:410
  21.0 121.7 %all-gather.7.cloned.1.call-start = ((), (), s32[]{:S(2)}) async-start(), calls=%async_computation.5 | async-start | bytes 1310720 | tf_op jit(solution)/shard_map/all_gather | solution.py:413
  21.0 42.1 %collective-permute-start.7 = (s32[1,1024]{1,0:T(1,128)S(1)}, s32[1,1024]{1,0:T(1,128)S(1)}, u32[]{:S(2)}, u32[]{:S(2)}) collective-permute-start(s32[1,1024]{1,0:T(1,128)S(1)} %copy-done.14), channel_id=1, source_target_pairs={{0,4},{1,5},{2,6},{3,7},{4,0},{5,1},{6,2},{7,3},{8,12},{9,13},{10,... | collective-permute-start | bytes 12296 | tf_op jit(solution)/shard_map/ppermute | solution.py:410
  24.9 25.3 %collective-permute-start.1 = (bf16[256,2048]{1,0:T(8,128)(2,1)S(1)}, bf16[256,2048]{1,0:T(8,128)(2,1)}, u32[]{:S(2)}, u32[]{:S(2)}) collective-permute-start(bf16[256,2048]{1,0:T(8,128)(2,1)S(1)} %get-tuple-element.109), channel_id=1, source_target_pairs={{0,4},{1,5},{2,6},{3,7},{4,0},{5,1},{6,2},{7,3},{8,12},{9,13},{10,... | collective-permute-start | bytes 3145736 | tf_op jit(solution)/shard_map/ppermute | solution.py:410
  36.5 16.2 %collective-permute-start.4 = (bf16[256,256]{1,0:T(8,128)(2,1)S(1)}, bf16[256,256]{1,0:T(8,128)(2,1)S(1)}, u32[]{:S(2)}, u32[]{:S(2)}) collective-permute-start(bf16[256,256]{1,0:T(8,128)(2,1)S(1)} %dynamic-slice_bitcast_fusion.41), channel_id=1, source_target_pairs={{0,4},{1,5},{2,6},{3,7},{4,0},{5,1},{6,2},{7,3},{8,12},{9,13},{10,... | collective-permute-start | bytes 393224 | tf_op jit(solution)/shard_map/ppermute | solution.py:410
  50.2 21.7 %collective-permute-start.2 = (bf16[256,2048]{1,0:T(8,128)(2,1)}, bf16[256,2048]{1,0:T(8,128)(2,1)}, u32[]{:S(2)}, u32[]{:S(2)}) collective-permute-start(bf16[256,2048]{1,0:T(8,128)(2,1)} %collective-permute-done.1), channel_id=1, source_target_pairs={{0,2},{1,3},{2,0},{3,1},{4,6},{5,7},{6,4},{7,5},{8,10},{9,11},{10,... | collective-permute-start | bytes 3145736 | tf_op jit(solution)/shard_map/ppermute | solution.py:410
  52.6 17.9 %collective-permute-start.5 = (bf16[256,1536]{1,0:T(8,128)(2,1)}, bf16[256,1536]{1,0:T(8,128)(2,1)}, u32[]{:S(2)}, u32[]{:S(2)}) collective-permute-start(bf16[256,1536]{1,0:T(8,128)(2,1)} %pad_maximum_fusion.18), channel_id=1, source_target_pairs={{0,4},{1,5},{2,6},{3,7},{4,0},{5,1},{6,2},{7,3},{8,12},{9,13},{10,... | collective-permute-start | bytes 2359304 | tf_op jit(solution)/shard_map/ppermute | solution.py:410
  65.0 202.0 %all-gather.9.cloned.1.call-start = ((), (), s32[]{:S(2)}) async-start(), calls=%async_computation.6 | async-start | bytes 7864320 | tf_op jit(solution)/shard_map/all_gather | solution.py:413
  70.6 21.0 %collective-permute-start.6 = (bf16[256,2048]{1,0:T(8,128)(2,1)S(1)}, bf16[256,2048]{1,0:T(8,128)(2,1)}, u32[]{:S(2)}, u32[]{:S(2)}) collective-permute-start(bf16[256,2048]{1,0:T(8,128)(2,1)S(1)} %get-tuple-element.115), channel_id=1, source_target_pairs={{0,4},{1,5},{2,6},{3,7},{4,0},{5,1},{6,2},{7,3},{8,12},{9,13},{10,... | collective-permute-start | bytes 3145736 | tf_op jit(solution)/shard_map/ppermute | solution.py:410
  75.1 41.5 %collective-permute-start.3 = (bf16[2,256,2048]{2,1,0:T(8,128)(2,1)}, bf16[2,256,2048]{2,1,0:T(8,128)(2,1)}, u32[]{:S(2)}, u32[]{:S(2)}) collective-permute-start(bf16[2,256,2048]{2,1,0:T(8,128)(2,1)} %pad_maximum_fusion.9), channel_id=1, source_target_pairs={{0,1},{1,0},{2,3},{3,2},{4,5},{5,4},{6,7},{7,6},{8,9},{9,8},{10,11... | collective-permute-start | bytes 6291464 | tf_op jit(solution)/shard_map/ppermute | solution.py:410
  91.6 23.1 %collective-permute-start.8 = (bf16[256,2048]{1,0:T(8,128)(2,1)}, bf16[256,2048]{1,0:T(8,128)(2,1)}, u32[]{:S(2)}, u32[]{:S(2)}) collective-permute-start(bf16[256,2048]{1,0:T(8,128)(2,1)} %collective-permute-done.6), channel_id=1, source_target_pairs={{0,2},{1,3},{2,0},{3,1},{4,6},{5,7},{6,4},{7,5},{8,10},{9,11},{10,... | collective-permute-start | bytes 3145736 | tf_op jit(solution)/shard_map/ppermute | solution.py:410
  94.4 231.6 %all-gather.11.cloned.1.call-start = ((), (), s32[]{:S(2)}) async-start(), calls=%async_computation.7 | async-start | bytes 7864320 | tf_op jit(solution)/shard_map/all_gather | solution.py:413
  114.2 26.9 %collective-permute-start.10 = (bf16[256,1536]{1,0:T(8,128)(2,1)}, bf16[256,1536]{1,0:T(8,128)(2,1)}, u32[]{:S(2)}, u32[]{:S(2)}) collective-permute-start(bf16[256,1536]{1,0:T(8,128)(2,1)} %pad_maximum_fusion.19), channel_id=1, source_target_pairs={{0,4},{1,5},{2,6},{3,7},{4,0},{5,1},{6,2},{7,3},{8,12},{9,13},{10,... | collective-permute-start | bytes 2359304 | tf_op jit(solution)/shard_map/ppermute | solution.py:410
  116.5 23.0 %collective-permute-start.9 = (bf16[2,256,2048]{2,1,0:T(8,128)(2,1)S(1)}, bf16[2,256,2048]{2,1,0:T(8,128)(2,1)S(1)}, u32[]{:S(2)}, u32[]{:S(2)}) collective-permute-start(bf16[2,256,2048]{2,1,0:T(8,128)(2,1)S(1)} %pad_maximum_fusion.10), channel_id=1, source_target_pairs={{0,1},{1,0},{2,3},{3,2},{4,5},{5,4},{6,7},{7,6},{8,9},{9,8},{10,11... | collective-permute-start | bytes 6291464 | tf_op jit(solution)/shard_map/ppermute | solution.py:410
  155.9 25.8 %collective-permute-start.12 = (bf16[256,2048]{1,0:T(8,128)(2,1)}, bf16[256,2048]{1,0:T(8,128)(2,1)}, u32[]{:S(2)}, u32[]{:S(2)}) collective-permute-start(bf16[256,2048]{1,0:T(8,128)(2,1)} %get-tuple-element.252), channel_id=1, source_target_pairs={{0,2},{1,3},{2,0},{3,1},{4,6},{5,7},{6,4},{7,5},{8,10},{9,11},{10,... | collective-permute-start | bytes 3145736 | tf_op jit(solution)/shard_map/ppermute | solution.py:410
  156.7 26.3 %collective-permute-start.13 = (bf16[256,2048]{1,0:T(8,128)(2,1)}, bf16[256,2048]{1,0:T(8,128)(2,1)}, u32[]{:S(2)}, u32[]{:S(2)}) collective-permute-start(bf16[256,2048]{1,0:T(8,128)(2,1)} %get-tuple-element.254), channel_id=1, source_target_pairs={{0,4},{1,5},{2,6},{3,7},{4,0},{5,1},{6,2},{7,3},{8,12},{9,13},{10,... | collective-permute-start | bytes 3145736 | tf_op jit(solution)/shard_map/ppermute | solution.py:410
  157.8 47.4 %collective-permute-start.14 = (bf16[256,2048]{1,0:T(8,128)(2,1)}, bf16[256,2048]{1,0:T(8,128)(2,1)}, u32[]{:S(2)}, u32[]{:S(2)}) collective-permute-start(bf16[256,2048]{1,0:T(8,128)(2,1)} %get-tuple-element.253), channel_id=1, source_target_pairs={{0,6},{1,7},{2,4},{3,5},{4,2},{5,3},{6,0},{7,1},{8,14},{9,15},{10,... | collective-permute-start | bytes 3145736 | tf_op jit(solution)/shard_map/ppermute | solution.py:410
  162.0 327.3 %reduce-scatter.5.cloned.1.call-start = ((), (), s32[]{:S(2)}) async-start(), calls=%async_computation.8 | async-start | bytes 7864320 | tf_op jit(solution)/shard_map/reduce_scatter | solution.py:416
  209.3 25.3 %collective-permute-start.15 = (bf16[256,2048]{1,0:T(8,128)(2,1)S(1)}, bf16[256,2048]{1,0:T(8,128)(2,1)S(1)}, u32[]{:S(2)}, u32[]{:S(2)}) collective-permute-start(bf16[256,2048]{1,0:T(8,128)(2,1)S(1)} %multiply_convert_fusion), channel_id=1, source_target_pairs={{0,2},{1,3},{2,0},{3,1},{4,6},{5,7},{6,4},{7,5},{8,10},{9,11},{10,... | collective-permute-start | bytes 3145736 | tf_op jit(solution)/shard_map/ppermute | solution.py:410
  210.2 26.1 %collective-permute-start.16 = (bf16[256,2048]{1,0:T(8,128)(2,1)S(1)}, bf16[256,2048]{1,0:T(8,128)(2,1)S(1)}, u32[]{:S(2)}, u32[]{:S(2)}) collective-permute-start(bf16[256,2048]{1,0:T(8,128)(2,1)S(1)} %multiply_convert_fusion), channel_id=1, source_target_pairs={{0,4},{1,5},{2,6},{3,7},{4,0},{5,1},{6,2},{7,3},{8,12},{9,13},{10,... | collective-permute-start | bytes 3145736 | tf_op jit(solution)/shard_map/ppermute | solution.py:410
  211.3 46.0 %collective-permute-start.17 = (bf16[256,2048]{1,0:T(8,128)(2,1)S(1)}, bf16[256,2048]{1,0:T(8,128)(2,1)S(1)}, u32[]{:S(2)}, u32[]{:S(2)}) collective-permute-start(bf16[256,2048]{1,0:T(8,128)(2,1)S(1)} %multiply_convert_fusion), channel_id=1, source_target_pairs={{0,6},{1,7},{2,4},{3,5},{4,2},{5,3},{6,0},{7,1},{8,14},{9,15},{10,... | collective-permute-start | bytes 3145736 | tf_op jit(solution)/shard_map/ppermute | solution.py:410
  259.8 24.2 %collective-permute-start.18 = (bf16[4,256,2048]{2,1,0:T(8,128)(2,1)}, bf16[4,256,2048]{2,1,0:T(8,128)(2,1)}, u32[]{:S(2)}, u32[]{:S(2)}) collective-permute-start(bf16[4,256,2048]{2,1,0:T(8,128)(2,1)} %pad_maximum_fusion.2), channel_id=1, source_target_pairs={{0,1},{1,0},{2,3},{3,2},{4,5},{5,4},{6,7},{7,6},{8,9},{9,8},{10,11... | collective-permute-start | bytes 12582920 | tf_op jit(solution)/shard_map/ppermute | solution.py:410
  321.9 342.7 %reduce-scatter.7.cloned.1.call-start = ((), (), s32[]{:S(2)}) async-start(), calls=%async_computation.9 | async-start | bytes 7864320 | tf_op jit(solution)/shard_map/reduce_scatter | solution.py:416
  345.4 18.3 %collective-permute-start.19 = (bf16[4,256,2048]{2,1,0:T(8,128)(2,1)}, bf16[4,256,2048]{2,1,0:T(8,128)(2,1)S(1)}, u32[]{:S(2)}, u32[]{:S(2)}) collective-permute-start(bf16[4,256,2048]{2,1,0:T(8,128)(2,1)} %bitcast.303), channel_id=1, source_target_pairs={{0,1},{1,0},{2,3},{3,2},{4,5},{5,4},{6,7},{7,6},{8,9},{9,8},{10,11... | collective-permute-start | bytes 12582920 | tf_op jit(solution)/shard_map/ppermute | solution.py:410
  370.1 27.3 %collective-permute-start.20 = (bf16[256,2048]{1,0:T(8,128)(2,1)}, bf16[256,2048]{1,0:T(8,128)(2,1)}, u32[]{:S(2)}, u32[]{:S(2)}) collective-permute-start(bf16[256,2048]{1,0:T(8,128)(2,1)} %get-tuple-element.251), channel_id=1, source_target_pairs={{0,6},{1,7},{2,4},{3,5},{4,2},{5,3},{6,0},{7,1},{8,14},{9,15},{10,... | collective-permute-start | bytes 3145736 | tf_op jit(solution)/shard_map/ppermute | solution.py:410
  372.5 46.5 %collective-permute-start.21 = (bf16[256,2048]{1,0:T(8,128)(2,1)}, bf16[256,2048]{1,0:T(8,128)(2,1)}, u32[]{:S(2)}, u32[]{:S(2)}) collective-permute-start(bf16[256,2048]{1,0:T(8,128)(2,1)} %get-tuple-element.250), channel_id=1, source_target_pairs={{0,2},{1,3},{2,0},{3,1},{4,6},{5,7},{6,4},{7,5},{8,10},{9,11},{10,... | collective-permute-start | bytes 3145736 | tf_op jit(solution)/shard_map/ppermute | solution.py:410
  373.1 46.0 %collective-permute-start.22 = (bf16[256,2048]{1,0:T(8,128)(2,1)}, bf16[256,2048]{1,0:T(8,128)(2,1)}, u32[]{:S(2)}, u32[]{:S(2)}) collective-permute-start(bf16[256,2048]{1,0:T(8,128)(2,1)} %get-tuple-element.249), channel_id=1, source_target_pairs={{0,4},{1,5},{2,6},{3,7},{4,0},{5,1},{6,2},{7,3},{8,12},{9,13},{10,... | collective-permute-start | bytes 3145736 | tf_op jit(solution)/shard_map/ppermute | solution.py:410
  425.6 27.0 %collective-permute-start.23 = (bf16[256,2048]{1,0:T(8,128)(2,1)S(1)}, bf16[256,2048]{1,0:T(8,128)(2,1)S(1)}, u32[]{:S(2)}, u32[]{:S(2)}) collective-permute-start(bf16[256,2048]{1,0:T(8,128)(2,1)S(1)} %get-tuple-element.238), channel_id=1, source_target_pairs={{0,6},{1,7},{2,4},{3,5},{4,2},{5,3},{6,0},{7,1},{8,14},{9,15},{10,... | collective-permute-start | bytes 3145736 | tf_op jit(solution)/shard_map/ppermute | solution.py:410
  427.3 46.7 %collective-permute-start.24 = (bf16[256,2048]{1,0:T(8,128)(2,1)S(1)}, bf16[256,2048]{1,0:T(8,128)(2,1)S(1)}, u32[]{:S(2)}, u32[]{:S(2)}) collective-permute-start(bf16[256,2048]{1,0:T(8,128)(2,1)S(1)} %get-tuple-element.238), channel_id=1, source_target_pairs={{0,2},{1,3},{2,0},{3,1},{4,6},{5,7},{6,4},{7,5},{8,10},{9,11},{10,... | collective-permute-start | bytes 3145736 | tf_op jit(solution)/shard_map/ppermute | solution.py:410
  428.6 45.5 %collective-permute-start.25 = (bf16[256,2048]{1,0:T(8,128)(2,1)S(1)}, bf16[256,2048]{1,0:T(8,128)(2,1)S(1)}, u32[]{:S(2)}, u32[]{:S(2)}) collective-permute-start(bf16[256,2048]{1,0:T(8,128)(2,1)S(1)} %get-tuple-element.238), channel_id=1, source_target_pairs={{0,4},{1,5},{2,6},{3,7},{4,0},{5,1},{6,2},{7,3},{8,12},{9,13},{10,... | collective-permute-start | bytes 3145736 | tf_op jit(solution)/shard_map/ppermute | solution.py:410
  476.4 198.4 %reduce-scatter.11.cloned.1.call-start = ((), (), s32[]{:S(2)}) async-start(), calls=%async_computation.11 | async-start | bytes 1310720 | tf_op jit(solution)/shard_map/reduce_scatter | solution.py:416
  483.8 54.4 %collective-permute-start.31 = (bf16[4,256,2048]{2,1,0:T(8,128)(2,1)}, bf16[4,256,2048]{2,1,0:T(8,128)(2,1)}, u32[]{:S(2)}, u32[]{:S(2)}) collective-permute-start(bf16[4,256,2048]{2,1,0:T(8,128)(2,1)} %bitcast.86), channel_id=1, source_target_pairs={{0,1},{1,0},{2,3},{3,2},{4,5},{5,4},{6,7},{7,6},{8,9},{9,8},{10,11... | collective-permute-start | bytes 12582920 | tf_op jit(solution)/shard_map/ppermute | solution.py:410
  537.7 59.2 %collective-permute-start.27 = (bf16[4,256,2048]{2,1,0:T(8,128)(2,1)}, bf16[4,256,2048]{2,1,0:T(8,128)(2,1)}, u32[]{:S(2)}, u32[]{:S(2)}) collective-permute-start(bf16[4,256,2048]{2,1,0:T(8,128)(2,1)} %convolution_convert_fusion), channel_id=1, source_target_pairs={{0,1},{1,0},{2,3},{3,2},{4,5},{5,4},{6,7},{7,6},{8,9},{9,8},{10,11... | collective-permute-start | bytes 12582920 | tf_op jit(solution)/shard_map/ppermute | solution.py:410
  542.7 25.5 %collective-permute-start.32 = (bf16[256,2048]{1,0:T(8,128)(2,1)}, bf16[256,2048]{1,0:T(8,128)(2,1)}, u32[]{:S(2)}, u32[]{:S(2)}) collective-permute-start(bf16[256,2048]{1,0:T(8,128)(2,1)} %get-tuple-element.243), channel_id=1, source_target_pairs={{0,2},{1,3},{2,0},{3,1},{4,6},{5,7},{6,4},{7,5},{8,10},{9,11},{10,... | collective-permute-start | bytes 3145736 | tf_op jit(solution)/shard_map/ppermute | solution.py:410
  544.1 26.4 %collective-permute-start.33 = (bf16[256,2048]{1,0:T(8,128)(2,1)}, bf16[256,2048]{1,0:T(8,128)(2,1)}, u32[]{:S(2)}, u32[]{:S(2)}) collective-permute-start(bf16[256,2048]{1,0:T(8,128)(2,1)} %get-tuple-element.245), channel_id=1, source_target_pairs={{0,4},{1,5},{2,6},{3,7},{4,0},{5,1},{6,2},{7,3},{8,12},{9,13},{10,... | collective-permute-start | bytes 3145736 | tf_op jit(solution)/shard_map/ppermute | solution.py:410
  544.7 47.2 %collective-permute-start.34 = (bf16[256,2048]{1,0:T(8,128)(2,1)S(1)}, bf16[256,2048]{1,0:T(8,128)(2,1)}, u32[]{:S(2)}, u32[]{:S(2)}) collective-permute-start(bf16[256,2048]{1,0:T(8,128)(2,1)S(1)} %get-tuple-element.244), channel_id=1, source_target_pairs={{0,6},{1,7},{2,4},{3,5},{4,2},{5,3},{6,0},{7,1},{8,14},{9,15},{10,... | collective-permute-start | bytes 3145736 | tf_op jit(solution)/shard_map/ppermute | solution.py:410
  554.5 140.3 %reduce-scatter.9.cloned.1.call-start = ((), (), s32[]{:S(2)}) async-start(), calls=%async_computation.10 | async-start | bytes 1966080 | tf_op jit(solution)/shard_map/reduce_scatter | solution.py:416
  595.6 48.7 %collective-permute-start.35 = (bf16[256,2048]{1,0:T(8,128)(2,1)S(1)}, bf16[256,2048]{1,0:T(8,128)(2,1)}, u32[]{:S(2)}, u32[]{:S(2)}) collective-permute-start(bf16[256,2048]{1,0:T(8,128)(2,1)S(1)} %fusion.24), channel_id=1, source_target_pairs={{0,2},{1,3},{2,0},{3,1},{4,6},{5,7},{6,4},{7,5},{8,10},{9,11},{10,... | collective-permute-start | bytes 3145736 | tf_op jit(solution)/shard_map/ppermute | solution.py:410
  601.4 45.7 %collective-permute-start.28 = (bf16[256,2048]{1,0:T(8,128)(2,1)}, bf16[256,2048]{1,0:T(8,128)(2,1)}, u32[]{:S(2)}, u32[]{:S(2)}) collective-permute-start(bf16[256,2048]{1,0:T(8,128)(2,1)} %get-tuple-element.248), channel_id=1, source_target_pairs={{0,6},{1,7},{2,4},{3,5},{4,2},{5,3},{6,0},{7,1},{8,14},{9,15},{10,... | collective-permute-start | bytes 3145736 | tf_op jit(solution)/shard_map/ppermute | solution.py:410
  602.9 61.7 %collective-permute-start.29 = (bf16[256,2048]{1,0:T(8,128)(2,1)}, bf16[256,2048]{1,0:T(8,128)(2,1)}, u32[]{:S(2)}, u32[]{:S(2)}) collective-permute-start(bf16[256,2048]{1,0:T(8,128)(2,1)} %get-tuple-element.247), channel_id=1, source_target_pairs={{0,2},{1,3},{2,0},{3,1},{4,6},{5,7},{6,4},{7,5},{8,10},{9,11},{10,... | collective-permute-start | bytes 3145736 | tf_op jit(solution)/shard_map/ppermute | solution.py:410
  603.5 61.2 %collective-permute-start.30 = (bf16[256,2048]{1,0:T(8,128)(2,1)}, bf16[256,2048]{1,0:T(8,128)(2,1)}, u32[]{:S(2)}, u32[]{:S(2)}) collective-permute-start(bf16[256,2048]{1,0:T(8,128)(2,1)} %get-tuple-element.246), channel_id=1, source_target_pairs={{0,4},{1,5},{2,6},{3,7},{4,0},{5,1},{6,2},{7,3},{8,12},{9,13},{10,... | collective-permute-start | bytes 3145736 | tf_op jit(solution)/shard_map/ppermute | solution.py:410
  615.6 59.1 %collective-permute-start.37 = (bf16[256,1536]{1,0:T(8,128)(2,1)}, bf16[256,1536]{1,0:T(8,128)(2,1)}, u32[]{:S(2)}, u32[]{:S(2)}) collective-permute-start(bf16[256,1536]{1,0:T(8,128)(2,1)} %get-tuple-element.287), channel_id=1, source_target_pairs={{0,4},{1,5},{2,6},{3,7},{4,0},{5,1},{6,2},{7,3},{8,12},{9,13},{10,... | collective-permute-start | bytes 2359304 | tf_op jit(solution)/shard_map/ppermute | solution.py:410
  647.1 54.3 %collective-permute-start.36 = (bf16[2,256,2048]{2,1,0:T(8,128)(2,1)}, bf16[2,256,2048]{2,1,0:T(8,128)(2,1)}, u32[]{:S(2)}, u32[]{:S(2)}) collective-permute-start(bf16[2,256,2048]{2,1,0:T(8,128)(2,1)} %pad_maximum_fusion.11), channel_id=1, source_target_pairs={{0,1},{1,0},{2,3},{3,2},{4,5},{5,4},{6,7},{7,6},{8,9},{9,8},{10,11... | collective-permute-start | bytes 6291464 | tf_op jit(solution)/shard_map/ppermute | solution.py:410
  667.2 17.7 %collective-permute-start.38 = (bf16[256,1536]{1,0:T(8,128)(2,1)}, bf16[256,1536]{1,0:T(8,128)(2,1)}, u32[]{:S(2)}, u32[]{:S(2)}) collective-permute-start(bf16[256,1536]{1,0:T(8,128)(2,1)} %get-tuple-element.285), channel_id=1, source_target_pairs={{0,4},{1,5},{2,6},{3,7},{4,0},{5,1},{6,2},{7,3},{8,12},{9,13},{10,... | collective-permute-start | bytes 2359304 | tf_op jit(solution)/shard_map/ppermute | solution.py:410
  673.4 25.2 %collective-permute-start.41 = (bf16[256,2048]{1,0:T(8,128)(2,1)S(1)}, bf16[256,2048]{1,0:T(8,128)(2,1)}, u32[]{:S(2)}, u32[]{:S(2)}) collective-permute-start(bf16[256,2048]{1,0:T(8,128)(2,1)S(1)} %fusion.15), channel_id=1, source_target_pairs={{0,2},{1,3},{2,0},{3,1},{4,6},{5,7},{6,4},{7,5},{8,10},{9,11},{10,... | collective-permute-start | bytes 3145736 | tf_op jit(solution)/shard_map/ppermute | solution.py:410
  696.4 27.9 %collective-permute-start.40 = (bf16[256,384]{1,0:T(8,128)(2,1)}, bf16[256,384]{1,0:T(8,128)(2,1)}, u32[]{:S(2)}, u32[]{:S(2)}) collective-permute-start(bf16[256,384]{1,0:T(8,128)(2,1)} %constant_dynamic-slice_fusion.5), channel_id=1, source_target_pairs={{0,4},{1,5},{2,6},{3,7},{4,0},{5,1},{6,2},{7,3},{8,12},{9,13},{10,... | collective-permute-start | bytes 589832 | tf_op jit(solution)/shard_map/ppermute | solution.py:410
  701.3 33.0 %collective-permute-start.42 = (bf16[2,256,2048]{2,1,0:T(8,128)(2,1)}, bf16[2,256,2048]{2,1,0:T(8,128)(2,1)}, u32[]{:S(2)}, u32[]{:S(2)}) collective-permute-start(bf16[2,256,2048]{2,1,0:T(8,128)(2,1)} %pad_maximum_fusion.12), channel_id=1, source_target_pairs={{0,1},{1,0},{2,3},{3,2},{4,5},{5,4},{6,7},{7,6},{8,9},{9,8},{10,11... | collective-permute-start | bytes 6291464 | tf_op jit(solution)/shard_map/ppermute | solution.py:410
  (122 other events, 864.7 us)
Sparse Core Ops, SparseCore 0:
  21.1 40.1 all-gather.4
  65.1 28.2 all-gather.6
  95.5 114.8 all-gather.8
  212.4 113.5 all-gather.10
  328.1 108.9 reduce-scatter.4
  476.5 108.5 reduce-scatter.6
  587.4 27.6 reduce-scatter.10
  618.0 33.9 reduce-scatter.8

commit v4 on v3

--- a/solution.py
+++ b/solution.py
@@ -132,9 +132,62 @@
         name="attend",
     )(q, k, v, brow, bcol)
 
-def bwd_body(limits, q_ref, k_ref, v_ref, brow_ref, bcol_ref, lse_ref, do_ref, cos_ref, sin_ref, kcos_ref, ksin_ref, dq_ref, dkv_ref, dk_acc, dv_acc):
+def bwd_body(
+    limits,
+    q_ref,
+    k_ref,
+    v_ref,
+    brow_ref,
+    bcol_ref,
+    lse_ref,
+    do_ref,
+    cos_ref,
+    sin_ref,
+    kcos_ref,
+    ksin_ref,
+    even,
+    odd,
+    hidden_ref,
+    piece,
+    dq_ref,
+    dkv_ref,
+    out_ref,
+    theirs,
+    dk_acc,
+    dv_acc,
+    *scratch
+):
     heads, tile, _ = q_ref.shape
     i = pl.program_id(1)
+    turn = pl.program_id(0) * pl.num_programs(1) + i
+    targets = neighbours()
+    job = Job(even, odd, scratch[:8], targets)
+    swapped = trade(piece, theirs, scratch[8])
+    blocks = range(PARTS)
+
+    @pl.when(turn == 0)
+    def _():
+        meet(targets)
+        job.start()
+        for s in blocks:
+            job.first(s)
+
+    @pl.when(turn == 1)
+    def _():
+        swapped.start()
+
+    for s in blocks:
+
+        @pl.when(turn == 2 + s)
+        def _(s=s):
+            job.second(s)
+
+    @pl.when(turn == 6)
+    def _():
+        for s in blocks:
+            job.own[job.span(s)] = (hidden_ref[job.span(s)] + job.total(s)).astype(BF)
+            job.line_start(s, out_ref)
+
     @pl.when(i == 0)
     def _():
         dk_acc[...] = jnp.zeros_like(dk_acc)
@@ -167,12 +220,22 @@
         @pl.when(i == n)
         def _(keys=keys):
             run(keys)
+
+    @pl.when(turn == 7)
+    def _():
+        for s in blocks:
+            job.line_core(s, out_ref)
+        job.line_end(out_ref)
+        swapped.wait()
+
     @pl.when(i == len(limits) - 1)
     def _():
         both = jnp.concatenate([dk_acc[...], dv_acc[...]], axis=0).T
         dkv_ref[...] = (both * kcos_ref[...] - swap_halves(both) * ksin_ref[...]).astype(BF)
 
-def attend_back(q, k, v, brow, bcol, lse, do, cos, sin, length, tile=256, most=256):
+def attend_back(
+    q, k, v, brow, bcol, lse, do, cos, sin, length, even, odd, hidden, piece, tile=256, most=256
+):
     heads, count, _ = q.shape
     seqs = count // length
     per = length // tile
@@ -194,20 +257,32 @@
             pl.BlockSpec((tile, qc), lambda b, i: (i, 0)),
             pl.BlockSpec((length, 2 * HD), lambda b, i: (0, qc // (2 * HD))),
             pl.BlockSpec((length, 2 * HD), lambda b, i: (0, qc // (2 * HD))),
+            IN_VMEM,
+            ANY,
+            IN_VMEM,
+            ANY,
         ],
         out_specs=[
             pl.BlockSpec((tile, qc), rowm),
             pl.BlockSpec((length, 2 * HD), lambda b, i: (b, 0)),
+            ANY,
+            ANY,
         ],
         out_shape=[
             jax.ShapeDtypeStruct((count, qc), BF),
             jax.ShapeDtypeStruct((count, 2 * HD), BF),
-        ],
-        scratch_shapes=[pltpu.VMEM((HD, length), F32), pltpu.VMEM((HD, length), F32)],
-        compiler_params=pltpu.CompilerParams(vmem_limit_bytes=VMEM),
+            jax.ShapeDtypeStruct((length, even.shape[2]), BF),
+            jax.ShapeDtypeStruct((piece.shape[0] // 2, piece.shape[1]), BF),
+        ],
+        scratch_shapes=[pltpu.VMEM((HD, length), F32), pltpu.VMEM((HD, length), F32)]
+        + Job.scratch(even.shape[1], even.shape[2])
+        + [pltpu.SemaphoreType.DMA((2, 1))],
+        compiler_params=pltpu.CompilerParams(
+            collective_id=7, has_side_effects=True, vmem_limit_bytes=VMEM
+        ),
         cost_estimate=pl.CostEstimate(flops=10 * heads * count * length * HD * 4, bytes_accessed=count * 4096, transcendentals=heads * count * length),
         name="attend_back",
-    )(q, k, v, brow, bcol, lse, do, cos, sin, cos, sin)
+    )(q, k, v, brow, bcol, lse, do, cos, sin, cos, sin, even, odd, hidden, piece)
 
 def rope_tables(length, heads):
     positions = jnp.arange(length, dtype=jnp.int32).astype(F32)
@@ -290,6 +365,42 @@
     )(*n2, *cot, *dgu, *act)
 
 
+def attn_grad_body(na, ga, ha, hb, ma, mb, o_ref):
+    cols = ga.shape[1]
+    o_ref[:, :cols] = dot(na[...], ga[...], 0, 0).astype(BF)
+    o_ref[:, cols:] = (dot(ha[...], ma[...], 0, 0) + dot(hb[...], mb[...], 0, 0)).astype(BF)
+
+
+def attn_grads(normed, grads, hidden, mixed, tile=256):
+    width = normed.shape[1]
+    col = lambda i: (0, i)
+    ins = [normed, grads, *hidden, *mixed]
+    cols = grads.shape[1] + mixed[0].shape[1]
+
+    def tiled(value):
+        return pl.BlockSpec((value.shape[0], tile), col)
+
+    def whole(value):
+        return pl.BlockSpec(value.shape, lambda i: (0, 0), pipeline_mode=pl.Buffered(1))
+
+    return pl.pallas_call(
+        attn_grad_body,
+        grid=(width // tile,),
+        in_specs=[tiled(normed), whole(grads)]
+        + [tiled(v) for v in hidden]
+        + [whole(v) for v in mixed],
+        out_specs=pl.BlockSpec((tile, cols), lambda i: (i, 0)),
+        out_shape=jax.ShapeDtypeStruct((width, cols), BF),
+        compiler_params=pltpu.CompilerParams(vmem_limit_bytes=VMEM),
+        cost_estimate=pl.CostEstimate(
+            flops=2 * normed.shape[0] * width * cols,
+            bytes_accessed=8 * normed.shape[0] * width,
+            transcendentals=0,
+        ),
+        name="attn_grads",
+    )(*ins)
+
+
 def out_body(*refs):
     count = len(refs) // 2
     total = dot(refs[0][...], refs[count][...], 1, 1)
@@ -322,80 +433,668 @@
     )(*acts, *weights)
 
 
-def sum_body(dps, shards, x_ref, o_ref, slots, send, recv):
-    total = dps * shards
-    me = lax.axis_index("dp") * shards + lax.axis_index("shard")
+def peers(dps, shards):
+    dp, sh = lax.axis_index("dp"), lax.axis_index("shard")
+    groups = dps // 2
+    near = []
+    for r in range(1, 2 * shards):
+        there = sh
+        for bit in (1, 2):
+            there = flip(there, bit) if r % shards & bit else there
+        near.append((flip(dp, 1) if r >= shards else dp, there))
+    far = [
+        (lax.rem(dp // 2 + p, groups) * 2 + lax.rem(dp, 2), sh) for p in range(1, groups)
+    ]
+    return near, far, lax.rem(dp, 2) * shards + sh, dp // 2
+
+
+def meet(targets):
     barrier = pltpu.get_barrier_semaphore()
-
-    def device(p):
-        target = lax.rem(me + p, total)
-        return (target // shards, lax.rem(target, shards))
-
-    def greet(p, carry):
-        pl.semaphore_signal(barrier, inc=1, device_id=device(p), device_id_type=MESH)
-        return carry
-
-    lax.fori_loop(1, total, greet, 0)
-    slots[me] = x_ref[...]
-    pl.semaphore_wait(barrier, total - 1)
-
-    def copy(p):
-        return pltpu.make_async_remote_copy(
-            src_ref=x_ref,
-            dst_ref=slots.at[me],
-            send_sem=send.at[p],
-            recv_sem=recv.at[p],
-            device_id=device(p),
+    for target in targets:
+        pl.semaphore_signal(barrier, inc=1, device_id=target, device_id_type=MESH)
+    pl.semaphore_wait(barrier, len(targets))
+
+
+def exchange(values, slots, mine, targets, source, send, recv, base):
+    source[...] = values
+    slots[mine] = values
+    copies = [
+        pltpu.make_async_remote_copy(
+            src_ref=source,
+            dst_ref=slots.at[mine],
+            send_sem=send.at[base + n],
+            recv_sem=recv.at[base + n],
+            device_id=target,
             device_id_type=MESH,
         )
-
-    def start(p, carry):
-        copy(p).start()
-        return carry
-
-    def finish(p, carry):
-        copy(p).wait()
-        return carry
-
-    lax.fori_loop(1, total, start, 0)
-    lax.fori_loop(1, total, finish, 0)
-    o_ref[...] = lax.fori_loop(
-        0, total, lambda i, acc: acc + slots[i], jnp.zeros(x_ref.shape, F32)
+        for n, target in enumerate(targets)
+    ]
+    for copy in copies:
+        copy.start()
+    for copy in copies:
+        copy.wait()
+    total = slots[0]
+    for n in range(1, slots.shape[0]):
+        total = total + slots[n]
+    return total
+
+
+def two_stages(values, near, far, me, outer, bufs):
+    slots_near, slots_far, from_near, from_far, send, recv = bufs
+    total = exchange(values, slots_near, me, near, from_near, send, recv, 0)
+    return exchange(total, slots_far, outer, far, from_far, send, recv, len(near))
+
+
+def sum_scratch(shape, dps, shards):
+    count = 2 * shards - 1 + dps // 2 - 1
+    return [
+        pltpu.VMEM((2 * shards,) + shape, F32),
+        pltpu.VMEM((dps // 2,) + shape, F32),
+        pltpu.VMEM(shape, F32),
+        pltpu.VMEM(shape, F32),
+        pltpu.SemaphoreType.DMA((count,)),
+        pltpu.SemaphoreType.DMA((count,)),
+    ]
+
+
+def pick(x, first, second):
+    low = jnp.where(x == 0, first.astype(F32), second.astype(F32)).astype(BF)
+    high = jnp.where(x == 0, second.astype(F32), first.astype(F32)).astype(BF)
+    return low, high
+
+
+def finish_body(
+    dps, shards, piece_ref, sq_ref, q_ref, k_ref, v_ref, o_ref, norm_ref, theirs, pair, *bufs
+):
+    near, far, me, outer = peers(dps, shards)
+    rows = piece_ref.shape[0] // 2
+    qc = q_ref.shape[1] // 2
+    x = lax.rem(lax.axis_index("dp"), 2)
+    meet(near + far)
+    copy = pltpu.make_async_remote_copy(
+        src_ref=piece_ref.at[pl.ds(pl.multiple_of((1 - x) * rows, rows), rows)],
+        dst_ref=theirs,
+        send_sem=pair.at[0],
+        recv_sem=pair.at[1],
+        device_id=(flip(lax.axis_index("dp"), 1), lax.axis_index("shard")),
+        device_id_type=MESH,
     )
-
-
-def sum_all(values, dps, shards, number):
-    total = dps * shards
+    copy.start()
+    mine = piece_ref[pl.ds(pl.multiple_of(x * rows, rows), rows), :]
+    wide = mine.astype(F32)
+    squares = jnp.sum(wide * wide)
+    copy.wait()
+    got = theirs[...]
+    wide = got.astype(F32)
+    squares = squares + jnp.sum(wide * wide)
+    low, high = pick(x, mine, got)
+    q_ref[:, :qc] = low[:, :qc]
+    q_ref[:, qc:] = high[:, :qc]
+    k_ref[...] = jnp.concatenate([low[:, qc : qc + HD], high[:, qc : qc + HD]], axis=1)
+    vc, oc = qc + HD, qc + 2 * HD
+    v_ref[...] = jnp.concatenate([low[:, vc:oc], high[:, vc:oc]], axis=1)
+    o_ref[:qc] = low[:, oc:].astype(F32).T.astype(BF)
+    o_ref[qc:] = high[:, oc:].astype(F32).T.astype(BF)
+    norm_ref[...] = jnp.sqrt(
+        two_stages(sq_ref[...] + squares, near, far, me, outer, bufs)
+    )
+
+
+def finish(piece, squares, dps, shards, number):
+    rows, cols = piece.shape[0] // 2, piece.shape[1]
+    qc = (cols - 2 * HD) // 2
+    vmem = pl.BlockSpec(memory_space=pltpu.VMEM)
     return pl.pallas_call(
-        functools.partial(sum_body, dps, shards),
-        in_specs=[pl.BlockSpec(memory_space=pltpu.VMEM)],
-        out_specs=pl.BlockSpec(memory_space=pltpu.VMEM),
-        out_shape=jax.ShapeDtypeStruct(values.shape, F32),
+        functools.partial(finish_body, dps, shards),
+        in_specs=[vmem, vmem],
+        out_specs=[vmem] * 5,
+        out_shape=[
+            jax.ShapeDtypeStruct((rows, 2 * qc), BF),
+            jax.ShapeDtypeStruct((rows, 2 * HD), BF),
+            jax.ShapeDtypeStruct((rows, 2 * HD), BF),
+            jax.ShapeDtypeStruct((2 * qc, rows), BF),
+            jax.ShapeDtypeStruct(squares.shape, F32),
+        ],
+        scratch_shapes=[pltpu.VMEM((rows, cols), BF), pltpu.SemaphoreType.DMA((2,))]
+        + sum_scratch(squares.shape, dps, shards),
+        compiler_params=pltpu.CompilerParams(collective_id=number, has_side_effects=True),
+        name="finish",
+    )(piece, squares)
+
+
+def collect_body(count, size, x_ref, *refs):
+    ins, (g_ref, u_ref, d_ref, sq_ref) = refs[: 2 * count], refs[2 * count :]
+    x = x_ref[0]
+    total = jnp.zeros((1, 1), F32)
+    for j in range(count):
+        size_in = ins[2 * j + 1].shape[0]
+        mine = ins[2 * j][pl.ds(pl.multiple_of(x * size_in, size_in), size_in), :]
+        theirs = ins[2 * j + 1][...]
+        for h, piece in enumerate(pick(x, mine, theirs)):
+            wide = piece.astype(F32)
+            total = total + jnp.sum(wide * wide, keepdims=True)
+            span = pl.ds((h * count + j) * size, size)
+            g_ref[:, span] = piece[:, :size]
+            u_ref[:, span] = piece[:, size : 2 * size]
+            d_ref[span, :] = wide[:, 2 * size :].T.astype(BF)
+    sq_ref[...] = jnp.broadcast_to(total, sq_ref.shape)
+
+
+def collect(x, pairs):
+    rows, size = pairs[0][1].shape[0], pairs[0][1].shape[1] // 3
+    wide = 2 * len(pairs) * size
+    vmem = pl.BlockSpec(memory_space=pltpu.VMEM)
+    ins = [v for pair in pairs for v in pair]
+    return pl.pallas_call(
+        functools.partial(collect_body, len(pairs), size),
+        in_specs=[pl.BlockSpec(memory_space=pltpu.SMEM)] + [vmem] * len(ins),
+        out_specs=[vmem] * 4,
+        out_shape=[
+            jax.ShapeDtypeStruct((rows, wide), BF),
+            jax.ShapeDtypeStruct((rows, wide), BF),
+            jax.ShapeDtypeStruct((wide, rows), BF),
+            jax.ShapeDtypeStruct((8, 128), F32),
+        ],
+        compiler_params=pltpu.CompilerParams(vmem_limit_bytes=VMEM),
+        name="collect",
+    )(x.reshape(1), *ins)
+
+
+PARTS = 4
+
+
+def flip(value, bit):
+    return value + bit * (1 - 2 * lax.rem(value // bit, 2))
+
+
+def neighbours():
+    dp, sh = lax.axis_index("dp"), lax.axis_index("shard")
+    return (flip(dp, 1), sh), (dp, flip(sh, 2)), (dp, flip(sh, 1))
+
+
+def remote(src, dst, sems, n, target):
+    return pltpu.make_async_remote_copy(
+        src_ref=src,
+        dst_ref=dst,
+        send_sem=sems.at[0, n],
+        recv_sem=sems.at[1, n],
+        device_id=target,
+        device_id_type=MESH,
+    )
+
+
+class Job:
+
+    def __init__(self, even, odd, scratch, targets, y_first=()):
+        self.y_first = y_first
+        self.even, self.odd = even, odd
+        self.got, self.out1, self.in1, self.out2, self.in2, self.own, self.sems, self.local = scratch
+        self.x, self.y, self.core = targets
+        self.rows = even.shape[1] // PARTS
+
+    @staticmethod
+    def scratch(rows, width):
+        part = rows // PARTS
+        return [
+            pltpu.VMEM((4, rows, width), BF),
+            pltpu.VMEM((PARTS, 2, part, width), BF),
+            pltpu.VMEM((PARTS, 2, part, width), BF),
+            pltpu.VMEM((PARTS, part, width), BF),
+            pltpu.VMEM((PARTS, part, width), BF),
+            pltpu.VMEM((rows, width), BF),
+            pltpu.SemaphoreType.DMA((2, 6 * PARTS)),
+            pltpu.SemaphoreType.DMA((PARTS,)),
+        ]
+
+    def span(self, s):
+        return pl.ds(s * self.rows, self.rows)
+
+    def over_x(self, s):
+        return s not in self.y_first
+
+    def copy(self, stage, s, src, dst, target):
+        return remote(src, dst, self.sems, stage * PARTS + s, target)
+
+    def to_core(self, s):
+        span = self.span(s)
+        return self.copy(0, s, self.odd.at[:, span], self.got.at[:, span], self.core)
+
+    def to_first(self, s):
+        target = self.x if self.over_x(s) else self.y
+        return self.copy(1, s, self.out1.at[s], self.in1.at[s], target)
+
+    def to_second(self, s):
+        target = self.y if self.over_x(s) else self.x
+        return self.copy(2, s, self.out2.at[s], self.in2.at[s], target)
+
+    def start(self):
+        for s in range(PARTS):
+            self.to_core(s).start()
+
+    def pair(self, k, s):
+        return self.even[k, self.span(s)].astype(F32) + self.got[k, self.span(s)].astype(F32)
+
+    def first(self, s):
+        self.to_core(s).wait_recv()
+        self.out1[s, 0] = self.pair(2 if self.over_x(s) else 1, s).astype(BF)
+        self.out1[s, 1] = self.pair(3, s).astype(BF)
+        self.to_first(s).start()
+
+    def second(self, s):
+        self.to_first(s).wait_recv()
+        near = self.pair(1 if self.over_x(s) else 2, s)
+        self.out2[s] = (near + self.in1[s, 1].astype(F32)).astype(BF)
+        self.to_second(s).start()
+
+    def total(self, s):
+        self.to_second(s).wait_recv()
+        return self.pair(0, s) + self.in1[s, 0].astype(F32) + self.in2[s].astype(F32)
+
+    def sent(self):
+        for s in range(PARTS):
+            self.to_core(s).wait_send()
+            self.to_first(s).wait_send()
+            self.to_second(s).wait_send()
+
+
+    def keep(self, s, place):
+        return pltpu.make_async_copy(self.own.at[self.span(s)], place, self.local.at[s])
+
+    def spread_copies(self, s, mine, theirs):
+        span = self.span(s)
+        own = self.own.at[span]
+        if self.over_x(s):
+            near = self.copy(3, s, own, mine.at[1, 0, span], self.x)
+            far = self.copy(4, s, mine.at[:, 0, span], mine.at[:, 1, span], self.y)
+        else:
+            near = self.copy(3, s, own, mine.at[0, 1, span], self.y)
+            far = self.copy(4, s, mine.at[0, :, span], mine.at[1, :, span], self.x)
+        core = self.copy(5, s, mine.at[:, :, span], theirs.at[:, :, span], self.core)
+        return self.keep(s, mine.at[0, 0, span]), near, far, core
+
+
+    def line_copies(self, s, whole):
+        me = lax.axis_index("shard")
+        size = self.rows * PARTS
+
+        def place(owner):
+            at = pl.multiple_of(owner * size + s * self.rows, self.rows)
+            return whole.at[pl.ds(at, self.rows)]
+
+        own = self.own.at[self.span(s)]
+        near = self.copy(3, s, own, place(me), self.y)
+        core = self.copy(4, s, own, place(me), self.core)
+        other = place(flip(me, 2))
+        return self.keep(s, place(me)), near, core, self.copy(5, s, other, other, self.core)
+
+    def line_start(self, s, whole):
+        for copy in self.line_copies(s, whole)[:3]:
+            copy.start()
+
+    def line_core(self, s, whole):
+        keep, near, core, far = self.line_copies(s, whole)
+        keep.wait()
+        near.wait_recv()
+        far.start()
+
+    def line_end(self, whole):
+        for s in range(PARTS):
+            _, near, core, far = self.line_copies(s, whole)
+            core.wait_recv()
+            far.wait_recv()
+            for copy in (near, core, far):
+                copy.wait_send()
+        self.sent()
+
+
+def run_job(job, mine, theirs, produce, filler=None):
+    blocks = range(PARTS)
+    job.start()
+    for s in blocks:
+        job.first(s)
+    if filler is not None:
+        filler(0)
+    for s in blocks:
+        job.second(s)
+    if filler is not None:
+        filler(1)
+    copies = [job.spread_copies(s, mine, theirs) for s in blocks]
+    for s in blocks:
+        job.own[job.span(s)] = produce(s, job.total(s)).astype(BF)
+        copies[s][0].start()
+        copies[s][1].start()
+    for keep, near, far, core in copies:
+        keep.wait()
+        near.wait_recv()
+        far.start()
+    for keep, near, far, core in copies:
+        far.wait_recv()
+        core.start()
+    if filler is not None:
+        filler(2)
+    for keep, near, far, core in copies:
+        core.wait_recv()
+        for copy in (near, far, core):
+            copy.wait_send()
+    job.sent()
+
+
+def rms_of(values):
+    return lax.rsqrt(jnp.mean(values * values, axis=1, keepdims=True) + EPS)
+
+
+def norm_back_of(values, gain, grad):
+    inverse = rms_of(values)
+    scaled = grad * gain
+    total = jnp.sum(grad * values * inverse, axis=0, keepdims=True)
+    mean = jnp.mean(scaled * values, axis=1, keepdims=True)
+    return total, inverse * scaled - values * (inverse * inverse * inverse * mean)
+
+
+def mid_body(
+    even, odd, tok_ref, gain_ref, cot_ref, mine, theirs, hidden_ref, cot_mine, cot_theirs, *scratch
+):
+    targets = neighbours()
+    xs, ys, core = targets
+    sh = lax.axis_index("shard")
+    quarter = cot_ref.shape[0] // 4
+    cot_sem, keeps = scratch[8:]
+    local = []
+    for n, (half, dy, owner) in enumerate(
+        (
+            (cot_mine, 0, sh),
+            (cot_mine, 1, flip(sh, 2)),
+            (cot_theirs, 0, flip(sh, 1)),
+            (cot_theirs, 1, flip(flip(sh, 1), 2)),
+        )
+    ):
+        src = cot_ref.at[pl.ds(pl.multiple_of(owner * quarter, quarter), quarter)]
+        local.append(pltpu.make_async_copy(src, half.at[0, dy], keeps.at[n]))
+    for copy in local:
+        copy.start()
+    meet(targets)
+    job = Job(even, odd, scratch[:8], targets, (1, 3))
+    rows = quarter // PARTS
+    over_x, over_y, over_core, over_far = [], [], [], []
+    for s in range(PARTS):
+        span = pl.ds(s * rows, rows)
+        own = cot_ref.at[pl.ds(pl.multiple_of(sh * quarter + s * rows, rows), rows)]
+        near, far = cot_mine.at[1, 0, span], cot_mine.at[1, 1, span]
+        over_x.append(remote(own, near, cot_sem, s, xs))
+        over_y.append(remote(near, far, cot_sem, PARTS + s, ys))
+        over_core.append(remote(near, cot_theirs.at[1, 0, span], cot_sem, 2 * PARTS + s, core))
+        over_far.append(remote(far, cot_theirs.at[1, 1, span], cot_sem, 3 * PARTS + s, core))
+
+    def cotangents(part):
+        for s in range(PARTS):
+            if part == 0:
+                over_x[s].start()
+            elif part == 1:
+                over_x[s].wait_recv()
+                over_y[s].start()
+                over_core[s].start()
+            else:
+                over_y[s].wait_recv()
+                over_far[s].start()
+
+    def produce(s, total):
+        hidden = tok_ref[job.span(s)].astype(F32) + total
+        hidden_ref[job.span(s)] = hidden
+        return hidden * rms_of(hidden) * gain_ref[...]
+
+    run_job(job, mine, theirs, produce, cotangents)
+    for copy in local:
+        copy.wait()
+    for copies in (over_core, over_far):
+        for copy in copies:
+            copy.wait_recv()
+    for copies in (over_x, over_y, over_core, over_far):
+        for copy in copies:
+            copy.wait_send()
+
+
+def back_body(even, odd, hidden_ref, cot_ref, gain_ref, *rest):
+    ins, (mine, theirs, gh_ref, gg_ref, dw_ref), scratch = rest[:8], rest[8:13], rest[13:]
+    held, (tiles, load, store) = scratch[8:16], scratch[16:]
+    targets = neighbours()
+    loads = [
+        pltpu.make_async_copy(src, dst, load.at[n]) for n, (src, dst) in enumerate(zip(ins, held))
+    ]
+    for copy in loads:
+        copy.start()
+    meet(targets)
+    job = Job(even, odd, scratch[:8], targets, (1, 3))
+    na, nb, ca, cb, ga, gb, aa, ab = held
+    size = aa.shape[1]
+    step = tiles.shape[1]
+    half = dw_ref.shape[0] // step // 2
+
+    def filler(part):
+        if part == 2:
+            return
+        if part == 0:
+            for copy in loads:
+                copy.wait()
+
+        def tile(n, carry):
+            i = part * half + n
+            cols = pl.ds(pl.multiple_of(i * step, step), step)
+            slot = lax.rem(n, 2)
+            copy = pltpu.make_async_copy(tiles.at[slot], dw_ref.at[cols], store.at[slot])
+
+            @pl.when(n >= 2)
+            def _():
+                copy.wait()
+
+            gu = dot(na[:, cols], ga[...], 0, 0) + dot(nb[:, cols], gb[...], 0, 0)
+            tiles[slot, :, : 2 * size] = gu.astype(BF)
+            dt = dot(ca[:, cols], aa[...], 0, 0) + dot(cb[:, cols], ab[...], 0, 0)
+            tiles[slot, :, 2 * size :] = dt.astype(BF)
+            copy.start()
+            return carry
+
+        lax.fori_loop(0, half, tile, 0)
+        for n in (0, 1):
+            cols = pl.ds(part * half * step, step)
+            pltpu.make_async_copy(tiles.at[n], dw_ref.at[cols], store.at[n]).wait()
+
+    totals = []
+
+    def produce(s, total):
+        gain_total, through = norm_back_of(hidden_ref[job.span(s)], gain_ref[...], total)
+        totals.append(gain_total)
+        grad_hidden = cot_ref[job.span(s)].astype(F32) + through
+        gh_ref[job.span(s)] = grad_hidden
+        return grad_hidden
+
+    run_job(job, mine, theirs, produce, filler)
+    gg_ref[...] = sum(totals[1:], totals[0])
+
+
+def trade(piece, theirs, sems):
+    size = theirs.shape[0]
+    x = lax.rem(lax.axis_index("dp"), 2)
+    src = piece.at[pl.ds(pl.multiple_of((1 - x) * size, size), size)]
+    return remote(src, theirs, sems, 0, neighbours()[0])
+
+
+def end_body(
+    dps, shards, even, odd, tok_ref, gh_ref, gain_ref, gg_ref, piece, in_ref, sum_ref, theirs, *scratch
+):
+    near, far, me, outer = peers(dps, shards)
+    meet(near + far)
+    job = Job(even, odd, scratch[:8], neighbours())
+    swapped = trade(piece, theirs, scratch[8])
+    blocks = range(PARTS)
+    totals = []
+    job.start()
+    for s in blocks:
+        job.first(s)
+    swapped.start()
+    for s in blocks:
+        job.second(s)
+    for s in blocks:
+        span = job.span(s)
+        values = tok_ref[span].astype(F32)
+        gain_total, through = norm_back_of(values, gain_ref[...], job.total(s))
+        totals.append(gain_total)
+        job.own[span] = (gh_ref[span] + through).astype(BF)
+        job.line_start(s, in_ref)
+    gains = jnp.concatenate([sum(totals[1:], totals[0]), gg_ref[...]], axis=0)
+    sum_ref[...] = two_stages(gains, near, far, me, outer, scratch[9:])
+    for s in blocks:
+        job.line_core(s, in_ref)
+    job.line_end(in_ref)
+    swapped.wait()
+
+
+def entry_body(tok_ref, keep_ref, send_ref, both, piece, hop_x, hop_y, hop_core, weight_sem, keeps):
+    xs, ys, core = neighbours()
+    sh = lax.axis_index("shard")
+    x = lax.rem(lax.axis_index("dp"), 2)
+    length = tok_ref.shape[0]
+    quarter = length // 4
+    rows = quarter // PARTS
+    size = keep_ref.shape[0]
+    mine = piece.at[pl.ds(pl.multiple_of(x * size, size), size)]
+    local = [
+        pltpu.make_async_copy(keep_ref, mine, keeps.at[0]),
+        pltpu.make_async_copy(tok_ref, both.at[pl.ds(0, length)], keeps.at[1]),
+    ]
+    for copy in local:
+        copy.start()
+    meet((xs, ys, core))
+
+    def rows_of(ref, base, owner, s):
+        return ref.at[pl.ds(pl.multiple_of(base + owner * quarter + s * rows, rows), rows)]
+
+    over_x, over_y, over_core, over_far = [], [], [], []
+    for s in range(PARTS):
+        near, far = rows_of(both, length, sh, s), rows_of(both, length, flip(sh, 2), s)
+        over_x.append(remote(rows_of(tok_ref, 0, sh, s), near, hop_x, s, xs))
+        over_y.append(remote(near, near, hop_y, s, ys))
+        over_core.append(remote(near, near, hop_core, s, core))
+        over_far.append(remote(far, far, hop_core, PARTS + s, core))
+    moving = remote(send_ref, mine, weight_sem, 0, xs)
+    for copy in over_x:
+        copy.start()
+    moving.start()
+    for s in range(PARTS):
+        over_x[s].wait_recv()
+        over_y[s].start()
+        over_core[s].start()
+    for s in range(PARTS):
+        over_y[s].wait_recv()
+        over_far[s].start()
+    moving.wait()
+    for copy in over_core + over_far:
+        copy.wait()
+    for copy in over_x + over_y:
+        copy.wait_send()
+    for copy in local:
+        copy.wait()
+
+
+def entry(tokens, keep, sent):
+    length, width = tokens.shape
+    dma = pltpu.SemaphoreType.DMA
+    return pl.pallas_call(
+        entry_body,
+        in_specs=[ANY] * 3,
+        out_specs=[ANY] * 2,
+        out_shape=[
+            jax.ShapeDtypeStruct((2 * length, width), BF),
+            jax.ShapeDtypeStruct((2 * keep.shape[0], keep.shape[1]), BF),
+        ],
         scratch_shapes=[
-            pltpu.VMEM((total,) + values.shape, F32),
-            pltpu.SemaphoreType.DMA((total,)),
-            pltpu.SemaphoreType.DMA((total,)),
-        ],
-        compiler_params=pltpu.CompilerParams(collective_id=number, has_side_effects=True),
-        name="sum_all",
-    )(values)
+            dma((2, PARTS)),
+            dma((2, PARTS)),
+            dma((2, 2 * PARTS)),
+            dma((2, 1)),
+            dma((2,)),
+        ],
+        compiler_params=pltpu.CompilerParams(
+            collective_id=6, has_side_effects=True, vmem_limit_bytes=8 << 20
+        ),
+        name="entry",
+    )(tokens, keep, sent)
+
+
+ANY = pl.BlockSpec(memory_space=pl.ANY)
+IN_VMEM = pl.BlockSpec(memory_space=pltpu.VMEM)
+BIG = 60 << 20
+
+
+def mid_stage(even, odd, tokens_own, gain, cotangent):
+    _, rows, width = even.shape
+    half = jax.ShapeDtypeStruct((2, 2, rows, width), BF)
+    return pl.pallas_call(
+        mid_body,
+        in_specs=[IN_VMEM, ANY, IN_VMEM, IN_VMEM, ANY],
+        out_specs=[ANY, ANY, IN_VMEM, ANY, ANY],
+        out_shape=[half, half, jax.ShapeDtypeStruct((rows, width), F32), half, half],
+        scratch_shapes=Job.scratch(rows, width)
+        + [pltpu.SemaphoreType.DMA((2, 4 * PARTS)), pltpu.SemaphoreType.DMA((4,))],
+        compiler_params=pltpu.CompilerParams(
+            collective_id=3, has_side_effects=True, vmem_limit_bytes=VMEM
+        ),
+        name="mid_stage",
+    )(even, odd, tokens_own, gain, cotangent)
+
+
+def back_stage(even, odd, hidden, cot_own, gain, *filling, tile=256):
+    _, rows, width = even.shape
+    size = filling[-1].shape[1]
+    spread_shape = jax.ShapeDtypeStruct((2, 2, rows, width), BF)
+    return pl.pallas_call(
+        back_body,
+        in_specs=[IN_VMEM, ANY, IN_VMEM, IN_VMEM, IN_VMEM] + [ANY] * 8,
+        out_specs=[ANY, ANY, IN_VMEM, IN_VMEM, ANY],
+        out_shape=[
+            spread_shape,
+            spread_shape,
+            jax.ShapeDtypeStruct((rows, width), F32),
+            jax.ShapeDtypeStruct((1, width), F32),
+            jax.ShapeDtypeStruct((width, 3 * size), BF),
+        ],
+        scratch_shapes=Job.scratch(rows, width)
+        + [pltpu.VMEM(value.shape, BF) for value in filling]
+        + [
+            pltpu.VMEM((2, tile, 3 * size), BF),
+            pltpu.SemaphoreType.DMA((8,)),
+            pltpu.SemaphoreType.DMA((2,)),
+        ],
+        compiler_params=pltpu.CompilerParams(
+            collective_id=4, has_side_effects=True, vmem_limit_bytes=BIG
+        ),
+        name="back_stage",
+    )(even, odd, hidden, cot_own, gain, *filling)
+
+
+def end_stage(even, odd, tokens_own, grad_hidden, gain, gain_grad, piece, dps, shards):
+    _, rows, width = even.shape
+    theirs = jax.ShapeDtypeStruct((piece.shape[0] // 2, piece.shape[1]), BF)
+    return pl.pallas_call(
+        functools.partial(end_body, dps, shards),
+        in_specs=[IN_VMEM, ANY] + [IN_VMEM] * 4 + [ANY],
+        out_specs=[ANY, IN_VMEM, ANY],
+        out_shape=[
+            jax.ShapeDtypeStruct((shards * rows, width), BF),
+            jax.ShapeDtypeStruct((2, width), F32),
+            theirs,
+        ],
+        scratch_shapes=Job.scratch(rows, width)
+        + [pltpu.SemaphoreType.DMA((2, 1))]
+        + sum_scratch((2, width), dps, shards),
+        compiler_params=pltpu.CompilerParams(
+            collective_id=5, has_side_effects=True, vmem_limit_bytes=VMEM
+        ),
+        name="end_stage",
+    )(even, odd, tokens_own, grad_hidden, gain, gain_grad, piece)
 
 
 def after(*values):
     return lax.optimization_barrier(values)
-
-
-def inverse_rms(values):
-    return lax.rsqrt(jnp.mean(values * values, axis=-1, keepdims=True) + EPS)
-
-
-def norm_back(values, inverse, gain, grad_normed):
-    scaled = grad_normed * gain
-    gain_grad = jnp.sum(grad_normed * values * inverse, axis=0)
-    grad_values = inverse * scaled - values * inverse**3 * jnp.mean(
-        scaled * values, axis=-1, keepdims=True
-    )
-    return (gain_grad, grad_values)
 
 
 def build(dps, shards):
@@ -417,34 +1116,6 @@
             whole, "dp", scatter_dimension=0, tiled=True, axis_index_groups=zgroups
         )
 
-
-    def sum_to_owner(even, odd, between=None):
-        got = swap(odd, 0, 1)
-
-        def pair(k):
-            return even[k].astype(F32) + got[k].astype(F32)
-
-        from_d = swap(pair(3).astype(BF), 1, 2)
-        from_y = swap(pair(1).astype(BF), 0, 2)
-        from_x = swap(pair(2).astype(BF), 1, 0)
-        filler = None
-        if between is not None:
-            filler = between(got)
-            from_d, from_y, from_x, filler = after(from_d, from_y, from_x, filler)
-        result = pair(0) + from_y.astype(F32) + from_x.astype(F32) + from_d.astype(F32)
-        return result if between is None else (result, filler)
-
-    def spread(own, between=None):
-        from_d = swap(own, 1, 2)
-        from_y = swap(own, 0, 2)
-        from_x = swap(own, 1, 0)
-        if between is not None:
-            filler = between(own)
-            from_d, from_y, from_x, filler = after(from_d, from_y, from_x, filler)
-            mine = jnp.stack([own, from_y, from_x, from_d])
-            return mine, swap(mine, 0, 1), filler
-        mine = jnp.stack([own, from_y, from_x, from_d])
-        return mine, swap(mine, 0, 1)
 
     def on_device(
         tokens,
@@ -519,34 +1190,25 @@
         low_q = w_query.astype(BF)
         low_k = w_key.astype(BF)
         low_v = w_value.astype(BF)
+        low_o = w_output.astype(BF).T
+        qc = group * HD
+        cols = qc + 2 * HD
 
         def attn_half(which):
-            return jnp.concatenate(
-                [half(low_q, which), half(low_k, which), half(low_v, which)], axis=1
-            )
-
-        cols = low_q.shape[1] // 2 + low_k.shape[1]
+            return jnp.concatenate([half(low, which) for low in (low_q, low_k, low_v, low_o)], axis=1)
+
         gains = jnp.stack([gain_first, gain_second]).astype(BF)
-        gains = jnp.pad(gains, ((0, 14), (0, cols - rows)))
+        gains = jnp.pad(gains, ((0, 14), (0, cols + qc - rows)))
         sent = swap(jnp.concatenate([attn_half(1 - x), gains], axis=0), 1, 0)
         piece = jnp.concatenate(
             [ordered(attn_half(x), sent[:rows]), ordered(gains, sent[rows:])], axis=0
         )
         groups = dps // 2
-        packed = gather(piece).reshape(groups, 2 * rows + 32, cols)
-        qkv_weight = packed[:, : 2 * rows].reshape(width, cols)
-        tails = packed[:, 2 * rows :].reshape(groups, 2, 16, cols)
-        gain_one = tails[:, :, 0, :rows].reshape(1, width).astype(F32)
-        gain_two = tails[:, :, 1, :rows].reshape(1, width).astype(F32)
-
-        low_o, w_g, w_u, w_d = after((w_output, w_gate, w_up, w_down), sent)[0]
-        low_o = low_o.astype(BF).T
-        low_g = w_g.astype(BF)
-        low_u = w_u.astype(BF)
-        low_d = w_d.astype(BF).T
-        tokens_x = swap(after(cut(tokens, 0), sent)[0], 1, 0)
+
         blocks_x = swap(block_ids, 1, 0)
-        out_x = swap(half(low_o, 1 - x), 1, 0)
+        low_g = w_gate.astype(BF)
+        low_u = w_up.astype(BF)
+        low_d = w_down.astype(BF).T
         size = low_g.shape[1] // 2 // CHUNKS
 
         def ffn_part(which, j):
@@ -555,52 +1217,45 @@
                 axis=1,
             )
 
-        def rest_of(from_x):
-            from_xy = swap(from_x, 0, 2)
-            other = swap(jnp.stack([from_x, from_xy]), 0, 1)
-            return [from_x, other[0], from_xy, other[1]]
-
-        out_weight = gather(ordered(half(low_o, x), out_x))
-        send_first, _, _ = after(ffn_part(1 - x, 0), tokens_x, out_x)
-        first_x = swap(send_first, 1, 0)
-        ffn_weights = [gather(ordered(ffn_part(x, 0), first_x))]
-        cot_x = swap(after(cut(cotangent, 0), first_x)[0], 1, 0)
-        second_x = swap(after(ffn_part(1 - x, 1), cot_x)[0], 1, 0)
-        ffn_weights.append(gather(ordered(ffn_part(x, 1), second_x)))
+        both, first_part = entry(
+            after(tokens, piece)[0], ffn_part(x, 0), ffn_part(1 - x, 0)
+        )
+        ffn_weights = [gather(first_part)]
+        packed, both, send_second = after(gather(piece), both, ffn_part(1 - x, 1))
+        second_part = ordered(ffn_part(x, 1), swap(send_second, 1, 0))
+        packed = packed.reshape(groups, 2 * rows + 32, cols + qc)
+        qkv_weight = packed[:, : 2 * rows, :cols].reshape(width, cols)
+        out_weight = packed[:, : 2 * rows, cols:].reshape(width, qc)
+        tails = packed[:, 2 * rows :].reshape(groups, 2, 16, cols + qc)
+        gain_one = tails[:, :, 0, :rows].reshape(1, width).astype(F32)
+        gain_two = tails[:, :, 1, :rows].reshape(1, width).astype(F32)
 
         cosine, sine = rope_tables(length, group)
 
-        def forward(own_tokens, own_blocks):
-            normed, query, key, value = qkv(own_tokens, gain_one, qkv_weight, cosine, sine, group)
-            block_rows = own_blocks[:, None, :]
-            block_cols = own_blocks.reshape(length, 1)
-            mixed, lse = attend(query, key, value, block_rows, block_cols, length)
-            return normed, mixed, (query, key, value, block_rows, block_cols, lse)
-
-        normed_own, mixed_own, saved_own = forward(tokens, block_ids)
-        other_tokens = natural(rest_of(tokens_x))
-        other_tokens, _, _ = after(other_tokens, cot_x, mixed_own)
-        normed_other, mixed_other, saved_other = forward(other_tokens, blocks_x)
-        cot_rest = rest_of(cot_x)
-        mixed_own, mixed_other, cot_rest, second_x = after(
-            mixed_own, mixed_other, cot_rest, second_x
-        )
-        cot_mine = flat(jnp.stack([cut(cotangent, 0), cut(cotangent, 2), cot_rest[0], cot_rest[2]]))
-        cot_theirs = flat(
-            jnp.stack([cut(cotangent, 1), cut(cotangent, 3), cot_rest[1], cot_rest[3]])
-        )
+        normed, query, key, value = qkv(both, gain_one, qkv_weight, cosine, sine, group)
+        blocks = jnp.concatenate([block_ids, blocks_x], axis=0)
+        block_rows = blocks[:, None, :]
+        block_cols = blocks.reshape(2 * length, 1)
+        mixed, lse = attend(query, key, value, block_rows, block_cols, length)
+        mixed, second_part = after(mixed, second_part)
+        ffn_weights.append(gather(second_part))
+        mixed_own, mixed_other = mixed[:length], mixed[length:]
         mixed_mine, mixed_theirs = halves(mixed_own, mixed_other)
 
         def project(values, weight):
             partial = jnp.einsum("atk,dk->atd", values, weight, preferred_element_type=F32)
             return partial.astype(BF)
 
-        summed = sum_to_owner(project(mixed_mine, out_weight), project(mixed_theirs, out_weight))
-        tokens_own = cut(tokens, 0).astype(F32)
-        hidden = tokens_own + summed
-        inverse_second = inverse_rms(hidden)
-        mine, theirs = spread((hidden * inverse_second * gain_two).astype(BF))
+        tokens_own = cut(tokens, 0)
+        mine, theirs, hidden, cot_mine, cot_theirs = mid_stage(
+            project(mixed_mine, out_weight),
+            project(mixed_theirs, out_weight),
+            tokens_own,
+            gain_two,
+            cotangent,
+        )
         two_mine, two_theirs = flat(mine), flat(theirs)
+        cot_mine, cot_theirs = flat(cot_mine), flat(cot_theirs)
 
         shape = (4, quarter, width)
         acts_mine = []
@@ -623,115 +1278,86 @@
             acts_mine.append(act_mine)
             acts_theirs.append(act_theirs)
 
-            def part_grads(token=None):
-                gu = gu_mine if token is None else after(gu_mine, token)[0]
-                return ffn_grads(
+            if not last:
+                first_grads = ffn_grads(
                     (two_mine, two_theirs),
                     (cot_mine, cot_theirs),
-                    (gu, gu_theirs),
+                    (gu_mine, gu_theirs),
                     (act_mine, act_theirs),
                 )
-
-            if not last:
-                first_grads = part_grads()
-        grad_normed_two, last_grads = sum_to_owner(
-            part_mine.reshape(shape), part_theirs.reshape(shape), part_grads
+        mine, theirs, grad_hidden, gain_grad_two, last_grads = back_stage(
+            part_mine.reshape(shape),
+            part_theirs.reshape(shape),
+            hidden,
+            cut(cotangent, 0),
+            gain_two,
+            two_mine,
+            two_theirs,
+            cot_mine,
+            cot_theirs,
+            gu_mine,
+            gu_theirs,
+            act_mine,
+            act_theirs,
         )
+        gh_mine = mine.reshape(shape)
+        gh_theirs = theirs.reshape(shape)
         first_piece = scatter(first_grads)
         last_piece = scatter(last_grads)
-        gain_grad_two, grad_through = norm_back(hidden, inverse_second, gain_two, grad_normed_two)
-        grad_hidden = cut(cotangent, 0).astype(F32) + grad_through
-
-        def outputs(token):
-            return tuple(
-                down([after(a, token)[0] for a in acts], ffn_weights)
-                for acts in (acts_mine, acts_theirs)
-            )
-
-        gh_mine, gh_theirs, (out_mine, out_theirs) = spread(grad_hidden.astype(BF), outputs)
-
-        def to_sequence(own):
-            pair = jnp.stack([own, swap(own, 0, 2)])
-            other = swap(pair, 0, 1)
-            return natural([pair[0], other[0], pair[1], other[1]])
-
         grad_mixed_mine = project(gh_mine, out_weight.T)
         grad_mixed_theirs = project(gh_theirs, out_weight.T)
         grad_mixed = streams(grad_mixed_mine, grad_mixed_theirs)
         grad_mixed, first_piece = after(grad_mixed, first_piece)
-        backs = [
-            attend_back(*saved, grad_mixed[k], cosine, sine, length)
-            for k, saved in enumerate((saved_own, saved_other))
-        ]
-        grad_qkv = [jnp.concatenate(pair, axis=1) for pair in backs]
-        d_out = jnp.einsum("atd,atk->dk", gh_mine, mixed_mine, preferred_element_type=F32)
-        d_out = d_out + jnp.einsum(
-            "atd,atk->dk", gh_theirs, mixed_theirs, preferred_element_type=F32
+        grad_q, grad_kv, output, first_theirs = attend_back(
+            query,
+            key,
+            value,
+            block_rows,
+            block_cols,
+            lse,
+            jnp.concatenate(grad_mixed, axis=0),
+            cosine,
+            sine,
+            length,
+            down(acts_mine, ffn_weights).reshape(shape),
+            down(acts_theirs, ffn_weights).reshape(shape),
+            hidden,
+            first_piece,
         )
-        grad_out = scatter(d_out.astype(BF))
-        d_qkv = jnp.einsum("tc,tk->ck", normed_own, grad_qkv[0], preferred_element_type=F32)
-        d_qkv = d_qkv + jnp.einsum(
-            "tc,tk->ck", normed_other, grad_qkv[1], preferred_element_type=F32
+        grad_qkv = jnp.concatenate([grad_q, grad_kv], axis=1)
+        d_attn = attn_grads(
+            normed,
+            grad_qkv,
+            (flat(gh_mine), flat(gh_theirs)),
+            (flat(mixed_mine), flat(mixed_theirs)),
         )
-        d_qkv = d_qkv.astype(BF)
-        grad_qkv_w = scatter(d_qkv)
-        gq_mine, gq_theirs = halves(*grad_qkv)
-        gq_mine, gq_theirs, _ = after(gq_mine, gq_theirs, d_qkv)
-        grad_normed, last_piece = sum_to_owner(
-            project(gq_mine, qkv_weight), project(gq_theirs, qkv_weight), lambda token: last_piece
+        grad_attn = scatter(d_attn)
+        gq_mine, gq_theirs = halves(grad_qkv[:length], grad_qkv[length:])
+        gq_mine, gq_theirs, d_attn = after(gq_mine, gq_theirs, d_attn)
+        input_grad, gain_grads, last_theirs = end_stage(
+            project(gq_mine, qkv_weight),
+            project(gq_theirs, qkv_weight),
+            tokens_own,
+            grad_hidden,
+            gain_one,
+            gain_grad_two,
+            last_piece,
+            dps,
+            shards,
         )
-
-        out_theirs, _ = after(out_theirs, gh_theirs)
-        output_own = hidden + sum_to_owner(out_mine.reshape(shape), out_theirs.reshape(shape))
-        output = to_sequence(output_own.astype(BF))
-
-        inverse_own = inverse_rms(tokens_own)
-        gain_grad_one, grad_inner = norm_back(tokens_own, inverse_own, gain_one, grad_normed)
-        input_grad = to_sequence((grad_hidden + grad_inner).astype(BF)).astype(F32)
-
-        def owned_halves(piece):
-            keep = lax.dynamic_slice_in_dim(piece, x * rows, rows, axis=0)
-            send = lax.dynamic_slice_in_dim(piece, (1 - x) * rows, rows, axis=0)
-            return keep, swap(send, 1, 0)
-
-        def joined(mine, theirs):
-            return ordered(mine, theirs, axis=1).astype(F32)
-
-        first_piece, _ = after(first_piece, d_qkv)
-        pairs = [owned_halves(first_piece), owned_halves(last_piece)]
-        grad_out, pairs = after(grad_out, pairs)
-        mine, theirs = owned_halves(grad_out)
-        grad_qkv_w, theirs = after(grad_qkv_w, theirs)
-        own_o = joined(mine, theirs).T
-        own_gud = []
-        for part in range(3):
-            span = slice(part * size, (part + 1) * size)
-            own_gud.append(
-                joined(
-                    jnp.concatenate([m[:, span] for m, t in pairs], axis=1),
-                    jnp.concatenate([t[:, span] for m, t in pairs], axis=1),
-                )
-            )
-        own_g, own_u, own_d = own_gud[0], own_gud[1], own_gud[2].T
-        gain_grads = jnp.stack([gain_grad_one, gain_grad_two]).reshape(-1, 128)
-        gain_grads, output = after(gain_grads, output)
-        gain_grads = sum_all(gain_grads, dps, shards, 1).reshape(2, width)
+        input_grad = input_grad.astype(F32)
+
+        pairs = [(first_piece, first_theirs), (last_piece, last_theirs)]
+        own_g, own_u, own_d, squares = collect(x, pairs)
         gain_grads = lax.dynamic_slice_in_dim(gain_grads, dp * rows, rows, axis=1)
-        mine, theirs = owned_halves(grad_qkv_w)
-        qc = group * HD
-        own_q = joined(mine[:, :qc], theirs[:, :qc])
-        own_k = joined(mine[:, qc : qc + HD], theirs[:, qc : qc + HD])
-        own_v = joined(mine[:, qc + HD :], theirs[:, qc + HD :])
+        first_shard = (me == 0).astype(F32)
+        squares = squares + first_shard * jnp.sum(gain_grads * gain_grads)
+        grad_attn, squares, output, own_g, own_u, own_d = after(
+            grad_attn, squares, output, own_g, own_u, own_d
+        )
+        own_q, own_k, own_v, own_o, norm = finish(grad_attn, squares, dps, shards, 2)
+        global_norm = norm[0, 0]
         owned = (gain_grads[0], own_q, own_k, own_v, own_o, gain_grads[1], own_g, own_u, own_d)
-
-        first_shard = (me == 0).astype(F32)
-        squares = first_shard * (jnp.sum(owned[0] * owned[0]) + jnp.sum(owned[5] * owned[5]))
-        for position in (1, 2, 3, 4, 6, 7, 8):
-            squares = squares + jnp.sum(owned[position] * owned[position])
-        squares = jnp.broadcast_to(squares, (8, 128))
-        squares, input_grad = after(squares, input_grad)
-        squares = sum_all(squares, dps, shards, 2)
-        global_norm = jnp.sqrt(squares[0, 0])
         factor = jnp.minimum(1.0, CLIP / global_norm)
         rate_now = rate * jnp.minimum(1.0, (step.astype(F32) + 1.0) / WARMUP)
         masters = (gain_first, w_query, w_key, w_value, w_output, gain_second, w_gate, w_up, w_down)

time: 798 us -> 756 us (0.947)
  Pallas kernels: 214 us -> 613 us
  waiting for transfers between devices: 277 us -> 8.28 us
  other arithmetic: 124 us -> 37.5 us
  starting transfers between devices: 41.2 us -> 6.17 us
  local copies, waits for them, and re-layouts: 76.7 us -> 48.7 us
  matrix products: 33.7 us -> 20.5 us
    pallas_call x2 -> x7, Pallas kernels: 27.4 us -> 387 us  [the longest x1 131 us: mid_stage(): pl.pallas_call(mid_body, in_specs=[IN_VMEM, ANY, IN_VMEM, IN_VMEM, ANY],...]
    ppermute x43 -> x3, waiting for transfers between devices: 272 us -> 8.15 us  [swap(): return lax.ppermute(values, axes, pairs)]
    pallas_call x2 -> x1, Pallas kernels: 29.6 us -> 88.1 us  [attend_back(): pl.pallas_call(functools.partial(bwd_body, limits), grid=(seqs, per), in_...]
    ppermute x43 -> x3, starting transfers between devices: 39.9 us -> 5.16 us  [swap(): return lax.ppermute(values, axes, pairs)]
    convert_element_type x11 -> x4, other arithmetic: 32.9 us -> 8.97 us  [the longest x1 6.94 us: on_device(): input_grad = input_grad.astype(F32)]
    another operation x12 -> x2, other arithmetic: 22.4 us -> 0.01 us  [the longest x2 5.47 us: to_sequence(): pair = jnp.stack([own, swap(own, 0, 2)])]
    reduce_sum x12 -> x1, other arithmetic: 21.4 us -> 0.6 us  [on_device(): squares = squares + first_shard * jnp.sum(gain_grads * gain_grads)]
    pallas_call x2 -> x1, Pallas kernels: 36.3 us -> 18.1 us  [ffn_grads(): pl.pallas_call(grad_body, grid=(width // tile,), in_specs=[pl.BlockSpec((...]
  transfers between devices with their start and end apart: 51 -> 9, of which waited for: 24 -> 1; matrix products, arithmetic and copies ran while one was open for 23% -> 8% of each run, Pallas kernels for 25% -> 79%
where the time goes in v4:
time: 756 us; the launch traced here: 752 us
  Pallas kernels  613 us (81%)
  local copies, waits for them, and re-layouts  48.7 us (6%)
  other arithmetic  37.5 us (5%)
  matrix products  20.5 us (3%)
  between operations  18.1 us (2%)
  waiting for transfers between devices  8.28 us (1%)
    pallas_call x1, Pallas kernels, mid_stage(): pl.pallas_call(mid_body, in_specs=[IN_VMEM, ANY, IN_VMEM, IN_VMEM, ANY],...  131 us
    pallas_call x1, Pallas kernels, end_stage(): pl.pallas_call(functools.partial(end_body, dps, shards), in_specs=[IN_VME...  93.5 us
    pallas_call x1, Pallas kernels, attend_back(): pl.pallas_call(functools.partial(bwd_body, limits), grid=(seqs, per), in_...  88.1 us
    pallas_call x1, Pallas kernels, back_stage(): pl.pallas_call(back_body, in_specs=[IN_VMEM, ANY, IN_VMEM, IN_VMEM, IN_VM...  83.7 us
    pallas_call x4, Pallas kernels, up_back(): pl.pallas_call(functools.partial(up_body, prev is None, last), grid=(coun...  71 us
    pallas_call x1, Pallas kernels, entry(): pl.pallas_call(entry_body, in_specs=[ANY] * 3, out_specs=[ANY] * 2, out_s...  43.2 us
    unnamed x162, local copies, waits for them, and re-layouts  30.8 us
    pallas_call x1, Pallas kernels, finish(): pl.pallas_call(functools.partial(finish_body, dps, shards), in_specs=[vme...  20.5 us
  transfers between devices with their start and end apart: 9, of which 1 were waited for; matrix products, arithmetic and copies ran while one was open for 8% of the time, Pallas kernels for 79%

profile of v4, /device:TPU:0, one launch (start us, length us, event | category | flops | bytes accessed | tf_op | source)
XLA Modules:
  0.0 751.9 jit_solution(15884226836231534198)
XLA Ops:
  10.1 3.0 collective-permute-start
  13.1 8.1 %collective-permute-done = bf16[272,640]{1,0:T(8,128)(2,1)S(1)} collective-permute-done((bf16[272,640]{1,0:T(8,128)(2,1)S(1)}, bf16[272,640]{1,0:T(8,128)(2,1)S(1)}, u32[]{:S(2)}, u32[]{:S(2)}) %collective-permute-start) | collective-permute-done | bytes 348192 | tf_op jit(solution)/shard_map/ppermute | solution.py:1109
  23.1 1.9 convert_element_type.97
  26.8 2.0 copy-done.2
  28.8 43.2 %entry.1 = (bf16[2048,2048]{1,0:T(8,128)(2,1)S(1)}, bf16[512,1536]{1,0:T(8,128)(2,1)}) custom-call(bf16[1024,2048]{1,0:T(8,128)(2,1)S(1)} %copy-done.2, bf16[256,1536]{1,0:T(8,128)(2,1)S(1)} %pad_maximum_fusion.2.keep_ref, bf16[256,1536]{1,0:T(8,128)(2,1)S(1)} %pad_maximum_fusion.3.send_ref), custom_call_target="tpu_custom_call" | custom-call | tf_op jit(solution)/shard_map/entry/pallas_call | solution.py:1001
  72.0 3.4 copy-done.1
  77.7 1.6 copy.52
  79.5 1.6 copy.53
  81.1 1.6 concatenate.62.cos_ref.kcos_ref
  83.0 1.3 concatenate.64.sin_ref.ksin_ref
  84.8 2.0 slice.143
  87.9 1.8 collective-permute-start.2
  89.7 1.6 copy-done.7
  91.4 13.6 %qkv_rope.1 = (bf16[2048,2048]{1,0:T(8,128)(2,1)}, bf16[4,2048,64]{2,1,0:T(8,128)(2,1)}, bf16[2048,64]{1,0:T(8,128)(2,1)S(1)}, bf16[2048,64]{1,0:T(8,128)(2,1)S(1)}) custom-call(bf16[2048,2048]{1,0:T(8,128)(2,1)} %copy-done.1, f32[1,2048]{1,0:T(1,128)S(1)} %convert.12.gain_ref, bf16[2048,384]{1,0:T(8,128)(2,1)S(1)} %bitcast.103, ...), custom_call_target="tpu_custom_call" | custom-call | flops 3221225472 | bytes 16777216 | tf_op jit(solution)/shard_map/qkv_rope/pallas_call | solution.py:55
  105.0 17.6 %attend.1 = (bf16[2048,256]{1,0:T(8,128)(2,1)S(1)}, f32[2048,4]{1,0:T(8,128)S(1)}) custom-call(bf16[4,2048,64]{2,1,0:T(8,128)(2,1)} %get-tuple-element.93.q_ref, bf16[2048,64]{1,0:T(8,128)(2,1)S(1)} %get-tuple-element.94.k_ref, bf16[2048,64]{1,0:T(8,128)(2,1)S(1)} %get-tuple-element.95.v_ref, s32[2,1,1024]{2,1,0:T(1,128)S(1)} %broadcast_in_dim.2.brow_ref, ...), custom_call_target="tpu_custom_call" | custom-call | flops 8589934592 | bytes 4194304 | tf_op jit(solution)/shard_map/attend/pallas_call | solution.py:112
  127.0 1.3 slice.145
  128.6 3.3 convolution_convert_fusion.2.odd
  132.0 3.3 convolution_convert_fusion.3.even
  135.3 131.2 %mid_stage.1 = (bf16[2,2,256,2048]{3,2,1,0:T(8,128)(2,1)}, bf16[2,2,256,2048]{3,2,1,0:T(8,128)(2,1)}, f32[256,2048]{1,0:T(8,128)S(1)}, bf16[2,2,256,2048]{3,2,1,0:T(8,128)(2,1)}, bf16[2,2,256,2048]{3,2,1,0:T(8,128)(2,1)}) custom-call(bf16[4,256,2048]{2,1,0:T(8,128)(2,1)} %convolution_convert_fusion.3.even, ...), custom_call_target="tpu_custom_call" | custom-call | tf_op jit(solution)/shard_map/mid_stage/pallas_call | solution.py:1031
  266.4 1.3 copy-done.13
  267.8 17.0 %swiglu_part.5 = (bf16[1024,512]{1,0:T(8,128)(2,1)S(1)}, bf16[1024,1024]{1,0:T(8,128)(2,1)S(1)}, f32[1024,2048]{1,0:T(8,128)}) custom-call(bf16[1024,2048]{1,0:T(8,128)(2,1)} %bitcast.120, bf16[1024,2048]{1,0:T(8,128)(2,1)} %bitcast.128, bf16[2048,1536]{1,0:T(8,128)(2,1)} %all-gather.6.cloned.1.call-done.w_ref.refs_2_), custom_call_target="tpu_custom_call" | custom-call | flops 10737418240 | bytes 25165824 | tf_op jit(solution)/shard_map/swiglu_part/pallas_call | solution.py:326
  284.8 1.3 copy-done.31
  286.1 17.4 %swiglu_part.4 = (bf16[1024,512]{1,0:T(8,128)(2,1)S(1)}, bf16[1024,1024]{1,0:T(8,128)(2,1)S(1)}, f32[1024,2048]{1,0:T(8,128)}) custom-call(bf16[1024,2048]{1,0:T(8,128)(2,1)} %bitcast.116, bf16[1024,2048]{1,0:T(8,128)(2,1)} %bitcast.124, bf16[2048,1536]{1,0:T(8,128)(2,1)} %all-gather.6.cloned.1.call-done.w_ref.refs_2_), custom_call_target="tpu_custom_call" | custom-call | flops 10737418240 | bytes 25165824 | tf_op jit(solution)/shard_map/swiglu_part/pallas_call | solution.py:326
  303.5 18.1 %swiglu_grads.1 = bf16[2048,1536]{1,0:T(8,128)(2,1)} custom-call(bf16[1024,2048]{1,0:T(8,128)(2,1)} %bitcast.117, bf16[1024,2048]{1,0:T(8,128)(2,1)} %bitcast.121, bf16[1024,2048]{1,0:T(8,128)(2,1)} %bitcast.125, bf16[1024,2048]{1,0:T(8,128)(2,1)} %bitcast.129, bf16[1024,1024]{1,0:T(8,128)(2,1)S(1)} %get-tuple-element.105.dgua, ...), custom_call_target="tpu_custom_call" | custom-call | flops 12884901888 | bytes 33554432 | tf_op jit(solution)/shard_map/swiglu_grads/pallas_call | solution.py:350
  321.9 2.3 constant_dynamic-slice_fusion.6.cot_ref
  324.2 18.6 %swiglu_part.6 = (bf16[1024,512]{1,0:T(8,128)(2,1)S(1)}, bf16[1024,1024]{1,0:T(8,128)(2,1)S(1)}, bf16[1024,2048]{1,0:T(8,128)(2,1)}) custom-call(bf16[1024,2048]{1,0:T(8,128)(2,1)} %bitcast.122, bf16[1024,2048]{1,0:T(8,128)(2,1)} %bitcast.130, bf16[2048,1536]{1,0:T(8,128)(2,1)} %all-gather.8.cloned.1.call-done.w_ref.refs_3_, ...), custom_call_target="tpu_custom_call" | custom-call | flops 10737418240 | bytes 25165824 | tf_op jit(solution)/shard_map/swiglu_part/pallas_call | solution.py:326
  343.8 1.3 copy-done.14
  345.1 18.0 %swiglu_part.7 = (bf16[1024,512]{1,0:T(8,128)(2,1)S(1)}, bf16[1024,1024]{1,0:T(8,128)(2,1)S(1)}, bf16[1024,2048]{1,0:T(8,128)(2,1)}) custom-call(bf16[1024,2048]{1,0:T(8,128)(2,1)} %bitcast.118, bf16[1024,2048]{1,0:T(8,128)(2,1)} %bitcast.126, bf16[2048,1536]{1,0:T(8,128)(2,1)} %all-gather.8.cloned.1.call-done.w_ref.refs_3_, ...), custom_call_target="tpu_custom_call" | custom-call | flops 10737418240 | bytes 25165824 | tf_op jit(solution)/shard_map/swiglu_part/pallas_call | solution.py:326
  364.2 1.3 copy-done.15
  365.5 83.7 %back_stage.1 = (bf16[2,2,256,2048]{3,2,1,0:T(8,128)(2,1)}, bf16[2,2,256,2048]{3,2,1,0:T(8,128)(2,1)}, f32[256,2048]{1,0:T(8,128)}, f32[1,2048]{1,0:T(1,128)}, bf16[2048,1536]{1,0:T(8,128)(2,1)}) custom-call(bf16[4,256,2048]{2,1,0:T(8,128)(2,1)} %bitcast.133, bf16[4,256,2048]{2,1,0:T(8,128)(2,1)} %bitcast.132, f32[256,2048]{1,0:T(8,128)} %copy-done.13, ...), custom_call_target="tpu_custom_call" | custom-call | tf_op jit(solution)/shard_map/back_stage/pallas_call | solution.py:1049
  452.0 3.9 convolution_convert_fusion.5
  459.4 8.5 %swiglu_down.3 = bf16[1024,2048]{1,0:T(8,128)(2,1)} custom-call(bf16[1024,512]{1,0:T(8,128)(2,1)S(1)} %copy-done.18, bf16[1024,512]{1,0:T(8,128)(2,1)S(1)} %copy-done.9, bf16[2048,1536]{1,0:T(8,128)(2,1)} %all-gather.6.cloned.1.call-done.w_ref.refs_2_, bf16[2048,1536]{1,0:T(8,128)(2,1)} %all-gather.8.cloned.1.call-done.w_ref.refs_3_), custom_call_target="tpu_custom_call" | custom-call | flops 4294967296 | bytes 16777216 | tf_op jit(solution)/shard_map/swiglu_down/pallas_call | solution.py:416
  467.9 8.5 %swiglu_down.2 = bf16[1024,2048]{1,0:T(8,128)(2,1)} custom-call(bf16[1024,512]{1,0:T(8,128)(2,1)S(1)} %get-tuple-element.107.acta.refs_0_, bf16[1024,512]{1,0:T(8,128)(2,1)S(1)} %copy-done.11, bf16[2048,1536]{1,0:T(8,128)(2,1)} %all-gather.6.cloned.1.call-done.w_ref.refs_2_, bf16[2048,1536]{1,0:T(8,128)(2,1)} %all-gather.8.cloned.1.call-done.w_ref.refs_3_), custom_call_target="tpu_custom_call" | custom-call | flops 4294967296 | bytes 16777216 | tf_op jit(solution)/shard_map/swiglu_down/pallas_call | solution.py:416
  476.4 2.4 pad_maximum_fusion.1.do_ref
  480.1 88.1 %attend_back.1 = (bf16[2048,256]{1,0:T(8,128)(2,1)S(1)}, bf16[2048,128]{1,0:T(8,128)(2,1)S(1)}, bf16[1024,2048]{1,0:T(8,128)(2,1)}, bf16[256,1536]{1,0:T(8,128)(2,1)S(1)}) custom-call(bf16[4,2048,64]{2,1,0:T(8,128)(2,1)} %get-tuple-element.93.q_ref, bf16[2048,64]{1,0:T(8,128)(2,1)S(1)} %copy-done.28, bf16[2048,64]{1,0:T(8,128)(2,1)S(1)} %copy-done.30, ...), custom_call_target="tpu_custom_call" | custom-call | flops 21474836480 | bytes 8388608 | tf_op jit(solution)/shard_map/attend_back/pallas_call | solution.py:245
  570.1 11.6 %attn_grads.1 = bf16[2048,640]{1,0:T(8,128)(2,1)S(1)} custom-call(bf16[2048,2048]{1,0:T(8,128)(2,1)} %get-tuple-element.92.na, bf16[2048,384]{1,0:T(8,128)(2,1)S(1)} %constant_dynamic-update-slice_fusion.ga, bf16[1024,2048]{1,0:T(8,128)(2,1)} %bitcast.135, bf16[1024,2048]{1,0:T(8,128)(2,1)} %bitcast.136, bf16[1024,256]{1,0:T(8,128)(2,1)S(1)} %bitcast.107, ...), custom_call_target="tpu_custom_call" | custom-call | flops 5368709120 | bytes 33554432 | tf_op jit(solution)/shard_map/attn_grads/pallas_call | solution.py:386
  581.7 1.5 copy-done
  586.2 4.4 convolution_convert_fusion.odd
  590.6 4.4 convolution_convert_fusion.1.even
  595.0 1.4 copy-done.3
  596.4 93.5 %end_stage.1 = (bf16[1024,2048]{1,0:T(8,128)(2,1)}, f32[2,2048]{1,0:T(2,128)S(1)}, bf16[256,1536]{1,0:T(8,128)(2,1)S(1)}) custom-call(bf16[4,256,2048]{2,1,0:T(8,128)(2,1)} %convolution_convert_fusion.1.even, bf16[4,256,2048]{2,1,0:T(8,128)(2,1)} %convolution_convert_fusion.odd, bf16[256,2048]{1,0:T(8,128)(2,1)S(1)} %constant_dynamic-slice_fusion.7.tok_ref, ...), custom_call_target="tpu_custom_call" | custom-call | tf_op jit(solution)/shard_map/end_stage/pallas_call | solution.py:1077
  690.0 6.9 convert_element_type.111
  700.4 3.5 collect.1
  704.5 20.5 %finish.1 = (bf16[256,512]{1,0:T(8,128)(2,1)}, bf16[256,128]{1,0:T(8,128)(2,1)}, bf16[256,128]{1,0:T(8,128)(2,1)}, bf16[512,256]{1,0:T(8,128)(2,1)}, f32[8,128]{1,0:T(8,128)}) custom-call(bf16[512,640]{1,0:T(8,128)(2,1)} %reduce-scatter.6.cloned.1.call-done.piece_ref, f32[8,128]{1,0:T(8,128)} %broadcast_add_fusion.sq_ref), custom_call_target="tpu_custom_call" | custom-call | tf_op jit(solution)/shard_map/finish/pallas_call | solution.py:547
  727.0 4.8 multiply_subtract_fusion
  731.9 2.9 multiply_subtract_fusion.1
  735.0 2.9 multiply_subtract_fusion.2
  742.9 2.0 copy.62
  (240 shorter events, 38.1 us)
Async XLA Ops:
  7.2 77.5 %all-gather.4.cloned.1.call-start = ((), (), s32[]{:S(2)}) async-start(), calls=%async_computation.3 | async-start | bytes 3481600 | tf_op jit(solution)/shard_map/all_gather | solution.py:1112
  10.0 12.5 %copy-start.36 = (f32[2048,256]{1,0:T(8,128)S(1)}, f32[2048,256]{1,0:T(8,128)}, u32[]{:S(2)}) copy-start(f32[2048,256]{1,0:T(8,128)} %param.34) | copy-start | bytes 6291460
  10.1 11.2 %collective-permute-start = (bf16[272,640]{1,0:T(8,128)(2,1)S(1)}, bf16[272,640]{1,0:T(8,128)(2,1)S(1)}, u32[]{:S(2)}, u32[]{:S(2)}) collective-permute-start(bf16[272,640]{1,0:T(8,128)(2,1)S(1)} %pad_maximum_fusion.15), channel_id=1, source_target_pairs={{0,4},{1,5},{2,6},{3,7},{4,0},{5,1},{6,2},{7,3},{8,12},{9,13},{10,... | collective-permute-start | bytes 1044488 | tf_op jit(solution)/shard_map/ppermute | solution.py:1109
  22.4 245.3 %all-gather.6.cloned.1.call-start = ((), (), s32[]{:S(2)}) async-start(), calls=%async_computation.4 | async-start | bytes 7864320 | tf_op jit(solution)/shard_map/all_gather | solution.py:1112
  28.8 46.8 %copy-start.71 = (s32[1,1024]{1,0:T(1,128)S(1)}, s32[1,1024]{1,0:T(1,128)}, u32[]{:S(2)}) copy-start(s32[1,1024]{1,0:T(1,128)} %param.24) | copy-start | bytes 12292
  72.0 3.4 copy-start.1
  75.4 248.8 %all-gather.8.cloned.1.call-start = ((), (), s32[]{:S(2)}) async-start(), calls=%async_computation.5 | async-start | bytes 7864320 | tf_op jit(solution)/shard_map/all_gather | solution.py:1112
  75.6 8.6 %collective-permute-start.1 = (s32[1,1024]{1,0:T(1,128)S(1)}, s32[1,1024]{1,0:T(1,128)S(1)}, u32[]{:S(2)}, u32[]{:S(2)}) collective-permute-start(s32[1,1024]{1,0:T(1,128)S(1)} %copy-done.71), channel_id=1, source_target_pairs={{0,4},{1,5},{2,6},{3,7},{4,0},{5,1},{6,2},{7,3},{8,12},{9,13},{10,... | collective-permute-start | bytes 12296 | tf_op jit(solution)/shard_map/ppermute | solution.py:1109
  83.0 6.8 copy-start.6
  84.7 20.3 %copy-start.19 = (s32[1,2048]{0,1:T(8,128)}, s32[1,2048]{0,1:T(8,128)S(1)}, u32[]{:S(2)}) copy-start(s32[1,2048]{0,1:T(8,128)S(1)} %copy.57) | copy-start | bytes 24580
  84.7 3.1 copy-start.58
  86.7 18.3 %copy-start.4 = (bf16[4,512,384]{2,1,0:T(8,128)(2,1)}, bf16[4,512,384]{2,1,0:T(8,128)(2,1)S(1)}, u32[]{:S(2)}) copy-start(bf16[4,512,384]{2,1,0:T(8,128)(2,1)S(1)} %slice.143) | copy-start | bytes 4718596
  87.9 35.8 %collective-permute-start.2 = (bf16[256,1536]{1,0:T(8,128)(2,1)S(1)}, bf16[256,1536]{1,0:T(8,128)(2,1)S(1)}, u32[]{:S(2)}, u32[]{:S(2)}) collective-permute-start(bf16[256,1536]{1,0:T(8,128)(2,1)S(1)} %copy-done.58), channel_id=1, source_target_pairs={{0,4},{1,5},{2,6},{3,7},{4,0},{5,1},{6,2},{7,3},{8,12},{9,13},{10,... | collective-permute-start | bytes 2359304 | tf_op jit(solution)/shard_map/ppermute | solution.py:1109
  105.0 17.7 %copy-start.27 = (bf16[2048,64]{1,0:T(8,128)(2,1)}, bf16[2048,64]{1,0:T(8,128)(2,1)S(1)}, u32[]{:S(2)}) copy-start(bf16[2048,64]{1,0:T(8,128)(2,1)S(1)} %get-tuple-element.94.k_ref) | copy-start | bytes 786436
  105.0 17.7 %copy-start.29 = (bf16[2048,64]{1,0:T(8,128)(2,1)}, bf16[2048,64]{1,0:T(8,128)(2,1)S(1)}, u32[]{:S(2)}) copy-start(bf16[2048,64]{1,0:T(8,128)(2,1)S(1)} %get-tuple-element.95.v_ref) | copy-start | bytes 786436
  105.0 18.7 %copy-start.56 = (bf16[256,512]{1,0:T(8,128)(2,1)S(1)}, bf16[256,512]{1,0:T(8,128)(2,1)}, u32[]{:S(2)}) copy-start(bf16[256,512]{1,0:T(8,128)(2,1)} %get-tuple-element.171) | copy-start | bytes 786436
  105.0 18.6 %copy-start.57 = (bf16[256,512]{1,0:T(8,128)(2,1)S(1)}, bf16[256,512]{1,0:T(8,128)(2,1)}, u32[]{:S(2)}) copy-start(bf16[256,512]{1,0:T(8,128)(2,1)} %get-tuple-element.251) | copy-start | bytes 786436
  125.2 351.2 %reduce-scatter.4.cloned.1.call-start = ((), (), s32[]{:S(2)}) async-start(), calls=%async_computation.6 | async-start | bytes 7864320 | tf_op jit(solution)/shard_map/reduce_scatter | solution.py:1115
  128.3 3.6 copy-start.34
  128.3 6.9 copy-start.25
  128.5 3.4 copy-start.47
  128.6 3.4 copy-start.53
  128.6 3.3 copy-start.55
  128.6 3.3 copy-start.49
  128.6 3.3 copy-start.51
  286.1 17.4 %copy-start.17 = (bf16[1024,512]{1,0:T(8,128)(2,1)}, bf16[1024,512]{1,0:T(8,128)(2,1)S(1)}, u32[]{:S(2)}) copy-start(bf16[1024,512]{1,0:T(8,128)(2,1)S(1)} %get-tuple-element.108.actb.refs_0_) | copy-start | bytes 3145732
  321.6 273.4 %reduce-scatter.8.cloned.1.call-start = ((), (), s32[]{:S(2)}) async-start(), calls=%async_computation.8 | async-start | bytes 7864320 | tf_op jit(solution)/shard_map/reduce_scatter | solution.py:1115
  449.3 255.3 %reduce-scatter.6.cloned.1.call-start = ((), (), s32[]{:S(2)}) async-start(), calls=%async_computation.7 | async-start | bytes 3276800 | tf_op jit(solution)/shard_map/reduce_scatter | solution.py:1115
  452.0 3.9 copy-start.35
  452.0 4.2 copy-start.42
  459.4 8.5 %copy-start.11 = (bf16[1024,512]{1,0:T(8,128)(2,1)S(1)}, bf16[1024,512]{1,0:T(8,128)(2,1)}, u32[]{:S(2)}) copy-start(bf16[1024,512]{1,0:T(8,128)(2,1)} %copy-done.10) | copy-start | bytes 3145732
  590.6 4.4 copy-start.12
  590.6 4.4 copy-start.26
  690.0 7.0 copy-start.23
  727.0 4.8 copy-start.38
  727.0 4.8 copy-start.43
  731.8 2.9 copy-start.39
  731.9 3.1 copy-start.44
  735.0 3.0 copy-start.45
  735.0 3.0 copy-start.63
  735.0 3.0 copy-start.66
  735.0 4.1 copy-start.70
  735.0 4.8 copy-start.68
  735.0 6.7 copy-start.73
  735.0 6.7 copy-start.74
  735.0 7.3 copy-start.76
  735.0 7.3 copy-start.77
  738.0 4.9 copy-start.41
  (39 other events, 66.7 us)
Sparse Core Ops, SparseCore 0:
  22.5 59.0 all-gather.3
  83.2 114.0 all-gather.5
  199.4 113.5 all-gather.7
  321.7 111.2 reduce-scatter.3
  449.4 111.4 reduce-scatter.7
  583.4 52.6 reduce-scatter.5

commit v5 on v4

--- a/solution.py
+++ b/solution.py
@@ -21,7 +21,7 @@
 HD = 64
 EPS = 1e-05
 NEGATIVE = -1e30
-VMEM = 48 << 20
+VMEM = 60 << 20
 
 def dot(a, b, ca, cb):
     return lax.dot_general(a, b, (((ca,), (cb,)), ((), ())), preferred_element_type=F32)
@@ -148,11 +148,9 @@
     even,
     odd,
     hidden_ref,
-    piece,
     dq_ref,
     dkv_ref,
     out_ref,
-    theirs,
     dk_acc,
     dv_acc,
     *scratch
@@ -161,32 +159,20 @@
     i = pl.program_id(1)
     turn = pl.program_id(0) * pl.num_programs(1) + i
     targets = neighbours()
-    job = Job(even, odd, scratch[:8], targets)
-    swapped = trade(piece, theirs, scratch[8])
-    blocks = range(PARTS)
+    job = Job(even, odd, scratch, targets)
+
+    def produce(s, total):
+        return hidden_ref[job.span(s)] + total
 
     @pl.when(turn == 0)
     def _():
         meet(targets)
-        job.start()
-        for s in blocks:
-            job.first(s)
-
-    @pl.when(turn == 1)
-    def _():
-        swapped.start()
-
-    for s in blocks:
-
-        @pl.when(turn == 2 + s)
-        def _(s=s):
-            job.second(s)
-
-    @pl.when(turn == 6)
-    def _():
-        for s in blocks:
-            job.own[job.span(s)] = (hidden_ref[job.span(s)] + job.total(s)).astype(BF)
-            job.line_start(s, out_ref)
+
+    for t in range(8):
+
+        @pl.when(turn == t)
+        def _(t=t):
+            line_turn(job, t, out_ref, produce)
 
     @pl.when(i == 0)
     def _():
@@ -223,10 +209,9 @@
 
     @pl.when(turn == 7)
     def _():
-        for s in blocks:
-            job.line_core(s, out_ref)
+        for t in range(8, TURNS):
+            line_turn(job, t, out_ref, produce)
         job.line_end(out_ref)
-        swapped.wait()
 
     @pl.when(i == len(limits) - 1)
     def _():
@@ -234,7 +219,7 @@
         dkv_ref[...] = (both * kcos_ref[...] - swap_halves(both) * ksin_ref[...]).astype(BF)
 
 def attend_back(
-    q, k, v, brow, bcol, lse, do, cos, sin, length, even, odd, hidden, piece, tile=256, most=256
+    q, k, v, brow, bcol, lse, do, cos, sin, length, even, odd, hidden, tile=256, most=256
 ):
     heads, count, _ = q.shape
     seqs = count // length
@@ -260,29 +245,25 @@
             IN_VMEM,
             ANY,
             IN_VMEM,
-            ANY,
         ],
         out_specs=[
             pl.BlockSpec((tile, qc), rowm),
             pl.BlockSpec((length, 2 * HD), lambda b, i: (b, 0)),
-            ANY,
             ANY,
         ],
         out_shape=[
             jax.ShapeDtypeStruct((count, qc), BF),
             jax.ShapeDtypeStruct((count, 2 * HD), BF),
             jax.ShapeDtypeStruct((length, even.shape[2]), BF),
-            jax.ShapeDtypeStruct((piece.shape[0] // 2, piece.shape[1]), BF),
         ],
         scratch_shapes=[pltpu.VMEM((HD, length), F32), pltpu.VMEM((HD, length), F32)]
-        + Job.scratch(even.shape[1], even.shape[2])
-        + [pltpu.SemaphoreType.DMA((2, 1))],
+        + Job.scratch(even.shape[1], even.shape[2]),
         compiler_params=pltpu.CompilerParams(
             collective_id=7, has_side_effects=True, vmem_limit_bytes=VMEM
         ),
         cost_estimate=pl.CostEstimate(flops=10 * heads * count * length * HD * 4, bytes_accessed=count * 4096, transcendentals=heads * count * length),
         name="attend_back",
-    )(q, k, v, brow, bcol, lse, do, cos, sin, cos, sin, even, odd, hidden, piece)
+    )(q, k, v, brow, bcol, lse, do, cos, sin, cos, sin, even, odd, hidden)
 
 def rope_tables(length, heads):
     positions = jnp.arange(length, dtype=jnp.int32).astype(F32)
@@ -401,38 +382,6 @@
     )(*ins)
 
 
-def out_body(*refs):
-    count = len(refs) // 2
-    total = dot(refs[0][...], refs[count][...], 1, 1)
-    for j in range(1, count):
-        total = total + dot(refs[j][...], refs[count + j][...], 1, 1)
-    refs[-1][...] = total.astype(BF)
-
-
-def down(acts, weights, tile=256):
-    count, size = acts[0].shape
-    width = weights[0].shape[0]
-    row = lambda i: (i, 0)
-    return pl.pallas_call(
-        out_body,
-        grid=(count // tile,),
-        in_specs=[pl.BlockSpec((tile, size), row) for _ in acts]
-        + [
-            pl.BlockSpec((width, size), lambda i: (0, 2), pipeline_mode=pl.Buffered(1))
-            for _ in weights
-        ],
-        out_specs=pl.BlockSpec((tile, width), row),
-        out_shape=jax.ShapeDtypeStruct((count, width), BF),
-        compiler_params=pltpu.CompilerParams(vmem_limit_bytes=VMEM),
-        cost_estimate=pl.CostEstimate(
-            flops=2 * count * width * size * len(acts),
-            bytes_accessed=8 * count * width,
-            transcendentals=0,
-        ),
-        name="swiglu_down",
-    )(*acts, *weights)
-
-
 def peers(dps, shards):
     dp, sh = lax.axis_index("dp"), lax.axis_index("shard")
     groups = dps // 2
@@ -503,30 +452,37 @@
     return low, high
 
 
-def finish_body(
-    dps, shards, piece_ref, sq_ref, q_ref, k_ref, v_ref, o_ref, norm_ref, theirs, pair, *bufs
-):
+def finish_body(dps, shards, count, piece_ref, theirs, sq_ref, *refs):
+    ins, outs, scratch = refs[: 2 * count], refs[2 * count : 2 * count + 8], refs[2 * count + 8 :]
+    q_ref, k_ref, v_ref, o_ref, g_ref, u_ref, d_ref, norm_ref = outs
+    bufs = scratch
     near, far, me, outer = peers(dps, shards)
     rows = piece_ref.shape[0] // 2
     qc = q_ref.shape[1] // 2
     x = lax.rem(lax.axis_index("dp"), 2)
-    meet(near + far)
-    copy = pltpu.make_async_remote_copy(
-        src_ref=piece_ref.at[pl.ds(pl.multiple_of((1 - x) * rows, rows), rows)],
-        dst_ref=theirs,
-        send_sem=pair.at[0],
-        recv_sem=pair.at[1],
-        device_id=(flip(lax.axis_index("dp"), 1), lax.axis_index("shard")),
-        device_id_type=MESH,
-    )
-    copy.start()
-    mine = piece_ref[pl.ds(pl.multiple_of(x * rows, rows), rows), :]
+    here = pl.ds(pl.multiple_of(x * rows, rows), rows)
+    squares = jnp.zeros((1, 1), F32)
+    half = g_ref.shape[1] // 2
+    at = 0
+    for j in range(count):
+        size = ins[2 * j].shape[1] // 3
+        for h, piece in enumerate(pick(x, ins[2 * j][here, :], ins[2 * j + 1][...])):
+            wide = piece.astype(F32)
+            squares = squares + jnp.sum(wide * wide, keepdims=True)
+            span = pl.ds(h * half + at, size)
+            g_ref[:, span] = piece[:, :size]
+            u_ref[:, span] = piece[:, size : 2 * size]
+            d_ref[span, :] = wide[:, 2 * size :].T.astype(BF)
+        at = at + size
+    mine = piece_ref[here, :]
     wide = mine.astype(F32)
-    squares = jnp.sum(wide * wide)
-    copy.wait()
+    squares = squares + jnp.sum(wide * wide, keepdims=True)
     got = theirs[...]
     wide = got.astype(F32)
-    squares = squares + jnp.sum(wide * wide)
+    squares = squares + jnp.sum(wide * wide, keepdims=True)
+    values = sq_ref[...] + jnp.broadcast_to(squares, sq_ref.shape)
+    meet(near + far)
+    norm_ref[...] = jnp.sqrt(two_stages(values, near, far, me, outer, bufs))
     low, high = pick(x, mine, got)
     q_ref[:, :qc] = low[:, :qc]
     q_ref[:, qc:] = high[:, :qc]
@@ -535,72 +491,31 @@
     v_ref[...] = jnp.concatenate([low[:, vc:oc], high[:, vc:oc]], axis=1)
     o_ref[:qc] = low[:, oc:].astype(F32).T.astype(BF)
     o_ref[qc:] = high[:, oc:].astype(F32).T.astype(BF)
-    norm_ref[...] = jnp.sqrt(
-        two_stages(sq_ref[...] + squares, near, far, me, outer, bufs)
-    )
-
-
-def finish(piece, squares, dps, shards, number):
+
+
+def finish(piece, theirs, squares, pairs, dps, shards, number):
     rows, cols = piece.shape[0] // 2, piece.shape[1]
     qc = (cols - 2 * HD) // 2
-    vmem = pl.BlockSpec(memory_space=pltpu.VMEM)
-    return pl.pallas_call(
-        functools.partial(finish_body, dps, shards),
-        in_specs=[vmem, vmem],
-        out_specs=[vmem] * 5,
-        out_shape=[
-            jax.ShapeDtypeStruct((rows, 2 * qc), BF),
-            jax.ShapeDtypeStruct((rows, 2 * HD), BF),
-            jax.ShapeDtypeStruct((rows, 2 * HD), BF),
-            jax.ShapeDtypeStruct((2 * qc, rows), BF),
-            jax.ShapeDtypeStruct(squares.shape, F32),
-        ],
-        scratch_shapes=[pltpu.VMEM((rows, cols), BF), pltpu.SemaphoreType.DMA((2,))]
-        + sum_scratch(squares.shape, dps, shards),
-        compiler_params=pltpu.CompilerParams(collective_id=number, has_side_effects=True),
-        name="finish",
-    )(piece, squares)
-
-
-def collect_body(count, size, x_ref, *refs):
-    ins, (g_ref, u_ref, d_ref, sq_ref) = refs[: 2 * count], refs[2 * count :]
-    x = x_ref[0]
-    total = jnp.zeros((1, 1), F32)
-    for j in range(count):
-        size_in = ins[2 * j + 1].shape[0]
-        mine = ins[2 * j][pl.ds(pl.multiple_of(x * size_in, size_in), size_in), :]
-        theirs = ins[2 * j + 1][...]
-        for h, piece in enumerate(pick(x, mine, theirs)):
-            wide = piece.astype(F32)
-            total = total + jnp.sum(wide * wide, keepdims=True)
-            span = pl.ds((h * count + j) * size, size)
-            g_ref[:, span] = piece[:, :size]
-            u_ref[:, span] = piece[:, size : 2 * size]
-            d_ref[span, :] = wide[:, 2 * size :].T.astype(BF)
-    sq_ref[...] = jnp.broadcast_to(total, sq_ref.shape)
-
-
-def collect(x, pairs):
-    rows, size = pairs[0][1].shape[0], pairs[0][1].shape[1] // 3
-    wide = 2 * len(pairs) * size
+    wide = 2 * sum(other.shape[1] // 3 for _, other in pairs)
     vmem = pl.BlockSpec(memory_space=pltpu.VMEM)
     ins = [v for pair in pairs for v in pair]
+    shapes = ((rows, 2 * qc), (rows, 2 * HD), (rows, 2 * HD), (2 * qc, rows))
+    shapes = shapes + ((rows, wide), (rows, wide), (wide, rows))
     return pl.pallas_call(
-        functools.partial(collect_body, len(pairs), size),
-        in_specs=[pl.BlockSpec(memory_space=pltpu.SMEM)] + [vmem] * len(ins),
-        out_specs=[vmem] * 4,
-        out_shape=[
-            jax.ShapeDtypeStruct((rows, wide), BF),
-            jax.ShapeDtypeStruct((rows, wide), BF),
-            jax.ShapeDtypeStruct((wide, rows), BF),
-            jax.ShapeDtypeStruct((8, 128), F32),
-        ],
-        compiler_params=pltpu.CompilerParams(vmem_limit_bytes=VMEM),
-        name="collect",
-    )(x.reshape(1), *ins)
-
-
-PARTS = 4
+        functools.partial(finish_body, dps, shards, len(pairs)),
+        in_specs=[vmem] * (3 + len(ins)),
+        out_specs=[vmem] * 8,
+        out_shape=[jax.ShapeDtypeStruct(shape, BF) for shape in shapes]
+        + [jax.ShapeDtypeStruct(squares.shape, F32)],
+        scratch_shapes=sum_scratch(squares.shape, dps, shards),
+        compiler_params=pltpu.CompilerParams(
+            collective_id=number, has_side_effects=True, vmem_limit_bytes=VMEM
+        ),
+        name="finish",
+    )(piece, theirs, squares, *ins)
+
+
+PARTS = 8
 
 
 def flip(value, bit):
@@ -668,7 +583,7 @@
         return self.copy(2, s, self.out2.at[s], self.in2.at[s], target)
 
     def start(self):
-        for s in range(PARTS):
+        for s in range(4):
             self.to_core(s).start()
 
     def pair(self, k, s):
@@ -676,6 +591,8 @@
 
     def first(self, s):
         self.to_core(s).wait_recv()
+        if s + 4 < PARTS:
+            self.to_core(s + 4).start()
         self.out1[s, 0] = self.pair(2 if self.over_x(s) else 1, s).astype(BF)
         self.out1[s, 1] = self.pair(3, s).astype(BF)
         self.to_first(s).start()
@@ -747,36 +664,56 @@
         self.sent()
 
 
-def run_job(job, mine, theirs, produce, filler=None):
-    blocks = range(PARTS)
+def run_job(job, mine, theirs, produce, hook, window=4, lag=2):
+    copies = [job.spread_copies(s, mine, theirs) for s in range(PARTS)]
     job.start()
-    for s in blocks:
+    for s in range(window):
         job.first(s)
-    if filler is not None:
-        filler(0)
-    for s in blocks:
-        job.second(s)
-    if filler is not None:
-        filler(1)
-    copies = [job.spread_copies(s, mine, theirs) for s in blocks]
-    for s in blocks:
-        job.own[job.span(s)] = produce(s, job.total(s)).astype(BF)
-        copies[s][0].start()
-        copies[s][1].start()
-    for keep, near, far, core in copies:
-        keep.wait()
-        near.wait_recv()
-        far.start()
-    for keep, near, far, core in copies:
-        far.wait_recv()
-        core.start()
-    if filler is not None:
-        filler(2)
-    for keep, near, far, core in copies:
+    for t in range(PARTS + 3 * lag):
+        hook(t)
+        if t < PARTS:
+            job.second(t)
+            if t + window < PARTS:
+                job.first(t + window)
+        if 0 <= t - lag < PARTS:
+            s = t - lag
+            job.own[job.span(s)] = produce(s, job.total(s)).astype(BF)
+            copies[s][0].start()
+            copies[s][1].start()
+        if 0 <= t - 2 * lag < PARTS:
+            keep, near, far, _ = copies[t - 2 * lag]
+            keep.wait()
+            near.wait_recv()
+            far.start()
+        if 0 <= t - 3 * lag < PARTS:
+            _, _, far, core = copies[t - 3 * lag]
+            far.wait_recv()
+            core.start()
+    for _, near, far, core in copies:
         core.wait_recv()
         for copy in (near, far, core):
             copy.wait_send()
     job.sent()
+
+
+def line_turn(job, t, whole, produce, window=4, lag=2):
+    if t == 0:
+        job.start()
+        for s in range(window):
+            job.first(s)
+    if 0 <= t - 1 < PARTS:
+        job.second(t - 1)
+        if t - 1 + window < PARTS:
+            job.first(t - 1 + window)
+    if 0 <= t - 1 - lag < PARTS:
+        s = t - 1 - lag
+        job.own[job.span(s)] = produce(s, job.total(s)).astype(BF)
+        job.line_start(s, whole)
+    if 0 <= t - 1 - 2 * lag < PARTS:
+        job.line_core(t - 1 - 2 * lag, whole)
+
+
+TURNS = PARTS + 5
 
 
 def rms_of(values):
@@ -791,112 +728,81 @@
     return total, inverse * scaled - values * (inverse * inverse * inverse * mean)
 
 
-def mid_body(
-    even, odd, tok_ref, gain_ref, cot_ref, mine, theirs, hidden_ref, cot_mine, cot_theirs, *scratch
-):
+def mid_body(even, odd, tok_ref, gain_ref, mine, theirs, hidden_ref, *scratch):
     targets = neighbours()
-    xs, ys, core = targets
-    sh = lax.axis_index("shard")
-    quarter = cot_ref.shape[0] // 4
-    cot_sem, keeps = scratch[8:]
-    local = []
-    for n, (half, dy, owner) in enumerate(
-        (
-            (cot_mine, 0, sh),
-            (cot_mine, 1, flip(sh, 2)),
-            (cot_theirs, 0, flip(sh, 1)),
-            (cot_theirs, 1, flip(flip(sh, 1), 2)),
-        )
-    ):
-        src = cot_ref.at[pl.ds(pl.multiple_of(owner * quarter, quarter), quarter)]
-        local.append(pltpu.make_async_copy(src, half.at[0, dy], keeps.at[n]))
-    for copy in local:
-        copy.start()
     meet(targets)
-    job = Job(even, odd, scratch[:8], targets, (1, 3))
-    rows = quarter // PARTS
-    over_x, over_y, over_core, over_far = [], [], [], []
-    for s in range(PARTS):
-        span = pl.ds(s * rows, rows)
-        own = cot_ref.at[pl.ds(pl.multiple_of(sh * quarter + s * rows, rows), rows)]
-        near, far = cot_mine.at[1, 0, span], cot_mine.at[1, 1, span]
-        over_x.append(remote(own, near, cot_sem, s, xs))
-        over_y.append(remote(near, far, cot_sem, PARTS + s, ys))
-        over_core.append(remote(near, cot_theirs.at[1, 0, span], cot_sem, 2 * PARTS + s, core))
-        over_far.append(remote(far, cot_theirs.at[1, 1, span], cot_sem, 3 * PARTS + s, core))
-
-    def cotangents(part):
-        for s in range(PARTS):
-            if part == 0:
-                over_x[s].start()
-            elif part == 1:
-                over_x[s].wait_recv()
-                over_y[s].start()
-                over_core[s].start()
-            else:
-                over_y[s].wait_recv()
-                over_far[s].start()
+    job = Job(even, odd, scratch, targets, range(1, PARTS, 2))
 
     def produce(s, total):
         hidden = tok_ref[job.span(s)].astype(F32) + total
         hidden_ref[job.span(s)] = hidden
         return hidden * rms_of(hidden) * gain_ref[...]
 
-    run_job(job, mine, theirs, produce, cotangents)
-    for copy in local:
-        copy.wait()
-    for copies in (over_core, over_far):
-        for copy in copies:
-            copy.wait_recv()
-    for copies in (over_x, over_y, over_core, over_far):
-        for copy in copies:
-            copy.wait_send()
+    run_job(job, mine, theirs, produce, lambda t: None)
 
 
 def back_body(even, odd, hidden_ref, cot_ref, gain_ref, *rest):
-    ins, (mine, theirs, gh_ref, gg_ref, dw_ref), scratch = rest[:8], rest[8:13], rest[13:]
-    held, (tiles, load, store) = scratch[8:16], scratch[16:]
+    chunks = CHUNKS
+    count = 6 + 3 * chunks
+    ins, outs, scratch = rest[:count], rest[count : count + 7], rest[count + 7 :]
+    mine, theirs, gh_ref, gg_ref, dw_ref, down_a, down_b = outs
+    held = scratch[8 : 8 + count]
+    tiles, store, load, down_tiles, down_store = scratch[8 + count :]
     targets = neighbours()
-    loads = [
-        pltpu.make_async_copy(src, dst, load.at[n]) for n, (src, dst) in enumerate(zip(ins, held))
-    ]
+    loads = []
+    for n, (src, dst) in enumerate(zip(ins, held)):
+        wide = src.shape[1] - dst.shape[1]
+        src = src.at[:, pl.ds(wide, dst.shape[1])] if wide else src
+        loads.append(pltpu.make_async_copy(src, dst, load.at[n]))
     for copy in loads:
         copy.start()
     meet(targets)
-    job = Job(even, odd, scratch[:8], targets, (1, 3))
-    na, nb, ca, cb, ga, gb, aa, ab = held
+    job = Job(even, odd, scratch[:8], targets, range(1, PARTS, 2))
+    na, nb, ca, cb, ga, gb = held[:6]
+    acts_a, acts_b, downs = held[6 : 6 + chunks], held[6 + chunks : 6 + 2 * chunks], held[6 + 2 * chunks :]
+    aa, ab = acts_a[-1], acts_b[-1]
     size = aa.shape[1]
     step = tiles.shape[1]
-    half = dw_ref.shape[0] // step // 2
+    sites = 4
+    half = dw_ref.shape[0] // step // sites
+    rows = down_tiles.shape[1]
 
     def filler(part):
-        if part == 2:
-            return
         if part == 0:
             for copy in loads:
                 copy.wait()
 
         def tile(n, carry):
-            i = part * half + n
-            cols = pl.ds(pl.multiple_of(i * step, step), step)
-            slot = lax.rem(n, 2)
-            copy = pltpu.make_async_copy(tiles.at[slot], dw_ref.at[cols], store.at[slot])
-
-            @pl.when(n >= 2)
-            def _():
-                copy.wait()
-
+            cols = pl.ds(pl.multiple_of((part * half + n) * step, step), step)
             gu = dot(na[:, cols], ga[...], 0, 0) + dot(nb[:, cols], gb[...], 0, 0)
-            tiles[slot, :, : 2 * size] = gu.astype(BF)
+            tiles[n, :, : 2 * size] = gu.astype(BF)
             dt = dot(ca[:, cols], aa[...], 0, 0) + dot(cb[:, cols], ab[...], 0, 0)
-            tiles[slot, :, 2 * size :] = dt.astype(BF)
-            copy.start()
+            tiles[n, :, 2 * size :] = dt.astype(BF)
+            pltpu.make_async_copy(tiles.at[n], dw_ref.at[cols], store.at[n]).start()
             return carry
 
         lax.fori_loop(0, half, tile, 0)
-        for n in (0, 1):
-            cols = pl.ds(part * half * step, step)
+        span = pl.ds(part * rows, rows)
+        for n, (acts, out) in enumerate(((acts_a, down_a), (acts_b, down_b))):
+            total = dot(acts[0][span], downs[0][...], 1, 1)
+            for j in range(1, chunks):
+                total = total + dot(acts[j][span], downs[j][...], 1, 1)
+            down_tiles[n] = total.astype(BF)
+            pltpu.make_async_copy(down_tiles.at[n], out.at[span], down_store.at[n]).start()
+
+    def settle(part):
+        span = pl.ds(part * rows, rows)
+        for n in range(half):
+            cols = pl.ds((part * half + n) * step, step)
             pltpu.make_async_copy(tiles.at[n], dw_ref.at[cols], store.at[n]).wait()
+        for n, out in enumerate((down_a, down_b)):
+            pltpu.make_async_copy(down_tiles.at[n], out.at[span], down_store.at[n]).wait()
+
+    def hook(t):
+        if t % 2 == 0 and t // 2 < sites:
+            if t > 0:
+                settle(t // 2 - 1)
+            filler(t // 2)
 
     totals = []
 
@@ -907,7 +813,8 @@
         gh_ref[job.span(s)] = grad_hidden
         return grad_hidden
 
-    run_job(job, mine, theirs, produce, filler)
+    run_job(job, mine, theirs, produce, hook)
+    settle(sites - 1)
     gg_ref[...] = sum(totals[1:], totals[0])
 
 
@@ -923,27 +830,22 @@
 ):
     near, far, me, outer = peers(dps, shards)
     meet(near + far)
-    job = Job(even, odd, scratch[:8], neighbours())
+    job = Job(even, odd, scratch[:8], neighbours(), (1, 4, 7))
     swapped = trade(piece, theirs, scratch[8])
-    blocks = range(PARTS)
     totals = []
-    job.start()
-    for s in blocks:
-        job.first(s)
-    swapped.start()
-    for s in blocks:
-        job.second(s)
-    for s in blocks:
+
+    def produce(s, total):
         span = job.span(s)
-        values = tok_ref[span].astype(F32)
-        gain_total, through = norm_back_of(values, gain_ref[...], job.total(s))
+        gain_total, through = norm_back_of(tok_ref[span].astype(F32), gain_ref[...], total)
         totals.append(gain_total)
-        job.own[span] = (gh_ref[span] + through).astype(BF)
-        job.line_start(s, in_ref)
+        return gh_ref[span] + through
+
+    for t in range(TURNS):
+        line_turn(job, t, in_ref, produce)
+        if t == 4:
+            swapped.start()
     gains = jnp.concatenate([sum(totals[1:], totals[0]), gg_ref[...]], axis=0)
     sum_ref[...] = two_stages(gains, near, far, me, outer, scratch[9:])
-    for s in blocks:
-        job.line_core(s, in_ref)
     job.line_end(in_ref)
     swapped.wait()
 
@@ -1025,44 +927,53 @@
 BIG = 60 << 20
 
 
-def mid_stage(even, odd, tokens_own, gain, cotangent):
+def mid_stage(even, odd, tokens_own, gain):
     _, rows, width = even.shape
     half = jax.ShapeDtypeStruct((2, 2, rows, width), BF)
     return pl.pallas_call(
         mid_body,
-        in_specs=[IN_VMEM, ANY, IN_VMEM, IN_VMEM, ANY],
-        out_specs=[ANY, ANY, IN_VMEM, ANY, ANY],
-        out_shape=[half, half, jax.ShapeDtypeStruct((rows, width), F32), half, half],
-        scratch_shapes=Job.scratch(rows, width)
-        + [pltpu.SemaphoreType.DMA((2, 4 * PARTS)), pltpu.SemaphoreType.DMA((4,))],
+        in_specs=[IN_VMEM, ANY, IN_VMEM, IN_VMEM],
+        out_specs=[ANY, ANY, IN_VMEM],
+        out_shape=[half, half, jax.ShapeDtypeStruct((rows, width), F32)],
+        scratch_shapes=Job.scratch(rows, width),
         compiler_params=pltpu.CompilerParams(
             collective_id=3, has_side_effects=True, vmem_limit_bytes=VMEM
         ),
         name="mid_stage",
-    )(even, odd, tokens_own, gain, cotangent)
-
-
-def back_stage(even, odd, hidden, cot_own, gain, *filling, tile=256):
+    )(even, odd, tokens_own, gain)
+
+
+def back_stage(even, odd, hidden, cot_own, gain, halves, acts, weights, tile=256):
     _, rows, width = even.shape
-    size = filling[-1].shape[1]
+    count = halves[0].shape[0]
+    sizes = [act.shape[1] for act in acts[0]]
+    filling = list(halves) + list(acts[0]) + list(acts[1]) + list(weights)
+    held = [pltpu.VMEM(v.shape, BF) for v in filling[: 6 + 2 * len(sizes)]]
+    held += [pltpu.VMEM((width, size), BF) for size in sizes]
     spread_shape = jax.ShapeDtypeStruct((2, 2, rows, width), BF)
+    down_shape = jax.ShapeDtypeStruct((count, width), BF)
+    dma = pltpu.SemaphoreType.DMA
     return pl.pallas_call(
         back_body,
-        in_specs=[IN_VMEM, ANY, IN_VMEM, IN_VMEM, IN_VMEM] + [ANY] * 8,
-        out_specs=[ANY, ANY, IN_VMEM, IN_VMEM, ANY],
+        in_specs=[IN_VMEM, ANY, IN_VMEM, IN_VMEM, IN_VMEM] + [ANY] * len(filling),
+        out_specs=[ANY, ANY, IN_VMEM, IN_VMEM, ANY, ANY, ANY],
         out_shape=[
             spread_shape,
             spread_shape,
             jax.ShapeDtypeStruct((rows, width), F32),
             jax.ShapeDtypeStruct((1, width), F32),
-            jax.ShapeDtypeStruct((width, 3 * size), BF),
+            jax.ShapeDtypeStruct((width, 3 * sizes[-1]), BF),
+            down_shape,
+            down_shape,
         ],
         scratch_shapes=Job.scratch(rows, width)
-        + [pltpu.VMEM(value.shape, BF) for value in filling]
+        + held
         + [
-            pltpu.VMEM((2, tile, 3 * size), BF),
-            pltpu.SemaphoreType.DMA((8,)),
-            pltpu.SemaphoreType.DMA((2,)),
+            pltpu.VMEM((width // tile // 4, tile, 3 * sizes[-1]), BF),
+            dma((width // tile // 4,)),
+            dma((len(filling),)),
+            pltpu.VMEM((2, count // 4, width), BF),
+            dma((2,)),
         ],
         compiler_params=pltpu.CompilerParams(
             collective_id=4, has_side_effects=True, vmem_limit_bytes=BIG
@@ -1091,6 +1002,43 @@
         ),
         name="end_stage",
     )(even, odd, tokens_own, grad_hidden, gain, gain_grad, piece)
+
+
+def update_body(count, norm_ref, rate_ref, *refs):
+    factor = jnp.minimum(1.0, CLIP / norm_ref[0:1, 0:1])
+    rate = rate_ref[0]
+    for n in range(count):
+        master, moment, grad = (refs[3 * n + k] for k in range(3))
+        new_moment, new_master = refs[3 * count + 2 * n], refs[3 * count + 2 * n + 1]
+        momentum = 0.5 * moment[...] + 0.5 * (factor * grad[...].astype(F32))
+        new_moment[...] = momentum
+        new_master[...] = master[...] - rate * momentum
+
+
+def update(norm, rate, masters, moments, grads, steps=8):
+    count = len(masters)
+
+    def block(value):
+        if value.shape[0] == 1:
+            return pl.BlockSpec(value.shape, lambda i: (0, 0))
+        return pl.BlockSpec((value.shape[0] // steps, value.shape[1]), lambda i: (i, 0))
+
+    ins = [v for triple in zip(masters, moments, grads) for v in triple]
+    outs = [v for master in masters for v in (master, master)]
+    values = pl.pallas_call(
+        functools.partial(update_body, count),
+        grid=(steps,),
+        in_specs=[
+            pl.BlockSpec(norm.shape, lambda i: (0, 0)),
+            pl.BlockSpec(memory_space=pltpu.SMEM),
+        ]
+        + [block(v) for v in ins],
+        out_specs=[block(v) for v in outs],
+        out_shape=[jax.ShapeDtypeStruct(v.shape, F32) for v in outs],
+        compiler_params=pltpu.CompilerParams(vmem_limit_bytes=VMEM),
+        name="update",
+    )(norm, rate.reshape(1), *ins)
+    return values[0::2], values[1::2]
 
 
 def after(*values):
@@ -1209,11 +1157,16 @@
         low_g = w_gate.astype(BF)
         low_u = w_up.astype(BF)
         low_d = w_down.astype(BF).T
-        size = low_g.shape[1] // 2 // CHUNKS
+        units = low_g.shape[1] // 2
+        sizes = (units * 5 // 8, units * 3 // 8)
+        offsets = (0, sizes[0])
 
         def ffn_part(which, j):
             return jnp.concatenate(
-                [half(low, which)[:, j * size : (j + 1) * size] for low in (low_g, low_u, low_d)],
+                [
+                    lax.dynamic_slice_in_dim(low, which * units + offsets[j], sizes[j], axis=1)
+                    for low in (low_g, low_u, low_d)
+                ],
                 axis=1,
             )
 
@@ -1221,8 +1174,9 @@
             after(tokens, piece)[0], ffn_part(x, 0), ffn_part(1 - x, 0)
         )
         ffn_weights = [gather(first_part)]
-        packed, both, send_second = after(gather(piece), both, ffn_part(1 - x, 1))
-        second_part = ordered(ffn_part(x, 1), swap(send_second, 1, 0))
+        cot_own = [cut(cotangent, ds) for ds in range(shards)]
+        packed, both, send_cot = after(gather(piece), both, cot_own[0])
+        cot_x = swap(send_cot, 1, 0)
         packed = packed.reshape(groups, 2 * rows + 32, cols + qc)
         qkv_weight = packed[:, : 2 * rows, :cols].reshape(width, cols)
         out_weight = packed[:, : 2 * rows, cols:].reshape(width, qc)
@@ -1233,11 +1187,18 @@
         cosine, sine = rope_tables(length, group)
 
         normed, query, key, value = qkv(both, gain_one, qkv_weight, cosine, sine, group)
+        query, cot_x, send_second = after(query, cot_x, ffn_part(1 - x, 1))
+        second_part = ordered(ffn_part(x, 1), swap(send_second, 1, 0))
+        cot_xy = swap(cot_x, 0, 2)
         blocks = jnp.concatenate([block_ids, blocks_x], axis=0)
         block_rows = blocks[:, None, :]
         block_cols = blocks.reshape(2 * length, 1)
         mixed, lse = attend(query, key, value, block_rows, block_cols, length)
-        mixed, second_part = after(mixed, second_part)
+        mixed, second_part, cot_xy = after(mixed, second_part, cot_xy)
+        cot_x = jnp.stack([cot_x, cot_xy])
+        cot_core = swap(cot_x, 0, 1)
+        cot_mine = flat(jnp.concatenate([jnp.stack([cot_own[0], cot_own[2]]), cot_x], axis=0))
+        cot_theirs = flat(jnp.concatenate([jnp.stack([cot_own[1], cot_own[3]]), cot_core], axis=0))
         ffn_weights.append(gather(second_part))
         mixed_own, mixed_other = mixed[:length], mixed[length:]
         mixed_mine, mixed_theirs = halves(mixed_own, mixed_other)
@@ -1247,15 +1208,13 @@
             return partial.astype(BF)
 
         tokens_own = cut(tokens, 0)
-        mine, theirs, hidden, cot_mine, cot_theirs = mid_stage(
+        mine, theirs, hidden = mid_stage(
             project(mixed_mine, out_weight),
             project(mixed_theirs, out_weight),
             tokens_own,
             gain_two,
-            cotangent,
         )
         two_mine, two_theirs = flat(mine), flat(theirs)
-        cot_mine, cot_theirs = flat(cot_mine), flat(cot_theirs)
 
         shape = (4, quarter, width)
         acts_mine = []
@@ -1285,20 +1244,15 @@
                     (gu_mine, gu_theirs),
                     (act_mine, act_theirs),
                 )
-        mine, theirs, grad_hidden, gain_grad_two, last_grads = back_stage(
+        mine, theirs, grad_hidden, gain_grad_two, last_grads, out_mine, out_theirs = back_stage(
             part_mine.reshape(shape),
             part_theirs.reshape(shape),
             hidden,
             cut(cotangent, 0),
             gain_two,
-            two_mine,
-            two_theirs,
-            cot_mine,
-            cot_theirs,
-            gu_mine,
-            gu_theirs,
-            act_mine,
-            act_theirs,
+            (two_mine, two_theirs, cot_mine, cot_theirs, gu_mine, gu_theirs),
+            (acts_mine, acts_theirs),
+            ffn_weights,
         )
         gh_mine = mine.reshape(shape)
         gh_theirs = theirs.reshape(shape)
@@ -1307,8 +1261,7 @@
         grad_mixed_mine = project(gh_mine, out_weight.T)
         grad_mixed_theirs = project(gh_theirs, out_weight.T)
         grad_mixed = streams(grad_mixed_mine, grad_mixed_theirs)
-        grad_mixed, first_piece = after(grad_mixed, first_piece)
-        grad_q, grad_kv, output, first_theirs = attend_back(
+        grad_q, grad_kv, output = attend_back(
             query,
             key,
             value,
@@ -1319,10 +1272,13 @@
             cosine,
             sine,
             length,
-            down(acts_mine, ffn_weights).reshape(shape),
-            down(acts_theirs, ffn_weights).reshape(shape),
+            out_mine.reshape(shape),
+            out_theirs.reshape(shape),
             hidden,
-            first_piece,
+        )
+        grad_q, first_piece = after(grad_q, first_piece)
+        first_theirs = swap(
+            lax.dynamic_slice_in_dim(first_piece, (1 - x) * rows, rows, axis=0), 1, 0
         )
         grad_qkv = jnp.concatenate([grad_q, grad_kv], axis=1)
         d_attn = attn_grads(
@@ -1334,9 +1290,12 @@
         grad_attn = scatter(d_attn)
         gq_mine, gq_theirs = halves(grad_qkv[:length], grad_qkv[length:])
         gq_mine, gq_theirs, d_attn = after(gq_mine, gq_theirs, d_attn)
+        even_in, odd_in, first_theirs = after(
+            project(gq_mine, qkv_weight), project(gq_theirs, qkv_weight), first_theirs
+        )
         input_grad, gain_grads, last_theirs = end_stage(
-            project(gq_mine, qkv_weight),
-            project(gq_theirs, qkv_weight),
+            even_in,
+            odd_in,
             tokens_own,
             grad_hidden,
             gain_one,
@@ -1345,20 +1304,23 @@
             dps,
             shards,
         )
-        input_grad = input_grad.astype(F32)
+        grad_attn, input_grad, gain_grads = after(grad_attn, input_grad, gain_grads)
+        attn_theirs = swap(
+            lax.dynamic_slice_in_dim(grad_attn, (1 - x) * rows, rows, axis=0), 1, 0
+        )
+        input_grad, gain_grads, attn_theirs = after(
+            input_grad.astype(F32), gain_grads, attn_theirs
+        )
 
         pairs = [(first_piece, first_theirs), (last_piece, last_theirs)]
-        own_g, own_u, own_d, squares = collect(x, pairs)
         gain_grads = lax.dynamic_slice_in_dim(gain_grads, dp * rows, rows, axis=1)
         first_shard = (me == 0).astype(F32)
-        squares = squares + first_shard * jnp.sum(gain_grads * gain_grads)
-        grad_attn, squares, output, own_g, own_u, own_d = after(
-            grad_attn, squares, output, own_g, own_u, own_d
-        )
-        own_q, own_k, own_v, own_o, norm = finish(grad_attn, squares, dps, shards, 2)
+        squares = jnp.broadcast_to(first_shard * jnp.sum(gain_grads * gain_grads), (8, 128))
+        own_q, own_k, own_v, own_o, own_g, own_u, own_d, norm = finish(
+            grad_attn, attn_theirs, squares, pairs, dps, shards, 2
+        )
         global_norm = norm[0, 0]
         owned = (gain_grads[0], own_q, own_k, own_v, own_o, gain_grads[1], own_g, own_u, own_d)
-        factor = jnp.minimum(1.0, CLIP / global_norm)
         rate_now = rate * jnp.minimum(1.0, (step.astype(F32) + 1.0) / WARMUP)
         masters = (gain_first, w_query, w_key, w_value, w_output, gain_second, w_gate, w_up, w_down)
         moments = (
@@ -1372,10 +1334,14 @@
             moment_up,
             moment_down,
         )
-        momenta = [
-            0.5 * moment + 0.5 * (factor * gradient) for moment, gradient in zip(moments, owned)
+        lists = [
+            [v.reshape(1, -1) if v.ndim == 1 else v for v in values]
+            for values in (masters, moments, owned)
         ]
-        updated = [master - rate_now * momentum for master, momentum in zip(masters, momenta)]
+        momenta, updated = (
+            [v.reshape(-1) if v.shape[0] == 1 else v for v in values]
+            for values in update(norm, rate_now, *lists)
+        )
         return (output, input_grad, global_norm, *momenta, *updated)
 
     return on_device

time: 756 us -> 694 us (0.918)
  Pallas kernels: 613 us -> 537 us
  waiting for transfers between devices: 8.28 us -> 22 us
    pallas_call x5 -> x3, Pallas kernels: 172 us -> 111 us  [the longest x1 82.7 us: mid_stage(): pl.pallas_call(mid_body, in_specs=[IN_VMEM, ANY, IN_VMEM, IN_VMEM], out_s...]
    pallas_call x1, Pallas kernels: 88.1 us -> 70.4 us  [attend_back(): pl.pallas_call(functools.partial(bwd_body, limits), grid=(seqs, per), in_...]
    sub x9 -> x0, other arithmetic: 15.4 us -> none  [on_device(): master - rate_now * momentum]
    pallas_call x1, Pallas kernels: 93.5 us -> 79.3 us  [end_stage(): pl.pallas_call(functools.partial(end_body, dps, shards), in_specs=[IN_VME...]
    ppermute x3 -> x8, waiting for transfers between devices: 8.15 us -> 21.2 us  [swap(): return lax.ppermute(values, axes, pairs)]
    unnamed x162 -> x83, local copies, waits for them, and re-layouts: 30.8 us -> 20.8 us
  transfers between devices with their start and end apart: 9 -> 14, of which waited for: 1 -> 4; matrix products, arithmetic and copies ran while one was open for 8% -> 11% of each run, Pallas kernels for 79% -> 74%
where the time goes in v5:
time: 694 us; the launch traced here: 689 us
  Pallas kernels  537 us (77%)
  local copies, waits for them, and re-layouts  49.7 us (7%)
  other arithmetic  31.8 us (5%)
  waiting for transfers between devices  22 us (3%)
  matrix products  20.2 us (3%)
  between operations  17.1 us (2%)
  starting transfers between devices  10.6 us (2%)
    pallas_call x1, Pallas kernels, back_stage(): pl.pallas_call(back_body, in_specs=[IN_VMEM, ANY, IN_VMEM, IN_VMEM, IN_VM...  84.3 us
    pallas_call x1, Pallas kernels, mid_stage(): pl.pallas_call(mid_body, in_specs=[IN_VMEM, ANY, IN_VMEM, IN_VMEM], out_s...  82.7 us
    pallas_call x1, Pallas kernels, end_stage(): pl.pallas_call(functools.partial(end_body, dps, shards), in_specs=[IN_VME...  79.3 us
    pallas_call x4, Pallas kernels, up_back(): pl.pallas_call(functools.partial(up_body, prev is None, last), grid=(coun...  72.4 us
    pallas_call x1, Pallas kernels, attend_back(): pl.pallas_call(functools.partial(bwd_body, limits), grid=(seqs, per), in_...  70.4 us
    pallas_call x1, Pallas kernels, entry(): pl.pallas_call(entry_body, in_specs=[ANY] * 3, out_specs=[ANY] * 2, out_s...  47.7 us
    pallas_call x1, Pallas kernels, ffn_grads(): pl.pallas_call(grad_body, grid=(width // tile,), in_specs=[pl.BlockSpec((...  24.4 us
    ppermute x8, waiting for transfers between devices, swap(): return lax.ppermute(values, axes, pairs)  21.2 us
  transfers between devices with their start and end apart: 14, of which 4 were waited for; matrix products, arithmetic and copies ran while one was open for 11% of the time, Pallas kernels for 74%

profile of v5, /device:TPU:0, one launch (start us, length us, event | category | flops | bytes accessed | tf_op | source)
XLA Modules:
  0.0 688.6 jit_solution(10117096546704654678)
XLA Ops:
  13.8 2.9 collective-permute-start
  16.7 8.4 %collective-permute-done = bf16[272,640]{1,0:T(8,128)(2,1)S(1)} collective-permute-done((bf16[272,640]{1,0:T(8,128)(2,1)}, bf16[272,640]{1,0:T(8,128)(2,1)S(1)}, u32[]{:S(2)}, u32[]{:S(2)}) %collective-permute-start) | collective-permute-done | bytes 348192 | tf_op jit(solution)/shard_map/ppermute | solution.py:1057
  26.9 1.9 convert_element_type.77
  29.7 1.9 copy-done.1
  31.6 47.7 %entry.1 = (bf16[2048,2048]{1,0:T(8,128)(2,1)S(1)}, bf16[512,1920]{1,0:T(8,128)(2,1)}) custom-call(bf16[1024,2048]{1,0:T(8,128)(2,1)S(1)} %copy-done.1, bf16[256,1920]{1,0:T(8,128)(2,1)S(1)} %pad_maximum_fusion.4.keep_ref, bf16[256,1920]{1,0:T(8,128)(2,1)S(1)} %pad_maximum_fusion.5.send_ref), custom_call_target="tpu_custom_call" | custom-call | tf_op jit(solution)/shard_map/entry/pallas_call | solution.py:903
  79.3 3.4 copy-done
  85.6 4.0 dynamic-slice_bitcast_fusion.1
  89.6 1.7 collective-permute-start.1
  92.7 1.6 copy.51
  95.5 1.6 copy.52
  97.1 2.9 concatenate.62.cos_ref.kcos_ref
  101.9 1.4 copy.59
  104.3 2.8 slice.92
  107.7 15.3 %qkv_rope.1 = (bf16[2048,2048]{1,0:T(8,128)(2,1)}, bf16[4,2048,64]{2,1,0:T(8,128)(2,1)}, bf16[2048,64]{1,0:T(8,128)(2,1)}, bf16[2048,64]{1,0:T(8,128)(2,1)}) custom-call(bf16[2048,2048]{1,0:T(8,128)(2,1)} %copy-done, f32[1,2048]{1,0:T(1,128)} %reshape.185.gain_ref, bf16[2048,384]{1,0:T(8,128)(2,1)} %bitcast.135, f32[1024,384]{1,0:T(8,128)} %concatenate.62.cos_ref.kcos_ref, ...), custom_call_target="tpu_custom_call" | custom-call | flops 3221225472 | bytes 16777216 | tf_op jit(solution)/shard_map/qkv_rope/pallas_call | solution.py:55
  123.2 1.8 collective-permute-start.4
  125.0 18.5 %attend.1 = (bf16[2048,256]{1,0:T(8,128)(2,1)}, f32[2048,4]{1,0:T(8,128)}) custom-call(bf16[4,2048,64]{2,1,0:T(8,128)(2,1)} %get-tuple-element.116.q_ref, bf16[2048,64]{1,0:T(8,128)(2,1)} %get-tuple-element.117.k_ref, bf16[2048,64]{1,0:T(8,128)(2,1)} %get-tuple-element.118.v_ref, s32[2,1,1024]{2,1,0:T(1,128)} %broadcast_in_dim.4.brow_ref, s32[2048,1]{1,0:T(8,128)} %bitcast.163), custom_call_target="tpu_custom_call" | custom-call | flops 8589934592 | bytes 4194304 | tf_op jit(solution)/shard_map/attend/pallas_call | solution.py:112
  143.6 1.3 broadcast_select_fusion.1
  147.5 1.5 pad_maximum_fusion.2
  149.0 2.4 constant_dynamic-slice_fusion.4.tok_ref
  151.4 1.3 slice.93
  153.7 3.3 convolution_convert_fusion.3.even
  157.0 3.3 convolution_convert_fusion.2.odd
  160.3 82.7 %mid_stage.1 = (bf16[2,2,256,2048]{3,2,1,0:T(8,128)(2,1)}, bf16[2,2,256,2048]{3,2,1,0:T(8,128)(2,1)}, f32[256,2048]{1,0:T(8,128)}) custom-call(bf16[4,256,2048]{2,1,0:T(8,128)(2,1)} %convolution_convert_fusion.3.even, bf16[4,256,2048]{2,1,0:T(8,128)(2,1)} %convolution_convert_fusion.2.odd, bf16[256,2048]{1,0:T(8,128)(2,1)} %constant_dynamic-slice_fusion.4.tok_ref, ...), custom_call_target="tpu_custom_call" | custom-call | tf_op jit(solution)/shard_map/mid_stage/pallas_call | solution.py:933
  243.1 3.8 pad_maximum_fusion
  246.9 3.5 pad_maximum_fusion.1
  250.4 20.5 %swiglu_part.4 = (bf16[1024,640]{1,0:T(8,128)(2,1)}, bf16[1024,1280]{1,0:T(8,128)(2,1)}, f32[1024,2048]{1,0:T(8,128)}) custom-call(bf16[1024,2048]{1,0:T(8,128)(2,1)} %bitcast.140, bf16[1024,2048]{1,0:T(8,128)(2,1)} %bitcast.122, bf16[2048,1920]{1,0:T(8,128)(2,1)} %all-gather.6.cloned.1.call-done.w_ref.rest_10_), custom_call_target="tpu_custom_call" | custom-call | flops 13421772800 | bytes 25165824 | tf_op jit(solution)/shard_map/swiglu_part/pallas_call | solution.py:307
  270.9 20.6 %swiglu_part.5 = (bf16[1024,640]{1,0:T(8,128)(2,1)}, bf16[1024,1280]{1,0:T(8,128)(2,1)}, f32[1024,2048]{1,0:T(8,128)}) custom-call(bf16[1024,2048]{1,0:T(8,128)(2,1)} %bitcast.144, bf16[1024,2048]{1,0:T(8,128)(2,1)} %bitcast.126, bf16[2048,1920]{1,0:T(8,128)(2,1)} %all-gather.6.cloned.1.call-done.w_ref.rest_10_), custom_call_target="tpu_custom_call" | custom-call | flops 13421772800 | bytes 25165824 | tf_op jit(solution)/shard_map/swiglu_part/pallas_call | solution.py:307
  291.5 24.4 %swiglu_grads.1 = bf16[2048,1920]{1,0:T(8,128)(2,1)} custom-call(bf16[1024,2048]{1,0:T(8,128)(2,1)} %bitcast.141, bf16[1024,2048]{1,0:T(8,128)(2,1)} %bitcast.145, bf16[1024,2048]{1,0:T(8,128)(2,1)} %bitcast.123, bf16[1024,2048]{1,0:T(8,128)(2,1)} %bitcast.127, bf16[1024,1280]{1,0:T(8,128)(2,1)} %get-tuple-element.128.dgua, ...), custom_call_target="tpu_custom_call" | custom-call | flops 16106127360 | bytes 33554432 | tf_op jit(solution)/shard_map/swiglu_grads/pallas_call | solution.py:331
  316.7 15.9 %swiglu_part.6 = (bf16[1024,384]{1,0:T(8,128)(2,1)}, bf16[1024,768]{1,0:T(8,128)(2,1)}, bf16[1024,2048]{1,0:T(8,128)(2,1)}) custom-call(bf16[1024,2048]{1,0:T(8,128)(2,1)} %bitcast.146, bf16[1024,2048]{1,0:T(8,128)(2,1)} %bitcast.128, bf16[2048,1152]{1,0:T(8,128)(2,1)} %all-gather.8.cloned.1.call-done.w_ref.rest_11_, f32[1024,2048]{1,0:T(8,128)} %get-tuple-element.134.rest_0_), custom_call_target="tpu_custom_call" | custom-call | flops 8053063680 | bytes 25165824 | tf_op jit(solution)/shard_map/swiglu_part/pallas_call | solution.py:307
  332.6 15.3 %swiglu_part.7 = (bf16[1024,384]{1,0:T(8,128)(2,1)}, bf16[1024,768]{1,0:T(8,128)(2,1)}, bf16[1024,2048]{1,0:T(8,128)(2,1)}) custom-call(bf16[1024,2048]{1,0:T(8,128)(2,1)} %bitcast.142, bf16[1024,2048]{1,0:T(8,128)(2,1)} %bitcast.124, bf16[2048,1152]{1,0:T(8,128)(2,1)} %all-gather.8.cloned.1.call-done.w_ref.rest_11_, f32[1024,2048]{1,0:T(8,128)} %get-tuple-element.137.rest_0_), custom_call_target="tpu_custom_call" | custom-call | flops 8053063680 | bytes 25165824 | tf_op jit(solution)/shard_map/swiglu_part/pallas_call | solution.py:307
  348.0 84.3 %back_stage.1 = (bf16[2,2,256,2048]{3,2,1,0:T(8,128)(2,1)}, bf16[2,2,256,2048]{3,2,1,0:T(8,128)(2,1)}, f32[256,2048]{1,0:T(8,128)}, f32[1,2048]{1,0:T(1,128)}, b...) custom-call(bf16[4,256,2048]{2,1,0:T(8,128)(2,1)} %bitcast.149, ...), custom_call_target="tpu_custom_call" | custom-call | tf_op jit(solution)/shard_map/back_stage/pallas_call | solution.py:956
  435.0 3.6 convolution_convert_fusion.4
  438.7 1.3 convolution_convert_fusion.5
  441.3 70.4 %attend_back.1 = (bf16[2048,256]{1,0:T(8,128)(2,1)}, bf16[2048,128]{1,0:T(8,128)(2,1)}, bf16[1024,2048]{1,0:T(8,128)(2,1)}) custom-call(bf16[4,2048,64]{2,1,0:T(8,128)(2,1)} %get-tuple-element.116.q_ref, bf16[2048,64]{1,0:T(8,128)(2,1)} %get-tuple-element.117.k_ref, bf16[2048,64]{1,0:T(8,128)(2,1)} %get-tuple-element.118.v_ref, ...), custom_call_target="tpu_custom_call" | custom-call | flops 21474836480 | bytes 8388608 | tf_op jit(solution)/shard_map/attend_back/pallas_call | solution.py:230
  511.8 1.3 constant_dynamic-update-slice_fusion.1
  514.4 13.8 %attn_grads.1 = bf16[2048,640]{1,0:T(8,128)(2,1)} custom-call(bf16[2048,2048]{1,0:T(8,128)(2,1)} %get-tuple-element.150.na, bf16[2048,384]{1,0:T(8,128)(2,1)} %copy-done.2, bf16[1024,2048]{1,0:T(8,128)(2,1)} %bitcast.150, bf16[1024,2048]{1,0:T(8,128)(2,1)} %bitcast.153, bf16[1024,256]{1,0:T(8,128)(2,1)} %bitcast.161, bf16[1024,256]{1,0:T(8,128)(2,1)} %bitcast.162), custom_call_target="tpu_custom_call" | custom-call | flops 5368709120 | bytes 33554432 | tf_op jit(solution)/shard_map/attn_grads/pallas_call | solution.py:367
  528.2 1.6 copy-done.9
  529.9 1.7 collective-permute-start.6
  533.2 4.4 convolution_convert_fusion.1.even
  537.6 4.4 convolution_convert_fusion.odd
  542.0 11.8 %collective-permute-done.6.refs_1_ = bf16[256,1920]{1,0:T(8,128)(2,1)S(1)} collective-permute-done((bf16[256,1920]{1,0:T(8,128)(2,1)S(1)}, bf16[256,1920]{1,0:T(8,128)(2,1)S(1)}, u32[]{:S(2)}, u32[]{:S(2)}) %collective-permute-start.6) | collective-permute-done | bytes 983072 | tf_op jit(solution)/shard_map/ppermute | solution.py:1057
  553.8 79.3 %end_stage.1 = (bf16[1024,2048]{1,0:T(8,128)(2,1)}, f32[2,2048]{1,0:T(2,128)}, bf16[256,1152]{1,0:T(8,128)(2,1)}) custom-call(bf16[4,256,2048]{2,1,0:T(8,128)(2,1)} %convolution_convert_fusion.1.even, bf16[4,256,2048]{2,1,0:T(8,128)(2,1)} %convolution_convert_fusion.odd, bf16[256,2048]{1,0:T(8,128)(2,1)} %constant_dynamic-slice_fusion.4.tok_ref, ...), custom_call_target="tpu_custom_call" | custom-call | tf_op jit(solution)/shard_map/end_stage/pallas_call | solution.py:988
  636.6 6.7 convert_element_type.90
  643.2 1.3 fusion.8
  645.8 15.1 %finish.1 = (bf16[256,512]{1,0:T(8,128)(2,1)}, bf16[256,128]{1,0:T(8,128)(2,1)}, bf16[256,128]{1,0:T(8,128)(2,1)}, bf16[512,256]{1,0:T(8,128)(2,1)}, bf16[256,20...) custom-call(bf16[512,640]{1,0:T(8,128)(2,1)} %reduce-scatter.6.cloned.1.call-done.piec, ...), custom_call_target="tpu_custom_call" | custom-call | tf_op jit(solution)/shard_map/finish/pallas_call | solution.py:504
  662.1 1.4 fusion.15
  663.5 13.2 %update.1 = (f32[1,256]{1,0:T(1,128)}, f32[1,256]{1,0:T(1,128)}, f32[256,512]{1,0:T(8,128)}, f32[256,512]{1,0:T(8,128)}, f32[256,128]{1,0:T(8,128)}, /*index=5*/...) custom-call(f32[8,128]{1,0:T(8,128)} %get-tuple-element.173.norm_ref, ...), custom_call_target="tpu_custom_call" | custom-call | tf_op jit(solution)/shard_map/update/pallas_call | solution.py:1028
  676.7 4.8 copy.73
  (162 shorter events, 33.5 us)
Async XLA Ops:
  7.2 82.4 %all-gather.4.cloned.1.call-start = ((), (), s32[]{:S(2)}) async-start(), calls=%async_computation.3 | async-start | bytes 3481600 | tf_op jit(solution)/shard_map/all_gather | solution.py:1060
  13.0 13.4 %copy-start.5 = (f32[2048,256]{1,0:T(8,128)S(1)}, f32[2048,256]{1,0:T(8,128)}, u32[]{:S(2)}) copy-start(f32[2048,256]{1,0:T(8,128)} %refs_24_.1) | copy-start | bytes 6291460
  13.8 11.3 %collective-permute-start = (bf16[272,640]{1,0:T(8,128)(2,1)}, bf16[272,640]{1,0:T(8,128)(2,1)S(1)}, u32[]{:S(2)}, u32[]{:S(2)}) collective-permute-start(bf16[272,640]{1,0:T(8,128)(2,1)} %pad_maximum_fusion.15), channel_id=1, source_target_pairs={{0,4},{1,5},{2,6},{3,7},{4,0},{5,1},{6,2},{7,3},{8,12},{9,13},{10,... | collective-permute-start | bytes 1044488 | tf_op jit(solution)/shard_map/ppermute | solution.py:1057
  26.3 224.1 %all-gather.6.cloned.1.call-start = ((), (), s32[]{:S(2)}) async-start(), calls=%async_computation.4 | async-start | bytes 9830400 | tf_op jit(solution)/shard_map/all_gather | solution.py:1060
  26.9 2.2 copy-start.6
  29.4 2.2 copy-start.1
  31.6 51.2 %copy-start.34 = (s32[1,1024]{1,0:T(1,128)S(1)}, s32[1,1024]{1,0:T(1,128)}, u32[]{:S(2)}) copy-start(s32[1,1024]{1,0:T(1,128)} %param.24) | copy-start | bytes 12292
  79.3 3.4 copy-start
  82.7 233.9 %all-gather.8.cloned.1.call-start = ((), (), s32[]{:S(2)}) async-start(), calls=%async_computation.5 | async-start | bytes 5898240 | tf_op jit(solution)/shard_map/all_gather | solution.py:1060
  82.8 18.5 %collective-permute-start.2 = (s32[1,1024]{1,0:T(1,128)S(1)}, s32[1,1024]{1,0:T(1,128)S(1)}, u32[]{:S(2)}, u32[]{:S(2)}) collective-permute-start(s32[1,1024]{1,0:T(1,128)S(1)} %copy-done.34), channel_id=1, source_target_pairs={{0,4},{1,5},{2,6},{3,7},{4,0},{5,1},{6,2},{7,3},{8,12},{9,13},{10,... | collective-permute-start | bytes 12296 | tf_op jit(solution)/shard_map/ppermute | solution.py:1057
  89.5 153.5 %copy-start.4 = (bf16[256,2048]{1,0:T(8,128)(2,1)}, bf16[256,2048]{1,0:T(8,128)(2,1)S(1)}, u32[]{:S(2)}) copy-start(bf16[256,2048]{1,0:T(8,128)(2,1)S(1)} %get-tuple-element.115.cot_ref) | copy-start | bytes 3145732
  89.6 33.5 %collective-permute-start.1 = (bf16[256,2048]{1,0:T(8,128)(2,1)S(1)}, bf16[256,2048]{1,0:T(8,128)(2,1)S(1)}, u32[]{:S(2)}, u32[]{:S(2)}) collective-permute-start(bf16[256,2048]{1,0:T(8,128)(2,1)S(1)} %get-tuple-element.115.cot_ref), channel_id=1, source_target_pairs={{0,4},{1,5},{2,6},{3,7},{4,0},{5,1},{6,2},{7,3},{8,12},{9,13},{10,... | collective-permute-start | bytes 3145736 | tf_op jit(solution)/shard_map/ppermute | solution.py:1057
  97.1 2.9 copy-start.7
  123.0 24.5 %copy-start.14 = (bf16[256,2048]{1,0:T(8,128)(2,1)}, bf16[256,2048]{1,0:T(8,128)(2,1)S(1)}, u32[]{:S(2)}) copy-start(bf16[256,2048]{1,0:T(8,128)(2,1)S(1)} %collective-permute-done.1) | copy-start | bytes 3145732
  123.0 20.5 %collective-permute-start.3 = (bf16[256,1152]{1,0:T(8,128)(2,1)}, bf16[256,1152]{1,0:T(8,128)(2,1)}, u32[]{:S(2)}, u32[]{:S(2)}) collective-permute-start(bf16[256,1152]{1,0:T(8,128)(2,1)} %pad_maximum_fusion.9), channel_id=1, source_target_pairs={{0,4},{1,5},{2,6},{3,7},{4,0},{5,1},{6,2},{7,3},{8,12},{9,13},{10,... | collective-permute-start | bytes 1769480 | tf_op jit(solution)/shard_map/ppermute | solution.py:1057
  123.2 23.7 %collective-permute-start.4 = (bf16[256,2048]{1,0:T(8,128)(2,1)S(1)}, bf16[256,2048]{1,0:T(8,128)(2,1)S(1)}, u32[]{:S(2)}, u32[]{:S(2)}) collective-permute-start(bf16[256,2048]{1,0:T(8,128)(2,1)S(1)} %collective-permute-done.1), channel_id=1, source_target_pairs={{0,2},{1,3},{2,0},{3,1},{4,6},{5,7},{6,4},{7,5},{8,10},{9,11},{10,... | collective-permute-start | bytes 3145736 | tf_op jit(solution)/shard_map/ppermute | solution.py:1057
  125.0 18.5 %copy-start.28 = (bf16[256,384]{1,0:T(8,128)(2,1)S(1)}, bf16[256,384]{1,0:T(8,128)(2,1)}, u32[]{:S(2)}) copy-start(bf16[256,384]{1,0:T(8,128)(2,1)} %get-tuple-element.213) | copy-start | bytes 589828
  125.0 18.5 %copy-start.29 = (bf16[256,384]{1,0:T(8,128)(2,1)S(1)}, bf16[256,384]{1,0:T(8,128)(2,1)}, u32[]{:S(2)}) copy-start(bf16[256,384]{1,0:T(8,128)(2,1)} %get-tuple-element.211) | copy-start | bytes 589828
  125.0 18.5 %copy-start.30 = (bf16[256,384]{1,0:T(8,128)(2,1)S(1)}, bf16[256,384]{1,0:T(8,128)(2,1)}, u32[]{:S(2)}) copy-start(bf16[256,384]{1,0:T(8,128)(2,1)} %get-tuple-element.273) | copy-start | bytes 589828
  146.9 2.1 copy-start.15
  146.9 364.8 %reduce-scatter.4.cloned.1.call-start = ((), (), s32[]{:S(2)}) async-start(), calls=%async_computation.6 | async-start | bytes 9830400 | tf_op jit(solution)/shard_map/reduce_scatter | solution.py:1063
  149.0 97.8 %collective-permute-start.5 = (bf16[2,256,2048]{2,1,0:T(8,128)(2,1)}, bf16[2,256,2048]{2,1,0:T(8,128)(2,1)}, u32[]{:S(2)}, u32[]{:S(2)}) collective-permute-start(bf16[2,256,2048]{2,1,0:T(8,128)(2,1)} %pad_maximum_fusion.2), channel_id=1, source_target_pairs={{0,1},{1,0},{2,3},{3,2},{4,5},{5,4},{6,7},{7,6},{8,9},{9,8},{10,11... | collective-permute-start | bytes 6291464 | tf_op jit(solution)/shard_map/ppermute | solution.py:1057
  149.0 4.4 copy-start.26
  153.5 3.4 copy-start.16
  153.6 3.4 copy-start.22
  153.6 3.4 copy-start.24
  153.6 3.3 copy-start.18
  153.6 3.3 copy-start.20
  160.3 82.8 %copy-start.13 = (bf16[1,256,2048]{2,1,0:T(8,128)(2,1)S(1)}, bf16[1,256,2048]{2,1,0:T(8,128)(2,1)}, u32[]{:S(2)}) copy-start(bf16[1,256,2048]{2,1,0:T(8,128)(2,1)} %get-tuple-element.200) | copy-start | bytes 3145732
  243.1 3.8 copy-start.11
  243.1 3.8 copy-start.12
  315.9 237.9 %reduce-scatter.8.cloned.1.call-start = ((), (), s32[]{:S(2)}) async-start(), calls=%async_computation.8 | async-start | bytes 5898240 | tf_op jit(solution)/shard_map/reduce_scatter | solution.py:1063
  432.2 1.0 copy-start.23
  432.2 1.0 copy-start.25
  432.3 1.9 copy-start.19
  432.3 1.9 copy-start.21
  432.3 200.9 %reduce-scatter.6.cloned.1.call-start = ((), (), s32[]{:S(2)}) async-start(), calls=%async_computation.7 | async-start | bytes 3276800 | tf_op jit(solution)/shard_map/reduce_scatter | solution.py:1063
  435.0 3.6 copy-start.10
  440.3 1.0 copy-start.33
  511.7 1.4 copy-start.31
  513.2 1.1 copy-start.2
  528.2 1.6 copy-start.9
  528.2 3.4 copy-start.3
  529.9 24.0 %collective-permute-start.6 = (bf16[256,1920]{1,0:T(8,128)(2,1)S(1)}, bf16[256,1920]{1,0:T(8,128)(2,1)S(1)}, u32[]{:S(2)}, u32[]{:S(2)}) collective-permute-start(bf16[256,1920]{1,0:T(8,128)(2,1)S(1)} %constant_dynamic-slice_fusion.3), channel_id=1, source_target_pairs={{0,4},{1,5},{2,6},{3,7},{4,0},{5,1},{6,2},{7,3},{8,12},{9,13},{10,... | collective-permute-start | bytes 2949128 | tf_op jit(solution)/shard_map/ppermute | solution.py:1057
  531.8 1.4 copy-start.8
  553.8 79.3 %copy-start.27 = (bf16[256,1920]{1,0:T(8,128)(2,1)}, bf16[256,1920]{1,0:T(8,128)(2,1)S(1)}, u32[]{:S(2)}) copy-start(bf16[256,1920]{1,0:T(8,128)(2,1)S(1)} %collective-permute-done.6.refs_1_) | copy-start | bytes 2949124
  634.2 9.1 %collective-permute-start.7 = (bf16[256,640]{1,0:T(8,128)(2,1)S(1)}, bf16[256,640]{1,0:T(8,128)(2,1)S(1)}, u32[]{:S(2)}, u32[]{:S(2)}) collective-permute-start(bf16[256,640]{1,0:T(8,128)(2,1)S(1)} %constant_dynamic-slice_fusion.2), channel_id=1, source_target_pairs={{0,4},{1,5},{2,6},{3,7},{4,0},{5,1},{6,2},{7,3},{8,12},{9,13},{10,... | collective-permute-start | bytes 983048 | tf_op jit(solution)/shard_map/ppermute | solution.py:1057
  643.2 2.5 copy-start.32
  (1 other events, 0.9 us)
Sparse Core Ops, SparseCore 0:
  26.4 59.0 all-gather.3
  87.0 139.7 all-gather.5
  229.0 87.6 all-gather.7
  318.8 134.6 reduce-scatter.3
  455.7 85.7 reduce-scatter.7
  543.7 52.6 reduce-scatter.5

commit v6 on v5

--- a/solution.py
+++ b/solution.py
@@ -2,6 +2,7 @@
 
 import jax
 import jax.numpy as jnp
+import numpy as np
 from jax import lax
 from jax.experimental import pallas as pl
 from jax.experimental.pallas import tpu as pltpu
@@ -31,24 +32,45 @@
     lane = lax.broadcasted_iota(jnp.int32, v.shape, 1)
     return jnp.where(lane % HD < HD // 2, pltpu.roll(v, n - HD // 2, 1), pltpu.roll(v, HD // 2, 1))
 
-def qkv_body(tok_ref, gain_ref, w_ref, cos_ref, sin_ref, normed_ref, q_ref, k_ref, v_ref):
+def qkv_body(
+    tok_ref, gain_ref, w_ref, cos_ref, sin_ref, cot_ref, normed_ref, q_ref, k_ref, v_ref, near, sems
+):
+    rows = near.shape[0]
+    at = pl.multiple_of(lax.axis_index("shard") * rows, rows)
+    target = neighbours()[0]
+    moving = remote(cot_ref.at[pl.ds(at, rows)], near, sems, 0, target)
+
+    @pl.when(pl.program_id(0) == 0)
+    def _():
+        meet((target,))
+        moving.start()
+
     x = tok_ref[...].astype(F32)
     inv = lax.rsqrt(jnp.mean(x * x, axis=1, keepdims=True) + EPS)
     normed = (x * inv * gain_ref[...]).astype(BF)
     normed_ref[...] = normed
-    lin = dot(normed, w_ref[...], 1, 0)
     heads = q_ref.shape[0]
     qc = heads * HD
+    groups, cols = w_ref.shape[0], qc + 2 * HD
+    deep = normed.shape[1] // groups
+    lin = sum(
+        dot(normed[:, g * deep : (g + 1) * deep], w_ref[g, :deep, :cols], 1, 0)
+        for g in range(groups)
+    )
     rot = lin * cos_ref[...] + swap_halves(lin) * sin_ref[...]
     for h in range(heads):
         q_ref[h] = (rot[:, h * HD : (h + 1) * HD]).astype(BF)
     k_ref[...] = rot[:, qc : qc + HD].astype(BF)
     v_ref[...] = rot[:, qc + HD :].astype(BF)
 
-def qkv(tokens, gain, weight, cos, sin, heads, tile=256):
+    @pl.when(pl.program_id(0) == pl.num_programs(0) - 1)
+    def _():
+        moving.wait()
+
+
+def qkv(tokens, gain, weight, cos, sin, cotangent, heads, tile=256):
     count, width = tokens.shape
-    cols = weight.shape[1]
-    length = cos.shape[0]
+    length, cols = cos.shape
     per = length // tile
     full = lambda i: (0, 0)
     row = lambda i: (i, 0)
@@ -58,30 +80,66 @@
         in_specs=[
             pl.BlockSpec((tile, width), row),
             pl.BlockSpec((1, width), full),
-            pl.BlockSpec((width, cols), full),
+            pl.BlockSpec(weight.shape, lambda i: (0, 0, 0)),
             pl.BlockSpec((tile, cols), lambda i: (i % per, 0)),
             pl.BlockSpec((tile, cols), lambda i: (i % per, 0)),
+            ANY,
         ],
         out_specs=[
             pl.BlockSpec((tile, width), row),
             pl.BlockSpec((heads, tile, HD), lambda i: (0, i, 0)),
             pl.BlockSpec((tile, HD), row),
             pl.BlockSpec((tile, HD), row),
+            ANY,
         ],
         out_shape=[
             jax.ShapeDtypeStruct((count, width), BF),
             jax.ShapeDtypeStruct((heads, count, HD), BF),
             jax.ShapeDtypeStruct((count, HD), BF),
             jax.ShapeDtypeStruct((count, HD), BF),
-        ],
-        compiler_params=pltpu.CompilerParams(vmem_limit_bytes=VMEM),
+            jax.ShapeDtypeStruct((cotangent.shape[0] // 4, width), BF),
+        ],
+        scratch_shapes=[pltpu.SemaphoreType.DMA((2, 1))],
+        compiler_params=pltpu.CompilerParams(
+            collective_id=10, has_side_effects=True, vmem_limit_bytes=VMEM
+        ),
         cost_estimate=pl.CostEstimate(flops=2 * count * width * cols, bytes_accessed=4 * count * width, transcendentals=0),
         name="qkv_rope",
-    )(tokens, gain, weight, cos, sin)
-
-def fwd_body(limits, q_ref, k_ref, v_ref, brow_ref, bcol_ref, o_ref, lse_ref):
+    )(tokens, gain, weight, cos, sin, cotangent)
+
+def fwd_body(
+    limits,
+    q_ref,
+    k_ref,
+    v_ref,
+    brow_ref,
+    bcol_ref,
+    near,
+    sent,
+    o_ref,
+    lse_ref,
+    far,
+    near_core,
+    far_core,
+    theirs,
+    sems
+):
     heads, tile, _ = q_ref.shape
     i = pl.program_id(1)
+    turn = pl.program_id(0) * pl.num_programs(1) + i
+    targets = neighbours()
+    over_y = remote(near, far, sems, 0, targets[1])
+    over_core = remote(near, near_core, sems, 1, targets[2])
+    last = remote(far, far_core, sems, 2, targets[2])
+    over_x = remote(sent, theirs, sems, 3, targets[0])
+
+    @pl.when(turn == 0)
+    def _():
+        meet(targets)
+        over_y.start()
+        over_x.start()
+        over_core.start()
+
     def run(keys):
         k = k_ref[:keys]
         v = v_ref[:keys]
@@ -104,7 +162,17 @@
         def _(keys=keys):
             run(keys)
 
-def attend(q, k, v, brow, bcol, length, tile=256, most=256):
+    @pl.when(turn == pl.num_programs(0) * pl.num_programs(1) - 1)
+    def _():
+        over_y.wait_recv()
+        last.start()
+        over_x.wait()
+        over_core.wait()
+        over_y.wait_send()
+        last.wait()
+
+
+def attend(q, k, v, brow, bcol, near, sent, length, tile=256, most=256):
     heads, count, _ = q.shape
     seqs = count // length
     per = length // tile
@@ -118,19 +186,30 @@
             pl.BlockSpec((length, HD), lambda b, i: (b, 0)),
             pl.BlockSpec((1, 1, length), lambda b, i: (b, 0, 0)),
             pl.BlockSpec((tile, 1), lambda b, i: (b * per + i, 0)),
+            ANY,
+            ANY,
         ],
         out_specs=[
             pl.BlockSpec((tile, heads * HD), lambda b, i: (b * per + i, 0)),
             pl.BlockSpec((tile, heads), lambda b, i: (b * per + i, 0)),
+            ANY,
+            ANY,
+            ANY,
+            ANY,
         ],
         out_shape=[
             jax.ShapeDtypeStruct((count, heads * HD), BF),
             jax.ShapeDtypeStruct((count, heads), F32),
-        ],
-        compiler_params=pltpu.CompilerParams(vmem_limit_bytes=VMEM),
+            *[jax.ShapeDtypeStruct(near.shape, BF)] * 3,
+            jax.ShapeDtypeStruct(sent.shape, BF),
+        ],
+        scratch_shapes=[pltpu.SemaphoreType.DMA((2, 4))],
+        compiler_params=pltpu.CompilerParams(
+            collective_id=11, has_side_effects=True, vmem_limit_bytes=VMEM
+        ),
         cost_estimate=pl.CostEstimate(flops=4 * heads * count * length * HD * 4, bytes_accessed=count * 2048, transcendentals=heads * count * length),
         name="attend",
-    )(q, k, v, brow, bcol)
+    )(q, k, v, brow, bcol, near, sent)
 
 def bwd_body(
     limits,
@@ -266,13 +345,15 @@
     )(q, k, v, brow, bcol, lse, do, cos, sin, cos, sin, even, odd, hidden)
 
 def rope_tables(length, heads):
-    positions = jnp.arange(length, dtype=jnp.int32).astype(F32)
-    powers = -2.0 * jnp.arange(HD // 2, dtype=F32) / HD
-    angles = positions[:, None] * jnp.power(THETA, powers)[None, :]
-    c = jnp.cos(angles); s = jnp.sin(angles)
-    cos = jnp.concatenate([jnp.tile(jnp.concatenate([c, c], axis=1), (1, heads + 1)), jnp.ones((length, HD), F32)], axis=1)
-    sin = jnp.concatenate([jnp.tile(jnp.concatenate([-s, s], axis=1), (1, heads + 1)), jnp.zeros((length, HD), F32)], axis=1)
-    return cos, sin
+    positions = np.arange(length, dtype=np.float32)
+    powers = np.float32(-2.0) * np.arange(HD // 2, dtype=np.float32) / np.float32(HD)
+    angles = positions[:, None] * np.power(np.float32(THETA), powers)[None, :]
+    c, s = np.cos(angles), np.sin(angles)
+    zeros = np.zeros((length, HD), np.float32)
+    cos = [c, c] * (heads + 1) + [zeros + 1]
+    sin = [-s, s] * (heads + 1) + [zeros]
+    return (jnp.asarray(np.concatenate(v, axis=1).astype(np.float32)) for v in (cos, sin))
+
 
 def up_body(first, last, n2_ref, cot_ref, w_ref, *rest):
     if first:
@@ -346,17 +427,36 @@
     )(*n2, *cot, *dgu, *act)
 
 
-def attn_grad_body(na, ga, ha, hb, ma, mb, o_ref):
+def attn_grad_body(
+    na, ga, ha, hb, ma, mb, qa, qb, w_ref, piece, o_ref, even, odd, theirs, sems
+):
     cols = ga.shape[1]
+    step = pl.program_id(0)
+    swapped = trade(piece, theirs, sems)
+
+    @pl.when(step == 0)
+    def _():
+        meet(neighbours()[:1])
+        swapped.start()
+
     o_ref[:, :cols] = dot(na[...], ga[...], 0, 0).astype(BF)
     o_ref[:, cols:] = (dot(ha[...], ma[...], 0, 0) + dot(hb[...], mb[...], 0, 0)).astype(BF)
-
-
-def attn_grads(normed, grads, hidden, mixed, tile=256):
+    even[...] = dot(qa[...], w_ref[0], 1, 1).astype(BF)
+    odd[...] = dot(qb[...], w_ref[0], 1, 1).astype(BF)
+
+    @pl.when(step == pl.num_programs(0) - 1)
+    def _():
+        swapped.wait()
+
+
+def attn_grads(normed, grads, hidden, mixed, halves, packed, piece, tile=256):
     width = normed.shape[1]
+    count, cols = halves[0].shape
     col = lambda i: (0, i)
-    ins = [normed, grads, *hidden, *mixed]
-    cols = grads.shape[1] + mixed[0].shape[1]
+    tile = min(tile, width // packed.shape[0])
+    per = width // packed.shape[0] // tile
+    ins = [normed, grads, *hidden, *mixed, *halves, packed, piece]
+    wide = cols + mixed[0].shape[1]
 
     def tiled(value):
         return pl.BlockSpec((value.shape[0], tile), col)
@@ -369,14 +469,23 @@
         grid=(width // tile,),
         in_specs=[tiled(normed), whole(grads)]
         + [tiled(v) for v in hidden]
-        + [whole(v) for v in mixed],
-        out_specs=pl.BlockSpec((tile, cols), lambda i: (i, 0)),
-        out_shape=jax.ShapeDtypeStruct((width, cols), BF),
-        compiler_params=pltpu.CompilerParams(vmem_limit_bytes=VMEM),
-        cost_estimate=pl.CostEstimate(
-            flops=2 * normed.shape[0] * width * cols,
-            bytes_accessed=8 * normed.shape[0] * width,
-            transcendentals=0,
+        + [whole(v) for v in (*mixed, *halves)]
+        + [pl.BlockSpec((1, tile, cols), lambda i: (i // per, i % per, 0)), ANY],
+        out_specs=[
+            pl.BlockSpec((tile, wide), lambda i: (i, 0)),
+            pl.BlockSpec((count, tile), col),
+            pl.BlockSpec((count, tile), col),
+            ANY,
+        ],
+        out_shape=[
+            jax.ShapeDtypeStruct((width, wide), BF),
+            jax.ShapeDtypeStruct((count, width), BF),
+            jax.ShapeDtypeStruct((count, width), BF),
+            jax.ShapeDtypeStruct((piece.shape[0] // 2, piece.shape[1]), BF),
+        ],
+        scratch_shapes=[pltpu.SemaphoreType.DMA((2, 1))],
+        compiler_params=pltpu.CompilerParams(
+            collective_id=9, has_side_effects=True, vmem_limit_bytes=VMEM
         ),
         name="attn_grads",
     )(*ins)
@@ -397,11 +506,15 @@
     return near, far, lax.rem(dp, 2) * shards + sh, dp // 2
 
 
-def meet(targets):
+def greet(targets):
     barrier = pltpu.get_barrier_semaphore()
     for target in targets:
         pl.semaphore_signal(barrier, inc=1, device_id=target, device_id_type=MESH)
-    pl.semaphore_wait(barrier, len(targets))
+
+
+def meet(targets):
+    greet(targets)
+    pl.semaphore_wait(pltpu.get_barrier_semaphore(), len(targets))
 
 
 def exchange(values, slots, mine, targets, source, send, recv, base):
@@ -452,16 +565,23 @@
     return low, high
 
 
-def finish_body(dps, shards, count, piece_ref, theirs, sq_ref, *refs):
-    ins, outs, scratch = refs[: 2 * count], refs[2 * count : 2 * count + 8], refs[2 * count + 8 :]
-    q_ref, k_ref, v_ref, o_ref, g_ref, u_ref, d_ref, norm_ref = outs
-    bufs = scratch
+def finish_body(dps, shards, count, piece_ref, gain_ref, *refs):
+    ins, outs, scratch = refs[: 2 * count], refs[2 * count : 2 * count + 10], refs[2 * count + 10 :]
+    q_ref, k_ref, v_ref, o_ref, g_ref, u_ref, d_ref, norm_ref, first_ref, second_ref = outs
+    theirs, pair, *bufs = scratch
     near, far, me, outer = peers(dps, shards)
     rows = piece_ref.shape[0] // 2
     qc = q_ref.shape[1] // 2
     x = lax.rem(lax.axis_index("dp"), 2)
     here = pl.ds(pl.multiple_of(x * rows, rows), rows)
-    squares = jnp.zeros((1, 1), F32)
+    meet(near + far)
+    swapped = trade(piece_ref, theirs, pair)
+    swapped.start()
+    gains = gain_ref[lax.axis_index("dp")]
+    first_ref[...] = gains[0:1]
+    second_ref[...] = gains[1:2]
+    once = jnp.where(lax.axis_index("shard") == 0, 1.0, 0.0)
+    squares = once * jnp.sum(gains * gains, keepdims=True)
     half = g_ref.shape[1] // 2
     at = 0
     for j in range(count):
@@ -477,11 +597,11 @@
     mine = piece_ref[here, :]
     wide = mine.astype(F32)
     squares = squares + jnp.sum(wide * wide, keepdims=True)
+    swapped.wait()
     got = theirs[...]
     wide = got.astype(F32)
     squares = squares + jnp.sum(wide * wide, keepdims=True)
-    values = sq_ref[...] + jnp.broadcast_to(squares, sq_ref.shape)
-    meet(near + far)
+    values = jnp.broadcast_to(squares, norm_ref.shape)
     norm_ref[...] = jnp.sqrt(two_stages(values, near, far, me, outer, bufs))
     low, high = pick(x, mine, got)
     q_ref[:, :qc] = low[:, :qc]
@@ -493,7 +613,7 @@
     o_ref[qc:] = high[:, oc:].astype(F32).T.astype(BF)
 
 
-def finish(piece, theirs, squares, pairs, dps, shards, number):
+def finish(piece, gains, pairs, dps, shards, number):
     rows, cols = piece.shape[0] // 2, piece.shape[1]
     qc = (cols - 2 * HD) // 2
     wide = 2 * sum(other.shape[1] // 3 for _, other in pairs)
@@ -503,16 +623,17 @@
     shapes = shapes + ((rows, wide), (rows, wide), (wide, rows))
     return pl.pallas_call(
         functools.partial(finish_body, dps, shards, len(pairs)),
-        in_specs=[vmem] * (3 + len(ins)),
-        out_specs=[vmem] * 8,
+        in_specs=[vmem] * (2 + len(ins)),
+        out_specs=[vmem] * 10,
         out_shape=[jax.ShapeDtypeStruct(shape, BF) for shape in shapes]
-        + [jax.ShapeDtypeStruct(squares.shape, F32)],
-        scratch_shapes=sum_scratch(squares.shape, dps, shards),
+        + [jax.ShapeDtypeStruct(v, F32) for v in ((8, 128), (1, rows), (1, rows))],
+        scratch_shapes=[pltpu.VMEM((rows, cols), BF), pltpu.SemaphoreType.DMA((2, 1))]
+        + sum_scratch((8, 128), dps, shards),
         compiler_params=pltpu.CompilerParams(
             collective_id=number, has_side_effects=True, vmem_limit_bytes=VMEM
         ),
         name="finish",
-    )(piece, theirs, squares, *ins)
+    )(piece, gains, *ins)
 
 
 PARTS = 8
@@ -850,6 +971,63 @@
     swapped.wait()
 
 
+def open_body(q_ref, k_ref, v_ref, o_ref, gain_ref, piece, sent, sems):
+    rows = q_ref.shape[0]
+    qc = q_ref.shape[1] // 2
+    x = lax.rem(lax.axis_index("dp"), 2)
+    target = neighbours()[0]
+    barrier = pltpu.get_barrier_semaphore()
+    pl.semaphore_signal(barrier, inc=1, device_id=target, device_id_type=MESH)
+
+    def fill(ref, base, which):
+        at = pl.ds(pl.multiple_of(base, 16), rows)
+
+        def narrow(value):
+            return jnp.where(which == 0, value[:, :HD], value[:, HD:]).astype(BF)
+
+        ref[at, :qc] = q_ref[:, pl.ds(pl.multiple_of(which * qc, qc), qc)].astype(BF)
+        ref[at, qc : qc + HD] = narrow(k_ref[...])
+        ref[at, qc + HD : qc + 2 * HD] = narrow(v_ref[...])
+        out = o_ref[pl.ds(pl.multiple_of(which * qc, qc), qc), :]
+        ref[at, qc + 2 * HD :] = out.T.astype(BF)
+
+    fill(sent, 0, 1 - x)
+    sent[rows:] = gain_ref[...]
+    pl.semaphore_wait(barrier, 1)
+    spots = (
+        piece.at[pl.ds(pl.multiple_of(x * rows, 16), rows)],
+        piece.at[pl.ds(pl.multiple_of(2 * rows + x * 16, 16), 16)],
+    )
+    copies = [
+        remote(sent.at[pl.ds(0, rows)], spots[0], sems, 0, target),
+        remote(sent.at[pl.ds(rows, 16)], spots[1], sems, 1, target),
+    ]
+    for copy in copies:
+        copy.start()
+    fill(piece, x * rows, x)
+    piece[pl.ds(pl.multiple_of(2 * rows + x * 16, 16), 16)] = gain_ref[...]
+    for copy in copies:
+        copy.wait()
+
+
+def opening(w_query, w_key, w_value, w_output, gains):
+    rows, cols = w_query.shape[0], gains.shape[1]
+    return pl.pallas_call(
+        open_body,
+        in_specs=[IN_VMEM] * 5,
+        out_specs=IN_VMEM,
+        out_shape=jax.ShapeDtypeStruct((2 * rows + 32, cols), BF),
+        scratch_shapes=[
+            pltpu.VMEM((rows + 16, cols), BF),
+            pltpu.SemaphoreType.DMA((2, 2)),
+        ],
+        compiler_params=pltpu.CompilerParams(
+            collective_id=8, has_side_effects=True, vmem_limit_bytes=16 << 20
+        ),
+        name="opening",
+    )(w_query, w_key, w_value, w_output, gains)
+
+
 def entry_body(tok_ref, keep_ref, send_ref, both, piece, hop_x, hop_y, hop_core, weight_sem, keeps):
     xs, ys, core = neighbours()
     sh = lax.axis_index("shard")
@@ -1004,7 +1182,10 @@
     )(even, odd, tokens_own, grad_hidden, gain, gain_grad, piece)
 
 
-def update_body(count, norm_ref, rate_ref, *refs):
+def update_body(count, norm_ref, rate_ref, out_ref, in_ref, *refs):
+    refs, (new_out, new_in) = refs[:-2], refs[-2:]
+    new_out[...] = out_ref[...]
+    new_in[...] = in_ref[...].astype(F32)
     factor = jnp.minimum(1.0, CLIP / norm_ref[0:1, 0:1])
     rate = rate_ref[0]
     for n in range(count):
@@ -1015,7 +1196,7 @@
         new_master[...] = master[...] - rate * momentum
 
 
-def update(norm, rate, masters, moments, grads, steps=8):
+def update(norm, rate, output, input_grad, masters, moments, grads, steps=8):
     count = len(masters)
 
     def block(value):
@@ -1031,14 +1212,21 @@
         in_specs=[
             pl.BlockSpec(norm.shape, lambda i: (0, 0)),
             pl.BlockSpec(memory_space=pltpu.SMEM),
+            block(output),
+            block(input_grad),
         ]
         + [block(v) for v in ins],
-        out_specs=[block(v) for v in outs],
-        out_shape=[jax.ShapeDtypeStruct(v.shape, F32) for v in outs],
+        out_specs=[block(v) for v in (*outs, output, input_grad)],
+        out_shape=[jax.ShapeDtypeStruct(v.shape, F32) for v in outs]
+        + [
+            jax.ShapeDtypeStruct(output.shape, BF),
+            jax.ShapeDtypeStruct(input_grad.shape, F32),
+        ],
         compiler_params=pltpu.CompilerParams(vmem_limit_bytes=VMEM),
         name="update",
-    )(norm, rate.reshape(1), *ins)
-    return values[0::2], values[1::2]
+    )(norm, rate.reshape(1), output, input_grad, *ins)
+    *values, output, input_grad = values
+    return values[0::2], values[1::2], output, input_grad
 
 
 def after(*values):
@@ -1135,22 +1323,11 @@
         def flat(values):
             return values.reshape(-1, values.shape[-1])
 
-        low_q = w_query.astype(BF)
-        low_k = w_key.astype(BF)
-        low_v = w_value.astype(BF)
-        low_o = w_output.astype(BF).T
         qc = group * HD
         cols = qc + 2 * HD
-
-        def attn_half(which):
-            return jnp.concatenate([half(low, which) for low in (low_q, low_k, low_v, low_o)], axis=1)
-
         gains = jnp.stack([gain_first, gain_second]).astype(BF)
         gains = jnp.pad(gains, ((0, 14), (0, cols + qc - rows)))
-        sent = swap(jnp.concatenate([attn_half(1 - x), gains], axis=0), 1, 0)
-        piece = jnp.concatenate(
-            [ordered(attn_half(x), sent[:rows]), ordered(gains, sent[rows:])], axis=0
-        )
+        piece = opening(w_query, w_key, w_value, w_output, gains)
         groups = dps // 2
 
         blocks_x = swap(block_ids, 1, 0)
@@ -1171,14 +1348,11 @@
             )
 
         both, first_part = entry(
-            after(tokens, piece)[0], ffn_part(x, 0), ffn_part(1 - x, 0)
+            after(tokens, piece[:16, :128])[0], ffn_part(x, 0), ffn_part(1 - x, 0)
         )
         ffn_weights = [gather(first_part)]
-        cot_own = [cut(cotangent, ds) for ds in range(shards)]
-        packed, both, send_cot = after(gather(piece), both, cot_own[0])
-        cot_x = swap(send_cot, 1, 0)
+        packed = gather(piece)
         packed = packed.reshape(groups, 2 * rows + 32, cols + qc)
-        qkv_weight = packed[:, : 2 * rows, :cols].reshape(width, cols)
         out_weight = packed[:, : 2 * rows, cols:].reshape(width, qc)
         tails = packed[:, 2 * rows :].reshape(groups, 2, 16, cols + qc)
         gain_one = tails[:, :, 0, :rows].reshape(1, width).astype(F32)
@@ -1186,20 +1360,20 @@
 
         cosine, sine = rope_tables(length, group)
 
-        normed, query, key, value = qkv(both, gain_one, qkv_weight, cosine, sine, group)
-        query, cot_x, send_second = after(query, cot_x, ffn_part(1 - x, 1))
-        second_part = ordered(ffn_part(x, 1), swap(send_second, 1, 0))
-        cot_xy = swap(cot_x, 0, 2)
+        normed, query, key, value, cot_near = qkv(
+            both, gain_one, packed, cosine, sine, cotangent, group
+        )
         blocks = jnp.concatenate([block_ids, blocks_x], axis=0)
         block_rows = blocks[:, None, :]
         block_cols = blocks.reshape(2 * length, 1)
-        mixed, lse = attend(query, key, value, block_rows, block_cols, length)
-        mixed, second_part, cot_xy = after(mixed, second_part, cot_xy)
-        cot_x = jnp.stack([cot_x, cot_xy])
-        cot_core = swap(cot_x, 0, 1)
-        cot_mine = flat(jnp.concatenate([jnp.stack([cot_own[0], cot_own[2]]), cot_x], axis=0))
-        cot_theirs = flat(jnp.concatenate([jnp.stack([cot_own[1], cot_own[3]]), cot_core], axis=0))
-        ffn_weights.append(gather(second_part))
+        mixed, lse, cot_far, core_near, core_far, second_x = attend(
+            query, key, value, block_rows, block_cols, cot_near, ffn_part(1 - x, 1), length
+        )
+        ffn_weights.append(gather(ordered(ffn_part(x, 1), second_x)))
+        late, _ = after(cotangent, mixed[:16, :128])
+        cot_own = [cut(late, ds) for ds in range(shards)]
+        cot_mine = jnp.concatenate([cot_own[0], cot_own[2], cot_near, cot_far], axis=0)
+        cot_theirs = jnp.concatenate([cot_own[1], cot_own[3], core_near, core_far], axis=0)
         mixed_own, mixed_other = mixed[:length], mixed[length:]
         mixed_mine, mixed_theirs = halves(mixed_own, mixed_other)
 
@@ -1276,26 +1450,21 @@
             out_theirs.reshape(shape),
             hidden,
         )
-        grad_q, first_piece = after(grad_q, first_piece)
-        first_theirs = swap(
-            lax.dynamic_slice_in_dim(first_piece, (1 - x) * rows, rows, axis=0), 1, 0
-        )
         grad_qkv = jnp.concatenate([grad_q, grad_kv], axis=1)
-        d_attn = attn_grads(
+        gq_mine, gq_theirs = halves(grad_qkv[:length], grad_qkv[length:])
+        d_attn, even_in, odd_in, first_theirs = attn_grads(
             normed,
             grad_qkv,
             (flat(gh_mine), flat(gh_theirs)),
             (flat(mixed_mine), flat(mixed_theirs)),
+            (flat(gq_mine), flat(gq_theirs)),
+            packed,
+            first_piece,
         )
         grad_attn = scatter(d_attn)
-        gq_mine, gq_theirs = halves(grad_qkv[:length], grad_qkv[length:])
-        gq_mine, gq_theirs, d_attn = after(gq_mine, gq_theirs, d_attn)
-        even_in, odd_in, first_theirs = after(
-            project(gq_mine, qkv_weight), project(gq_theirs, qkv_weight), first_theirs
-        )
         input_grad, gain_grads, last_theirs = end_stage(
-            even_in,
-            odd_in,
+            even_in.reshape(shape),
+            odd_in.reshape(shape),
             tokens_own,
             grad_hidden,
             gain_one,
@@ -1304,23 +1473,13 @@
             dps,
             shards,
         )
-        grad_attn, input_grad, gain_grads = after(grad_attn, input_grad, gain_grads)
-        attn_theirs = swap(
-            lax.dynamic_slice_in_dim(grad_attn, (1 - x) * rows, rows, axis=0), 1, 0
-        )
-        input_grad, gain_grads, attn_theirs = after(
-            input_grad.astype(F32), gain_grads, attn_theirs
-        )
-
         pairs = [(first_piece, first_theirs), (last_piece, last_theirs)]
-        gain_grads = lax.dynamic_slice_in_dim(gain_grads, dp * rows, rows, axis=1)
-        first_shard = (me == 0).astype(F32)
-        squares = jnp.broadcast_to(first_shard * jnp.sum(gain_grads * gain_grads), (8, 128))
-        own_q, own_k, own_v, own_o, own_g, own_u, own_d, norm = finish(
-            grad_attn, attn_theirs, squares, pairs, dps, shards, 2
+        gain_rows = gain_grads.reshape(2, dps, rows).transpose(1, 0, 2)
+        own_q, own_k, own_v, own_o, own_g, own_u, own_d, norm, own_first, own_second = finish(
+            grad_attn, gain_rows, pairs, dps, shards, 2
         )
         global_norm = norm[0, 0]
-        owned = (gain_grads[0], own_q, own_k, own_v, own_o, gain_grads[1], own_g, own_u, own_d)
+        owned = (own_first, own_q, own_k, own_v, own_o, own_second, own_g, own_u, own_d)
         rate_now = rate * jnp.minimum(1.0, (step.astype(F32) + 1.0) / WARMUP)
         masters = (gain_first, w_query, w_key, w_value, w_output, gain_second, w_gate, w_up, w_down)
         moments = (
@@ -1338,9 +1497,9 @@
             [v.reshape(1, -1) if v.ndim == 1 else v for v in values]
             for values in (masters, moments, owned)
         ]
+        *parts, output, input_grad = update(norm, rate_now, output, input_grad, *lists)
         momenta, updated = (
-            [v.reshape(-1) if v.shape[0] == 1 else v for v in values]
-            for values in update(norm, rate_now, *lists)
+            [v.reshape(-1) if v.shape[0] == 1 else v for v in values] for values in parts
         )
         return (output, input_grad, global_norm, *momenta, *updated)
 

time: 694 us -> 684 us (0.986)
  Pallas kernels: 537 us -> 599 us
  local copies, waits for them, and re-layouts: 49.7 us -> 26.6 us
  waiting for transfers between devices: 22 us -> 2.22 us
  other arithmetic: 31.8 us -> 17.5 us
  starting transfers between devices: 10.6 us -> 1.31 us
  matrix products: 20.2 us -> 11.4 us
    ppermute x8 -> x1, waiting for transfers between devices: 21.2 us -> 2.05 us  [swap(): return lax.ppermute(values, axes, pairs)]
    pallas_call x1, Pallas kernels: 13.8 us -> 28.4 us  [attn_grads(): pl.pallas_call(attn_grad_body, grid=(width // tile,), in_specs=[tiled(nor...]
    pallas_call x1, Pallas kernels: 18.5 us -> 31.4 us  [attend(): pl.pallas_call(functools.partial(fwd_body, limits), grid=(seqs, per), in_...]
    pallas_call x0 -> x1, Pallas kernels: none -> 12.2 us  [opening(): pl.pallas_call(open_body, in_specs=[IN_VMEM] * 5, out_specs=IN_VMEM, out_...]
    pallas_call x1, Pallas kernels: 15.3 us -> 26.6 us  [qkv(): pl.pallas_call(qkv_body, grid=(count // tile,), in_specs=[pl.BlockSpec((t...]
    convert_element_type x5 -> x0, other arithmetic: 9.56 us -> none  [the longest x1 6.66 us: on_device(): input_grad.astype(F32)]
    ppermute x8 -> x1, starting transfers between devices: 9.79 us -> 0.59 us  [swap(): return lax.ppermute(values, axes, pairs)]
    dot_general x6 -> x4, matrix products: 20.2 us -> 11.4 us  [project(): jnp.einsum('atk,dk->atd', values, weight, preferred_element_type=F32)]
  transfers between devices with their start and end apart: 14 -> 7, of which waited for: 4 -> 1; matrix products, arithmetic and copies ran while one was open for 11% -> 6% of each run, Pallas kernels for 74% -> 81%
where the time goes in v6:
time: 684 us; the launch traced here: 675 us
  Pallas kernels  599 us (88%)
  local copies, waits for them, and re-layouts  26.6 us (4%)
  other arithmetic  17.5 us (3%)
  between operations  16.3 us (2%)
  matrix products  11.4 us (2%)
    pallas_call x1, Pallas kernels, back_stage(): pl.pallas_call(back_body, in_specs=[IN_VMEM, ANY, IN_VMEM, IN_VMEM, IN_VM...  83.6 us
    pallas_call x1, Pallas kernels, mid_stage(): pl.pallas_call(mid_body, in_specs=[IN_VMEM, ANY, IN_VMEM, IN_VMEM], out_s...  81.4 us
    pallas_call x1, Pallas kernels, end_stage(): pl.pallas_call(functools.partial(end_body, dps, shards), in_specs=[IN_VME...  78.8 us
    pallas_call x4, Pallas kernels, up_back(): pl.pallas_call(functools.partial(up_body, prev is None, last), grid=(coun...  72.3 us
    pallas_call x1, Pallas kernels, attend_back(): pl.pallas_call(functools.partial(bwd_body, limits), grid=(seqs, per), in_...  71.5 us
    pallas_call x1, Pallas kernels, entry(): pl.pallas_call(entry_body, in_specs=[ANY] * 3, out_specs=[ANY] * 2, out_s...  47.5 us
    pallas_call x1, Pallas kernels, attend(): pl.pallas_call(functools.partial(fwd_body, limits), grid=(seqs, per), in_...  31.4 us
    pallas_call x1, Pallas kernels, attn_grads(): pl.pallas_call(attn_grad_body, grid=(width // tile,), in_specs=[tiled(nor...  28.4 us
  transfers between devices with their start and end apart: 7, of which 1 were waited for; matrix products, arithmetic and copies ran while one was open for 6% of the time, Pallas kernels for 81%

profile of v6, /device:TPU:0, one launch (start us, length us, event | category | flops | bytes accessed | tf_op | source)
XLA Modules:
  0.0 674.8 jit_solution(2299421814306456779)
XLA Ops:
  7.2 0.7 convert.9
  8.6 1.0 copy-done.2
  9.7 1.0 copy-done.3
  10.7 0.9 copy-done.4
  11.6 0.9 copy-done.5
  12.5 12.2 %opening.1 = bf16[544,640]{1,0:T(8,128)(2,1)} custom-call(f32[256,512]{1,0:T(8,128)S(1)} %copy-done.2, f32[256,128]{1,0:T(8,128)S(1)} %copy-done.4, f32[256,128]{1,0:T(8,128)S(1)} %copy-done.5, f32[512,256]{1,0:T(8,128)S(1)} %copy-done.3, bf16[16,640]{1,0:T(8,128)(2,1)S(1)} %fusion.5.gain_ref), custom_call_target="tpu_custom_call" | custom-call | tf_op jit(solution)/shard_map/opening/pallas_call | solution.py:1015
  25.5 1.9 convert_element_type.38
  28.3 1.8 copy-done.1
  30.0 47.5 %entry.1 = (bf16[2048,2048]{1,0:T(8,128)(2,1)S(1)}, bf16[512,1920]{1,0:T(8,128)(2,1)}) custom-call(bf16[1024,2048]{1,0:T(8,128)(2,1)S(1)} %copy-done.1, bf16[256,1920]{1,0:T(8,128)(2,1)S(1)} %pad_maximum_fusion.3.keep_ref, bf16[256,1920]{1,0:T(8,128)(2,1)S(1)} %pad_maximum_fusion.4.send_ref), custom_call_target="tpu_custom_call" | custom-call | tf_op jit(solution)/shard_map/entry/pallas_call | solution.py:1081
  77.5 3.4 copy-done
  81.7 0.9 pad_maximum_fusion.7.sent
  82.6 2.1 collective-permute-done
  85.3 1.3 copy.54
  86.6 0.9 slice.70
  88.2 26.6 %qkv_rope.1 = (bf16[2048,2048]{1,0:T(8,128)(2,1)}, bf16[4,2048,64]{2,1,0:T(8,128)(2,1)}, bf16[2048,64]{1,0:T(8,128)(2,1)}, bf16[2048,64]{1,0:T(8,128)(2,1)}, bf16[256,2048]{1,0:T(8,128)(2,1)}) custom-call(bf16[2048,2048]{1,0:T(8,128)(2,1)} %copy-done, f32[1,2048]{1,0:T(1,128)} %reshape.176.gain_ref, bf16[4,544,640]{2,1,0:T(8,128)(2,1)} %bitcast.106, ...), custom_call_target="tpu_custom_call" | custom-call | flops 3221225472 | bytes 16777216 | tf_op jit(solution)/shard_map/qkv_rope/pallas_call | solution.py:77
  114.8 31.4 %attend.1 = (bf16[2048,256]{1,0:T(8,128)(2,1)}, f32[2048,4]{1,0:T(8,128)}, bf16[256,2048]{1,0:T(8,128)(2,1)}, bf16[256,2048]{1,0:T(8,128)(2,1)}, bf16[256,2048]{1,0:T(8,128)(2,1)}, /*index=5*/bf16[256,1152]{1,0:T(8,128)(2,1)}) custom-call(bf16[4,2048,64]{2,1,0:T(8,128)(2,1)} %get-tuple-element.102.q_ref, bf16[2048,64]{1,0:T(8,128)(2,1)} %get-tuple-element.103.k_ref, ...), custom_call_target="tpu_custom_call" | custom-call | flops 8589934592 | bytes 4194304 | tf_op jit(solution)/shard_map/attend/pallas_call | solution.py:180
  146.2 1.3 broadcast_select_fusion.1
  147.5 1.1 pad_maximum_fusion.2
  149.2 3.3 constant_dynamic-slice_fusion
  152.5 1.8 constant_dynamic-slice_fusion.4
  154.3 1.3 slice.72
  156.4 3.3 convolution_convert_fusion.1.even
  159.8 3.3 convolution_convert_fusion.odd
  163.1 81.4 %mid_stage.1 = (bf16[2,2,256,2048]{3,2,1,0:T(8,128)(2,1)}, bf16[2,2,256,2048]{3,2,1,0:T(8,128)(2,1)}, f32[256,2048]{1,0:T(8,128)}) custom-call(bf16[4,256,2048]{2,1,0:T(8,128)(2,1)} %convolution_convert_fusion.1.even, bf16[4,256,2048]{2,1,0:T(8,128)(2,1)} %convolution_convert_fusion.odd, bf16[256,2048]{1,0:T(8,128)(2,1)} %get-tuple-element.234.tok_ref, ...), custom_call_target="tpu_custom_call" | custom-call | tf_op jit(solution)/shard_map/mid_stage/pallas_call | solution.py:1111
  244.5 4.0 pad_maximum_fusion.cot_ref.cota.rest_2_
  248.5 2.2 pad_maximum_fusion.1.cot_ref.cotb.rest_3_
  250.8 20.6 %swiglu_part.4 = (bf16[1024,640]{1,0:T(8,128)(2,1)}, bf16[1024,1280]{1,0:T(8,128)(2,1)}, f32[1024,2048]{1,0:T(8,128)}) custom-call(bf16[1024,2048]{1,0:T(8,128)(2,1)} %bitcast.117, bf16[1024,2048]{1,0:T(8,128)(2,1)} %pad_maximum_fusion.cot_ref.cota.rest_2_, bf16[2048,1920]{1,0:T(8,128)(2,1)} %all-gather.6.cloned.1.call-done.w_ref.rest_10_), custom_call_target="tpu_custom_call" | custom-call | flops 13421772800 | bytes 25165824 | tf_op jit(solution)/shard_map/swiglu_part/pallas_call | solution.py:388
  271.4 20.6 %swiglu_part.5 = (bf16[1024,640]{1,0:T(8,128)(2,1)}, bf16[1024,1280]{1,0:T(8,128)(2,1)}, f32[1024,2048]{1,0:T(8,128)}) custom-call(bf16[1024,2048]{1,0:T(8,128)(2,1)} %bitcast.121, bf16[1024,2048]{1,0:T(8,128)(2,1)} %pad_maximum_fusion.1.cot_ref.cotb.rest_3_, bf16[2048,1920]{1,0:T(8,128)(2,1)} %all-gather.6.cloned.1.call-done.w_ref.rest_10_), custom_call_target="tpu_custom_call" | custom-call | flops 13421772800 | bytes 25165824 | tf_op jit(solution)/shard_map/swiglu_part/pallas_call | solution.py:388
  291.9 24.4 %swiglu_grads.1 = bf16[2048,1920]{1,0:T(8,128)(2,1)} custom-call(bf16[1024,2048]{1,0:T(8,128)(2,1)} %bitcast.118, bf16[1024,2048]{1,0:T(8,128)(2,1)} %bitcast.122, bf16[1024,2048]{1,0:T(8,128)(2,1)} %pad_maximum_fusion.cot_ref.cota.rest_2_, bf16[1024,2048]{1,0:T(8,128)(2,1)} %pad_maximum_fusion.1.cot_ref.cotb.rest_3_, ...), custom_call_target="tpu_custom_call" | custom-call | flops 16106127360 | bytes 33554432 | tf_op jit(solution)/shard_map/swiglu_grads/pallas_call | solution.py:412
  316.4 15.8 %swiglu_part.6 = (bf16[1024,384]{1,0:T(8,128)(2,1)}, bf16[1024,768]{1,0:T(8,128)(2,1)}, bf16[1024,2048]{1,0:T(8,128)(2,1)}) custom-call(bf16[1024,2048]{1,0:T(8,128)(2,1)} %bitcast.123, bf16[1024,2048]{1,0:T(8,128)(2,1)} %pad_maximum_fusion.1.cot_ref.cotb.rest_3_, bf16[2048,1152]{1,0:T(8,128)(2,1)} %all-gather.8.cloned.1.call-done.w_ref.rest_11_, ...), custom_call_target="tpu_custom_call" | custom-call | flops 8053063680 | bytes 25165824 | tf_op jit(solution)/shard_map/swiglu_part/pallas_call | solution.py:388
  332.2 15.3 %swiglu_part.7 = (bf16[1024,384]{1,0:T(8,128)(2,1)}, bf16[1024,768]{1,0:T(8,128)(2,1)}, bf16[1024,2048]{1,0:T(8,128)(2,1)}) custom-call(bf16[1024,2048]{1,0:T(8,128)(2,1)} %bitcast.119, bf16[1024,2048]{1,0:T(8,128)(2,1)} %pad_maximum_fusion.cot_ref.cota.rest_2_, bf16[2048,1152]{1,0:T(8,128)(2,1)} %all-gather.8.cloned.1.call-done.w_ref.rest_11_, ...), custom_call_target="tpu_custom_call" | custom-call | flops 8053063680 | bytes 25165824 | tf_op jit(solution)/shard_map/swiglu_part/pallas_call | solution.py:388
  347.5 83.6 %back_stage.1 = (bf16[2,2,256,2048]{3,2,1,0:T(8,128)(2,1)}, bf16[2,2,256,2048]{3,2,1,0:T(8,128)(2,1)}, f32[256,2048]{1,0:T(8,128)}, f32[1,2048]{1,0:T(1,128)}, b...) custom-call(bf16[4,256,2048]{2,1,0:T(8,128)(2,1)} %bitcast.126, ...), custom_call_target="tpu_custom_call" | custom-call | tf_op jit(solution)/shard_map/back_stage/pallas_call | solution.py:1134
  431.3 0.8 copy-done.12
  432.2 0.9 pad_maximum_fusion.9
  433.1 0.9 pad_maximum_fusion.10
  433.9 3.6 convolution_convert_fusion.2
  437.6 1.3 convolution_convert_fusion.3
  439.3 1.0 copy-done.24
  440.2 71.5 %attend_back.1 = (bf16[2048,256]{1,0:T(8,128)(2,1)}, bf16[2048,128]{1,0:T(8,128)(2,1)}, bf16[1024,2048]{1,0:T(8,128)(2,1)}) custom-call(bf16[4,2048,64]{2,1,0:T(8,128)(2,1)} %get-tuple-element.102.q_ref, bf16[2048,64]{1,0:T(8,128)(2,1)} %get-tuple-element.103.k_ref, bf16[2048,64]{1,0:T(8,128)(2,1)} %get-tuple-element.104.v_ref, ...), custom_call_target="tpu_custom_call" | custom-call | flops 21474836480 | bytes 8388608 | tf_op jit(solution)/shard_map/attend_back/pallas_call | solution.py:309
  511.7 1.3 constant_dynamic-update-slice_fusion.1
  513.0 1.2 constant_dynamic-update-slice_fusion.ga
  514.6 1.0 pad_maximum_fusion.5
  515.6 1.0 pad_maximum_fusion.6
  516.6 28.4 %attn_grads.1 = (bf16[2048,640]{1,0:T(8,128)(2,1)}, bf16[1024,2048]{1,0:T(8,128)(2,1)}, bf16[1024,2048]{1,0:T(8,128)(2,1)}, bf16[256,1920]{1,0:T(8,128)(2,1)}) custom-call(bf16[2048,2048]{1,0:T(8,128)(2,1)} %get-tuple-element.101.na, bf16[2048,384]{1,0:T(8,128)(2,1)} %copy-done.7, bf16[1024,2048]{1,0:T(8,128)(2,1)} %bitcast.113, ...), custom_call_target="tpu_custom_call" | custom-call | tf_op jit(solution)/shard_map/attn_grads/pallas_call | solution.py:467
  546.4 78.8 %end_stage.1 = (bf16[1024,2048]{1,0:T(8,128)(2,1)}, f32[2,2048]{1,0:T(2,128)}, bf16[256,1152]{1,0:T(8,128)(2,1)}) custom-call(bf16[4,256,2048]{2,1,0:T(8,128)(2,1)} %bitcast.127, bf16[4,256,2048]{2,1,0:T(8,128)(2,1)} %bitcast.128, bf16[256,2048]{1,0:T(8,128)(2,1)} %get-tuple-element.234.tok_ref, f32[256,2048]{1,0:T(8,128)} %get-tuple-element.141.gh_ref, ...), custom_call_target="tpu_custom_call" | custom-call | tf_op jit(solution)/shard_map/end_stage/pallas_call | solution.py:1166
  625.3 22.2 %finish.1 = (bf16[256,512]{1,0:T(8,128)(2,1)}, bf16[256,128]{1,0:T(8,128)(2,1)}, bf16[256,128]{1,0:T(8,128)(2,1)}, bf16[512,256]{1,0:T(8,128)(2,1)}, bf16[256,20...) custom-call(bf16[512,640]{1,0:T(8,128)(2,1)} %reduce-scatter.6.clone, ...), custom_call_target="tpu_custom_call" | custom-call | tf_op jit(solution)/shard_map/finish/pallas_call | solution.py:624
  647.5 1.2 slice.69
  648.6 19.0 %update.1 = (f32[1,256]{1,0:T(1,128)}, f32[1,256]{1,0:T(1,128)}, f32[256,512]{1,0:T(8,128)}, f32[256,512]{1,0:T(8,128)}, f32[256,128]{1,0:T(8,128)}, /*index=5*/...) custom-call(f32[8,128]{1,0:T(8,128)} %get-tuple-element.147.norm_ref, ...), custom_call_target="tpu_custom_call" | custom-call | tf_op jit(solution)/shard_map/update/pallas_call | solution.py:1209
  (98 shorter events, 6.8 us)
Async XLA Ops:
  7.2 79.5 %all-gather.4.cloned.1.call-start = ((), (), s32[]{:S(2)}) async-start(), calls=%async_computation.3 | async-start | bytes 3481600 | tf_op jit(solution)/shard_map/all_gather | solution.py:1248
  8.6 1.0 copy-start.2
  9.7 1.0 copy-start.3
  10.7 0.9 copy-start.4
  11.6 0.9 copy-start.5
  12.5 12.3 %copy-start.8 = (f32[2048,256]{1,0:T(8,128)S(1)}, f32[2048,256]{1,0:T(8,128)}, u32[]{:S(2)}) copy-start(f32[2048,256]{1,0:T(8,128)} %refs_24_.1) | copy-start | bytes 6291460
  24.8 226.0 %all-gather.6.cloned.1.call-start = ((), (), s32[]{:S(2)}) async-start(), calls=%async_computation.4 | async-start | bytes 9830400 | tf_op jit(solution)/shard_map/all_gather | solution.py:1248
  25.5 2.2 copy-start.9
  27.8 2.2 copy-start.1
  30.0 51.0 %copy-start.25 = (s32[1,1024]{1,0:T(1,128)S(1)}, s32[1,1024]{1,0:T(1,128)}, u32[]{:S(2)}) copy-start(s32[1,1024]{1,0:T(1,128)} %param.26) | copy-start | bytes 12292
  77.5 3.4 copy-start
  80.9 235.5 %all-gather.8.cloned.1.call-start = ((), (), s32[]{:S(2)}) async-start(), calls=%async_computation.5 | async-start | bytes 5898240 | tf_op jit(solution)/shard_map/all_gather | solution.py:1248
  81.0 3.7 collective-permute-start
  148.6 368.0 %reduce-scatter.4.cloned.1.call-start = ((), (), s32[]{:S(2)}) async-start(), calls=%async_computation.6 | async-start | bytes 9830400 | tf_op jit(solution)/shard_map/reduce_scatter | solution.py:1251
  149.2 3.3 copy-start.6
  152.5 3.7 copy-start.21
  156.3 6.7 copy-start.11
  156.4 6.7 copy-start.13
  156.4 6.7 copy-start.15
  156.4 6.6 copy-start.17
  156.4 6.6 copy-start.19
  244.5 4.0 copy-start.22
  244.5 4.0 copy-start.23
  316.3 230.0 %reduce-scatter.8.cloned.1.call-start = ((), (), s32[]{:S(2)}) async-start(), calls=%async_computation.8 | async-start | bytes 5898240 | tf_op jit(solution)/shard_map/reduce_scatter | solution.py:1251
  431.1 0.9 copy-start.12
  431.1 1.0 copy-start.18
  431.1 1.0 copy-start.20
  431.2 1.9 copy-start.14
  431.2 1.9 copy-start.16
  431.2 194.1 %reduce-scatter.6.cloned.1.call-start = ((), (), s32[]{:S(2)}) async-start(), calls=%async_computation.7 | async-start | bytes 3276800 | tf_op jit(solution)/shard_map/reduce_scatter | solution.py:1251
  433.9 3.6 copy-start.10
  439.2 1.0 copy-start.24
  514.2 2.4 copy-start.7
Sparse Core Ops, SparseCore 0:
  24.9 58.7 all-gather.3
  85.3 139.7 all-gather.5
  227.3 87.6 all-gather.7
  317.1 135.6 reduce-scatter.3
  454.9 85.7 reduce-scatter.7
  545.2 52.2 reduce-scatter.5

commit v7 on v6

--- a/solution.py
+++ b/solution.py
@@ -817,7 +817,7 @@
     job.sent()
 
 
-def line_turn(job, t, whole, produce, window=4, lag=2):
+def line_turn(job, t, whole, produce, window=3, lag=1):
     if t == 0:
         job.start()
         for s in range(window):
@@ -962,8 +962,8 @@
         return gh_ref[span] + through
 
     for t in range(TURNS):
-        line_turn(job, t, in_ref, produce)
-        if t == 4:
+        line_turn(job, t, in_ref, produce, lag=2)
+        if t == 6:
             swapped.start()
     gains = jnp.concatenate([sum(totals[1:], totals[0]), gg_ref[...]], axis=0)
     sum_ref[...] = two_stages(gains, near, far, me, outer, scratch[9:])

time: 684 us -> 677 us (0.990)
  Pallas kernels: 599 us -> 592 us
where the time goes in v7:
time: 677 us; the launch traced here: 668 us
  Pallas kernels  592 us (87%)
  local copies, waits for them, and re-layouts  26.6 us (4%)
  other arithmetic  17.5 us (3%)
  between operations  16.3 us (2%)
  matrix products  11.4 us (2%)
    pallas_call x1, Pallas kernels, back_stage(): pl.pallas_call(back_body, in_specs=[IN_VMEM, ANY, IN_VMEM, IN_VMEM, IN_VM...  83.6 us
    pallas_call x1, Pallas kernels, mid_stage(): pl.pallas_call(mid_body, in_specs=[IN_VMEM, ANY, IN_VMEM, IN_VMEM], out_s...  81.4 us
    pallas_call x1, Pallas kernels, end_stage(): pl.pallas_call(functools.partial(end_body, dps, shards), in_specs=[IN_VME...  74.6 us
    pallas_call x4, Pallas kernels, up_back(): pl.pallas_call(functools.partial(up_body, prev is None, last), grid=(coun...  72.3 us
    pallas_call x1, Pallas kernels, attend_back(): pl.pallas_call(functools.partial(bwd_body, limits), grid=(seqs, per), in_...  68.7 us
    pallas_call x1, Pallas kernels, entry(): pl.pallas_call(entry_body, in_specs=[ANY] * 3, out_specs=[ANY] * 2, out_s...  47.5 us
    pallas_call x1, Pallas kernels, attend(): pl.pallas_call(functools.partial(fwd_body, limits), grid=(seqs, per), in_...  31.4 us
    pallas_call x1, Pallas kernels, attn_grads(): pl.pallas_call(attn_grad_body, grid=(width // tile,), in_specs=[tiled(nor...  28.4 us
  transfers between devices with their start and end apart: 7, of which 1 were waited for; matrix products, arithmetic and copies ran while one was open for 6% of the time, Pallas kernels for 81%

profile of v7, /device:TPU:0, one launch (start us, length us, event | category | flops | bytes accessed | tf_op | source)
XLA Modules:
  0.0 667.7 jit_solution(10287794645959518169)
XLA Ops:
  7.2 0.7 convert.9
  8.6 1.0 copy-done.2
  9.7 1.0 copy-done.3
  10.7 0.9 copy-done.4
  11.6 0.9 copy-done.5
  12.5 12.2 %opening.1 = bf16[544,640]{1,0:T(8,128)(2,1)} custom-call(f32[256,512]{1,0:T(8,128)S(1)} %copy-done.2, f32[256,128]{1,0:T(8,128)S(1)} %copy-done.4, f32[256,128]{1,0:T(8,128)S(1)} %copy-done.5, f32[512,256]{1,0:T(8,128)S(1)} %copy-done.3, bf16[16,640]{1,0:T(8,128)(2,1)S(1)} %fusion.5.gain_ref), custom_call_target="tpu_custom_call" | custom-call | tf_op jit(solution)/shard_map/opening/pallas_call | solution.py:1015
  25.5 1.9 convert_element_type.38
  28.3 1.8 copy-done.1
  30.0 47.5 %entry.1 = (bf16[2048,2048]{1,0:T(8,128)(2,1)S(1)}, bf16[512,1920]{1,0:T(8,128)(2,1)}) custom-call(bf16[1024,2048]{1,0:T(8,128)(2,1)S(1)} %copy-done.1, bf16[256,1920]{1,0:T(8,128)(2,1)S(1)} %pad_maximum_fusion.3.keep_ref, bf16[256,1920]{1,0:T(8,128)(2,1)S(1)} %pad_maximum_fusion.4.send_ref), custom_call_target="tpu_custom_call" | custom-call | tf_op jit(solution)/shard_map/entry/pallas_call | solution.py:1081
  77.5 3.4 copy-done
  81.7 0.9 pad_maximum_fusion.7.sent
  82.6 2.1 collective-permute-done
  85.3 1.3 copy.54
  86.6 0.9 slice.70
  88.2 26.6 %qkv_rope.1 = (bf16[2048,2048]{1,0:T(8,128)(2,1)}, bf16[4,2048,64]{2,1,0:T(8,128)(2,1)}, bf16[2048,64]{1,0:T(8,128)(2,1)}, bf16[2048,64]{1,0:T(8,128)(2,1)}, bf16[256,2048]{1,0:T(8,128)(2,1)}) custom-call(bf16[2048,2048]{1,0:T(8,128)(2,1)} %copy-done, f32[1,2048]{1,0:T(1,128)} %reshape.176.gain_ref, bf16[4,544,640]{2,1,0:T(8,128)(2,1)} %bitcast.106, ...), custom_call_target="tpu_custom_call" | custom-call | flops 3221225472 | bytes 16777216 | tf_op jit(solution)/shard_map/qkv_rope/pallas_call | solution.py:77
  114.8 31.4 %attend.1 = (bf16[2048,256]{1,0:T(8,128)(2,1)}, f32[2048,4]{1,0:T(8,128)}, bf16[256,2048]{1,0:T(8,128)(2,1)}, bf16[256,2048]{1,0:T(8,128)(2,1)}, bf16[256,2048]{1,0:T(8,128)(2,1)}, /*index=5*/bf16[256,1152]{1,0:T(8,128)(2,1)}) custom-call(bf16[4,2048,64]{2,1,0:T(8,128)(2,1)} %get-tuple-element.102.q_ref, bf16[2048,64]{1,0:T(8,128)(2,1)} %get-tuple-element.103.k_ref, ...), custom_call_target="tpu_custom_call" | custom-call | flops 8589934592 | bytes 4194304 | tf_op jit(solution)/shard_map/attend/pallas_call | solution.py:180
  146.2 1.3 broadcast_select_fusion.1
  147.5 1.1 pad_maximum_fusion.2
  149.2 3.3 constant_dynamic-slice_fusion
  152.5 1.8 constant_dynamic-slice_fusion.4
  154.3 1.3 slice.72
  156.4 3.3 convolution_convert_fusion.1.even
  159.8 3.3 convolution_convert_fusion.odd
  163.1 81.4 %mid_stage.1 = (bf16[2,2,256,2048]{3,2,1,0:T(8,128)(2,1)}, bf16[2,2,256,2048]{3,2,1,0:T(8,128)(2,1)}, f32[256,2048]{1,0:T(8,128)}) custom-call(bf16[4,256,2048]{2,1,0:T(8,128)(2,1)} %convolution_convert_fusion.1.even, bf16[4,256,2048]{2,1,0:T(8,128)(2,1)} %convolution_convert_fusion.odd, bf16[256,2048]{1,0:T(8,128)(2,1)} %get-tuple-element.234.tok_ref, ...), custom_call_target="tpu_custom_call" | custom-call | tf_op jit(solution)/shard_map/mid_stage/pallas_call | solution.py:1111
  244.5 4.0 pad_maximum_fusion.cot_ref.cota.rest_2_
  248.5 2.2 pad_maximum_fusion.1.cot_ref.cotb.rest_3_
  250.8 20.6 %swiglu_part.4 = (bf16[1024,640]{1,0:T(8,128)(2,1)}, bf16[1024,1280]{1,0:T(8,128)(2,1)}, f32[1024,2048]{1,0:T(8,128)}) custom-call(bf16[1024,2048]{1,0:T(8,128)(2,1)} %bitcast.117, bf16[1024,2048]{1,0:T(8,128)(2,1)} %pad_maximum_fusion.cot_ref.cota.rest_2_, bf16[2048,1920]{1,0:T(8,128)(2,1)} %all-gather.6.cloned.1.call-done.w_ref.rest_10_), custom_call_target="tpu_custom_call" | custom-call | flops 13421772800 | bytes 25165824 | tf_op jit(solution)/shard_map/swiglu_part/pallas_call | solution.py:388
  271.4 20.6 %swiglu_part.5 = (bf16[1024,640]{1,0:T(8,128)(2,1)}, bf16[1024,1280]{1,0:T(8,128)(2,1)}, f32[1024,2048]{1,0:T(8,128)}) custom-call(bf16[1024,2048]{1,0:T(8,128)(2,1)} %bitcast.121, bf16[1024,2048]{1,0:T(8,128)(2,1)} %pad_maximum_fusion.1.cot_ref.cotb.rest_3_, bf16[2048,1920]{1,0:T(8,128)(2,1)} %all-gather.6.cloned.1.call-done.w_ref.rest_10_), custom_call_target="tpu_custom_call" | custom-call | flops 13421772800 | bytes 25165824 | tf_op jit(solution)/shard_map/swiglu_part/pallas_call | solution.py:388
  291.9 24.4 %swiglu_grads.1 = bf16[2048,1920]{1,0:T(8,128)(2,1)} custom-call(bf16[1024,2048]{1,0:T(8,128)(2,1)} %bitcast.118, bf16[1024,2048]{1,0:T(8,128)(2,1)} %bitcast.122, bf16[1024,2048]{1,0:T(8,128)(2,1)} %pad_maximum_fusion.cot_ref.cota.rest_2_, bf16[1024,2048]{1,0:T(8,128)(2,1)} %pad_maximum_fusion.1.cot_ref.cotb.rest_3_, ...), custom_call_target="tpu_custom_call" | custom-call | flops 16106127360 | bytes 33554432 | tf_op jit(solution)/shard_map/swiglu_grads/pallas_call | solution.py:412
  316.4 15.8 %swiglu_part.6 = (bf16[1024,384]{1,0:T(8,128)(2,1)}, bf16[1024,768]{1,0:T(8,128)(2,1)}, bf16[1024,2048]{1,0:T(8,128)(2,1)}) custom-call(bf16[1024,2048]{1,0:T(8,128)(2,1)} %bitcast.123, bf16[1024,2048]{1,0:T(8,128)(2,1)} %pad_maximum_fusion.1.cot_ref.cotb.rest_3_, bf16[2048,1152]{1,0:T(8,128)(2,1)} %all-gather.8.cloned.1.call-done.w_ref.rest_11_, ...), custom_call_target="tpu_custom_call" | custom-call | flops 8053063680 | bytes 25165824 | tf_op jit(solution)/shard_map/swiglu_part/pallas_call | solution.py:388
  332.2 15.3 %swiglu_part.7 = (bf16[1024,384]{1,0:T(8,128)(2,1)}, bf16[1024,768]{1,0:T(8,128)(2,1)}, bf16[1024,2048]{1,0:T(8,128)(2,1)}) custom-call(bf16[1024,2048]{1,0:T(8,128)(2,1)} %bitcast.119, bf16[1024,2048]{1,0:T(8,128)(2,1)} %pad_maximum_fusion.cot_ref.cota.rest_2_, bf16[2048,1152]{1,0:T(8,128)(2,1)} %all-gather.8.cloned.1.call-done.w_ref.rest_11_, ...), custom_call_target="tpu_custom_call" | custom-call | flops 8053063680 | bytes 25165824 | tf_op jit(solution)/shard_map/swiglu_part/pallas_call | solution.py:388
  347.5 83.6 %back_stage.1 = (bf16[2,2,256,2048]{3,2,1,0:T(8,128)(2,1)}, bf16[2,2,256,2048]{3,2,1,0:T(8,128)(2,1)}, f32[256,2048]{1,0:T(8,128)}, f32[1,2048]{1,0:T(1,128)}, b...) custom-call(bf16[4,256,2048]{2,1,0:T(8,128)(2,1)} %bitcast.126, ...), custom_call_target="tpu_custom_call" | custom-call | tf_op jit(solution)/shard_map/back_stage/pallas_call | solution.py:1134
  431.3 0.8 copy-done.12
  432.2 0.9 pad_maximum_fusion.9
  433.1 0.9 pad_maximum_fusion.10
  433.9 3.6 convolution_convert_fusion.2
  437.6 1.3 convolution_convert_fusion.3
  439.3 1.0 copy-done.24
  440.2 68.7 %attend_back.1 = (bf16[2048,256]{1,0:T(8,128)(2,1)}, bf16[2048,128]{1,0:T(8,128)(2,1)}, bf16[1024,2048]{1,0:T(8,128)(2,1)}) custom-call(bf16[4,2048,64]{2,1,0:T(8,128)(2,1)} %get-tuple-element.102.q_ref, bf16[2048,64]{1,0:T(8,128)(2,1)} %get-tuple-element.103.k_ref, bf16[2048,64]{1,0:T(8,128)(2,1)} %get-tuple-element.104.v_ref, ...), custom_call_target="tpu_custom_call" | custom-call | flops 21474836480 | bytes 8388608 | tf_op jit(solution)/shard_map/attend_back/pallas_call | solution.py:309
  508.9 1.3 constant_dynamic-update-slice_fusion.1
  510.2 1.2 constant_dynamic-update-slice_fusion.ga
  511.8 1.0 pad_maximum_fusion.5
  512.8 1.0 pad_maximum_fusion.6
  513.8 28.4 %attn_grads.1 = (bf16[2048,640]{1,0:T(8,128)(2,1)}, bf16[1024,2048]{1,0:T(8,128)(2,1)}, bf16[1024,2048]{1,0:T(8,128)(2,1)}, bf16[256,1920]{1,0:T(8,128)(2,1)}) custom-call(bf16[2048,2048]{1,0:T(8,128)(2,1)} %get-tuple-element.101.na, bf16[2048,384]{1,0:T(8,128)(2,1)} %copy-done.7, bf16[1024,2048]{1,0:T(8,128)(2,1)} %bitcast.113, ...), custom_call_target="tpu_custom_call" | custom-call | tf_op jit(solution)/shard_map/attn_grads/pallas_call | solution.py:467
  543.6 74.6 %end_stage.1 = (bf16[1024,2048]{1,0:T(8,128)(2,1)}, f32[2,2048]{1,0:T(2,128)}, bf16[256,1152]{1,0:T(8,128)(2,1)}) custom-call(bf16[4,256,2048]{2,1,0:T(8,128)(2,1)} %bitcast.127, bf16[4,256,2048]{2,1,0:T(8,128)(2,1)} %bitcast.128, bf16[256,2048]{1,0:T(8,128)(2,1)} %get-tuple-element.234.tok_ref, f32[256,2048]{1,0:T(8,128)} %get-tuple-element.141.gh_ref, ...), custom_call_target="tpu_custom_call" | custom-call | tf_op jit(solution)/shard_map/end_stage/pallas_call | solution.py:1166
  618.2 22.2 %finish.1 = (bf16[256,512]{1,0:T(8,128)(2,1)}, bf16[256,128]{1,0:T(8,128)(2,1)}, bf16[256,128]{1,0:T(8,128)(2,1)}, bf16[512,256]{1,0:T(8,128)(2,1)}, bf16[256,20...) custom-call(bf16[512,640]{1,0:T(8,128)(2,1)} %reduce-scatter.6.clone, ...), custom_call_target="tpu_custom_call" | custom-call | tf_op jit(solution)/shard_map/finish/pallas_call | solution.py:624
  640.4 1.2 slice.69
  641.6 19.0 %update.1 = (f32[1,256]{1,0:T(1,128)}, f32[1,256]{1,0:T(1,128)}, f32[256,512]{1,0:T(8,128)}, f32[256,512]{1,0:T(8,128)}, f32[256,128]{1,0:T(8,128)}, /*index=5*/...) custom-call(f32[8,128]{1,0:T(8,128)} %get-tuple-element.147.norm_ref, ...), custom_call_target="tpu_custom_call" | custom-call | tf_op jit(solution)/shard_map/update/pallas_call | solution.py:1209
  (98 shorter events, 6.8 us)
Async XLA Ops:
  7.2 79.5 %all-gather.4.cloned.1.call-start = ((), (), s32[]{:S(2)}) async-start(), calls=%async_computation.3 | async-start | bytes 3481600 | tf_op jit(solution)/shard_map/all_gather | solution.py:1248
  8.6 1.0 copy-start.2
  9.7 1.0 copy-start.3
  10.7 0.9 copy-start.4
  11.6 0.9 copy-start.5
  12.5 12.3 %copy-start.8 = (f32[2048,256]{1,0:T(8,128)S(1)}, f32[2048,256]{1,0:T(8,128)}, u32[]{:S(2)}) copy-start(f32[2048,256]{1,0:T(8,128)} %refs_24_.1) | copy-start | bytes 6291460
  24.8 226.0 %all-gather.6.cloned.1.call-start = ((), (), s32[]{:S(2)}) async-start(), calls=%async_computation.4 | async-start | bytes 9830400 | tf_op jit(solution)/shard_map/all_gather | solution.py:1248
  25.5 2.2 copy-start.9
  27.8 2.2 copy-start.1
  30.0 51.0 %copy-start.25 = (s32[1,1024]{1,0:T(1,128)S(1)}, s32[1,1024]{1,0:T(1,128)}, u32[]{:S(2)}) copy-start(s32[1,1024]{1,0:T(1,128)} %param.26) | copy-start | bytes 12292
  77.5 3.4 copy-start
  80.9 235.5 %all-gather.8.cloned.1.call-start = ((), (), s32[]{:S(2)}) async-start(), calls=%async_computation.5 | async-start | bytes 5898240 | tf_op jit(solution)/shard_map/all_gather | solution.py:1248
  81.0 3.7 collective-permute-start
  148.6 365.2 %reduce-scatter.4.cloned.1.call-start = ((), (), s32[]{:S(2)}) async-start(), calls=%async_computation.6 | async-start | bytes 9830400 | tf_op jit(solution)/shard_map/reduce_scatter | solution.py:1251
  149.2 3.3 copy-start.6
  152.5 3.7 copy-start.21
  156.3 6.7 %copy-start.11 = (bf16[1,256,256]{2,1,0:T(8,128)(2,1)}, bf16[1,256,256]{2,1,0:T(8,128)(2,1)S(1)}, u32[]{:S(2)}) copy-start(bf16[1,256,256]{2,1,0:T(8,128)(2,1)S(1)} %get-tuple-element.224) | copy-start | bytes 393220
  156.4 6.7 copy-start.13
  156.4 6.7 copy-start.15
  156.4 6.6 copy-start.17
  156.4 6.6 copy-start.19
  244.5 4.0 copy-start.22
  244.5 4.0 copy-start.23
  316.3 227.2 %reduce-scatter.8.cloned.1.call-start = ((), (), s32[]{:S(2)}) async-start(), calls=%async_computation.8 | async-start | bytes 5898240 | tf_op jit(solution)/shard_map/reduce_scatter | solution.py:1251
  431.1 0.9 copy-start.12
  431.1 1.0 copy-start.18
  431.1 1.0 copy-start.20
  431.2 1.9 copy-start.14
  431.2 1.9 copy-start.16
  431.2 187.0 %reduce-scatter.6.cloned.1.call-start = ((), (), s32[]{:S(2)}) async-start(), calls=%async_computation.7 | async-start | bytes 3276800 | tf_op jit(solution)/shard_map/reduce_scatter | solution.py:1251
  433.9 3.6 copy-start.10
  439.2 1.0 copy-start.24
  511.4 2.4 copy-start.7
Sparse Core Ops, SparseCore 0:
  24.9 58.7 all-gather.3
  85.3 139.7 all-gather.5
  227.3 87.6 all-gather.7
  317.1 135.6 reduce-scatter.3
  454.9 85.7 reduce-scatter.7
  542.9 52.6 reduce-scatter.5
